TPU v7x, 32 devices: a whole 2x2x4 slice. The times are simulated.
32 devices in a mesh: slot: 2 (over core), ctx: 4 (over y, x), wsh: 4 (over z).
Axes of the slice: x: 2, y: 2, z: 4, core: 2. Of those that a mesh axis runs over, the one named last changes fastest.
Arguments:
- tokens: bfloat16 [2, 2048, 2048], P('slot', ('ctx', 'wsh')), may hold values from -6 to 6
- cotangent: bfloat16 [2, 2048, 2048], P('slot', ('ctx', 'wsh')), may hold values from -6 to 6
- lengths: int32 [2], P('slot'), may hold values from 512 to 2048, as said below
- positions: int32 [2, 2048], P('slot', ('ctx', 'wsh')), may hold values from 0 to 2047, as said below
- token_ids: int32 [2, 2048], P('slot', ('ctx', 'wsh')), may hold values from 0 to 131071
- per_layer_table: bfloat16 [131072, 256], P(('slot', 'ctx', 'wsh')), may hold values from -0.375 to 0.375
- w_query: bfloat16 [2048, 2048], P('wsh'), may hold values from -0.125 to 0.125
- w_key: bfloat16 [2048, 512], P('wsh'), may hold values from -0.125 to 0.125
- w_value: bfloat16 [2048, 512], P('wsh'), may hold values from -0.125 to 0.125
- w_output: bfloat16 [2048, 2048], P('wsh'), may hold values from -0.125 to 0.125
- laurel_left: bfloat16 [2048, 64], P('wsh'), may hold values from -0.125 to 0.125
- laurel_right: bfloat16 [2048, 64], P('wsh'), may hold values from -0.75 to 0.75
- w_gate: bfloat16 [2048, 8192], P('wsh'), may hold values from -0.125 to 0.125
- w_up: bfloat16 [2048, 8192], P('wsh'), may hold values from -0.125 to 0.125
- w_down: bfloat16 [8192, 2048], P('wsh'), may hold values from -0.0625 to 0.0625
- w_layer_gate: bfloat16 [2048, 256], P('wsh'), may hold values from -0.125 to 0.125
- w_layer_proj: bfloat16 [256, 2048], P('wsh'), may hold values from -0.375 to 0.375
- norm_gains: bfloat16 [2048, 6], P('wsh'), may hold values from 0.5 to 1.5
- query_gain: bfloat16 [256], P('wsh'), may hold values from 0.049804688 to 0.19921875
- key_gain: bfloat16 [256], P('wsh'), may hold values from 0.5 to 1.5
Outputs:
- layer_out: bfloat16 [2, 2048, 2048], P('slot', ('ctx', 'wsh'))
- tokens_grad: bfloat16 [2, 2048, 2048], P('slot', ('ctx', 'wsh'))
- table_grad: float32 [131072, 256], P(('slot', 'ctx', 'wsh'))
- query_grad: float32 [2048, 2048], P('wsh')
- key_grad: float32 [2048, 512], P('wsh')
- value_grad: float32 [2048, 512], P('wsh')
- output_grad: float32 [2048, 2048], P('wsh')
- left_grad: float32 [2048, 64], P('wsh')
- right_grad: float32 [2048, 64], P('wsh')
- gate_grad: float32 [2048, 8192], P('wsh')
- up_grad: float32 [2048, 8192], P('wsh')
- down_grad: float32 [8192, 2048], P('wsh')
- layer_gate_grad: float32 [2048, 256], P('wsh')
- layer_proj_grad: float32 [256, 2048], P('wsh')
- gains_grad: float32 [2048, 6], P('wsh')
- query_gain_grad: float32 [256], P('wsh')
- key_gain_grad: float32 [256], P('wsh')
Inputs may be any that keep to these rules, and one draw needn't show every extreme that they name: `lengths`: in every draw one slot holds 2048 valid tokens; the other holds at least 512. Within a slot every position 0 to 2047 appears once; each device's 128 tokens hold consecutive positions starting at a multiple of 128.
All inputs are finite; a program needn't handle non-finite values.
Results may differ from a plain program's by a relative error of at most 0.024.
Values may be sent and summed in bfloat16 or wider, within the bound.
No kernel may reach another device: no remote copies, remote signals or barrier semaphores. Data moves between devices by JAX's collectives and lax.ppermute only.
A program may use at most 512 MiB of HBM per device.

v0:
```python
import math

import jax
import jax.numpy as jnp
from jax import lax
from jax.sharding import PartitionSpec as P

HEADS = 8
KV_HEADS = 2
HEAD_DIM = 256


EPSILON = 1e-06
ROPE_BASE = 1000000.0
HALF_ROOT = 0.7071067811865476
TANH_SCALE = 0.7978845608028654
NEGATIVE = -1e30
EMBED_SCALE = 16.0


def rms_norm(value, gain):
    return value * lax.rsqrt(jnp.mean(value * value, axis=-1, keepdims=True) + EPSILON) * gain


def gelu_tanh(value):
    return 0.5 * value * (1.0 + jnp.tanh(TANH_SCALE * (value + 0.044715 * value * value * value)))


def gated_product(pre_gate, other_side):
    return gelu_tanh(pre_gate) * other_side


def rotate(value, places):
    width_all = value.shape[-1]
    half_width = width_all // 2
    inverse = jnp.exp(
        -math.log(ROPE_BASE) * (2.0 * jnp.arange(half_width, dtype=jnp.float32) / width_all)
    )
    angles = places.astype(jnp.float32)[:, None] * inverse[None, :]
    cosine = jnp.cos(angles)[:, None, :]
    sine = jnp.sin(angles)[:, None, :]
    front = value[..., :half_width]
    behind = value[..., half_width:]
    return jnp.concatenate(
        [front * cosine - behind * sine, behind * cosine + front * sine], axis=-1
    )


def matmul(left, right):
    return jnp.dot(left, right, preferred_element_type=jnp.float32)


def times_transposed(left, right):
    return lax.dot_general(
        left, right, (((1,), (1,)), ((), ())), preferred_element_type=jnp.float32
    )


def over_rows(left, right):
    return lax.dot_general(
        left, right, (((0,), (0,)), ((), ())), preferred_element_type=jnp.float32
    )


def shards(
    tokens,
    cotangent,
    lengths,
    positions,
    token_ids,
    per_layer_table,
    w_query,
    w_key,
    w_value,
    w_output,
    laurel_left,
    laurel_right,
    w_gate,
    w_up,
    w_down,
    w_layer_gate,
    w_layer_proj,
    norm_gains,
    query_gain,
    key_gain,
):
    rows_dev = tokens.shape[1]
    seq_len = rows_dev * lax.axis_size("ctx") * lax.axis_size("wsh")
    groups = HEADS // KV_HEADS
    gathered_ids, gathered_places = (
        lax.all_gather(token_ids, ("slot", "ctx", "wsh"), axis=1, tiled=True),
        lax.all_gather(positions, ("slot", "ctx", "wsh"), axis=1, tiled=True),
    )
    all_ids = gathered_ids[0]
    slot_places = lax.dynamic_slice_in_dim(
        gathered_places[0], lax.axis_index("slot") * seq_len, seq_len
    )
    vocab_rows = per_layer_table.shape[0]
    vocab_first = lax.axis_index(("slot", "ctx", "wsh")) * vocab_rows
    vocab_range = jnp.arange(vocab_rows, dtype=jnp.int32)

    def one_hot():
        return ((all_ids - vocab_first)[:, None] == vocab_range[None, :]).astype(jnp.bfloat16)

    layer_input = EMBED_SCALE * lax.psum_scatter(
        matmul(one_hot(), per_layer_table), ("slot", "ctx", "wsh"), scatter_dimension=0, tiled=True
    )
    params = (
        lax.all_gather(w_query, "wsh", axis=0, tiled=True),
        lax.all_gather(w_key, "wsh", axis=0, tiled=True),
        lax.all_gather(w_value, "wsh", axis=0, tiled=True),
        lax.all_gather(w_output, "wsh", axis=0, tiled=True),
        lax.all_gather(laurel_left, "wsh", axis=0, tiled=True),
        lax.all_gather(laurel_right, "wsh", axis=0, tiled=True),
        lax.all_gather(w_gate, "wsh", axis=0, tiled=True),
        lax.all_gather(w_up, "wsh", axis=0, tiled=True),
        lax.all_gather(w_down, "wsh", axis=0, tiled=True),
        lax.all_gather(w_layer_gate, "wsh", axis=0, tiled=True),
        lax.all_gather(w_layer_proj, "wsh", axis=0, tiled=True),
        lax.all_gather(norm_gains, "wsh", axis=0, tiled=True),
        lax.all_gather(query_gain, "wsh", axis=0, tiled=True),
        lax.all_gather(key_gain, "wsh", axis=0, tiled=True),
    )
    gains_full = params[11].astype(jnp.float32)
    query_gain_full = params[12].astype(jnp.float32)
    key_gain_full = params[13].astype(jnp.float32)
    tokens_f = tokens[0].astype(jnp.float32)
    query_places = positions[0]
    length = lengths[0]
    valid = (query_places < length).astype(jnp.float32)

    def query_path(raw, gain):
        return rotate(rms_norm(raw.reshape(rows_dev, HEADS, HEAD_DIM), gain), query_places)

    def key_path(raw, gain):
        return rotate(rms_norm(raw.reshape(rows_dev, KV_HEADS, HEAD_DIM), gain), query_places)

    def value_path(raw):
        return rms_norm(raw.reshape(rows_dev, KV_HEADS, HEAD_DIM), 1.0)

    normed = rms_norm(tokens_f, gains_full[:, 0])
    normed_low = normed.astype(jnp.bfloat16)
    query = matmul(normed_low, params[0])
    key = matmul(normed_low, params[1])
    value = matmul(normed_low, params[2])
    q_low = query_path(query, query_gain_full).astype(jnp.bfloat16)
    k_low = key_path(key, key_gain_full).astype(jnp.bfloat16)
    v_low = value_path(value).astype(jnp.bfloat16)
    q_group = q_low.reshape(rows_dev, KV_HEADS, groups, HEAD_DIM)
    keys_all, values_all = (
        lax.all_gather(k_low, ("ctx", "wsh"), axis=0, tiled=True),
        lax.all_gather(v_low, ("ctx", "wsh"), axis=0, tiled=True),
    )
    key_block = math.gcd(1024, seq_len)
    block_count = seq_len // key_block
    keys_blocked = keys_all.reshape(block_count, key_block, KV_HEADS, HEAD_DIM)
    values_blocked = values_all.reshape(block_count, key_block, KV_HEADS, HEAD_DIM)
    block_starts = jnp.arange(block_count, dtype=jnp.int32) * key_block

    def masked_scores(key_piece, begin):
        amount = key_piece.shape[0]
        key_places = lax.dynamic_slice_in_dim(slot_places, begin, amount)
        allowed = (key_places[None, :] <= query_places[:, None]) & (key_places < length)[None, :]
        raw_scores = jnp.einsum(
            "qkgd,tkd->qkgt", q_group, key_piece, preferred_element_type=jnp.float32
        )
        return jnp.where(allowed[:, None, None, :], raw_scores, NEGATIVE)

    def forward_step(carried, inputs):
        running_top, running_sum, running_out = carried
        key_piece, value_piece, begin = inputs
        scores = masked_scores(key_piece, begin)
        new_top = jnp.maximum(running_top, jnp.max(scores, axis=-1))
        factor = jnp.exp(running_top - new_top)
        weights = jnp.exp(scores - new_top[..., None])
        new_sum = running_sum * factor + jnp.sum(weights, axis=-1)
        new_out = running_out * factor[..., None] + jnp.einsum(
            "qkgt,tkd->qkgd",
            weights.astype(jnp.bfloat16),
            value_piece,
            preferred_element_type=jnp.float32,
        )
        return ((new_top, new_sum, new_out), None)

    start_state = (
        jnp.full((rows_dev, KV_HEADS, groups), NEGATIVE, jnp.float32),
        jnp.zeros((rows_dev, KV_HEADS, groups), jnp.float32),
        jnp.zeros((rows_dev, KV_HEADS, groups, HEAD_DIM), jnp.float32),
    )
    (final_top, final_sum, final_out), _ = lax.scan(
        forward_step, start_state, (keys_blocked, values_blocked, block_starts)
    )
    attended = final_out / final_sum[..., None]
    log_total = final_top + jnp.log(final_sum)
    attended_low = attended.reshape(rows_dev, HEADS * HEAD_DIM).astype(jnp.bfloat16)
    attn_proj = matmul(attended_low, params[3])
    first_sum = tokens_f + rms_norm(attn_proj, gains_full[:, 1])
    low_rank = matmul(normed_low, params[4])
    low_rank_low = low_rank.astype(jnp.bfloat16)
    laurel_out = times_transposed(low_rank_low, params[5])
    laurel = normed + rms_norm(laurel_out, gains_full[:, 2])
    mixed = (first_sum + laurel) * HALF_ROOT
    ff_in_low = rms_norm(mixed, gains_full[:, 3]).astype(jnp.bfloat16)
    gate = matmul(ff_in_low, params[6])
    upward = matmul(ff_in_low, params[7])
    hidden_low = gated_product(gate, upward).astype(jnp.bfloat16)
    ff_out = matmul(hidden_low, params[8])
    third_sum = mixed + rms_norm(ff_out, gains_full[:, 4])
    third_low = third_sum.astype(jnp.bfloat16)
    layer_gate = matmul(third_low, params[9])
    gated_low = gated_product(layer_gate, layer_input).astype(jnp.bfloat16)
    layer_proj = matmul(gated_low, params[10])
    result = third_sum + rms_norm(layer_proj, gains_full[:, 5])
    layer_out = result.astype(jnp.bfloat16)[None]
    grad_out = cotangent[0].astype(jnp.float32) * valid[:, None]
    _, pullback = jax.vjp(rms_norm, layer_proj, gains_full[:, 5])
    grad_proj, grad_gain_five = pullback(grad_out)
    grad_proj_low = grad_proj.astype(jnp.bfloat16)
    grad_gated = times_transposed(grad_proj_low, params[10])
    _, pullback = jax.vjp(gated_product, layer_gate, layer_input)
    grad_lgate, grad_input = pullback(grad_gated)
    grad_lgate_low = grad_lgate.astype(jnp.bfloat16)
    grad_input_low = grad_input.astype(jnp.bfloat16)
    grad_third = grad_out + times_transposed(grad_lgate_low, params[9])
    _, pullback = jax.vjp(rms_norm, ff_out, gains_full[:, 4])
    grad_ff, grad_gain_four = pullback(grad_third)
    grad_ff_low = grad_ff.astype(jnp.bfloat16)
    grad_hidden = times_transposed(grad_ff_low, params[8])
    _, pullback = jax.vjp(gated_product, gate, upward)
    grad_gate, grad_upward = pullback(grad_hidden)
    grad_gate_low = grad_gate.astype(jnp.bfloat16)
    grad_upward_low = grad_upward.astype(jnp.bfloat16)
    grad_ff_in = times_transposed(grad_gate_low, params[6]) + times_transposed(
        grad_upward_low, params[7]
    )
    _, pullback = jax.vjp(rms_norm, mixed, gains_full[:, 3])
    grad_mixed_norm, grad_gain_three = pullback(grad_ff_in)
    grad_branch = (grad_third + grad_mixed_norm) * HALF_ROOT
    _, pullback = jax.vjp(rms_norm, laurel_out, gains_full[:, 2])
    grad_laurel, grad_gain_two = pullback(grad_branch)
    grad_laurel_low = grad_laurel.astype(jnp.bfloat16)
    grad_rank_low = matmul(grad_laurel_low, params[5]).astype(jnp.bfloat16)
    _, pullback = jax.vjp(rms_norm, attn_proj, gains_full[:, 1])
    grad_attn, grad_gain_one = pullback(grad_branch)
    grad_attn_low = grad_attn.astype(jnp.bfloat16)
    grad_att_low = times_transposed(grad_attn_low, params[3]).astype(jnp.bfloat16)
    grad_att_group = grad_att_low.reshape(rows_dev, KV_HEADS, groups, HEAD_DIM)
    row_delta = jnp.sum(grad_att_group.astype(jnp.float32) * attended, axis=-1)

    def backward_step(grad_q_sum, inputs):
        key_piece, value_piece, begin = inputs
        scores = masked_scores(key_piece, begin)
        probs = jnp.exp(scores - log_total[..., None])
        grad_probs = jnp.einsum(
            "qkgd,tkd->qkgt", grad_att_group, value_piece, preferred_element_type=jnp.float32
        )
        grad_scores = (probs * (grad_probs - row_delta[..., None])).astype(jnp.bfloat16)
        grad_q_sum = grad_q_sum + jnp.einsum(
            "qkgt,tkd->qkgd", grad_scores, key_piece, preferred_element_type=jnp.float32
        )
        key_part = jnp.einsum(
            "qkgt,qkgd->tkd", grad_scores, q_group, preferred_element_type=jnp.float32
        )
        value_part = jnp.einsum(
            "qkgt,qkgd->tkd",
            probs.astype(jnp.bfloat16),
            grad_att_group,
            preferred_element_type=jnp.float32,
        )
        return (grad_q_sum, (key_part, value_part))

    grad_q_rot, (key_parts, value_parts) = lax.scan(
        backward_step,
        jnp.zeros((rows_dev, KV_HEADS, groups, HEAD_DIM), jnp.float32),
        (keys_blocked, values_blocked, block_starts),
    )
    grad_keys_all = key_parts.reshape(seq_len, KV_HEADS, HEAD_DIM)
    grad_values_all = value_parts.reshape(seq_len, KV_HEADS, HEAD_DIM)
    grad_k_rot, grad_v_norm = (
        lax.psum_scatter(grad_keys_all, ("ctx", "wsh"), scatter_dimension=0, tiled=True),
        lax.psum_scatter(grad_values_all, ("ctx", "wsh"), scatter_dimension=0, tiled=True),
    )
    _, pullback = jax.vjp(query_path, query, query_gain_full)
    grad_query, grad_query_gain = pullback(grad_q_rot.reshape(rows_dev, HEADS, HEAD_DIM))
    _, pullback = jax.vjp(key_path, key, key_gain_full)
    grad_key, grad_key_gain = pullback(grad_k_rot)
    _, pullback = jax.vjp(value_path, value)
    (grad_value,) = pullback(grad_v_norm)
    grad_query_low = grad_query.astype(jnp.bfloat16)
    grad_key_low = grad_key.astype(jnp.bfloat16)
    grad_value_low = grad_value.astype(jnp.bfloat16)
    grad_normed = (
        times_transposed(grad_query_low, params[0])
        + times_transposed(grad_key_low, params[1])
        + times_transposed(grad_value_low, params[2])
        + times_transposed(grad_rank_low, params[4])
        + grad_branch
    )
    _, pullback = jax.vjp(rms_norm, tokens_f, gains_full[:, 0])
    grad_tokens, grad_gain_zero = pullback(grad_normed)
    tokens_grad = (grad_tokens + grad_branch).astype(jnp.bfloat16)[None]
    every_grad = lax.all_gather(grad_input_low, ("slot", "ctx", "wsh"), axis=0, tiled=True)
    table_grad = EMBED_SCALE * over_rows(one_hot(), every_grad)
    grad_gains = jnp.stack(
        [
            grad_gain_zero,
            grad_gain_one,
            grad_gain_two,
            grad_gain_three,
            grad_gain_four,
            grad_gain_five,
        ],
        axis=1,
    )
    vectors = (grad_gains, grad_query_gain, grad_key_gain)
    shard_sizes = (
        w_query.shape[0],
        w_key.shape[0],
        w_value.shape[0],
        w_output.shape[0],
        laurel_left.shape[0],
        laurel_right.shape[0],
        w_gate.shape[0],
        w_up.shape[0],
        w_down.shape[0],
        w_layer_gate.shape[0],
        w_layer_proj.shape[0],
        norm_gains.shape[0],
        query_gain.shape[0],
        key_gain.shape[0],
    )
    shard_index = lax.axis_index("wsh")
    input_side = (
        normed_low,
        attended_low,
        grad_laurel_low,
        ff_in_low,
        hidden_low,
        third_low,
        gated_low,
    )
    output_side = (
        grad_query_low,
        grad_key_low,
        grad_value_low,
        grad_attn_low,
        grad_rank_low,
        low_rank_low,
        grad_gate_low,
        grad_upward_low,
        grad_ff_low,
        grad_lgate_low,
        grad_proj_low,
    )
    input_choice = (0, 0, 0, 1, 0, 2, 3, 3, 4, 5, 6)
    pieces = (
        lax.all_gather(input_side[0], "wsh", axis=0, tiled=True),
        lax.all_gather(input_side[1], "wsh", axis=0, tiled=True),
        lax.all_gather(input_side[2], "wsh", axis=0, tiled=True),
        lax.all_gather(input_side[3], "wsh", axis=0, tiled=True),
        lax.all_gather(input_side[4], "wsh", axis=0, tiled=True),
        lax.all_gather(input_side[5], "wsh", axis=0, tiled=True),
        lax.all_gather(input_side[6], "wsh", axis=0, tiled=True),
        lax.all_gather(output_side[0], "wsh", axis=0, tiled=True),
        lax.all_gather(output_side[1], "wsh", axis=0, tiled=True),
        lax.all_gather(output_side[2], "wsh", axis=0, tiled=True),
        lax.all_gather(output_side[3], "wsh", axis=0, tiled=True),
        lax.all_gather(output_side[4], "wsh", axis=0, tiled=True),
        lax.all_gather(output_side[5], "wsh", axis=0, tiled=True),
        lax.all_gather(output_side[6], "wsh", axis=0, tiled=True),
        lax.all_gather(output_side[7], "wsh", axis=0, tiled=True),
        lax.all_gather(output_side[8], "wsh", axis=0, tiled=True),
        lax.all_gather(output_side[9], "wsh", axis=0, tiled=True),
        lax.all_gather(output_side[10], "wsh", axis=0, tiled=True),
    )
    left_pieces = pieces[:7]
    right_pieces = pieces[7:]
    folded = tuple(
        (
            over_rows(
                lax.dynamic_slice_in_dim(
                    left_pieces[input_choice[number]],
                    shard_index * shard_sizes[number],
                    shard_sizes[number],
                    1,
                ),
                right_pieces[number],
            )
            for number in range(11)
        )
    )
    smaller = (
        lax.psum_scatter(
            vectors[0].astype(jnp.bfloat16), "wsh", scatter_dimension=0, tiled=True
        ).astype(jnp.float32),
        lax.psum_scatter(
            vectors[1].astype(jnp.bfloat16), "wsh", scatter_dimension=0, tiled=True
        ).astype(jnp.float32),
        lax.psum_scatter(
            vectors[2].astype(jnp.bfloat16), "wsh", scatter_dimension=0, tiled=True
        ).astype(jnp.float32),
    )
    summed = (
        lax.psum(folded[0].astype(jnp.bfloat16), ("slot", "ctx")).astype(jnp.float32),
        lax.psum(folded[1].astype(jnp.bfloat16), ("slot", "ctx")).astype(jnp.float32),
        lax.psum(folded[2].astype(jnp.bfloat16), ("slot", "ctx")).astype(jnp.float32),
        lax.psum(folded[3].astype(jnp.bfloat16), ("slot", "ctx")).astype(jnp.float32),
        lax.psum(folded[4].astype(jnp.bfloat16), ("slot", "ctx")).astype(jnp.float32),
        lax.psum(folded[5].astype(jnp.bfloat16), ("slot", "ctx")).astype(jnp.float32),
        lax.psum(folded[6].astype(jnp.bfloat16), ("slot", "ctx")).astype(jnp.float32),
        lax.psum(folded[7].astype(jnp.bfloat16), ("slot", "ctx")).astype(jnp.float32),
        lax.psum(folded[8].astype(jnp.bfloat16), ("slot", "ctx")).astype(jnp.float32),
        lax.psum(folded[9].astype(jnp.bfloat16), ("slot", "ctx")).astype(jnp.float32),
        lax.psum(folded[10].astype(jnp.bfloat16), ("slot", "ctx")).astype(jnp.float32),
        lax.psum(smaller[0].astype(jnp.bfloat16), ("slot", "ctx")).astype(jnp.float32),
        lax.psum(smaller[1].astype(jnp.bfloat16), ("slot", "ctx")).astype(jnp.float32),
        lax.psum(smaller[2].astype(jnp.bfloat16), ("slot", "ctx")).astype(jnp.float32),
    )
    return (
        layer_out,
        tokens_grad,
        table_grad,
        summed[0],
        summed[1],
        summed[2],
        summed[3],
        summed[4],
        summed[5],
        summed[6],
        summed[7],
        summed[8],
        summed[9],
        summed[10],
        summed[11],
        summed[12],
        summed[13],
    )


def solution(mesh):
    placed = (
        P("slot", ("ctx", "wsh"), None),
        P("slot", ("ctx", "wsh"), None),
        P("slot"),
        P("slot", ("ctx", "wsh")),
        P("slot", ("ctx", "wsh")),
        P(("slot", "ctx", "wsh"), None),
        P("wsh", None),
        P("wsh", None),
        P("wsh", None),
        P("wsh", None),
        P("wsh", None),
        P("wsh", None),
        P("wsh", None),
        P("wsh", None),
        P("wsh", None),
        P("wsh", None),
        P("wsh", None),
        P("wsh", None),
        P("wsh"),
        P("wsh"),
    )
    return jax.shard_map(
        shards,
        mesh=mesh,
        in_specs=placed,
        out_specs=(
            P("slot", ("ctx", "wsh"), None),
            P("slot", ("ctx", "wsh"), None),
            P(("slot", "ctx", "wsh"), None),
            P("wsh", None),
            P("wsh", None),
            P("wsh", None),
            P("wsh", None),
            P("wsh", None),
            P("wsh", None),
            P("wsh", None),
            P("wsh", None),
            P("wsh", None),
            P("wsh", None),
            P("wsh", None),
            P("wsh", None),
            P("wsh"),
            P("wsh"),
        ),
        check_vma=False,
    )
```

profile of v0, /device:TPU:0, one launch (start us, length us, event | category | flops | bytes accessed | tf_op | source)
XLA Modules:
  0.0 3872.0 jit_solution(9865923164609194438)
XLA Ops:
  13.3 13.6 all-reduce.11
  26.9 13.5 all_gather.112
  42.7 16.9 all-gather.25.cloned.1.call-done
  68.2 37.6 all-gather.31.cloned.1.call-done
  117.3 65.7 %all_gather.127 = s32[1,4096]{1,0:T(1,128)S(1)} all-gather(s32[1,128]{1,0:T(1,128)S(1)} %copy-done.82), channel_id=1, replica_groups=mesh['slot'=2,'ctx'=4,'wsh'=4] {'slot','ctx','wsh'}, dimensions={1}, use_global_device_ids=true | all-gather | bytes 16896 | tf_op jit(solution)/shard_map/all_gather | solution.py:91
  183.6 13.3 fusion.48
  198.9 78.4 %all_gather.111 = s32[1,4096]{1,0:T(1,128)S(1)} all-gather(s32[1,128]{1,0:T(1,128)S(1)} %copy-done.55), channel_id=1, replica_groups=mesh['slot'=2,'ctx'=4,'wsh'=4] {'slot','ctx','wsh'}, dimensions={1}, use_global_device_ids=true | all-gather | bytes 16896 | tf_op jit(solution)/shard_map/all_gather | solution.py:92
  277.2 17.8 all_gather.121
  296.5 17.4 all_gather.122
  319.0 13.8 all-gather.29.cloned.1.call-done
  332.7 12.2 copy.74
  352.5 51.6 %all-gather.33.cloned.1.call-done = bf16[2048,2,256]{2,0,1:T(8,128)(2,1)} async-done(((bf16[128,2,256]{2,0,1:T(8,128)(2,1)}), bf16[2048,2,256]{2,0,1:T(8,128)(2,1)}) %all-gather.33.cloned.1.call-update) | async-done | bytes 2097168 | tf_op jit(solution)/shard_map/all_gather | solution.py:152
  404.1 28.9 while.30
  433.1 126.7 %all-gather.35.cloned.1.call-done = bf16[2048,2048]{1,0:T(8,128)(2,1)} async-done(((bf16[512,2048]{1,0:T(8,128)(2,1)}), bf16[2048,2048]{1,0:T(8,128)(2,1)}) %all-gather.35.cloned.1.call-update) | async-done | bytes 8388624 | tf_op jit(solution)/shard_map/all_gather | solution.py:112
  565.8 563.6 %all-gather.37.cloned.1.call-done = bf16[2048,8192]{1,0:T(8,128)(2,1)} async-done(((bf16[512,8192]{1,0:T(8,128)(2,1)}), bf16[2048,8192]{1,0:T(8,128)(2,1)}) %all-gather.37.cloned.1.call-update) | async-done | bytes 33554448 | tf_op jit(solution)/shard_map/all_gather | solution.py:115
  1129.4 20.6 fusion.143
  1150.0 541.5 %all-gather.39.cloned.1.call-done = bf16[2048,8192]{1,0:T(8,128)(2,1)} async-done(((bf16[512,8192]{1,0:T(8,128)(2,1)}), bf16[2048,8192]{1,0:T(8,128)(2,1)}) %all-gather.39.cloned.1.call-update) | async-done | bytes 33554448 | tf_op jit(solution)/shard_map/all_gather | solution.py:116
  1691.5 21.8 multiply_convert_fusion.1
  1713.3 539.4 %all-gather.41.cloned.1.call-done = bf16[8192,2048]{1,0:T(8,128)(2,1)} async-done(((bf16[2048,2048]{1,0:T(8,128)(2,1)}), bf16[8192,2048]{1,0:T(8,128)(2,1)}) %all-gather.41.cloned.1.call-update) | async-done | bytes 33554448 | tf_op jit(solution)/shard_map/all_gather | solution.py:117
  2252.7 14.0 multiply_reduce_fusion.12
  2267.0 13.3 all-gather.43.cloned.1.call-done
  2282.5 26.8 all-gather.45.cloned.1.call-done
  2321.2 21.4 multiply_convert_fusion
  2342.6 16.3 fusion.144
  2358.9 19.4 multiply_reduce_fusion.2
  2395.8 46.7 %while.31 = (s32[]{:T(128)}, f32[128,2,4,256]{0,3,2,1:T(8,128)S(1)}, f32[2,1024,2,256]{3,1,0,2:T(8,128)}, f32[2,1024,2,256]{3,1,0,2:T(8,128)}, bf16[2,1024,2,256...) while((s32[]{:T(128)}, ...), condition=%wide.region_20.21_spmd.clone, body=%wide.region_19.20_spmd.clone.sunk | while | flops 2693530624 | bytes 83258216 | solution.py:272
  2456.8 12.6 all_gather.138
  2472.7 12.1 all_gather.136
  2484.8 16.8 all_gather.145
  2501.6 15.5 all_gather.146
  2532.5 44.0 %all-gather.51.cloned.1.call-done = bf16[512,2048]{0,1:T(8,128)(2,1)} async-done(((bf16[128,2048]{0,1:T(8,128)(2,1)}), bf16[512,2048]{0,1:T(8,128)(2,1)}) %all-gather.51.cloned.1.call-update) | async-done | bytes 2097168 | tf_op jit(solution)/shard_map/all_gather | solution.py:364
  2581.0 41.4 %all-gather.53.cloned.1.call-done = bf16[512,2048]{0,1:T(8,128)(2,1)} async-done(((bf16[128,2048]{0,1:T(8,128)(2,1)}), bf16[512,2048]{0,1:T(8,128)(2,1)}) %all-gather.53.cloned.1.call-update) | async-done | bytes 2097168 | tf_op jit(solution)/shard_map/all_gather | solution.py:358
  2622.4 45.6 %all-gather.55.cloned.1.call-done = bf16[512,2048]{1,0:T(8,128)(2,1)} async-done(((bf16[128,2048]{1,0:T(8,128)(2,1)}), bf16[512,2048]{1,0:T(8,128)(2,1)}) %all-gather.55.cloned.1.call-update) | async-done | bytes 2097168 | tf_op jit(solution)/shard_map/all_gather | solution.py:367
  2672.4 93.6 %reduce-scatter.7.cloned.1.call-done = f32[128,2,256]{2,0,1:T(8,128)} async-done(((f32[2048,2,256]{2,0,1:T(8,128)}), f32[128,2,256]{2,0,1:T(8,128)}) %reduce-scatter.7.cloned.1.call-update) | async-done | bytes 262160 | tf_op jit(solution)/shard_map/reduce_scatter | solution.py:280
  2767.5 95.9 %reduce-scatter.9.cloned.1.call-done = f32[128,2,256]{2,0,1:T(8,128)} async-done(((f32[2048,2,256]{2,0,1:T(8,128)}), f32[128,2,256]{2,0,1:T(8,128)}) %reduce-scatter.9.cloned.1.call-update) | async-done | bytes 262160 | tf_op jit(solution)/shard_map/reduce_scatter | solution.py:281
  2872.3 23.6 all_gather.132
  2895.9 29.9 all_gather.133
  2930.9 145.3 %all-gather.61.cloned.1.call-done = bf16[512,8192]{1,0:T(8,128)(2,1)} async-done(((bf16[128,8192]{1,0:T(8,128)(2,1)}), bf16[512,8192]{1,0:T(8,128)(2,1)}) %all-gather.61.cloned.1.call-update) | async-done | bytes 8388624 | tf_op jit(solution)/shard_map/all_gather | solution.py:370
  3076.2 11.8 convolution_convert_fusion.1
  3088.0 137.6 %all-gather.63.cloned.1.call-done = bf16[512,8192]{1,0:T(8,128)(2,1)} async-done(((bf16[128,8192]{1,0:T(8,128)(2,1)}), bf16[512,8192]{1,0:T(8,128)(2,1)}) %all-gather.63.cloned.1.call-update) | async-done | bytes 8388624 | tf_op jit(solution)/shard_map/all_gather | solution.py:371
  3237.2 34.1 all-gather.67.cloned.1.call-done
  3271.3 150.5 %all-gather.65.cloned.1.call-done = bf16[512,8192]{1,0:T(8,128)(2,1)} async-done(((bf16[128,8192]{1,0:T(8,128)(2,1)}), bf16[512,8192]{1,0:T(8,128)(2,1)}) %all-gather.65.cloned.1.call-update) | async-done | bytes 8388624 | tf_op jit(solution)/shard_map/all_gather | solution.py:361
  3432.9 59.8 %all-gather.47.cloned.1.call-done = bf16[4096,256]{1,0:T(8,128)(2,1)} async-done(((bf16[128,256]{1,0:T(8,128)(2,1)}), bf16[4096,256]{1,0:T(8,128)(2,1)}) %all-gather.47.cloned.1.call-update) | async-done | bytes 2097168 | tf_op jit(solution)/shard_map/all_gather | solution.py:302
  3492.8 24.2 fusion.51
  3529.0 16.5 all-reduce.8
  3547.2 269.5 %all-reduce.14.cloned.1.call-done = (bf16[512,2048]{1,0:T(8,128)(2,1)}, bf16[512,512]{1,0:T(8,128)(2,1)}, bf16[512,512]{1,0:T(8,128)(2,1)}, bf16[512,2048]{1,0:T...) async-done(((bf16[512,2048]{1,0:T(8,128)(2,1)}, ...) | async-done | bytes 31064080 | tf_op jit(solution)/shard_map/psum | solution.py:404
  3827.1 11.7 convert_element_type.297
  3850.6 11.8 convert_element_type.301
  (407 shorter events, 263.0 us)
Async XLA Ops:
  8.0 175.6 %copy-start = (bf16[4096,256]{1,0:T(8,128)(2,1)S(1)}, bf16[4096,256]{1,0:T(8,128)(2,1)}, u32[]{:S(2)}) copy-start(bf16[4096,256]{1,0:T(8,128)(2,1)} %param.29) | copy-start | bytes 6291460
  8.0 51.6 %all-gather.25.cloned.1.call-start = ((), (), s32[]{:S(2)}) async-start(), calls=%async_computation.4 | async-start | bytes 2621440 | tf_op jit(solution)/shard_map/all_gather | solution.py:110
  8.8 97.1 %all-gather.31.cloned.1.call-start = ((), (), s32[]{:S(2)}) async-start(), calls=%async_computation.7 | async-start | bytes 2621440 | tf_op jit(solution)/shard_map/all_gather | solution.py:111
  9.5 306.4 %all-gather.27.cloned.1.call-start = ((), (), s32[]{:S(2)}) async-start(), calls=%async_computation.5 | async-start | bytes 2228224 | tf_op jit(solution)/shard_map/all_gather | solution.py:151
  41.6 523.0 %copy-start.67 = (f32[128]{0:T(128)}, f32[128]{0:T(128)S(1)}, u32[]{:S(2)}) copy-start(f32[128]{0:T(128)S(1)} %fusion.127) | copy-start | bytes 1540
  42.6 309.0 %copy-start.34 = (f32[128,128]{1,0:T(8,128)}, f32[128,128]{1,0:T(8,128)S(1)}, u32[]{:S(2)}) copy-start(f32[128,128]{1,0:T(8,128)S(1)} %get-tuple-element.431) | copy-start | bytes 196612
  42.6 309.0 %copy-start.36 = (f32[128,128]{1,0:T(8,128)}, f32[128,128]{1,0:T(8,128)S(1)}, u32[]{:S(2)}) copy-start(f32[128,128]{1,0:T(8,128)S(1)} %get-tuple-element.432) | copy-start | bytes 196612
  42.7 522.0 %copy-start.41 = (f32[2048,1]{0,1:T(1,128)}, f32[2048,1]{0,1:T(1,128)S(1)}, u32[]{:S(2)}) copy-start(f32[2048,1]{0,1:T(1,128)S(1)} %get-tuple-element.429) | copy-start | bytes 24580
  67.6 265.1 %all-gather.29.cloned.1.call-start = ((), (), s32[]{:S(2)}) async-start(), calls=%async_computation.6 | async-start | bytes 10485760 | tf_op jit(solution)/shard_map/all_gather | solution.py:109
  68.2 335.8 %all-gather.33.cloned.1.call-start = ((), (), s32[]{:S(2)}) async-start(), calls=%async_computation.8 | async-start | bytes 2228224 | tf_op jit(solution)/shard_map/all_gather | solution.py:152
  113.8 445.9 %all-gather.35.cloned.1.call-start = ((), (), s32[]{:S(2)}) async-start(), calls=%async_computation.9 | async-start | bytes 10485760 | tf_op jit(solution)/shard_map/all_gather | solution.py:112
  114.4 1015.0 %all-gather.37.cloned.1.call-start = ((), (), s32[]{:S(2)}) async-start(), calls=%async_computation.10 | async-start | bytes 41943040 | tf_op jit(solution)/shard_map/all_gather | solution.py:115
  115.2 1576.3 %all-gather.39.cloned.1.call-start = ((), (), s32[]{:S(2)}) async-start(), calls=%async_computation.11 | async-start | bytes 41943040 | tf_op jit(solution)/shard_map/all_gather | solution.py:116
  115.9 2136.8 %all-gather.41.cloned.1.call-start = ((), (), s32[]{:S(2)}) async-start(), calls=%async_computation.12 | async-start | bytes 41943040 | tf_op jit(solution)/shard_map/all_gather | solution.py:117
  116.7 2163.6 %all-gather.43.cloned.1.call-start = ((), (), s32[]{:S(2)}) async-start(), calls=%async_computation.13 | async-start | bytes 1310720 | tf_op jit(solution)/shard_map/all_gather | solution.py:118
  117.2 2163.0 %reduce-scatter.5.cloned.1.call-start = ((), (), s32[]{:S(2)}) async-start(), calls=%async_computation.14 | async-start | bytes 4325376 | tf_op jit(solution)/shard_map/reduce_scatter | solution.py:105
  196.9 99.5 %copy-start.52 = (bf16[512,64]{0,1:T(8,128)(2,1)S(1)}, bf16[512,64]{0,1:T(8,128)(2,1)}, u32[]{:S(2)}) copy-start(bf16[512,64]{0,1:T(8,128)(2,1)} %param.35) | copy-start | bytes 196612
  197.0 2112.3 %all-gather.45.cloned.1.call-start = ((), (), s32[]{:S(2)}) async-start(), calls=%async_computation.15 | async-start | bytes 1310720 | tf_op jit(solution)/shard_map/all_gather | solution.py:119
  197.7 2326.0 %all-gather.49.cloned.1.call-start = ((), (), s32[]{:S(2)}) async-start(), calls=%async_computation.19 | async-start | bytes 2621440 | tf_op jit(solution)/shard_map/all_gather | solution.py:357
  198.8 2326.9 %all-gather.57.cloned.1.call-start = ((), (), s32[]{:S(2)}) async-start(), calls=%async_computation.23 | async-start | bytes 2621440 | tf_op jit(solution)/shard_map/all_gather | solution.py:359
  433.0 131.6 %copy-start.21 = (f32[128,2,4,256]{0,3,2,1:T(8,128)}, f32[128,2,4,256]{0,3,2,1:T(8,128)S(1)}, u32[]{:S(2)}) copy-start(f32[128,2,4,256]{0,3,2,1:T(8,128)S(1)} %get-tuple-element.150) | copy-start | bytes 3145732
  433.0 131.6 %copy-start.83 = (s32[2]{0:T(128)}, s32[2]{0:T(128)S(1)}, u32[]{:S(2)}) copy-start(s32[2]{0:T(128)S(1)} %get-tuple-element.884) | copy-start | bytes 28
  433.1 131.5 %copy-start.16 = (bf16[128,2,4,256]{0,3,2,1:T(8,128)(2,1)}, bf16[128,2,4,256]{0,3,2,1:T(8,128)(2,1)S(1)}, u32[]{:S(2)}) copy-start(bf16[128,2,4,256]{0,3,2,1:T(8,128)(2,1)S(1)} %fusion.97) | copy-start | bytes 1572868
  565.8 1125.7 %copy-start.15 = (bf16[128,2048]{1,0:T(8,128)(2,1)}, bf16[128,2048]{1,0:T(8,128)(2,1)S(1)}, u32[]{:S(2)}) copy-start(bf16[128,2048]{1,0:T(8,128)(2,1)S(1)} %multiply_convert_fusion.2) | copy-start | bytes 1572868
  2382.7 144.9 %all-gather.69.cloned.1.call-start = ((), (), s32[]{:S(2)}) async-start(), calls=%async_computation.29 | async-start | bytes 2621440 | tf_op jit(solution)/shard_map/all_gather | solution.py:362
  2383.2 146.4 %all-gather.71.cloned.1.call-start = ((), (), s32[]{:S(2)}) async-start(), calls=%async_computation.30 | async-start | bytes 2621440 | tf_op jit(solution)/shard_map/all_gather | solution.py:374
  2395.7 180.8 %all-gather.51.cloned.1.call-start = ((), (), s32[]{:S(2)}) async-start(), calls=%async_computation.20 | async-start | bytes 2621440 | tf_op jit(solution)/shard_map/all_gather | solution.py:364
  2450.6 171.8 %all-gather.53.cloned.1.call-start = ((), (), s32[]{:S(2)}) async-start(), calls=%async_computation.21 | async-start | bytes 2621440 | tf_op jit(solution)/shard_map/all_gather | solution.py:358
  2451.2 216.8 %all-gather.55.cloned.1.call-start = ((), (), s32[]{:S(2)}) async-start(), calls=%async_computation.22 | async-start | bytes 2621440 | tf_op jit(solution)/shard_map/all_gather | solution.py:367
  2451.8 314.2 %reduce-scatter.7.cloned.1.call-start = ((), (), s32[]{:S(2)}) async-start(), calls=%async_computation.16 | async-start | bytes 4456448 | tf_op jit(solution)/shard_map/reduce_scatter | solution.py:280
  2452.5 410.9 %reduce-scatter.9.cloned.1.call-start = ((), (), s32[]{:S(2)}) async-start(), calls=%async_computation.17 | async-start | bytes 4456448 | tf_op jit(solution)/shard_map/reduce_scatter | solution.py:281
  2453.2 477.7 %all-gather.59.cloned.1.call-start = ((), (), s32[]{:S(2)}) async-start(), calls=%async_computation.24 | async-start | bytes 2621440 | tf_op jit(solution)/shard_map/all_gather | solution.py:360
  2453.9 622.3 %all-gather.61.cloned.1.call-start = ((), (), s32[]{:S(2)}) async-start(), calls=%async_computation.25 | async-start | bytes 10485760 | tf_op jit(solution)/shard_map/all_gather | solution.py:370
  2454.7 771.0 %all-gather.63.cloned.1.call-start = ((), (), s32[]{:S(2)}) async-start(), calls=%async_computation.26 | async-start | bytes 10485760 | tf_op jit(solution)/shard_map/all_gather | solution.py:371
  2455.4 815.9 %all-gather.67.cloned.1.call-start = ((), (), s32[]{:S(2)}) async-start(), calls=%async_computation.28 | async-start | bytes 2621440 | tf_op jit(solution)/shard_map/all_gather | solution.py:372
  2456.0 965.8 %all-gather.65.cloned.1.call-start = ((), (), s32[]{:S(2)}) async-start(), calls=%async_computation.27 | async-start | bytes 10485760 | tf_op jit(solution)/shard_map/all_gather | solution.py:361
  2456.7 1036.1 %all-gather.47.cloned.1.call-start = ((), (), s32[]{:S(2)}) async-start(), calls=%async_computation.18 | async-start | bytes 2162688 | tf_op jit(solution)/shard_map/all_gather | solution.py:302
  2517.2 1011.8 %reduce-scatter.11.cloned.1.call-start = ((), (), s32[]{:S(2)}) async-start(), calls=%async_computation.31 | async-start | bytes 40960 | tf_op jit(solution)/shard_map/reduce_scatter | solution.py:393
  2580.9 186.1 %copy-start.29 = (f32[128,2,256]{2,0,1:T(8,128)S(1)}, f32[128,2,256]{2,0,1:T(8,128)}, u32[]{:S(2)}) copy-start(f32[128,2,256]{2,0,1:T(8,128)} %copy-done.28) | copy-start | bytes 786436
  2580.9 186.1 %copy-start.64 = (f32[128,2]{0,1:T(2,128)S(1)}, f32[128,2]{0,1:T(2,128)}, u32[]{:S(2)}) copy-start(f32[128,2]{0,1:T(2,128)} %copy-done.63) | copy-start | bytes 3076
  2580.9 186.1 %copy-start.70 = (f32[256]{0:T(256)S(1)}, f32[256]{0:T(256)}, u32[]{:S(2)}) copy-start(f32[256]{0:T(256)} %copy-done.69) | copy-start | bytes 3076
  2580.9 186.3 %copy-start.76 = (f32[128,2]{0,1:T(2,128)S(1)}, f32[128,2]{0,1:T(2,128)}, u32[]{:S(2)}) copy-start(f32[128,2]{0,1:T(2,128)} %copy-done.75) | copy-start | bytes 3076
  2580.9 282.5 %copy-start.31 = (f32[128,2,256]{2,0,1:T(8,128)S(1)}, f32[128,2,256]{2,0,1:T(8,128)}, u32[]{:S(2)}) copy-start(f32[128,2,256]{2,0,1:T(8,128)} %copy-done.30) | copy-start | bytes 786436
  2581.0 283.5 %copy-start.78 = (f32[128,2]{0,1:T(2,128)S(1)}, f32[128,2]{0,1:T(2,128)}, u32[]{:S(2)}) copy-start(f32[128,2]{0,1:T(2,128)} %copy-done.77) | copy-start | bytes 3076
  2581.0 283.5 %copy-start.74 = (f32[128,2]{0,1:T(2,128)S(1)}, f32[128,2]{0,1:T(2,128)}, u32[]{:S(2)}) copy-start(f32[128,2]{0,1:T(2,128)} %copy-done.73) | copy-start | bytes 3076
  2925.8 890.9 %all-reduce.14.cloned.1.call-start = ((), (), s32[]{:S(2)}) async-start(), calls=%async_computation.32 | async-start | bytes 62128128 | tf_op jit(solution)/shard_map/psum | solution.py:404
  3432.9 84.1 %copy-start.81 = (bf16[256]{0:T(256)(128)(2,1)S(1)}, bf16[256]{0:T(256)(128)(2,1)}, u32[]{:S(2)}) copy-start(bf16[256]{0:T(256)(128)(2,1)} %get-tuple-element.312) | copy-start | bytes 1540
  3432.9 94.8 %copy-start.80 = (f32[128]{0:T(128)S(1)}, f32[128]{0:T(128)}, u32[]{:S(2)}) copy-start(f32[128]{0:T(128)} %copy-done.79) | copy-start | bytes 1540
  (71 other events, 1164.7 us)
Sparse Core Ops, SparseCore 0:
  10.5 49.1 all-gather.24
  61.2 44.6 all-gather.30
  109.3 59.4 all-gather.26
  170.2 162.4 all-gather.28
  335.9 68.0 all-gather.32
  405.5 154.2 all-gather.34
  561.3 568.0 all-gather.36
  1131.0 560.4 all-gather.38
  1693.1 559.5 all-gather.40
  2254.1 26.1 all-gather.42
  2281.8 27.4 all-gather.44
  2311.3 45.4 all-gather.48
  2382.8 45.3 all-gather.56
  2429.6 45.8 all-gather.68
  2477.5 51.5 all-gather.70
  2531.1 45.3 all-gather.50
  2577.9 44.4 all-gather.52
  2623.8 44.1 all-gather.54
  2670.9 95.0 reduce-scatter.6
  2768.7 94.6 reduce-scatter.8
  2865.0 60.7 all-gather.58
  2927.9 148.1 all-gather.60
  3077.7 147.8 all-gather.62
  3227.1 44.1 all-gather.66
  3273.4 148.3 all-gather.64
  3425.2 67.5 all-gather.46
  3495.5 18.0 reduce-scatter.10
Sparse Core Ops, SparseCore 1:
  197.1 939.8 reduce-scatter.4
  3432.4 384.3 all-reduce.13
where the time goes:
time: 3880 us; the launch traced here: 3870 us
  waiting for transfers between devices  3060 us (79%)
  blocking collectives  344 us (9%)
  matrix products  303 us (8%)
  other arithmetic  87.1 us (2%)
  local copies, waits for them, and re-layouts  47.8 us (1%)
    all_gather x1, waiting for transfers between devices, shards(): lax.all_gather(w_gate, 'wsh', axis=0, tiled=True)  564 us
    all_gather x1, waiting for transfers between devices, shards(): lax.all_gather(w_up, 'wsh', axis=0, tiled=True)  542 us
    all_gather x1, waiting for transfers between devices, shards(): lax.all_gather(w_down, 'wsh', axis=0, tiled=True)  539 us
    psum x1, waiting for transfers between devices, shards(): lax.psum(folded[0].astype(jnp.bfloat16), ('slot', 'ctx'))  270 us
    all_gather x1, waiting for transfers between devices, shards(): lax.all_gather(input_side[4], 'wsh', axis=0, tiled=True)  151 us
    all_gather x1, waiting for transfers between devices, shards(): lax.all_gather(output_side[6], 'wsh', axis=0, tiled=True)  145 us
    all_gather x1, waiting for transfers between devices, shards(): lax.all_gather(output_side[7], 'wsh', axis=0, tiled=True)  138 us
    all_gather x1, waiting for transfers between devices, shards(): lax.all_gather(w_output, 'wsh', axis=0, tiled=True)  127 us
  transfers between devices with their start and end apart: 29, of which 21 were waited for; matrix products, arithmetic and copies ran while one was open for 10% of the time, Pallas kernels for 0%

commit v1 on v0

v1 whole, which is shorter than its diff:
```python
import functools
import math

import jax
import jax.numpy as jnp
from jax import lax
from jax.experimental import pallas as pl
from jax.experimental.pallas import tpu as pltpu
from jax.sharding import PartitionSpec as P

HEADS = 8
KV_HEADS = 2
HEAD_DIM = 256


EPSILON = 1e-06
ROPE_BASE = 1000000.0
HALF_ROOT = 0.7071067811865476
TANH_SCALE = 0.7978845608028654
NEGATIVE = -1e30
EMBED_SCALE = 16.0


def rms_norm(value, gain):
    return value * lax.rsqrt(jnp.mean(value * value, axis=-1, keepdims=True) + EPSILON) * gain


def gelu_tanh(value):
    return 0.5 * value * (1.0 + jnp.tanh(TANH_SCALE * (value + 0.044715 * value * value * value)))


def gated_product(pre_gate, other_side):
    return gelu_tanh(pre_gate) * other_side


def rotate(value, places):
    width_all = value.shape[-1]
    half_width = width_all // 2
    inverse = jnp.exp(
        -math.log(ROPE_BASE) * (2.0 * jnp.arange(half_width, dtype=jnp.float32) / width_all)
    )
    angles = places.astype(jnp.float32)[:, None] * inverse[None, :]
    cosine = jnp.cos(angles)[:, None, :]
    sine = jnp.sin(angles)[:, None, :]
    front = value[..., :half_width]
    behind = value[..., half_width:]
    return jnp.concatenate(
        [front * cosine - behind * sine, behind * cosine + front * sine], axis=-1
    )


def matmul(left, right):
    return jnp.dot(left, right, preferred_element_type=jnp.float32)


def times_transposed(left, right):
    return lax.dot_general(
        left, right, (((1,), (1,)), ((), ())), preferred_element_type=jnp.float32
    )


def over_rows(left, right):
    return lax.dot_general(
        left, right, (((0,), (0,)), ((), ())), preferred_element_type=jnp.float32
    )


LOW = jnp.bfloat16
WIDE = jnp.float32
EVERY = ("slot", "ctx", "wsh")


def swap(value, axis, bit):
    size = lax.axis_size(axis)
    return lax.ppermute(value, axis, [(i, i ^ bit) for i in range(size)])


def shift(value, amount):
    size = lax.axis_size("wsh")
    return lax.ppermute(value, "wsh", [(i, (i + amount) % size) for i in range(size)])


def ring_gather(value):
    return [value] + [shift(value, k) for k in range(1, lax.axis_size("wsh"))]


def ring_scatter(blocks):
    total = blocks[0].astype(WIDE)
    for k in range(1, len(blocks)):
        total = total + shift(blocks[k], -k).astype(WIDE)
    return total


def row_blocks(value, count):
    rows = value.shape[0] // count
    return [value[k * rows : (k + 1) * rows] for k in range(count)]


def add_low(left, right):
    return (left.astype(WIDE) + right.astype(WIDE)).astype(LOW)


def ctx_gather(piece):
    size = lax.axis_size("ctx")
    if size == 4:
        half = piece.shape[0] // 2
        one = swap(piece, "ctx", 1)
        two = swap(piece, "ctx", 2)
        front = swap(one[:half], "ctx", 2)
        behind = swap(two[half:], "ctx", 1)
        return [piece, one, two, jnp.concatenate([front, behind], axis=0)]
    pieces = [piece]
    bit = 1
    while bit < size:
        pieces = pieces + [swap(p, "ctx", bit) for p in pieces]
        bit *= 2
    return pieces


def ctx_reduce(pieces):
    size = len(pieces)
    if size == 4:
        half = pieces[0].shape[0] // 2
        front = swap(pieces[3][:half], "ctx", 1)
        behind = swap(pieces[3][half:], "ctx", 2)
        two = jnp.concatenate([add_low(pieces[2][:half], front), pieces[2][half:]], axis=0)
        one = jnp.concatenate([pieces[1][:half], add_low(pieces[1][half:], behind)], axis=0)
        one = swap(one, "ctx", 1)
        two = swap(two, "ctx", 2)
        return (pieces[0].astype(WIDE) + one.astype(WIDE) + two.astype(WIDE)).astype(LOW)
    while size > 1:
        size //= 2
        pieces = [add_low(pieces[i], swap(pieces[size + i], "ctx", size)) for i in range(size)]
    return pieces[0]


def chip_gather(piece):
    pieces = ctx_gather(piece)
    return pieces + [swap(p, "slot", 1) for p in pieces]


def assemble_kernel(extent, cuts, own, *refs):
    step = pl.program_id(0)
    ins, outs = refs[:extent], refs[extent:]
    for number in range(extent):

        @pl.when(step == number)
        def _(number=number):
            for (begin, width), out in zip(cuts, outs):
                out[:, 0] = ins[number][:, :, begin : begin + width].astype(out.dtype)


def assemble(pieces, own, kind, cuts=None):
    count = len(pieces)
    outer, inner, width = pieces[0].shape
    cuts = cuts or [(0, width)]
    results = pl.pallas_call(
        functools.partial(assemble_kernel, count, cuts),
        grid_spec=pltpu.PrefetchScalarGridSpec(
            num_scalar_prefetch=1,
            grid=(count,),
            in_specs=[pl.BlockSpec((outer, inner, width), lambda i, o: (0, 0, 0))] * count,
            out_specs=[
                pl.BlockSpec((outer, 1, inner, w), lambda i, o: (0, lax.bitwise_xor(i, o[0]), 0, 0))
                for _, w in cuts
            ],
        ),
        out_shape=[jax.ShapeDtypeStruct((outer, count, inner, w), kind) for _, w in cuts],
    )(own, *pieces)
    return results


def permute_kernel(own, source, out):
    out[0] = source[:, 0]


def relative(value, own):
    outer, count, inner, width = value.shape
    return pl.pallas_call(
        permute_kernel,
        grid_spec=pltpu.PrefetchScalarGridSpec(
            num_scalar_prefetch=1,
            grid=(count,),
            in_specs=[
                pl.BlockSpec(
                    (outer, 1, inner, width), lambda i, o: (0, lax.bitwise_xor(i, o[0]), 0, 0)
                )
            ],
            out_specs=pl.BlockSpec((1, outer, inner, width), lambda i, o: (i, 0, 0, 0)),
        ),
        out_shape=jax.ShapeDtypeStruct((count, outer, inner, width), value.dtype),
    )(own, value)


def pair_kernel(count, columns, *refs):
    step = pl.program_id(0)
    ins, gate, up = refs[:count], refs[count], refs[count + 1]
    inner = pl.num_programs(1)
    for number in range(count):

        @pl.when(step == number)
        def _(number=number):
            gate[...] = ins[number][0, 0].astype(gate.dtype)
            up[...] = ins[number][0, 1].astype(up.dtype)


def assemble_pair(pieces, columns):
    count = len(pieces)
    outer, _, rows, width = pieces[0].shape
    total = count * outer

    def source(number):
        def at(i, k, columns):
            return (jnp.where(i == number, k, jnp.where(i < number, 0, outer - 1)), 0, 0, 0)

        return pl.BlockSpec((1, 2, rows, width), at)

    def place(i, k, columns):
        return (0, columns[i * outer + k])

    return pl.pallas_call(
        lambda columns, *refs: pair_kernel(count, columns, *refs),
        grid_spec=pltpu.PrefetchScalarGridSpec(
            num_scalar_prefetch=1,
            grid=(count, outer),
            in_specs=[source(number) for number in range(count)],
            out_specs=[pl.BlockSpec((rows, width), place)] * 2,
        ),
        out_shape=[jax.ShapeDtypeStruct((rows, width * total), WIDE)] * 2,
    )(columns, *pieces)


def shards(
    tokens,
    cotangent,
    lengths,
    positions,
    token_ids,
    per_layer_table,
    w_query,
    w_key,
    w_value,
    w_output,
    laurel_left,
    laurel_right,
    w_gate,
    w_up,
    w_down,
    w_layer_gate,
    w_layer_proj,
    norm_gains,
    query_gain,
    key_gain,
):
    rows_dev, width = tokens.shape[1:]
    run = lax.axis_size("wsh")
    contexts = lax.axis_size("ctx")
    parts = 2 * contexts
    here = lax.axis_index("wsh")
    chip = lax.axis_index(("slot", "ctx"))
    own = jnp.full((1,), chip, jnp.int32)
    shard_rows = width // run
    heads_here = HEADS // run
    query_width = heads_here * HEAD_DIM
    groups = HEADS // KV_HEADS
    hidden_width = w_gate.shape[1] // run
    order = (here - jnp.arange(run, dtype=jnp.int32)) % run

    def absolute(stacked, axis=0):
        return jnp.take(stacked, order, axis=axis)

    tokens_run = jnp.concatenate(ring_gather(tokens[0]), axis=0)
    small = jnp.concatenate(
        [
            norm_gains.T,
            jnp.pad(
                jnp.concatenate([query_gain, key_gain])[None],
                ((0, 1), (0, shard_rows - 2 * query_gain.shape[0])),
            ),
        ],
        axis=0,
    )
    small_all = absolute(jnp.stack(ring_gather(small)))
    gains_full = small_all.transpose(1, 0, 2).reshape(8, width).astype(WIDE)
    gain_cut = query_gain.shape[0]
    query_gain_full = small_all[:, 6, :gain_cut].reshape(HEAD_DIM).astype(WIDE)
    key_gain_full = small_all[:, 6, gain_cut : 2 * gain_cut].reshape(HEAD_DIM).astype(WIDE)

    piece_rows = shard_rows // parts

    def share(weight):
        return lax.dynamic_slice_in_dim(weight, chip * piece_rows, piece_rows, 0)

    query_rows, key_rows, value_rows = share(w_query), share(w_key), share(w_value)

    def kv_head(index):
        return index * heads_here // groups

    received = []
    for k in range(run):
        target = (here + k) % run
        piece = jnp.concatenate(
            [
                lax.dynamic_slice_in_dim(query_rows, target * query_width, query_width, 1),
                lax.dynamic_slice_in_dim(key_rows, kv_head(target) * HEAD_DIM, HEAD_DIM, 1),
                lax.dynamic_slice_in_dim(value_rows, kv_head(target) * HEAD_DIM, HEAD_DIM, 1),
            ],
            axis=1,
        )
        received.append(piece if k == 0 else shift(piece, k))
    (w_heads,) = assemble(chip_gather(absolute(jnp.stack(received))), own, LOW)
    w_heads = w_heads.reshape(width, query_width + 2 * HEAD_DIM)

    indices = lax.all_gather(jnp.concatenate([token_ids, positions], axis=0), EVERY, axis=0)
    all_ids = indices[:, 0].reshape(-1)
    slot_places = lax.dynamic_index_in_dim(
        indices[:, 1].reshape(2, contexts, run, rows_dev), lax.axis_index("slot"), 0, False
    )
    context_order = jnp.bitwise_xor(
        jnp.arange(contexts, dtype=jnp.int32), lax.axis_index("ctx").astype(jnp.int32)
    )
    key_places = jnp.take(jnp.take(slot_places, context_order, axis=0), order, axis=1)
    run_places = key_places[0].reshape(run * rows_dev)
    key_places = key_places.reshape(-1)
    length = lengths[0]
    own_places = positions[0]

    piece_width = hidden_width // parts
    received = []
    for k in range(run):
        first = ((here + k) % run) * hidden_width + chip * piece_width
        piece = jnp.stack(
            [
                lax.dynamic_slice_in_dim(w_gate, first, piece_width, 1),
                lax.dynamic_slice_in_dim(w_up, first, piece_width, 1),
            ]
        )
        received.append(piece if k == 0 else shift(piece, k))
    mine = absolute(jnp.stack(received, axis=1), axis=1).reshape(2, width, piece_width)
    ff_pieces = chip_gather(mine)
    gate_weight = jnp.concatenate([p[0] for p in ff_pieces], axis=1)
    up_weight = jnp.concatenate([p[1] for p in ff_pieces], axis=1)
    down_weight = relative(w_down.reshape(1, parts, piece_width, width), own).reshape(
        hidden_width, width
    )
    laurel_weights = lax.all_gather(
        jnp.concatenate([laurel_left, laurel_right, w_layer_gate], axis=1), "wsh", axis=0, tiled=True
    )
    rank = laurel_left.shape[1]
    left_full = laurel_weights[:, :rank]
    right_full = laurel_weights[:, rank : 2 * rank]
    layer_gate_full = laurel_weights[:, 2 * rank :]
    layer_proj_full = lax.all_gather(w_layer_proj, "wsh", axis=0, tiled=True)

    vocab_rows = per_layer_table.shape[0]
    vocab_first = lax.axis_index(EVERY) * vocab_rows
    vocab_range = jnp.arange(vocab_rows, dtype=jnp.int32)

    def one_hot():
        return ((all_ids - vocab_first)[:, None] == vocab_range[None, :]).astype(LOW)

    layer_input = EMBED_SCALE * lax.psum_scatter(
        matmul(one_hot(), per_layer_table).astype(LOW), EVERY, scatter_dimension=0, tiled=True
    ).astype(WIDE)

    normed_run = rms_norm(tokens_run.astype(WIDE), gains_full[0])
    normed_low = normed_run.astype(LOW)
    tokens_f = tokens[0].astype(WIDE)
    normed = rms_norm(tokens_f, gains_full[0])
    normed_own = normed_low[:rows_dev]
    total_rows = run * rows_dev
    projected = matmul(normed_low, w_heads)
    query = projected[:, :query_width]
    key = projected[:, query_width : query_width + HEAD_DIM]
    value = projected[:, query_width + HEAD_DIM :]

    def query_path(raw, gain):
        return rotate(rms_norm(raw.reshape(total_rows, heads_here, HEAD_DIM), gain), run_places)

    def key_path(raw, gain):
        return rotate(rms_norm(raw.reshape(total_rows, 1, HEAD_DIM), gain), run_places)[:, 0]

    def value_path(raw):
        return rms_norm(raw, 1.0)

    q_low = query_path(query, query_gain_full).astype(LOW)
    k_low = key_path(key, key_gain_full).astype(LOW)
    v_low = value_path(value).astype(LOW)
    keys_values = jnp.concatenate(
        ctx_gather(jnp.concatenate([k_low, v_low], axis=1)), axis=0
    )
    keys_all = keys_values[:, :HEAD_DIM]
    values_all = keys_values[:, HEAD_DIM:]
    allowed = (key_places[None, :] <= run_places[:, None]) & (key_places < length)[None, :]
    scores = jnp.einsum("qhd,td->hqt", q_low, keys_all, preferred_element_type=WIDE)
    scores = jnp.where(allowed[None], scores, NEGATIVE)
    top = jnp.max(scores, axis=-1, keepdims=True)
    raised = jnp.exp(scores - top)
    probs = raised / jnp.sum(raised, axis=-1, keepdims=True)
    attended = jnp.einsum(
        "hqt,td->qhd", probs.astype(LOW), values_all, preferred_element_type=WIDE
    )
    attended_low = attended.astype(LOW).reshape(total_rows, query_width)
    attn_proj = ring_scatter(row_blocks(matmul(attended_low, w_output).astype(LOW), run))

    first_sum = tokens_f + rms_norm(attn_proj, gains_full[1])
    low_rank = matmul(normed_own, left_full)
    low_rank_low = low_rank.astype(LOW)
    laurel_out = times_transposed(low_rank_low, right_full)
    laurel = normed + rms_norm(laurel_out, gains_full[2])
    mixed = (first_sum + laurel) * HALF_ROOT
    ff_in_low = rms_norm(mixed, gains_full[3]).astype(LOW)

    ff_run = jnp.concatenate(ring_gather(ff_in_low), axis=0)
    gate = matmul(ff_run, gate_weight)
    upward = matmul(ff_run, up_weight)
    hidden_low = gated_product(gate, upward).astype(LOW)
    ff_out = ring_scatter(row_blocks(matmul(hidden_low, down_weight).astype(LOW), run))
    third_sum = mixed + rms_norm(ff_out, gains_full[4])
    third_low = third_sum.astype(LOW)

    layer_gate = matmul(third_low, layer_gate_full)
    gated_low = gated_product(layer_gate, layer_input).astype(LOW)
    layer_proj = matmul(gated_low, layer_proj_full)
    result = third_sum + rms_norm(layer_proj, gains_full[5])
    layer_out = result.astype(LOW)[None]

    valid = (own_places < length).astype(WIDE)
    grad_out = cotangent[0].astype(WIDE) * valid[:, None]
    _, pullback = jax.vjp(rms_norm, layer_proj, gains_full[5])
    grad_proj, grad_gain_five = pullback(grad_out)
    grad_proj_low = grad_proj.astype(LOW)
    grad_gated = times_transposed(grad_proj_low, layer_proj_full)
    _, pullback = jax.vjp(gated_product, layer_gate, layer_input)
    grad_lgate, grad_input = pullback(grad_gated)
    grad_lgate_low = grad_lgate.astype(LOW)
    grad_input_low = grad_input.astype(LOW)
    grad_third = grad_out + times_transposed(grad_lgate_low, layer_gate_full)
    _, pullback = jax.vjp(rms_norm, ff_out, gains_full[4])
    grad_ff, grad_gain_four = pullback(grad_third)
    grad_ff_low = grad_ff.astype(LOW)

    grad_ff_run = jnp.concatenate(ring_gather(grad_ff_low), axis=0)
    grad_hidden = times_transposed(grad_ff_run, down_weight)
    _, pullback = jax.vjp(gated_product, gate, upward)
    grad_gate, grad_upward = pullback(grad_hidden)
    grad_gate_low = grad_gate.astype(LOW)
    grad_upward_low = grad_upward.astype(LOW)
    grad_ff_in = ring_scatter(
        row_blocks(
            (
                times_transposed(grad_gate_low, gate_weight)
                + times_transposed(grad_upward_low, up_weight)
            ).astype(LOW),
            run,
        )
    )
    half = hidden_width // 2

    def slot_sum(make):
        other = swap(make(1), "slot", 1)
        return add_low(make(0), other)

    down_sum = slot_sum(
        lambda side: over_rows(hidden_low[:, side * half : (side + 1) * half], grad_ff_run).astype(LOW)
    )
    down_own = ctx_reduce(row_blocks(down_sum, contexts))
    (down_grad,) = assemble([p[None] for p in chip_gather(down_own)], own, WIDE)
    gate_sum = slot_sum(
        lambda side: over_rows(ff_run, grad_gate_low[:, side * half : (side + 1) * half]).astype(LOW)
    )
    up_sum = slot_sum(
        lambda side: over_rows(ff_run, grad_upward_low[:, side * half : (side + 1) * half]).astype(LOW)
    )
    pair_own = ctx_reduce(
        [
            jnp.stack(
                [
                    gate_sum[:, r * piece_width : (r + 1) * piece_width],
                    up_sum[:, r * piece_width : (r + 1) * piece_width],
                ]
            )
            for r in range(contexts)
        ]
    )
    received = []
    for k in range(run):
        piece = lax.dynamic_slice_in_dim(pair_own, ((here + k) % run) * shard_rows, shard_rows, 1)
        received.append(piece if k == 0 else shift(piece, k))
    pair_pieces = chip_gather(jnp.stack(received))
    part_range = jnp.arange(parts, dtype=jnp.int32)
    if piece_width % 128 == 0:
        columns = order[None, :] * parts + jnp.bitwise_xor(part_range, chip)[:, None]
        gate_grad, up_grad = assemble_pair(pair_pieces, columns.reshape(-1))
    else:
        stacked = absolute(jnp.stack(pair_pieces), axis=1)
        stacked = jnp.take(stacked, jnp.bitwise_xor(part_range, chip), axis=0)
        stacked = stacked.transpose(2, 3, 1, 0, 4).reshape(2, shard_rows, -1).astype(WIDE)
        gate_grad, up_grad = stacked[0], stacked[1]

    _, pullback = jax.vjp(rms_norm, mixed, gains_full[3])
    grad_mixed_norm, grad_gain_three = pullback(grad_ff_in)
    grad_branch = (grad_third + grad_mixed_norm) * HALF_ROOT
    _, pullback = jax.vjp(rms_norm, attn_proj, gains_full[1])
    grad_attn, grad_gain_one = pullback(grad_branch)
    grad_attn_low = grad_attn.astype(LOW)
    grad_attn_run = jnp.concatenate(ring_gather(grad_attn_low), axis=0)
    _, pullback = jax.vjp(rms_norm, laurel_out, gains_full[2])
    grad_laurel, grad_gain_two = pullback(grad_branch)
    grad_laurel_low = grad_laurel.astype(LOW)
    grad_rank_low = matmul(grad_laurel_low, right_full).astype(LOW)

    grad_att_low = times_transposed(grad_attn_run, w_output).astype(LOW)
    grad_att = grad_att_low.reshape(total_rows, heads_here, HEAD_DIM)
    row_delta = jnp.sum(grad_att.astype(WIDE) * attended, axis=-1)
    grad_probs = jnp.einsum("qhd,td->hqt", grad_att, values_all, preferred_element_type=WIDE)
    grad_scores = (probs * (grad_probs - row_delta.T[:, :, None])).astype(LOW)
    grad_q_rot = jnp.einsum("hqt,td->qhd", grad_scores, keys_all, preferred_element_type=WIDE)
    key_part = jnp.einsum("hqt,qhd->td", grad_scores, q_low, preferred_element_type=WIDE)
    value_part = jnp.einsum("hqt,qhd->td", probs.astype(LOW), grad_att, preferred_element_type=WIDE)
    kv_sum = ctx_reduce(
        row_blocks(jnp.concatenate([key_part, value_part], axis=1).astype(LOW), contexts)
    ).astype(WIDE)
    grad_k_rot, grad_v_norm = kv_sum[:, :HEAD_DIM], kv_sum[:, HEAD_DIM:]
    _, pullback = jax.vjp(query_path, query, query_gain_full)
    grad_query, grad_query_gain = pullback(grad_q_rot)
    _, pullback = jax.vjp(key_path, key, key_gain_full)
    grad_key, grad_key_gain = pullback(grad_k_rot)
    _, pullback = jax.vjp(value_path, value)
    (grad_value,) = pullback(grad_v_norm)
    grad_heads_low = jnp.concatenate([grad_query, grad_key, grad_value], axis=1).astype(LOW)
    grad_normed = (
        ring_scatter(row_blocks(times_transposed(grad_heads_low, w_heads).astype(LOW), run))
        + times_transposed(grad_rank_low, left_full)
        + grad_branch
    )
    _, pullback = jax.vjp(rms_norm, tokens_f, gains_full[0])
    grad_tokens, grad_gain_zero = pullback(grad_normed)
    tokens_grad = (grad_tokens + grad_branch).astype(LOW)[None]

    def group_sum(value):
        summed = add_low(value[:contexts], swap(value[contexts:], "slot", 1))
        return ctx_reduce([summed[r] for r in range(contexts)])

    output_part = over_rows(attended_low, grad_attn_run).astype(LOW)
    output_own = group_sum(
        relative(output_part.reshape(1, parts, query_width // parts, width), own)[:, 0]
    )
    (output_grad,) = assemble([p[None] for p in chip_gather(output_own)], own, WIDE)
    heads_part = over_rows(normed_low, grad_heads_low).astype(LOW)
    heads_own = group_sum(
        relative(heads_part.reshape(run, parts, piece_rows, query_width + 2 * HEAD_DIM), own)
    )
    received = []
    for k in range(run):
        piece = lax.dynamic_index_in_dim(heads_own, (here + k) % run, 0, False)
        received.append(piece if k == 0 else shift(piece, k))
    by_run = absolute(jnp.stack(received))
    query_piece = by_run[:, :, :query_width].transpose(1, 0, 2).reshape(piece_rows, -1)
    kv_pieces = []
    for begin in (query_width, query_width + HEAD_DIM):
        one = by_run[:, :, begin : begin + HEAD_DIM].astype(WIDE)
        one = one.reshape(KV_HEADS, run // KV_HEADS, piece_rows, HEAD_DIM).sum(axis=1)
        kv_pieces.append(one.astype(LOW).transpose(1, 0, 2).reshape(piece_rows, -1))
    heads_piece = jnp.concatenate([query_piece] + kv_pieces, axis=1)
    kv_width = KV_HEADS * HEAD_DIM
    query_all = HEADS * HEAD_DIM
    query_grad, key_grad, value_grad = assemble(
        [p[None] for p in chip_gather(heads_piece)],
        own,
        WIDE,
        [(0, query_all), (query_all, kv_width), (query_all + kv_width, kv_width)],
    )

    every_grad = lax.all_gather(grad_input_low, EVERY, axis=0, tiled=True)
    table_grad = EMBED_SCALE * over_rows(one_hot(), every_grad)
    left_grad = over_rows(normed_own, grad_rank_low)
    right_grad = over_rows(grad_laurel_low, low_rank_low)
    layer_gate_grad = over_rows(third_low, grad_lgate_low)
    layer_proj_grad = over_rows(gated_low, grad_proj_low)

    def all_sum(value):
        value = lax.psum_scatter(value.astype(LOW), "wsh", scatter_dimension=0, tiled=True)
        return lax.psum(value, ("slot", "ctx")).astype(WIDE)

    narrow = all_sum(jnp.concatenate([left_grad, right_grad, layer_gate_grad], axis=1))
    layer_proj_grad = all_sum(layer_proj_grad)
    vector = jnp.concatenate(
        [grad_query_gain.reshape(run, gain_cut), grad_key_gain.reshape(run, gain_cut)], axis=1
    )
    vector = jnp.pad(vector, ((0, 0), (0, shard_rows - 2 * gain_cut))).reshape(width)
    gain_sums = all_sum(
        jnp.stack(
            [
                grad_gain_zero,
                grad_gain_one,
                grad_gain_two,
                grad_gain_three,
                grad_gain_four,
                grad_gain_five,
                vector,
                jnp.zeros_like(vector),
            ],
            axis=1,
        )
    )
    return (
        layer_out,
        tokens_grad,
        table_grad,
        query_grad.reshape(shard_rows, query_all),
        key_grad.reshape(shard_rows, kv_width),
        value_grad.reshape(shard_rows, kv_width),
        output_grad.reshape(query_width, width),
        narrow[:, :rank],
        narrow[:, rank : 2 * rank],
        gate_grad,
        up_grad,
        down_grad.reshape(hidden_width, width),
        narrow[:, 2 * rank :],
        layer_proj_grad,
        gain_sums[:, :6],
        gain_sums[:gain_cut, 6],
        gain_sums[gain_cut : 2 * gain_cut, 6],
    )


def solution(mesh):
    placed = (
        P("slot", ("ctx", "wsh"), None),
        P("slot", ("ctx", "wsh"), None),
        P("slot"),
        P("slot", ("ctx", "wsh")),
        P("slot", ("ctx", "wsh")),
        P(("slot", "ctx", "wsh"), None),
        P("wsh", None),
        P("wsh", None),
        P("wsh", None),
        P("wsh", None),
        P("wsh", None),
        P("wsh", None),
        P("wsh", None),
        P("wsh", None),
        P("wsh", None),
        P("wsh", None),
        P("wsh", None),
        P("wsh", None),
        P("wsh"),
        P("wsh"),
    )
    return jax.shard_map(
        shards,
        mesh=mesh,
        in_specs=placed,
        out_specs=(
            P("slot", ("ctx", "wsh"), None),
            P("slot", ("ctx", "wsh"), None),
            P(("slot", "ctx", "wsh"), None),
            P("wsh", None),
            P("wsh", None),
            P("wsh", None),
            P("wsh", None),
            P("wsh", None),
            P("wsh", None),
            P("wsh", None),
            P("wsh", None),
            P("wsh", None),
            P("wsh", None),
            P("wsh", None),
            P("wsh", None),
            P("wsh"),
            P("wsh"),
        ),
        check_vma=False,
    )
```

time: 3880 us -> 1390 us (0.36)
  waiting for transfers between devices: 3060 us -> 574 us
  blocking collectives: 344 us -> 128 us
  starting transfers between devices: 1.52 us -> 175 us
  matrix products: 303 us -> 174 us
  Pallas kernels: 0 us -> 77.5 us
  local copies, waits for them, and re-layouts: 47.8 us -> 106 us
  other arithmetic: 87.1 us -> 128 us
    all_gather x24 -> x3, waiting for transfers between devices: 2590 us -> 0.02 us  [the longest x1 0.02 us: shards(): layer_proj_full = lax.all_gather(w_layer_proj, 'wsh', axis=0, tiled=True)]
    ppermute x0 -> x116, waiting for transfers between devices: none -> 574 us  [the longest x39 304 us: shift(): lax.ppermute(value, 'wsh', [(i, (i + amount) % size) for i in range(size)])]
    psum x1, waiting for transfers between devices: 270 us -> 0.03 us  [all_sum(): return lax.psum(value, ('slot', 'ctx')).astype(WIDE)]
    reduce_scatter x4, waiting for transfers between devices: 190 us -> 0.04 us  [the longest x1 0.03 us: shards(): lax.psum_scatter(matmul(one_hot(), per_layer_table).astype(LOW), EVERY, s...]
    all_gather x11 -> x1, blocking collectives: 303 us -> 114 us  [shards(): lax.all_gather(jnp.concatenate([token_ids, positions], axis=0), EVERY, ax...]
    ppermute x0 -> x116, starting transfers between devices: none -> 175 us  [the longest x39 107 us: shift(): lax.ppermute(value, 'wsh', [(i, (i + amount) % size) for i in range(size)])]
    pallas_call x0 -> x8, Pallas kernels: none -> 77.5 us  [the longest x1 29.4 us: assemble_pair(): pl.pallas_call(lambda columns, *refs: pair_kernel(count, columns, *refs),...]
    dot_general x12 -> x10, matrix products: 91.6 us -> 49.7 us  [matmul(): return jnp.dot(left, right, preferred_element_type=jnp.float32)]
  transfers between devices with their start and end apart: 29 -> 124, of which waited for: 21 -> 47; matrix products, arithmetic and copies ran while one was open for 10% -> 23% of each run, Pallas kernels for 0% -> 3%
where the time goes in v1:
time: 1390 us; the launch traced here: 1380 us
  waiting for transfers between devices  574 us (41%)
  starting transfers between devices  175 us (13%)
  matrix products  174 us (13%)
  other arithmetic  128 us (9%)
  blocking collectives  128 us (9%)
  local copies, waits for them, and re-layouts  106 us (8%)
  Pallas kernels  77.5 us (6%)
  between operations  19.4 us (1%)
    ppermute x39, waiting for transfers between devices, shift(): lax.ppermute(value, 'wsh', [(i, (i + amount) % size) for i in range(size)])  304 us
    ppermute x77, waiting for transfers between devices, swap(): return lax.ppermute(value, axis, [(i, i ^ bit) for i in range(size)])  270 us
    all_gather x1, blocking collectives, shards(): lax.all_gather(jnp.concatenate([token_ids, positions], axis=0), EVERY, ax...  114 us
    ppermute x39, starting transfers between devices, shift(): lax.ppermute(value, 'wsh', [(i, (i + amount) % size) for i in range(size)])  107 us
    ppermute x77, starting transfers between devices, swap(): return lax.ppermute(value, axis, [(i, i ^ bit) for i in range(size)])  67.8 us
    dot_general x13, matrix products, over_rows(): lax.dot_general(left, right, (((0,), (0,)), ((), ())), preferred_element_...  67 us
    dot_general x10, matrix products, matmul(): return jnp.dot(left, right, preferred_element_type=jnp.float32)  49.7 us
    dot_general x9, matrix products, times_transposed(): lax.dot_general(left, right, (((1,), (1,)), ((), ())), preferred_element_...  44.4 us
  transfers between devices with their start and end apart: 124, of which 47 were waited for; matrix products, arithmetic and copies ran while one was open for 23% of the time, Pallas kernels for 3%

profile of v1, /device:TPU:0, one launch (start us, length us, event | category | flops | bytes accessed | tf_op | source)
XLA Modules:
  0.0 1381.5 jit_solution(15568933286015988961)
XLA Ops:
  28.4 114.2 %all-gather.1 = s32[32,2,128]{2,1,0:T(2,128)S(1)} all-gather(s32[1,2,128]{2,1,0:T(2,128)S(1)} %add_bitcast_fusion), channel_id=2, replica_groups=mesh['slot'=2,'ctx'=4,'wsh'=4] {'slot','ctx','wsh'}, dimensions={0}, use_global_device_ids=true | all-gather | bytes 33792 | tf_op jit(solution)/shard_map/all_gather | solution.py:314
  143.3 14.8 %fusion.9 = bf16[4096,256]{1,0:T(8,128)(2,1)} fusion(bf16[4096,256]{1,0:T(8,128)(2,1)} %param.27, s32[4096]{0:T(1024)S(1)} %bitcast.476), kind=kOutput, calls=%fused_computation.28 | convolution fusion | flops 8607760384 | bytes 4210688 | tf_op jit(solution)/shard_map/dot_general | solution.py:53
  172.9 9.0 shard_map.324
  188.6 16.5 %collective-permute-done.8 = bf16[64,1024]{1,0:T(8,128)(2,1)} collective-permute-done((bf16[64,1024]{1,0:T(8,128)(2,1)S(1)}, bf16[64,1024]{1,0:T(8,128)(2,1)}, u32[]{:S(2)}, u32[]{:S(2)}) %collective-permute-start.8) | collective-permute-done | bytes 131104 | tf_op jit(solution)/shard_map/ppermute | solution.py:80
  205.7 6.1 collective-permute-done.7
  214.8 7.4 collective-permute-start.1
  226.4 7.2 collective-permute-start.9
  253.3 16.9 %collective-permute-done.1 = bf16[128,2048]{1,0:T(8,128)(2,1)} collective-permute-done((bf16[128,2048]{1,0:T(8,128)(2,1)S(1)}, bf16[128,2048]{1,0:T(8,128)(2,1)}, u32[]{:S(2)}, u32[]{:S(2)}) %collective-permute-start.1) | collective-permute-done | bytes 524320 | tf_op jit(solution)/shard_map/ppermute | solution.py:80
  272.6 42.4 %collective-permute-done.12 = bf16[2,64,1024]{2,1,0:T(8,128)(2,1)S(1)} collective-permute-done((bf16[2,64,1024]{2,1,0:T(8,128)(2,1)S(1)}, bf16[2,64,1024]{2,1,0:T(8,128)(2,1)S(1)}, u32[]{:S(2)}, u32[]{:S(2)}) %collective-permute-start.12) | collective-permute-done | bytes 262176 | tf_op jit(solution)/shard_map/ppermute | solution.py:75
  344.3 6.3 collective-permute-done.17
  353.6 26.6 %collective-permute-done.18 = bf16[512,512]{1,0:T(8,128)(2,1)} collective-permute-done((bf16[512,512]{1,0:T(8,128)(2,1)}, bf16[512,512]{1,0:T(8,128)(2,1)}, u32[]{:S(2)}, u32[]{:S(2)}) %collective-permute-start.18) | collective-permute-done | bytes 524320 | tf_op jit(solution)/shard_map/ppermute | solution.py:75
  393.9 12.7 fusion.175
  436.1 18.7 %collective-permute-done.22 = bf16[128,2048]{1,0:T(8,128)(2,1)} collective-permute-done((bf16[128,2048]{1,0:T(8,128)(2,1)}, bf16[128,2048]{1,0:T(8,128)(2,1)}, u32[]{:S(2)}, u32[]{:S(2)}) %collective-permute-start.22) | collective-permute-done | bytes 524320 | tf_op jit(solution)/shard_map/ppermute | solution.py:80
  463.0 9.3 collective-permute-start.25
  481.7 34.9 %collective-permute-done.25 = bf16[128,2048]{1,0:T(8,128)(2,1)S(1)} collective-permute-done((bf16[128,2048]{1,0:T(8,128)(2,1)S(1)}, bf16[128,2048]{1,0:T(8,128)(2,1)S(1)}, u32[]{:S(2)}, u32[]{:S(2)}) %collective-permute-start.25) | collective-permute-done | bytes 524320 | tf_op jit(solution)/shard_map/ppermute | solution.py:80
  522.7 12.3 multiply_convert_fusion.1
  544.4 12.4 collective-permute-done.40
  556.8 21.3 %collective-permute-done.39 = bf16[128,2048]{1,0:T(8,128)(2,1)S(1)} collective-permute-done((bf16[128,2048]{1,0:T(8,128)(2,1)S(1)}, bf16[128,2048]{1,0:T(8,128)(2,1)S(1)}, u32[]{:S(2)}, u32[]{:S(2)}) %collective-permute-start.39) | collective-permute-done | bytes 524320 | tf_op jit(solution)/shard_map/ppermute | solution.py:80
  588.7 9.8 collective-permute-start.43
  601.3 9.7 collective-permute-done.43
  611.0 34.8 %collective-permute-done.42 = bf16[128,2048]{1,0:T(8,128)(2,1)S(1)} collective-permute-done((bf16[128,2048]{1,0:T(8,128)(2,1)S(1)}, bf16[128,2048]{1,0:T(8,128)(2,1)S(1)}, u32[]{:S(2)}, u32[]{:S(2)}) %collective-permute-start.42) | collective-permute-done | bytes 524320 | tf_op jit(solution)/shard_map/ppermute | solution.py:80
  645.8 15.8 %fusion.16 = (bf16[512,2048]{1,0:T(8,128)(2,1)}, bf16[512,2048]{1,0:T(8,128)(2,1)S(1)}) fusion(f32[512,2048]{1,0:T(8,128)} %fusion.161, f32[512,2048]{1,0:T(8,128)} %get-tuple-element.294, bf16[2048,2048]{1,0:T(8,128)(2,1)} %bitcast.411, bf16[128,2048]{1,0:T(8,128)(2,1)S(1)} %collective-permute-done.43, bf16[128,2048]{1,0:T(8,128)(2,1)S(1)} %collective-permute-done.42, ...), kind=kOutput, calls=%fused_computation.35 | convolution fusion | flops 4332716032 | bytes 23068672 | tf_op jit(solution)/shard_map/dot_general | solution.py:57
  661.6 7.7 fusion.178
  669.5 8.3 add_convert_fusion.5
  681.8 12.9 collective-permute-done.46
  694.8 19.8 %collective-permute-done.45 = bf16[128,2048]{1,0:T(8,128)(2,1)S(1)} collective-permute-done((bf16[128,2048]{1,0:T(8,128)(2,1)S(1)}, bf16[128,2048]{1,0:T(8,128)(2,1)S(1)}, u32[]{:S(2)}, u32[]{:S(2)}) %collective-permute-start.45) | collective-permute-done | bytes 524320 | tf_op jit(solution)/shard_map/ppermute | solution.py:80
  719.1 11.8 collective-permute-start.49
  733.0 10.3 collective-permute-done.49
  743.3 32.7 %collective-permute-done.48 = bf16[128,2048]{1,0:T(8,128)(2,1)S(1)} collective-permute-done((bf16[128,2048]{1,0:T(8,128)(2,1)S(1)}, bf16[128,2048]{1,0:T(8,128)(2,1)S(1)}, u32[]{:S(2)}, u32[]{:S(2)}) %collective-permute-start.48) | collective-permute-done | bytes 524320 | tf_op jit(solution)/shard_map/ppermute | solution.py:80
  829.6 7.8 collective-permute-done.56
  837.4 17.4 %collective-permute-done.55 = bf16[128,2048]{1,0:T(8,128)(2,1)S(1)} collective-permute-done((bf16[128,2048]{1,0:T(8,128)(2,1)}, bf16[128,2048]{1,0:T(8,128)(2,1)S(1)}, u32[]{:S(2)}, u32[]{:S(2)}) %collective-permute-start.55) | collective-permute-done | bytes 524320 | tf_op jit(solution)/shard_map/ppermute | solution.py:80
  862.0 6.4 convolution_convert_fusion.1
  893.3 6.3 fusion.44
  908.5 6.6 shard_map.325
  972.8 9.9 collective-permute-done.90
  1004.5 47.0 %collective-permute-done.104 = bf16[128,2048]{1,0:T(8,128)(2,1)} collective-permute-done((bf16[128,2048]{1,0:T(8,128)(2,1)}, bf16[128,2048]{1,0:T(8,128)(2,1)}, u32[]{:S(2)}, u32[]{:S(2)}) %collective-permute-start.104) | collective-permute-done | bytes 524320 | tf_op jit(solution)/shard_map/ppermute | solution.py:75
  1052.2 8.6 collective-permute-done.106
  1073.7 13.2 collective-permute-start.64
  1100.9 12.3 collective-permute-start.92
  1116.2 20.5 %collective-permute-done.93 = bf16[2,512,256]{2,1,0:T(8,128)(2,1)} collective-permute-done((bf16[2,512,256]{2,1,0:T(8,128)(2,1)}, bf16[2,512,256]{2,1,0:T(8,128)(2,1)}, u32[]{:S(2)}, u32[]{:S(2)}) %collective-permute-start.93) | collective-permute-done | bytes 524320 | tf_op jit(solution)/shard_map/ppermute | solution.py:80
  1148.1 38.8 %collective-permute-done.80 = bf16[32,2048]{1,0:T(8,128)(2,1)S(1)} collective-permute-done((bf16[32,2048]{1,0:T(8,128)(2,1)S(1)}, bf16[32,2048]{1,0:T(8,128)(2,1)S(1)}, u32[]{:S(2)}, u32[]{:S(2)}) %collective-permute-start.80) | collective-permute-done | bytes 131104 | tf_op jit(solution)/shard_map/ppermute | solution.py:75
  1192.8 7.0 collective-permute-done.65
  1202.5 13.8 collective-permute-done.66
  1226.6 13.6 psum.23
  1267.0 20.9 %collective-permute-done.97 = bf16[2,2,512,256]{3,2,1,0:T(8,128)(2,1)} collective-permute-done((bf16[2,2,512,256]{3,2,1,0:T(8,128)(2,1)S(1)}, bf16[2,2,512,256]{3,2,1,0:T(8,128)(2,1)}, u32[]{:S(2)}, u32[]{:S(2)}) %collective-permute-start.97) | collective-permute-done | bytes 1048608 | tf_op jit(solution)/shard_map/ppermute | solution.py:75
  1297.2 24.2 %fusion.8 = f32[4096,256]{1,0:T(8,128)} fusion(bf16[4096,256]{1,0:T(8,128)(2,1)} %all-gather.10.cloned.1.call-done, s32[4096]{0:T(1024)S(1)} %bitcast.477), kind=kOutput, calls=%fused_computation.25 | convolution fusion | flops 8607760384 | bytes 6307840 | tf_op jit(solution)/shard_map/dot_general | solution.py:63
  1334.5 10.0 shard_map.330
  1344.6 29.4 %shard_map.329 = (f32[512,8192]{1,0:T(8,128)}, f32[512,8192]{1,0:T(8,128)}) custom-call(s32[32]{0:T(128)} %add.633.columns, bf16[4,2,512,256]{3,2,1,0:T(8,128)(2,1)} %pad_maximum_fusion.8.refs_0_, bf16[4,2,512,256]{3,2,1,0:T(8,128)(2,1)} %collective-permute-done.95.refs_1_, bf16[4,2,512,256]{3,2,1,0:T(8,128)(2,1)} %collective-permute-done.96.refs_2_, ...), custom_call_target="tpu_custom_call" | custom-call | tf_op jit(solution)/shard_map/pallas_call | solution.py:221
  (895 shorter events, 486.0 us)
Async XLA Ops:
  8.1 412.3 %all-gather.6.cloned.1.call-start = ((), (), s32[]{:S(2)}) async-start(), calls=%async_computation.4 | async-start | bytes 1966080 | tf_op jit(solution)/shard_map/all_gather | solution.py:346
  12.1 568.8 %all-gather.8.cloned.1.call-start = ((), (), s32[]{:S(2)}) async-start(), calls=%async_computation.6 | async-start | bytes 1310720 | tf_op jit(solution)/shard_map/all_gather | solution.py:353
  14.2 167.8 %collective-permute-start.5 = (bf16[8,512]{1,0:T(8,128)(2,1)}, bf16[8,512]{1,0:T(8,128)(2,1)}, u32[]{:S(2)}, u32[]{:S(2)}) collective-permute-start(bf16[8,512]{1,0:T(8,128)(2,1)} %fusion.130), channel_id=1, source_target_pairs={{0,3},{1,0},{2,1},{3,2},{4,7},{5,4},{6,5},{7,6},{8,11},{9,8},{10,9... | collective-permute-start | bytes 24584 | tf_op jit(solution)/shard_map/ppermute | solution.py:80
  19.2 162.8 %collective-permute-start.4 = (bf16[8,512]{1,0:T(8,128)(2,1)}, bf16[8,512]{1,0:T(8,128)(2,1)}, u32[]{:S(2)}, u32[]{:S(2)}) collective-permute-start(bf16[8,512]{1,0:T(8,128)(2,1)} %fusion.130), channel_id=1, source_target_pairs={{0,2},{1,3},{2,0},{3,1},{4,6},{5,7},{6,4},{7,5},{8,10},{9,11},{10,... | collective-permute-start | bytes 24584 | tf_op jit(solution)/shard_map/ppermute | solution.py:80
  19.2 166.6 %collective-permute-start.3 = (bf16[8,512]{1,0:T(8,128)(2,1)}, bf16[8,512]{1,0:T(8,128)(2,1)}, u32[]{:S(2)}, u32[]{:S(2)}) collective-permute-start(bf16[8,512]{1,0:T(8,128)(2,1)} %fusion.130), channel_id=1, source_target_pairs={{0,1},{1,2},{2,3},{3,0},{4,5},{5,6},{6,7},{7,4},{8,9},{9,10},{10,1... | collective-permute-start | bytes 24584 | tf_op jit(solution)/shard_map/ppermute | solution.py:80
  23.5 202.3 %collective-permute-start.29 = (bf16[2,512,256]{2,1,0:T(8,128)(2,1)}, bf16[2,512,256]{2,1,0:T(8,128)(2,1)}, u32[]{:S(2)}, u32[]{:S(2)}) collective-permute-start(bf16[2,512,256]{2,1,0:T(8,128)(2,1)} %pad_maximum_fusion.18), channel_id=1, source_target_pairs={{0,3},{1,0},{2,1},{3,2},{4,7},{5,4},{6,5},{7,6},{8,11},{9,8},{10,9... | collective-permute-start | bytes 1572872 | tf_op jit(solution)/shard_map/ppermute | solution.py:80
  27.1 199.3 %collective-permute-start.28 = (bf16[2,512,256]{2,1,0:T(8,128)(2,1)}, bf16[2,512,256]{2,1,0:T(8,128)(2,1)}, u32[]{:S(2)}, u32[]{:S(2)}) collective-permute-start(bf16[2,512,256]{2,1,0:T(8,128)(2,1)} %pad_maximum_fusion.17), channel_id=1, source_target_pairs={{0,2},{1,3},{2,0},{3,1},{4,6},{5,7},{6,4},{7,5},{8,10},{9,11},{10,... | collective-permute-start | bytes 1572872 | tf_op jit(solution)/shard_map/ppermute | solution.py:80
  28.4 552.5 %reduce-scatter.5.cloned.1.call-start = ((), (), s32[]{:S(2)}) async-start(), calls=%async_computation.5 | async-start | bytes 2162688 | tf_op jit(solution)/shard_map/reduce_scatter | solution.py:362
  158.1 1068.5 %reduce-scatter.11.cloned.1.call-start = ((), (), s32[]{:S(2)}) async-start(), calls=%async_computation.10 | async-start | bytes 40960 | tf_op jit(solution)/shard_map/reduce_scatter | solution.py:583
  182.0 51.7 %collective-permute-start.27 = (bf16[2,512,256]{2,1,0:T(8,128)(2,1)}, bf16[2,512,256]{2,1,0:T(8,128)(2,1)}, u32[]{:S(2)}, u32[]{:S(2)}) collective-permute-start(bf16[2,512,256]{2,1,0:T(8,128)(2,1)} %pad_maximum_fusion.16), channel_id=1, source_target_pairs={{0,1},{1,2},{2,3},{3,0},{4,5},{5,6},{6,7},{7,4},{8,9},{9,10},{10,1... | collective-permute-start | bytes 1572872 | tf_op jit(solution)/shard_map/ppermute | solution.py:80
  214.8 55.4 %collective-permute-start.1 = (bf16[128,2048]{1,0:T(8,128)(2,1)S(1)}, bf16[128,2048]{1,0:T(8,128)(2,1)}, u32[]{:S(2)}, u32[]{:S(2)}) collective-permute-start(bf16[128,2048]{1,0:T(8,128)(2,1)S(1)} %bitcast.405), channel_id=1, source_target_pairs={{0,2},{1,3},{2,0},{3,1},{4,6},{5,7},{6,4},{7,5},{8,10},{9,11},{10,... | collective-permute-start | bytes 1572872 | tf_op jit(solution)/shard_map/ppermute | solution.py:80
  225.9 44.3 %collective-permute-start = (bf16[128,2048]{1,0:T(8,128)(2,1)S(1)}, bf16[128,2048]{1,0:T(8,128)(2,1)}, u32[]{:S(2)}, u32[]{:S(2)}) collective-permute-start(bf16[128,2048]{1,0:T(8,128)(2,1)S(1)} %bitcast.406), channel_id=1, source_target_pairs={{0,1},{1,2},{2,3},{3,0},{4,5},{5,6},{6,7},{7,4},{8,9},{9,10},{10,1... | collective-permute-start | bytes 1572872 | tf_op jit(solution)/shard_map/ppermute | solution.py:80
  250.3 68.2 %collective-permute-start.13 = (bf16[4,64,1024]{2,1,0:T(8,128)(2,1)S(1)}, bf16[4,64,1024]{2,1,0:T(8,128)(2,1)S(1)}, u32[]{:S(2)}, u32[]{:S(2)}) collective-permute-start(bf16[4,64,1024]{2,1,0:T(8,128)(2,1)S(1)} %broadcast_select_fusion.2.refs_0_), channel_id=1, source_target_pairs={{0,16},{16,0},{1,17},{17,1},{2,18},{18,2},{3,19},{19,3},{4,20},{20... | collective-permute-start | bytes 1572872 | tf_op jit(solution)/shard_map/ppermute | solution.py:75
  251.3 172.2 %collective-permute-start.30 = (bf16[2,2048,256]{2,1,0:T(8,128)(2,1)}, bf16[2,2048,256]{2,1,0:T(8,128)(2,1)}, u32[]{:S(2)}, u32[]{:S(2)}) collective-permute-start(bf16[2,2048,256]{2,1,0:T(8,128)(2,1)} %bitcast_select_fusion.4), channel_id=1, source_target_pairs={{0,4},{4,0},{8,12},{12,8},{1,5},{5,1},{9,13},{13,9},{2,6},{6,2},{1... | collective-permute-start | bytes 6291464 | tf_op jit(solution)/shard_map/ppermute | solution.py:75
  270.2 44.8 %collective-permute-start.12 = (bf16[2,64,1024]{2,1,0:T(8,128)(2,1)S(1)}, bf16[2,64,1024]{2,1,0:T(8,128)(2,1)S(1)}, u32[]{:S(2)}, u32[]{:S(2)}) collective-permute-start(bf16[2,64,1024]{2,1,0:T(8,128)(2,1)S(1)} %slice.600), channel_id=1, source_target_pairs={{0,4},{4,0},{8,12},{12,8},{1,5},{5,1},{9,13},{13,9},{2,6},{6,2},{1... | collective-permute-start | bytes 786440 | tf_op jit(solution)/shard_map/ppermute | solution.py:75
  272.0 48.5 %collective-permute-start.14 = (bf16[4,64,1024]{2,1,0:T(8,128)(2,1)}, bf16[4,64,1024]{2,1,0:T(8,128)(2,1)S(1)}, u32[]{:S(2)}, u32[]{:S(2)}) collective-permute-start(bf16[4,64,1024]{2,1,0:T(8,128)(2,1)} %collective-permute-done.9.refs_1_), channel_id=1, source_target_pairs={{0,16},{16,0},{1,17},{17,1},{2,18},{18,2},{3,19},{19,3},{4,20},{20... | collective-permute-start | bytes 1572872 | tf_op jit(solution)/shard_map/ppermute | solution.py:75
  272.1 49.3 %collective-permute-start.15 = (bf16[4,64,1024]{2,1,0:T(8,128)(2,1)}, bf16[4,64,1024]{2,1,0:T(8,128)(2,1)}, u32[]{:S(2)}, u32[]{:S(2)}) collective-permute-start(bf16[4,64,1024]{2,1,0:T(8,128)(2,1)} %collective-permute-done.10.refs_2_), channel_id=1, source_target_pairs={{0,16},{16,0},{1,17},{17,1},{2,18},{18,2},{3,19},{19,3},{4,20},{20... | collective-permute-start | bytes 1572872 | tf_op jit(solution)/shard_map/ppermute | solution.py:75
  318.5 107.6 %collective-permute-start.31 = (bf16[2,2048,256]{2,1,0:T(8,128)(2,1)}, bf16[2,2048,256]{2,1,0:T(8,128)(2,1)}, u32[]{:S(2)}, u32[]{:S(2)}) collective-permute-start(bf16[2,2048,256]{2,1,0:T(8,128)(2,1)} %bitcast_select_fusion.4), channel_id=1, source_target_pairs={{0,8},{4,12},{8,0},{12,4},{1,9},{5,13},{9,1},{13,5},{2,10},{6,14},... | collective-permute-start | bytes 6291464 | tf_op jit(solution)/shard_map/ppermute | solution.py:75
  321.4 141.6 %collective-permute-start.33 = (bf16[2,2048,256]{2,1,0:T(8,128)(2,1)}, bf16[2,2048,256]{2,1,0:T(8,128)(2,1)}, u32[]{:S(2)}, u32[]{:S(2)}) collective-permute-start(bf16[2,2048,256]{2,1,0:T(8,128)(2,1)} %bitcast_select_fusion.4), channel_id=1, source_target_pairs={{0,16},{16,0},{1,17},{17,1},{2,18},{18,2},{3,19},{19,3},{4,20},{20... | collective-permute-start | bytes 6291464 | tf_op jit(solution)/shard_map/ppermute | solution.py:75
  463.0 53.6 %collective-permute-start.25 = (bf16[128,2048]{1,0:T(8,128)(2,1)S(1)}, bf16[128,2048]{1,0:T(8,128)(2,1)S(1)}, u32[]{:S(2)}, u32[]{:S(2)}) collective-permute-start(bf16[128,2048]{1,0:T(8,128)(2,1)S(1)} %multiply_convert_fusion.2), channel_id=1, source_target_pairs={{0,2},{1,3},{2,0},{3,1},{4,6},{5,7},{6,4},{7,5},{8,10},{9,11},{10,... | collective-permute-start | bytes 1572872 | tf_op jit(solution)/shard_map/ppermute | solution.py:80
  598.5 47.3 %collective-permute-start.42 = (bf16[128,2048]{1,0:T(8,128)(2,1)S(1)}, bf16[128,2048]{1,0:T(8,128)(2,1)S(1)}, u32[]{:S(2)}, u32[]{:S(2)}) collective-permute-start(bf16[128,2048]{1,0:T(8,128)(2,1)S(1)} %fusion.33), channel_id=1, source_target_pairs={{0,2},{1,3},{2,0},{3,1},{4,6},{5,7},{6,4},{7,5},{8,10},{9,11},{10,... | collective-permute-start | bytes 1572872 | tf_op jit(solution)/shard_map/ppermute | solution.py:80
  601.1 44.7 %collective-permute-start.41 = (bf16[128,2048]{1,0:T(8,128)(2,1)S(1)}, bf16[128,2048]{1,0:T(8,128)(2,1)S(1)}, u32[]{:S(2)}, u32[]{:S(2)}) collective-permute-start(bf16[128,2048]{1,0:T(8,128)(2,1)S(1)} %fusion.33), channel_id=1, source_target_pairs={{0,1},{1,2},{2,3},{3,0},{4,5},{5,6},{6,7},{7,4},{8,9},{9,10},{10,1... | collective-permute-start | bytes 1572872 | tf_op jit(solution)/shard_map/ppermute | solution.py:80
  730.9 45.1 %collective-permute-start.48 = (bf16[128,2048]{1,0:T(8,128)(2,1)S(1)}, bf16[128,2048]{1,0:T(8,128)(2,1)S(1)}, u32[]{:S(2)}, u32[]{:S(2)}) collective-permute-start(bf16[128,2048]{1,0:T(8,128)(2,1)S(1)} %get-tuple-element.249), channel_id=1, source_target_pairs={{0,2},{1,3},{2,0},{3,1},{4,6},{5,7},{6,4},{7,5},{8,10},{9,11},{10,... | collective-permute-start | bytes 1572872 | tf_op jit(solution)/shard_map/ppermute | solution.py:80
  731.4 44.6 %collective-permute-start.47 = (bf16[128,2048]{1,0:T(8,128)(2,1)S(1)}, bf16[128,2048]{1,0:T(8,128)(2,1)S(1)}, u32[]{:S(2)}, u32[]{:S(2)}) collective-permute-start(bf16[128,2048]{1,0:T(8,128)(2,1)S(1)} %get-tuple-element.249), channel_id=1, source_target_pairs={{0,1},{1,2},{2,3},{3,0},{4,5},{5,6},{6,7},{7,4},{8,9},{9,10},{10,1... | collective-permute-start | bytes 1572872 | tf_op jit(solution)/shard_map/ppermute | solution.py:80
  859.4 398.2 %reduce-scatter.9.cloned.1.call-start = ((), (), s32[]{:S(2)}) async-start(), calls=%async_computation.9 | async-start | bytes 1310720 | tf_op jit(solution)/shard_map/reduce_scatter | solution.py:583
  861.9 395.6 %reduce-scatter.7.cloned.1.call-start = ((), (), s32[]{:S(2)}) async-start(), calls=%async_computation.8 | async-start | bytes 1966080 | tf_op jit(solution)/shard_map/reduce_scatter | solution.py:583
  868.4 90.9 %collective-permute-start.87 = (bf16[2048,1024]{1,0:T(8,128)(2,1)}, bf16[2048,1024]{1,0:T(8,128)(2,1)}, u32[]{:S(2)}, u32[]{:S(2)}) collective-permute-start(bf16[2048,1024]{1,0:T(8,128)(2,1)} %convolution_convert_fusion.1), channel_id=1, source_target_pairs={{0,16},{16,0},{1,17},{17,1},{2,18},{18,2},{3,19},{19,3},{4,20},{20... | collective-permute-start | bytes 12582920 | tf_op jit(solution)/shard_map/ppermute | solution.py:75
  872.9 79.8 %collective-permute-start.86 = (bf16[2048,1024]{1,0:T(8,128)(2,1)}, bf16[2048,1024]{1,0:T(8,128)(2,1)}, u32[]{:S(2)}, u32[]{:S(2)}) collective-permute-start(bf16[2048,1024]{1,0:T(8,128)(2,1)} %convolution_convert_fusion.2), channel_id=1, source_target_pairs={{0,16},{16,0},{1,17},{17,1},{2,18},{18,2},{3,19},{19,3},{4,20},{20... | collective-permute-start | bytes 12582920 | tf_op jit(solution)/shard_map/ppermute | solution.py:75
  938.2 359.0 %all-gather.10.cloned.1.call-start = ((), (), s32[]{:S(2)}) async-start(), calls=%async_computation.7 | async-start | bytes 2162688 | tf_op jit(solution)/shard_map/all_gather | solution.py:575
  944.9 50.2 %collective-permute-start.78 = (bf16[64,2048]{1,0:T(8,128)(2,1)}, bf16[64,2048]{1,0:T(8,128)(2,1)S(1)}, u32[]{:S(2)}, u32[]{:S(2)}) collective-permute-start(bf16[64,2048]{1,0:T(8,128)(2,1)} %fusion.86), channel_id=1, source_target_pairs={{0,4},{4,0},{8,12},{12,8},{1,5},{5,1},{9,13},{13,9},{2,6},{6,2},{1... | collective-permute-start | bytes 786440 | tf_op jit(solution)/shard_map/ppermute | solution.py:75
  945.9 51.2 %collective-permute-start.79 = (bf16[64,2048]{1,0:T(8,128)(2,1)}, bf16[64,2048]{1,0:T(8,128)(2,1)S(1)}, u32[]{:S(2)}, u32[]{:S(2)}) collective-permute-start(bf16[64,2048]{1,0:T(8,128)(2,1)} %fusion.86), channel_id=1, source_target_pairs={{0,8},{4,12},{8,0},{12,4},{1,9},{5,13},{9,1},{13,5},{2,10},{6,14},... | collective-permute-start | bytes 786440 | tf_op jit(solution)/shard_map/ppermute | solution.py:75
  990.0 97.0 %collective-permute-start.91 = (bf16[2,2048,256]{2,1,0:T(8,128)(2,1)}, bf16[2,2048,256]{2,1,0:T(8,128)(2,1)}, u32[]{:S(2)}, u32[]{:S(2)}) collective-permute-start(bf16[2,2048,256]{2,1,0:T(8,128)(2,1)} %pad_maximum_fusion.7), channel_id=1, source_target_pairs={{0,8},{4,12},{8,0},{12,4},{1,9},{5,13},{9,1},{13,5},{2,10},{6,14},... | collective-permute-start | bytes 6291464 | tf_op jit(solution)/shard_map/ppermute | solution.py:75
  995.1 91.9 %collective-permute-start.89 = (bf16[2,2048,256]{2,1,0:T(8,128)(2,1)}, bf16[2,2048,256]{2,1,0:T(8,128)(2,1)}, u32[]{:S(2)}, u32[]{:S(2)}) collective-permute-start(bf16[2,2048,256]{2,1,0:T(8,128)(2,1)} %pad_maximum_fusion.6), channel_id=1, source_target_pairs={{0,4},{4,0},{8,12},{12,8},{1,5},{5,1},{9,13},{13,9},{2,6},{6,2},{1... | collective-permute-start | bytes 6291464 | tf_op jit(solution)/shard_map/ppermute | solution.py:75
  997.1 54.4 %collective-permute-start.104 = (bf16[128,2048]{1,0:T(8,128)(2,1)}, bf16[128,2048]{1,0:T(8,128)(2,1)}, u32[]{:S(2)}, u32[]{:S(2)}) collective-permute-start(bf16[128,2048]{1,0:T(8,128)(2,1)} %get-tuple-element.179), channel_id=1, source_target_pairs={{0,8},{4,12},{8,0},{12,4},{1,9},{5,13},{9,1},{13,5},{2,10},{6,14},... | collective-permute-start | bytes 1572872 | tf_op jit(solution)/shard_map/ppermute | solution.py:75
  997.1 63.6 %collective-permute-start.106 = (bf16[128,2048]{1,0:T(8,128)(2,1)}, bf16[128,2048]{1,0:T(8,128)(2,1)}, u32[]{:S(2)}, u32[]{:S(2)}) collective-permute-start(bf16[128,2048]{1,0:T(8,128)(2,1)} %get-tuple-element.178), channel_id=1, source_target_pairs={{0,4},{4,0},{8,12},{12,8},{1,5},{5,1},{9,13},{13,9},{2,6},{6,2},{1... | collective-permute-start | bytes 1572872 | tf_op jit(solution)/shard_map/ppermute | solution.py:75
  998.6 322.9 %all-reduce.9.cloned.1.call-start = ((), (), s32[]{:S(2)}) async-start(), calls=%async_computation.11 | async-start | bytes 1310720 | tf_op jit(solution)/shard_map/psum | solution.py:584
  1002.5 63.9 %collective-permute-start.61 = (bf16[4,64,1024]{2,1,0:T(8,128)(2,1)S(1)}, bf16[4,64,1024]{2,1,0:T(8,128)(2,1)S(1)}, u32[]{:S(2)}, u32[]{:S(2)}) collective-permute-start(bf16[4,64,1024]{2,1,0:T(8,128)(2,1)S(1)} %pad_maximum_fusion.21), channel_id=1, source_target_pairs={{0,8},{4,12},{8,0},{12,4},{1,9},{5,13},{9,1},{13,5},{2,10},{6,14},... | collective-permute-start | bytes 1572872 | tf_op jit(solution)/shard_map/ppermute | solution.py:75
  1063.8 78.9 %collective-permute-start.107 = (bf16[256,2048]{1,0:T(8,128)(2,1)}, bf16[256,2048]{1,0:T(8,128)(2,1)}, u32[]{:S(2)}, u32[]{:S(2)}) collective-permute-start(bf16[256,2048]{1,0:T(8,128)(2,1)} %pad_maximum_fusion.12), channel_id=1, source_target_pairs={{0,8},{4,12},{8,0},{12,4},{1,9},{5,13},{9,1},{13,5},{2,10},{6,14},... | collective-permute-start | bytes 3145736 | tf_op jit(solution)/shard_map/ppermute | solution.py:75
  1066.3 77.8 %collective-permute-start.105 = (bf16[256,2048]{1,0:T(8,128)(2,1)}, bf16[256,2048]{1,0:T(8,128)(2,1)}, u32[]{:S(2)}, u32[]{:S(2)}) collective-permute-start(bf16[256,2048]{1,0:T(8,128)(2,1)} %pad_maximum_fusion.11), channel_id=1, source_target_pairs={{0,4},{4,0},{8,12},{12,8},{1,5},{5,1},{9,13},{13,9},{2,6},{6,2},{1... | collective-permute-start | bytes 3145736 | tf_op jit(solution)/shard_map/ppermute | solution.py:75
  1139.8 82.3 %collective-permute-start.95 = (bf16[4,2,512,256]{3,2,1,0:T(8,128)(2,1)}, bf16[4,2,512,256]{3,2,1,0:T(8,128)(2,1)}, u32[]{:S(2)}, u32[]{:S(2)}) collective-permute-start(bf16[4,2,512,256]{3,2,1,0:T(8,128)(2,1)} %pad_maximum_fusion.8.refs_0_), channel_id=1, source_target_pairs={{0,4},{4,0},{8,12},{12,8},{1,5},{5,1},{9,13},{13,9},{2,6},{6,2},{1... | collective-permute-start | bytes 6291464 | tf_op jit(solution)/shard_map/ppermute | solution.py:75
  1140.4 83.3 %collective-permute-start.96 = (bf16[4,2,512,256]{3,2,1,0:T(8,128)(2,1)}, bf16[4,2,512,256]{3,2,1,0:T(8,128)(2,1)}, u32[]{:S(2)}, u32[]{:S(2)}) collective-permute-start(bf16[4,2,512,256]{3,2,1,0:T(8,128)(2,1)} %pad_maximum_fusion.8.refs_0_), channel_id=1, source_target_pairs={{0,8},{4,12},{8,0},{12,4},{1,9},{5,13},{9,1},{13,5},{2,10},{6,14},... | collective-permute-start | bytes 6291464 | tf_op jit(solution)/shard_map/ppermute | solution.py:75
  1141.5 45.4 %collective-permute-start.80 = (bf16[32,2048]{1,0:T(8,128)(2,1)S(1)}, bf16[32,2048]{1,0:T(8,128)(2,1)S(1)}, u32[]{:S(2)}, u32[]{:S(2)}) collective-permute-start(bf16[32,2048]{1,0:T(8,128)(2,1)S(1)} %copy-done.100), channel_id=1, source_target_pairs={{0,8},{4,12},{8,0},{12,4},{1,9},{5,13},{9,1},{13,5},{2,10},{6,14},... | collective-permute-start | bytes 393224 | tf_op jit(solution)/shard_map/ppermute | solution.py:75
  1142.7 48.7 %collective-permute-start.81 = (bf16[32,2048]{1,0:T(8,128)(2,1)S(1)}, bf16[32,2048]{1,0:T(8,128)(2,1)S(1)}, u32[]{:S(2)}, u32[]{:S(2)}) collective-permute-start(bf16[32,2048]{1,0:T(8,128)(2,1)S(1)} %copy-done.99), channel_id=1, source_target_pairs={{0,4},{4,0},{8,12},{12,8},{1,5},{5,1},{9,13},{13,9},{2,6},{6,2},{1... | collective-permute-start | bytes 393224 | tf_op jit(solution)/shard_map/ppermute | solution.py:75
  1144.1 55.7 %collective-permute-start.65 = (bf16[64,3072]{1,0:T(8,128)(2,1)S(1)}, bf16[64,3072]{1,0:T(8,128)(2,1)S(1)}, u32[]{:S(2)}, u32[]{:S(2)}) collective-permute-start(bf16[64,3072]{1,0:T(8,128)(2,1)S(1)} %constant_dynamic-update-slice_fusion.9), channel_id=1, source_target_pairs={{0,4},{4,0},{8,12},{12,8},{1,5},{5,1},{9,13},{13,9},{2,6},{6,2},{1... | collective-permute-start | bytes 1179656 | tf_op jit(solution)/shard_map/ppermute | solution.py:75
  1294.1 50.4 %collective-permute-start.99 = (bf16[4,2,512,256]{3,2,1,0:T(8,128)(2,1)}, bf16[4,2,512,256]{3,2,1,0:T(8,128)(2,1)}, u32[]{:S(2)}, u32[]{:S(2)}) collective-permute-start(bf16[4,2,512,256]{3,2,1,0:T(8,128)(2,1)} %pad_maximum_fusion.8.refs_0_), channel_id=1, source_target_pairs={{0,16},{16,0},{1,17},{17,1},{2,18},{18,2},{3,19},{19,3},{4,20},{20... | collective-permute-start | bytes 6291464 | tf_op jit(solution)/shard_map/ppermute | solution.py:75
  1294.2 50.3 %collective-permute-start.100 = (bf16[4,2,512,256]{3,2,1,0:T(8,128)(2,1)}, bf16[4,2,512,256]{3,2,1,0:T(8,128)(2,1)}, u32[]{:S(2)}, u32[]{:S(2)}) collective-permute-start(bf16[4,2,512,256]{3,2,1,0:T(8,128)(2,1)} %collective-permute-done.95.refs_1_), channel_id=1, source_target_pairs={{0,16},{16,0},{1,17},{17,1},{2,18},{18,2},{3,19},{19,3},{4,20},{20... | collective-permute-start | bytes 6291464 | tf_op jit(solution)/shard_map/ppermute | solution.py:75
  1294.6 49.9 %collective-permute-start.101 = (bf16[4,2,512,256]{3,2,1,0:T(8,128)(2,1)}, bf16[4,2,512,256]{3,2,1,0:T(8,128)(2,1)}, u32[]{:S(2)}, u32[]{:S(2)}) collective-permute-start(bf16[4,2,512,256]{3,2,1,0:T(8,128)(2,1)} %collective-permute-done.96.refs_2_), channel_id=1, source_target_pairs={{0,16},{16,0},{1,17},{17,1},{2,18},{18,2},{3,19},{19,3},{4,20},{20... | collective-permute-start | bytes 6291464 | tf_op jit(solution)/shard_map/ppermute | solution.py:75
  1296.7 47.8 %collective-permute-start.102 = (bf16[4,2,512,256]{3,2,1,0:T(8,128)(2,1)S(1)}, bf16[4,2,512,256]{3,2,1,0:T(8,128)(2,1)}, u32[]{:S(2)}, u32[]{:S(2)}) collective-permute-start(bf16[4,2,512,256]{3,2,1,0:T(8,128)(2,1)S(1)} %constant_dynamic-update-slice_fusion.16.refs_3_), channel_id=1, source_target_pairs={{0,16},{16,0},{1,17},{17,1},{2,18},{18,2},{3,19},{19,3},{4,20},{20... | collective-permute-start | bytes 6291464 | tf_op jit(solution)/shard_map/ppermute | solution.py:75
  (278 other events, 5539.6 us)
Sparse Core Ops, SparseCore 0:
  12.2 62.5 all-gather.5
  76.4 37.7 all-gather.7
  859.5 29.9 reduce-scatter.10
  891.6 25.2 reduce-scatter.8
  938.3 45.9 reduce-scatter.6
Sparse Core Ops, SparseCore 1:
  158.2 178.8 reduce-scatter.4
  998.7 71.0 all-gather.9
  1257.7 56.8 all-reduce.8

commit v2 on v1

v2 whole, which is shorter than its diff:
```python
import functools
import math

import jax
import jax.numpy as jnp
from jax import lax
from jax.experimental import pallas as pl
from jax.experimental.pallas import tpu as pltpu
from jax.sharding import PartitionSpec as P

HEADS = 8
KV_HEADS = 2
HEAD_DIM = 256


EPSILON = 1e-06
ROPE_BASE = 1000000.0
HALF_ROOT = 0.7071067811865476
TANH_SCALE = 0.7978845608028654
NEGATIVE = -1e30
EMBED_SCALE = 16.0


def rms_norm(value, gain):
    return value * lax.rsqrt(jnp.mean(value * value, axis=-1, keepdims=True) + EPSILON) * gain


def gelu_tanh(value):
    return 0.5 * value * (1.0 + jnp.tanh(TANH_SCALE * (value + 0.044715 * value * value * value)))


def gated_product(pre_gate, other_side):
    return gelu_tanh(pre_gate) * other_side


def rotate(value, places):
    width_all = value.shape[-1]
    half_width = width_all // 2
    inverse = jnp.exp(
        -math.log(ROPE_BASE) * (2.0 * jnp.arange(half_width, dtype=jnp.float32) / width_all)
    )
    angles = places.astype(jnp.float32)[:, None] * inverse[None, :]
    cosine = jnp.cos(angles)[:, None, :]
    sine = jnp.sin(angles)[:, None, :]
    front = value[..., :half_width]
    behind = value[..., half_width:]
    return jnp.concatenate(
        [front * cosine - behind * sine, behind * cosine + front * sine], axis=-1
    )


def matmul(left, right):
    return jnp.dot(left, right, preferred_element_type=jnp.float32)


def times_transposed(left, right):
    return lax.dot_general(
        left, right, (((1,), (1,)), ((), ())), preferred_element_type=jnp.float32
    )


def over_rows(left, right):
    return lax.dot_general(
        left, right, (((0,), (0,)), ((), ())), preferred_element_type=jnp.float32
    )


LOW = jnp.bfloat16
WIDE = jnp.float32
EVERY = ("slot", "ctx", "wsh")
COPIES = ("slot", "ctx")


def after(value, *others):
    return lax.optimization_barrier((value, others))[0]


def exchange(value, axis):
    return lax.all_to_all(value, axis, 0, 0, tiled=True)


def spread(value, axis):
    size = lax.axis_size(axis)
    copies = jnp.broadcast_to(value[None], (size,) + value.shape)
    return exchange(copies.reshape((size * value.shape[0],) + value.shape[1:]), axis)


def collect(parts, axis):
    size = lax.axis_size(axis)
    received = exchange(parts, axis)
    received = received.reshape((size, parts.shape[0] // size) + parts.shape[1:])
    return jnp.sum(received.astype(WIDE), axis=0)


def swap(value, axis, bit):
    size = lax.axis_size(axis)
    return lax.ppermute(value, axis, [(i, i ^ bit) for i in range(size)])


def add_low(left, right):
    return (left.astype(WIDE) + right.astype(WIDE)).astype(LOW)


def gather_first(piece):
    if lax.axis_size("ctx") == 4:
        return [swap(piece, "ctx", 1), swap(piece, "ctx", 2)]
    return []


def gather_second(piece, first):
    if first:
        one, two = first
        half = piece.shape[0] // 2
        front = swap(one[:half], "ctx", 2)
        behind = swap(two[half:], "ctx", 1)
        return [piece, one, two, jnp.concatenate([front, behind], axis=0)]
    pieces = [piece]
    bit = 1
    while bit < lax.axis_size("ctx"):
        pieces = pieces + [swap(p, "ctx", bit) for p in pieces]
        bit *= 2
    return pieces


def reduce_first(pieces):
    if len(pieces) == 4:
        half = pieces[0].shape[0] // 2
        return [swap(pieces[3][:half], "ctx", 1), swap(pieces[3][half:], "ctx", 2)]
    return []


def reduce_second(pieces, first):
    if first:
        front, behind = first
        half = pieces[0].shape[0] // 2
        two = jnp.concatenate([add_low(pieces[2][:half], front), pieces[2][half:]], axis=0)
        one = jnp.concatenate([pieces[1][:half], add_low(pieces[1][half:], behind)], axis=0)
        return [swap(one, "ctx", 1), swap(two, "ctx", 2)]
    return []


def reduce_last(pieces, second):
    if second:
        one, two = second
        return (pieces[0].astype(WIDE) + one.astype(WIDE) + two.astype(WIDE)).astype(LOW)
    size = len(pieces)
    while size > 1:
        size //= 2
        pieces = [add_low(pieces[i], swap(pieces[size + i], "ctx", size)) for i in range(size)]
    return pieces[0]


def assemble_kernel(extent, cuts, own, *refs):
    step = pl.program_id(0)
    ins, outs = refs[:extent], refs[extent:]
    for number in range(extent):

        @pl.when(step == number)
        def _(number=number):
            for (begin, width), out in zip(cuts, outs):
                out[:, 0] = ins[number][:, :, begin : begin + width].astype(out.dtype)


def assemble(pieces, own, kind, cuts=None):
    count = len(pieces)
    outer, inner, width = pieces[0].shape
    cuts = cuts or [(0, width)]
    results = pl.pallas_call(
        functools.partial(assemble_kernel, count, cuts),
        grid_spec=pltpu.PrefetchScalarGridSpec(
            num_scalar_prefetch=1,
            grid=(count,),
            in_specs=[pl.BlockSpec((outer, inner, width), lambda i, o: (0, 0, 0))] * count,
            out_specs=[
                pl.BlockSpec((outer, 1, inner, w), lambda i, o: (0, lax.bitwise_xor(i, o[0]), 0, 0))
                for _, w in cuts
            ],
        ),
        out_shape=[jax.ShapeDtypeStruct((outer, count, inner, w), kind) for _, w in cuts],
    )(own, *pieces)
    return results


def halves(blocks):
    count = blocks.shape[0] // 2
    slot = lax.axis_index("slot")
    kept = lax.dynamic_slice_in_dim(blocks, slot * count, count, 0)
    given = lax.dynamic_slice_in_dim(blocks, (1 - slot) * count, count, 0)
    return kept, swap(given, "slot", 1)


def nearest(blocks):
    here = lax.axis_index("ctx")
    count = blocks.shape[0]
    return [lax.dynamic_index_in_dim(blocks, here ^ r, 0, False) for r in range(count)]


def last_gather(pieces):
    return pieces + [swap(p, "slot", 1) for p in pieces]


def contract_last(left, right):
    return lax.dot_general(left, right, (((1,), (1,)), ((), ())), preferred_element_type=WIDE)


def gelu_and_slope(value):
    inner = jnp.tanh(TANH_SCALE * (value + 0.044715 * value * value * value))
    slope = 0.5 * (1.0 + inner) + 0.5 * value * (1.0 - inner * inner) * TANH_SCALE * (
        1.0 + 3.0 * 0.044715 * value * value
    )
    return 0.5 * value * (1.0 + inner), slope


def ff_forward_kernel(piece, count, x_ref, pair_ref, down_ref, both_ref, hidden_ref, out_ref):
    step = pl.program_id(0)

    @pl.when(step < count)
    def _():
        both = contract_last(x_ref[...], pair_ref[...])
        both_ref[...] = both
        hidden = (gelu_tanh(both[:, :piece]) * both[:, piece:]).astype(LOW)
        hidden_ref[:, pl.ds(pl.multiple_of(step * piece, piece), piece)] = hidden

    @pl.when(step >= count)
    def _():
        out_ref[...] = jnp.dot(
            hidden_ref[...], down_ref[...], preferred_element_type=WIDE
        ).astype(LOW)


def ff_forward(x, pair, down, piece):
    rows, width = x.shape
    hidden = down.shape[0]
    count = hidden // piece
    cut = math.gcd(width, 512)

    def now(i):
        return jnp.minimum(i, count - 1)

    def then(i):
        return jnp.maximum(i - count, 0)

    return pl.pallas_call(
        functools.partial(ff_forward_kernel, piece, count),
        grid=(count + width // cut,),
        in_specs=[
            pl.BlockSpec((rows, width), lambda i: (0, 0)),
            pl.BlockSpec((2 * piece, width), lambda i: (now(i), 0)),
            pl.BlockSpec((hidden, cut), lambda i: (0, then(i))),
        ],
        out_specs=[
            pl.BlockSpec((rows, 2 * piece), lambda i: (0, now(i))),
            pl.BlockSpec((rows, hidden), lambda i: (0, 0)),
            pl.BlockSpec((rows, cut), lambda i: (0, then(i))),
        ],
        out_shape=[
            jax.ShapeDtypeStruct((rows, 2 * hidden), WIDE),
            jax.ShapeDtypeStruct((rows, hidden), LOW),
            jax.ShapeDtypeStruct((rows, width), LOW),
        ],
        cost_estimate=pl.CostEstimate(
            flops=6 * rows * width * hidden,
            bytes_accessed=6 * width * hidden + 10 * rows * hidden,
            transcendentals=rows * hidden,
        ),
    )(x, pair, down)


def ff_backward_kernel(piece, count, grad_ref, down_ref, both_ref, pair_ref, grad_both_ref, out_ref):
    step = pl.program_id(0)

    @pl.when(step < count)
    def _():
        grad_hidden = contract_last(grad_ref[...], down_ref[...])
        value, slope = gelu_and_slope(both_ref[:, :piece])
        start = pl.multiple_of(step * 2 * piece, piece)
        grad_both_ref[:, pl.ds(start, piece)] = (grad_hidden * both_ref[:, piece:] * slope).astype(LOW)
        start = pl.multiple_of(step * 2 * piece + piece, piece)
        grad_both_ref[:, pl.ds(start, piece)] = (grad_hidden * value).astype(LOW)

    @pl.when(step >= count)
    def _():
        out_ref[...] = jnp.dot(
            grad_both_ref[...], pair_ref[...], preferred_element_type=WIDE
        ).astype(LOW)


def ff_backward(grad, pair, down, both, piece):
    rows, width = grad.shape
    hidden = down.shape[0]
    count = hidden // piece
    cut = math.gcd(width, 512)

    def now(i):
        return jnp.minimum(i, count - 1)

    def then(i):
        return jnp.maximum(i - count, 0)

    return pl.pallas_call(
        functools.partial(ff_backward_kernel, piece, count),
        grid=(count + width // cut,),
        in_specs=[
            pl.BlockSpec((rows, width), lambda i: (0, 0)),
            pl.BlockSpec((piece, width), lambda i: (now(i), 0)),
            pl.BlockSpec((rows, 2 * piece), lambda i: (0, now(i))),
            pl.BlockSpec((2 * hidden, cut), lambda i: (0, then(i))),
        ],
        out_specs=[
            pl.BlockSpec((rows, 2 * hidden), lambda i: (0, 0)),
            pl.BlockSpec((rows, cut), lambda i: (0, then(i))),
        ],
        out_shape=[
            jax.ShapeDtypeStruct((rows, 2 * hidden), LOW),
            jax.ShapeDtypeStruct((rows, width), LOW),
        ],
        cost_estimate=pl.CostEstimate(
            flops=6 * rows * width * hidden,
            bytes_accessed=6 * width * hidden + 12 * rows * hidden,
            transcendentals=rows * hidden,
        ),
    )(grad, down, both, pair)


def widen_kernel(places, source, gate, up):
    gate[...] = source[0, 0, 0].astype(WIDE)
    up[...] = source[0, 0, 1].astype(WIDE)


def widen_pair(pieces, places):
    parts, run, _, rows, width = pieces.shape
    return pl.pallas_call(
        widen_kernel,
        grid_spec=pltpu.PrefetchScalarGridSpec(
            num_scalar_prefetch=1,
            grid=(run, parts),
            in_specs=[pl.BlockSpec((1, 1, 2, rows, width), lambda k, r, p: (r, k, 0, 0, 0))],
            out_specs=[pl.BlockSpec((rows, width), lambda k, r, p: (0, p[k] * parts + r))] * 2,
        ),
        out_shape=[jax.ShapeDtypeStruct((rows, width * parts * run), WIDE)] * 2,
        cost_estimate=pl.CostEstimate(flops=0, bytes_accessed=6 * pieces.size, transcendentals=0),
    )(places, pieces)


def shift_blocks(make):
    run = lax.axis_size("wsh")
    here = lax.axis_index("wsh")
    received = []
    for k in range(run):
        block = make((here + k) % run)
        if k:
            block = lax.ppermute(block, "wsh", [(i, (i + k) % run) for i in range(run)])
        received.append(block)
    return received


def shift_exchange(make):
    run = lax.axis_size("wsh")
    order = (lax.axis_index("wsh") - jnp.arange(run, dtype=jnp.int32)) % run
    return jnp.take(jnp.stack(shift_blocks(make)), order, axis=0)


def place_kernel(places, *refs):
    step = pl.program_id(0)
    sources, out = refs[:-1], refs[-1]
    for number, source in enumerate(sources):

        @pl.when(step == number)
        def _(source=source):
            out[...] = source[...]


def place_columns(blocks, places):
    rows, width = blocks[0].shape
    count = len(blocks)
    return pl.pallas_call(
        place_kernel,
        grid_spec=pltpu.PrefetchScalarGridSpec(
            num_scalar_prefetch=1,
            grid=(count,),
            in_specs=[pl.BlockSpec((rows, width), lambda k, p: (0, 0))] * count,
            out_specs=pl.BlockSpec((rows, width), lambda k, p: (0, p[k])),
        ),
        out_shape=jax.ShapeDtypeStruct((rows, width * count), blocks[0].dtype),
        cost_estimate=pl.CostEstimate(
            flops=0, bytes_accessed=4 * count * blocks[0].size, transcendentals=0
        ),
    )(places, *blocks)


def entry(stacked):
    return lambda index: lax.dynamic_index_in_dim(stacked, index, 0, False)


def widen_heads_kernel(run, query_width, own, *refs):
    step = pl.program_id(0)
    sources, (query, key, value) = refs[:-3], refs[-3:]
    group = run // KV_HEADS
    for place, source in enumerate(sources):

        @pl.when(step == place)
        def _(source=source):
            for k in range(run):
                begin = k * query_width
                query[:, begin : begin + query_width] = source[k, :, :query_width].astype(WIDE)
            for number, out in enumerate((key, value)):
                begin = query_width + number * HEAD_DIM
                for head in range(KV_HEADS):
                    total = source[head * group, :, begin : begin + HEAD_DIM].astype(WIDE)
                    for k in range(1, group):
                        total += source[head * group + k, :, begin : begin + HEAD_DIM].astype(WIDE)
                    out[:, head * HEAD_DIM : (head + 1) * HEAD_DIM] = total


def widen_heads(pieces, own, query_width):
    parts = len(pieces)
    run, rows, columns = pieces[0].shape
    widths = (HEADS * HEAD_DIM, KV_HEADS * HEAD_DIM, KV_HEADS * HEAD_DIM)
    return pl.pallas_call(
        functools.partial(widen_heads_kernel, run, query_width),
        grid_spec=pltpu.PrefetchScalarGridSpec(
            num_scalar_prefetch=1,
            grid=(parts,),
            in_specs=[pl.BlockSpec((run, rows, columns), lambda r, o: (0, 0, 0))] * parts,
            out_specs=[
                pl.BlockSpec((rows, w), lambda r, o: (lax.bitwise_xor(r, o[0]), 0)) for w in widths
            ],
        ),
        out_shape=[jax.ShapeDtypeStruct((rows * parts, w), WIDE) for w in widths],
        cost_estimate=pl.CostEstimate(
            flops=0, bytes_accessed=6 * parts * pieces[0].size, transcendentals=0
        ),
    )(own, *pieces)


def shards(
    tokens,
    cotangent,
    lengths,
    positions,
    token_ids,
    per_layer_table,
    w_query,
    w_key,
    w_value,
    w_output,
    laurel_left,
    laurel_right,
    w_gate,
    w_up,
    w_down,
    w_layer_gate,
    w_layer_proj,
    norm_gains,
    query_gain,
    key_gain,
):
    rows_dev, width = tokens.shape[1:]
    run = lax.axis_size("wsh")
    contexts = lax.axis_size("ctx")
    parts = 2 * contexts
    chip = lax.axis_index(COPIES)
    shard_rows = width // run
    heads_here = HEADS // run
    groups = HEADS // KV_HEADS
    query_width = heads_here * HEAD_DIM
    head_width = query_width + 2 * HEAD_DIM
    hidden_width = w_gate.shape[1] // run
    head_piece = shard_rows // parts
    piece = hidden_width // parts
    rank = laurel_left.shape[1]
    places = ((lax.axis_index("wsh") - jnp.arange(run)) % run).astype(jnp.int32)
    gain_cut = query_gain.shape[0]

    def joined(make):
        return place_columns(shift_blocks(make), places)

    def share(weight):
        return lax.dynamic_slice_in_dim(weight, chip * head_piece, head_piece, 0)

    query_rows, key_rows, value_rows = share(w_query), share(w_key), share(w_value)

    indices = shift_exchange(lambda k: jnp.concatenate([token_ids, positions], axis=0))
    small = jnp.concatenate(
        [
            norm_gains.T,
            jnp.pad(
                jnp.concatenate([query_gain, key_gain])[None],
                ((0, 1), (0, shard_rows - 2 * gain_cut)),
            ),
        ],
        axis=0,
    )
    proj_rows = w_layer_proj.shape[0]
    proj_share = lax.dynamic_slice_in_dim(w_layer_proj, chip * (width // parts), width // parts, 1)
    common = jnp.concatenate(
        [
            share(laurel_left),
            share(laurel_right),
            share(w_layer_gate),
            proj_share.reshape(head_piece, -1),
        ],
        axis=1,
    )
    fetch_width = head_width + common.shape[1]
    small_flat = jnp.pad(small.reshape(-1), (0, -small.size % fetch_width)).reshape(-1, fetch_width)
    small_flat = jnp.pad(small_flat, ((0, 16 - small_flat.shape[0]), (0, 0)))
    common, query_rows, key_rows, value_rows, small_flat, indices = lax.optimization_barrier(
        (common, query_rows, key_rows, value_rows, small_flat, indices)
    )

    def head_block(index):
        kv = index * heads_here // groups * HEAD_DIM
        block = jnp.concatenate(
            [
                lax.dynamic_slice_in_dim(query_rows, index * query_width, query_width, 1),
                lax.dynamic_slice_in_dim(key_rows, kv, HEAD_DIM, 1),
                lax.dynamic_slice_in_dim(value_rows, kv, HEAD_DIM, 1),
                common,
            ],
            axis=1,
        )
        return jnp.concatenate([small_flat, block], axis=0)

    head_share = shift_exchange(head_block)
    small_all = head_share[:, :16].reshape(run, -1)[:, : small.size].reshape(run, 8, shard_rows)
    fetched = lax.all_gather(head_share[:, 16:], COPIES, axis=0)
    w_heads = fetched[:, :, :, :head_width]
    proj_at = head_width + 2 * rank + w_layer_gate.shape[1]
    layer_proj_full = fetched[:, :, :, proj_at:].reshape(parts, run, proj_rows, width // parts)
    layer_proj_full = layer_proj_full.transpose(1, 2, 0, 3).reshape(run * proj_rows, width)
    laurel_weights = fetched[:, :, :, head_width:proj_at].transpose(1, 0, 2, 3).reshape(width, -1)
    left_full = laurel_weights[:, :rank]
    right_full = laurel_weights[:, rank : 2 * rank]
    layer_gate_full = laurel_weights[:, 2 * rank :]
    w_heads = w_heads.transpose(1, 0, 2, 3).reshape(width, head_width)

    gains_full = small_all.transpose(1, 0, 2).reshape(8, width).astype(WIDE)
    query_gain_full = small_all[:, 6, :gain_cut].reshape(HEAD_DIM).astype(WIDE)
    key_gain_full = small_all[:, 6, gain_cut : 2 * gain_cut].reshape(HEAD_DIM).astype(WIDE)
    tokens_run = spread(tokens[0], "wsh")

    indices = indices[None]
    bit = 1
    while bit < contexts:
        indices = jnp.concatenate([indices, swap(indices, "ctx", bit)], axis=0)
        bit *= 2
    run_places = indices[0, :, 1].reshape(-1)
    here_ctx = lax.axis_index("ctx")
    context_order = jnp.bitwise_xor(jnp.arange(contexts, dtype=jnp.int32), here_ctx)
    key_places = jnp.take(indices[:, :, 1], context_order, axis=0).reshape(-1)
    own_ids = indices[:, :, 0].reshape(-1)
    all_ids = jnp.concatenate([own_ids, swap(own_ids, "slot", 1)])
    length = lengths[0]

    vocab_rows = per_layer_table.shape[0]
    vocab_first = lax.axis_index(EVERY) * vocab_rows
    vocab_range = jnp.arange(vocab_rows, dtype=jnp.int32)

    def one_hot():
        return ((all_ids - vocab_first)[:, None] == vocab_range[None, :]).astype(LOW)

    table_rows = matmul(one_hot(), per_layer_table).astype(LOW)
    def pair_block(index):
        first = index * hidden_width + chip * piece
        gate_cut = lax.dynamic_slice_in_dim(w_gate, first, piece, 1)
        up_cut = lax.dynamic_slice_in_dim(w_up, first, piece, 1)
        gate_cut, up_cut = after((gate_cut, up_cut), tokens_run)
        return jnp.concatenate([gate_cut.T, up_cut.T], axis=0)

    pair_share = joined(pair_block)
    normed_run = rms_norm(tokens_run.astype(WIDE), gains_full[0]).astype(LOW)
    tokens_f = tokens[0].astype(WIDE)
    normed = rms_norm(tokens_f, gains_full[0])
    normed_low = normed.astype(LOW)
    total_rows = run * rows_dev
    projected = matmul(normed_run, w_heads)
    query = projected[:, :query_width]
    key = projected[:, query_width : query_width + HEAD_DIM]
    value = projected[:, query_width + HEAD_DIM :]

    def query_path(raw, gain):
        return rotate(rms_norm(raw.reshape(total_rows, heads_here, HEAD_DIM), gain), run_places)

    def key_path(raw, gain):
        return rotate(rms_norm(raw.reshape(total_rows, 1, HEAD_DIM), gain), run_places)[:, 0]

    def value_path(raw):
        return rms_norm(raw, 1.0)

    k_low = key_path(key, key_gain_full).astype(LOW)
    v_low = value_path(value).astype(LOW)
    keys_values = spread(jnp.concatenate([k_low, v_low], axis=1), "ctx")
    keys_values, table_rows, pair_share = lax.optimization_barrier(
        (keys_values, table_rows, pair_share)
    )
    pair_weight = lax.all_gather(pair_share, COPIES, axis=0, tiled=True)
    half = table_rows.shape[0] // 2
    looked_up = add_low(table_rows[:half], swap(table_rows[half:], "slot", 1))
    bit = contexts // 2
    while bit:
        half = looked_up.shape[0] // 2
        looked_up = add_low(looked_up[:half], swap(looked_up[half:], "ctx", bit))
        bit //= 2
    looked_up = looked_up.reshape(run, rows_dev, -1)
    q_low = query_path(query, query_gain_full).astype(LOW)
    keys_all = keys_values[:, :HEAD_DIM]
    values_all = keys_values[:, HEAD_DIM:]
    allowed = (key_places[None, :] <= run_places[:, None]) & (key_places < length)[None, :]
    scores = jnp.einsum("qhd,td->hqt", q_low, keys_all, preferred_element_type=WIDE)
    scores = jnp.where(allowed[None], scores, NEGATIVE)
    top = jnp.max(scores, axis=-1, keepdims=True)
    raised = jnp.exp(scores - top)
    probs = raised / jnp.sum(raised, axis=-1, keepdims=True)
    attended = jnp.einsum(
        "hqt,td->qhd", probs.astype(LOW), values_all, preferred_element_type=WIDE
    )
    attended_low = attended.astype(LOW).reshape(total_rows, query_width)
    attn_proj = collect(matmul(attended_low, w_output).astype(LOW), "wsh")
    attn_proj, looked_up = lax.optimization_barrier((attn_proj, looked_up))
    layer_input = EMBED_SCALE * jnp.sum(shift_exchange(entry(looked_up)).astype(WIDE), axis=0)

    first_sum = tokens_f + rms_norm(attn_proj, gains_full[1])
    low_rank_low = matmul(normed_low, left_full).astype(LOW)
    laurel_out = times_transposed(low_rank_low, right_full)
    laurel = normed + rms_norm(laurel_out, gains_full[2])
    mixed = (first_sum + laurel) * HALF_ROOT
    ff_in_low = rms_norm(mixed, gains_full[3]).astype(LOW)

    ff_run = spread(ff_in_low, "wsh")
    aligned = piece % 128 == 0
    if aligned:
        both, hidden_low, ff_part = ff_forward(ff_run, pair_weight, w_down, piece)
    else:
        both = times_transposed(ff_run, pair_weight)
        both_parts = both.reshape(total_rows, parts, 2, piece)
        gate = both_parts[:, :, 0].reshape(total_rows, hidden_width)
        upward = both_parts[:, :, 1].reshape(total_rows, hidden_width)
        hidden_low = gated_product(gate, upward).astype(LOW)
        ff_part = matmul(hidden_low, w_down).astype(LOW)
    ff_out = collect(ff_part, "wsh")
    ff_out, layer_input = lax.optimization_barrier((ff_out, layer_input))
    third_sum = mixed + rms_norm(ff_out, gains_full[4])
    third_low = third_sum.astype(LOW)

    layer_gate = matmul(third_low, layer_gate_full)
    gated_low = gated_product(layer_gate, layer_input).astype(LOW)
    layer_proj = matmul(gated_low, layer_proj_full)
    result = third_sum + rms_norm(layer_proj, gains_full[5])
    layer_out = result.astype(LOW)[None]

    valid = (positions[0] < length).astype(WIDE)
    grad_out = cotangent[0].astype(WIDE) * valid[:, None]
    _, pullback = jax.vjp(rms_norm, layer_proj, gains_full[5])
    grad_proj, grad_gain_five = pullback(grad_out)
    grad_proj_low = grad_proj.astype(LOW)
    grad_gated = times_transposed(grad_proj_low, layer_proj_full)
    _, pullback = jax.vjp(gated_product, layer_gate, layer_input)
    grad_lgate, grad_input = pullback(grad_gated)
    grad_lgate_low = grad_lgate.astype(LOW)
    grad_input_low = grad_input.astype(LOW)
    grad_third = grad_out + times_transposed(grad_lgate_low, layer_gate_full)
    _, pullback = jax.vjp(rms_norm, ff_out, gains_full[4])
    grad_ff, grad_gain_four = pullback(grad_third)
    grad_ff_low = grad_ff.astype(LOW)

    grad_ff_run = spread(grad_ff_low, "wsh")
    if aligned:
        grad_both, ff_part = ff_backward(grad_ff_run, pair_weight, w_down, both, piece)
    else:
        grad_hidden = times_transposed(grad_ff_run, w_down)
        _, pullback = jax.vjp(gated_product, gate, upward)
        grad_gate, grad_upward = pullback(grad_hidden)
        grad_both = jnp.stack(
            [
                grad_gate.reshape(total_rows, parts, piece),
                grad_upward.reshape(total_rows, parts, piece),
            ],
            axis=2,
        )
        grad_both = grad_both.reshape(total_rows, 2 * hidden_width).astype(LOW)
        ff_part = matmul(grad_both, pair_weight).astype(LOW)
    grad_ff_in = collect(ff_part, "wsh")
    pair_part = over_rows(after(grad_both, ff_part), ff_run).astype(LOW)
    grad_ff_in, pair_part = lax.optimization_barrier((grad_ff_in, pair_part))
    grad_input_low = after(grad_input_low, pair_part)
    every_grad = shift_exchange(lambda k: grad_input_low).reshape(total_rows, -1)
    pair_own = lax.psum_scatter(pair_part, COPIES, scatter_dimension=0, tiled=True)
    _, pullback = jax.vjp(rms_norm, mixed, gains_full[3])
    grad_mixed_norm, grad_gain_three = pullback(grad_ff_in)
    grad_branch = (grad_third + grad_mixed_norm) * HALF_ROOT
    _, pullback = jax.vjp(rms_norm, attn_proj, gains_full[1])
    grad_attn, grad_gain_one = pullback(grad_branch)
    grad_attn_low = grad_attn.astype(LOW)
    grad_attn_run = spread(grad_attn_low, "wsh")
    down_part = over_rows(after(hidden_low, grad_attn_low), grad_ff_run).astype(LOW)
    grad_attn_run, down_part = lax.optimization_barrier((grad_attn_run, down_part))

    def pair_back(index):
        block = lax.dynamic_slice_in_dim(pair_own, index * shard_rows, shard_rows, 1)
        return block.reshape(2, piece, shard_rows).transpose(0, 2, 1)

    _, pullback = jax.vjp(rms_norm, laurel_out, gains_full[2])
    grad_laurel, grad_gain_two = pullback(grad_branch)
    grad_laurel_low = grad_laurel.astype(LOW)
    grad_rank_low = matmul(grad_laurel_low, right_full).astype(LOW)

    left_grad = over_rows(normed_low, grad_rank_low)
    right_grad = over_rows(grad_laurel_low, low_rank_low)
    layer_gate_grad = over_rows(third_low, grad_lgate_low)
    layer_proj_grad = over_rows(gated_low, grad_proj_low)

    narrow = jnp.concatenate([left_grad, right_grad, layer_gate_grad], axis=1)
    narrow = narrow.reshape(run, shard_rows, -1)
    narrow_columns = narrow.shape[2]
    layer_proj_grad = layer_proj_grad.reshape(run, shard_rows, -1)
    sums = jnp.concatenate([narrow, layer_proj_grad], axis=2).astype(LOW)
    sums = jnp.sum(shift_exchange(entry(after(sums, grad_attn_run))).astype(WIDE), axis=0).astype(LOW)

    grad_att_low = times_transposed(grad_attn_run, w_output).astype(LOW)
    grad_att = grad_att_low.reshape(total_rows, heads_here, HEAD_DIM)
    row_delta = jnp.sum(grad_att.astype(WIDE) * attended, axis=-1)
    grad_probs = jnp.einsum("qhd,td->hqt", grad_att, values_all, preferred_element_type=WIDE)
    grad_scores = (probs * (grad_probs - row_delta.T[:, :, None])).astype(LOW)
    key_part = jnp.einsum("hqt,qhd->td", grad_scores, q_low, preferred_element_type=WIDE)
    value_part = jnp.einsum("hqt,qhd->td", probs.astype(LOW), grad_att, preferred_element_type=WIDE)
    kv_part = jnp.concatenate([key_part, value_part], axis=1).astype(LOW)
    kv_part, pair_own = lax.optimization_barrier((kv_part, pair_own))
    kv_sum = collect(kv_part, "ctx")
    pair_blocks = jnp.stack(shift_blocks(pair_back))
    down_grad = lax.psum(after(down_part, pair_own), COPIES)
    output_part = over_rows(attended_low, grad_attn_run).astype(LOW)
    output_kept, output_given = halves(output_part.reshape(parts, -1, width))
    kv_sum, pair_blocks, output_kept, output_given, sums = lax.optimization_barrier(
        (kv_sum, pair_blocks, output_kept, output_given, sums)
    )
    pair_all = lax.all_gather(pair_blocks, COPIES, axis=0)
    output_pieces = nearest(add_low(output_kept, output_given))
    output_first = reduce_first(output_pieces)
    sums = add_low(sums, swap(sums, "slot", 1))
    grad_q_rot = jnp.einsum("hqt,td->qhd", grad_scores, keys_all, preferred_element_type=WIDE)
    _, pullback = jax.vjp(query_path, query, query_gain_full)
    grad_query, grad_query_gain = pullback(grad_q_rot)
    _, pullback = jax.vjp(key_path, key, key_gain_full)
    grad_key, grad_key_gain = pullback(kv_sum[:, :HEAD_DIM])
    _, pullback = jax.vjp(value_path, value)
    (grad_value,) = pullback(kv_sum[:, HEAD_DIM:])
    grad_heads = jnp.concatenate([grad_query, grad_key, grad_value], axis=1).astype(LOW)
    heads_part = over_rows(normed_run, grad_heads).astype(LOW)
    heads_part = heads_part.reshape(run, parts, head_piece, head_width).transpose(1, 0, 2, 3)
    heads_kept, heads_given = halves(heads_part)
    normed_part = times_transposed(grad_heads, w_heads).astype(LOW)
    normed_part, output_first, heads_kept, heads_given, sums = lax.optimization_barrier(
        (normed_part, output_first, heads_kept, heads_given, sums)
    )
    grad_run = collect(normed_part, "wsh")
    output_second = reduce_second(output_pieces, output_first)
    heads_pieces = nearest(add_low(heads_kept, heads_given))
    heads_second = reduce_second(heads_pieces, reduce_first(heads_pieces))
    heads_own = reduce_last(heads_pieces, heads_second)
    every_grad = after(every_grad, normed_part)
    bit = 1
    while bit < contexts:
        every_grad = jnp.concatenate([every_grad, swap(every_grad, "ctx", bit)], axis=0)
        bit *= 2
    every_grad = jnp.concatenate([every_grad, swap(every_grad, "slot", 1)], axis=0)
    table_grad = EMBED_SCALE * over_rows(one_hot(), every_grad)
    grad_run, output_second, heads_own, table_grad = lax.optimization_barrier(
        (grad_run, output_second, heads_own, table_grad)
    )
    if aligned:
        gate_grad, up_grad = widen_pair(pair_all, places)
    else:
        pair_all = jnp.take(pair_all, places, axis=1)
        pair_all = pair_all.transpose(2, 3, 1, 0, 4).reshape(2, shard_rows, -1).astype(WIDE)
        gate_grad, up_grad = pair_all[0], pair_all[1]
    output_own = reduce_last(output_pieces, output_second)
    own = jnp.full((1,), chip, jnp.int32)
    bit = 1
    while bit < contexts:
        sums = add_low(sums, swap(sums, "ctx", bit))
        bit *= 2
    sums = sums.astype(WIDE)
    narrow = sums[:, :narrow_columns]
    layer_proj_grad = sums[:, narrow_columns:].reshape(proj_rows, width)
    grad_normed = (
        grad_run
        + times_transposed(grad_rank_low, left_full)
        + grad_branch
    )
    _, pullback = jax.vjp(rms_norm, tokens_f, gains_full[0])
    grad_tokens, grad_gain_zero = pullback(grad_normed)
    tokens_grad = (grad_tokens + grad_branch).astype(LOW)[None]

    output_all = last_gather(gather_second(output_own, gather_first(output_own)))
    (output_grad,) = assemble([p[None] for p in output_all], own, WIDE)
    heads_own = shift_exchange(entry(heads_own))
    heads_all = last_gather(gather_second(heads_own, gather_first(heads_own)))
    query_grad, key_grad, value_grad = widen_heads(heads_all, own, query_width)

    vector = jnp.concatenate(
        [grad_query_gain.reshape(run, gain_cut), grad_key_gain.reshape(run, gain_cut)], axis=1
    )
    vector = jnp.pad(vector, ((0, 0), (0, shard_rows - 2 * gain_cut))).reshape(width)
    gain_sums = jnp.stack(
        [
            grad_gain_zero,
            grad_gain_one,
            grad_gain_two,
            grad_gain_three,
            grad_gain_four,
            grad_gain_five,
            vector,
            jnp.zeros_like(vector),
        ]
    )
    gain_sums = gain_sums.reshape(8, run, shard_rows).transpose(1, 0, 2)
    gain_sums = jnp.sum(shift_exchange(entry(gain_sums)), axis=0)
    gain_sums = gain_sums + swap(gain_sums, "slot", 1)
    bit = 1
    while bit < contexts:
        gain_sums = gain_sums + swap(gain_sums, "ctx", bit)
        bit *= 2
    return (
        layer_out,
        tokens_grad,
        table_grad,
        query_grad,
        key_grad,
        value_grad,
        output_grad.reshape(query_width, width),
        narrow[:, :rank],
        narrow[:, rank : 2 * rank],
        gate_grad,
        up_grad,
        down_grad.astype(WIDE),
        narrow[:, 2 * rank :],
        layer_proj_grad,
        gain_sums[:6].T,
        gain_sums[6, :gain_cut],
        gain_sums[6, gain_cut : 2 * gain_cut],
    )


def solution(mesh):
    placed = (
        P("slot", ("ctx", "wsh"), None),
        P("slot", ("ctx", "wsh"), None),
        P("slot"),
        P("slot", ("ctx", "wsh")),
        P("slot", ("ctx", "wsh")),
        P(("slot", "ctx", "wsh"), None),
        P("wsh", None),
        P("wsh", None),
        P("wsh", None),
        P("wsh", None),
        P("wsh", None),
        P("wsh", None),
        P("wsh", None),
        P("wsh", None),
        P("wsh", None),
        P("wsh", None),
        P("wsh", None),
        P("wsh", None),
        P("wsh"),
        P("wsh"),
    )
    return jax.shard_map(
        shards,
        mesh=mesh,
        in_specs=placed,
        out_specs=(
            P("slot", ("ctx", "wsh"), None),
            P("slot", ("ctx", "wsh"), None),
            P(("slot", "ctx", "wsh"), None),
            P("wsh", None),
            P("wsh", None),
            P("wsh", None),
            P("wsh", None),
            P("wsh", None),
            P("wsh", None),
            P("wsh", None),
            P("wsh", None),
            P("wsh", None),
            P("wsh", None),
            P("wsh", None),
            P("wsh", None),
            P("wsh"),
            P("wsh"),
        ),
        check_vma=False,
    )
```

time: 1390 us -> 1100 us (0.79)
  waiting for transfers between devices: 574 us -> 418 us
  starting transfers between devices: 175 us -> 103 us
  matrix products: 174 us -> 121 us
  blocking collectives: 128 us -> 102 us
    ppermute x39 -> x27, waiting for transfers between devices: 304 us -> 152 us  [shift_blocks(): block = lax.ppermute(block, 'wsh', [(i, (i + k) % run) for i in range(run)])]
    ppermute x77 -> x41, waiting for transfers between devices: 270 us -> 124 us  [swap(): return lax.ppermute(value, axis, [(i, i ^ bit) for i in range(size)])]
    all_gather x1 -> x0, blocking collectives: 114 us -> none  [shards(): lax.all_gather(jnp.concatenate([token_ids, positions], axis=0), EVERY, ax...]
    all_to_all x0 -> x8, waiting for transfers between devices: none -> 104 us  [exchange(): return lax.all_to_all(value, axis, 0, 0, tiled=True)]
    all_to_all x0 -> x2, blocking collectives: none -> 102 us  [exchange(): return lax.all_to_all(value, axis, 0, 0, tiled=True)]
    ppermute x39 -> x27, starting transfers between devices: 107 us -> 40.3 us  [shift_blocks(): block = lax.ppermute(block, 'wsh', [(i, (i + k) % run) for i in range(run)])]
    ppermute x77 -> x41, starting transfers between devices: 67.8 us -> 24.9 us  [swap(): return lax.ppermute(value, axis, [(i, i ^ bit) for i in range(size)])]
    reduce_scatter x4 -> x1, waiting for transfers between devices: 0.04 us -> 37.4 us  [shards(): lax.psum_scatter(pair_part, COPIES, scatter_dimension=0, tiled=True)]
  transfers between devices with their start and end apart: 124 -> 81, of which waited for: 47 -> 29; matrix products, arithmetic and copies ran while one was open for 23% -> 30% of each run, Pallas kernels for 3% -> 1%
where the time goes in v2:
time: 1100 us; the launch traced here: 1090 us
  waiting for transfers between devices  418 us (38%)
  other arithmetic  135 us (12%)
  matrix products  121 us (11%)
  local copies, waits for them, and re-layouts  106 us (10%)
  starting transfers between devices  103 us (9%)
  blocking collectives  102 us (9%)
  Pallas kernels  90.4 us (8%)
  between operations  17.6 us (2%)
    ppermute x27, waiting for transfers between devices, shift_blocks(): block = lax.ppermute(block, 'wsh', [(i, (i + k) % run) for i in range(run)])  152 us
    ppermute x41, waiting for transfers between devices, swap(): return lax.ppermute(value, axis, [(i, i ^ bit) for i in range(size)])  124 us
    all_to_all x8, waiting for transfers between devices, exchange(): return lax.all_to_all(value, axis, 0, 0, tiled=True)  104 us
    all_to_all x2, blocking collectives, exchange(): return lax.all_to_all(value, axis, 0, 0, tiled=True)  102 us
    dot_general x9, matrix products, over_rows(): lax.dot_general(left, right, (((0,), (0,)), ((), ())), preferred_element_...  62.1 us
    ppermute x27, starting transfers between devices, shift_blocks(): block = lax.ppermute(block, 'wsh', [(i, (i + k) % run) for i in range(run)])  40.3 us
    reduce_scatter x1, waiting for transfers between devices, shards(): lax.psum_scatter(pair_part, COPIES, scatter_dimension=0, tiled=True)  37.4 us
    all_to_all x8, starting transfers between devices, exchange(): return lax.all_to_all(value, axis, 0, 0, tiled=True)  36.4 us
  transfers between devices with their start and end apart: 81, of which 29 were waited for; matrix products, arithmetic and copies ran while one was open for 30% of the time, Pallas kernels for 1%

profile of v2, /device:TPU:0, one launch (start us, length us, event | category | flops | bytes accessed | tf_op | source)
XLA Modules:
  0.0 1092.0 jit_solution(17185721714300932434)
XLA Ops:
  8.1 5.0 collective-permute-start.2
  25.0 5.6 collective-permute-done.5
  30.6 16.6 %collective-permute-done.4 = bf16[80,1664]{1,0:T(8,128)(2,1)S(1)} collective-permute-done((bf16[80,1664]{1,0:T(8,128)(2,1)S(1)}, bf16[80,1664]{1,0:T(8,128)(2,1)S(1)}, u32[]{:S(2)}, u32[]{:S(2)}) %collective-permute-start.4) | collective-permute-done | bytes 266272 | tf_op jit(solution)/shard_map/ppermute | solution.py:352
  79.8 28.1 %all-to-all-done = bf16[4,128,2048]{2,1,0:T(8,128)(2,1)} async-done(((bf16[4,128,2048]{2,1,0:T(8,128)(2,1)}), bf16[4,128,2048]{2,1,0:T(8,128)(2,1)}, u32[]{:S(2)}, u32[]{:S(2)}) %all-to-all-start) | async-done | bytes 2097184 | tf_op jit(solution)/shard_map/all_to_all | solution.py:79
  133.2 4.6 all-to-all-start.1
  138.1 14.7 %fusion.9 = bf16[4096,256]{1,0:T(8,128)(2,1)} fusion(bf16[4096,256]{1,0:T(8,128)(2,1)} %param.27, s32[4096]{0:T(1024)S(1)} %copy-done.111), kind=kOutput, calls=%fused_computation.25 | convolution fusion | flops 8607760384 | bytes 4210688 | tf_op jit(solution)/shard_map/dot_general | solution.py:53
  176.3 6.1 fusion.53
  182.4 12.9 %fusion.146 = (f32[2,512]{1,0:T(2,128)S(1)}, f32[2,512,2048]{1,2,0:T(8,128)}) fusion(f32[2048,512,2]{1,0,2:T(8,128)} %fusion.53, pred[512,2048]{0,1:T(8,128)(4,1)S(1)} %copy-done.50), kind=kOutput, calls=%fused_computation.442 | output fusion | flops 8390655 | bytes 17829888 | tf_op jit(solution)/shard_map/sub | solution.py:613
  195.3 4.6 fusion.15
  206.7 4.7 all-to-all-start.2
  219.6 22.2 %collective-permute-done.13 = bf16[1024,256]{1,0:T(8,128)(2,1)S(1)} collective-permute-done((bf16[1024,256]{1,0:T(8,128)(2,1)S(1)}, bf16[1024,256]{1,0:T(8,128)(2,1)S(1)}, u32[]{:S(2)}, u32[]{:S(2)}) %collective-permute-start.13) | collective-permute-done | bytes 524320 | tf_op jit(solution)/shard_map/ppermute | solution.py:97
  244.7 9.6 collective-permute-done.14
  263.8 50.9 %all_to_all.88 = bf16[4,128,2048]{2,1,0:T(8,128)(2,1)} all-to-all(bf16[4,128,2048]{2,1,0:T(8,128)(2,1)S(1)} %broadcast_in_dim.239), channel_id=1, replica_groups=mesh['slot'=2,'ctx'=4,'wsh'=4] {'wsh'}, dimensions={0} | all-to-all | bytes 4194304 | tf_op jit(solution)/shard_map/all_to_all | solution.py:79
  314.7 23.8 %shard_map.324 = (f32[512,4096]{1,0:T(8,128)}, bf16[512,2048]{1,0:T(8,128)(2,1)}, bf16[512,2048]{1,0:T(8,128)(2,1)}) custom-call(bf16[512,2048]{1,0:T(8,128)(2,1)} %bitcast.401, bf16[4096,2048]{1,0:T(8,128)(2,1)} %all-gather.6.cloned.1.call-done.pair_ref, bf16[2048,2048]{1,0:T(8,128)(2,1)} %down_ref.3), custom_call_target="tpu_custom_call" | custom-call | flops 12884901888 | bytes 35651584 | tf_op jit(solution)/shard_map/pallas_call | solution.py:243
  338.5 4.6 all-to-all-start.4
  352.3 26.6 %collective-permute-done.17 = bf16[128,256]{1,0:T(8,128)(2,1)S(1)} collective-permute-done((bf16[128,256]{1,0:T(8,128)(2,1)S(1)}, bf16[128,256]{1,0:T(8,128)(2,1)S(1)}, u32[]{:S(2)}, u32[]{:S(2)}) %collective-permute-start.17) | collective-permute-done | bytes 65568 | tf_op jit(solution)/shard_map/ppermute | solution.py:352
  378.9 17.1 %collective-permute-done.16 = bf16[128,256]{1,0:T(8,128)(2,1)S(1)} collective-permute-done((bf16[128,256]{1,0:T(8,128)(2,1)S(1)}, bf16[128,256]{1,0:T(8,128)(2,1)S(1)}, u32[]{:S(2)}, u32[]{:S(2)}) %collective-permute-start.16) | collective-permute-done | bytes 65568 | tf_op jit(solution)/shard_map/ppermute | solution.py:352
  412.0 50.8 %all_to_all.89 = bf16[4,128,2048]{2,1,0:T(8,128)(2,1)} all-to-all(bf16[4,128,2048]{2,1,0:T(8,128)(2,1)S(1)} %broadcast_in_dim.243), channel_id=1, replica_groups=mesh['slot'=2,'ctx'=4,'wsh'=4] {'wsh'}, dimensions={0} | all-to-all | bytes 4194304 | tf_op jit(solution)/shard_map/all_to_all | solution.py:79
  462.9 25.4 %shard_map.325 = (bf16[512,4096]{1,0:T(8,128)(2,1)}, bf16[512,2048]{1,0:T(8,128)(2,1)}) custom-call(bf16[512,2048]{1,0:T(8,128)(2,1)} %bitcast.404, bf16[2048,2048]{1,0:T(8,128)(2,1)} %down_ref.3, f32[512,4096]{1,0:T(8,128)} %get-tuple-element.99.both_ref, bf16[4096,2048]{1,0:T(8,128)(2,1)} %all-gather.6.cloned.1.call-done.pair_ref), custom_call_target="tpu_custom_call" | custom-call | flops 12884901888 | bytes 37748736 | tf_op jit(solution)/shard_map/pallas_call | solution.py:300
  488.3 4.5 all-to-all-start.6
  492.8 15.1 %convolution_convert_fusion = bf16[4096,2048]{1,0:T(8,128)(2,1)} fusion(bf16[512,4096]{1,0:T(8,128)(2,1)} %get-tuple-element.101, bf16[512,2048]{1,0:T(8,128)(2,1)} %bitcast.402), kind=kOutput, calls=%fused_computation.14 | convolution fusion | flops 8598323200 | bytes 23068672 | tf_op jit(solution)/shard_map/dot_general | solution.py:63
  507.9 32.2 %all-to-all-done.6 = bf16[4,128,2048]{2,1,0:T(8,128)(2,1)} async-done(((bf16[4,128,2048]{2,1,0:T(8,128)(2,1)}), bf16[4,128,2048]{2,1,0:T(8,128)(2,1)}, u32[]{:S(2)}, u32[]{:S(2)}) %all-to-all-start.6) | async-done | bytes 2097184 | tf_op jit(solution)/shard_map/all_to_all | solution.py:79
  554.2 4.5 all-to-all-start.7
  559.2 11.2 %convolution_convert_fusion.1 = bf16[2048,2048]{1,0:T(8,128)(2,1)} fusion(bf16[512,2048]{1,0:T(8,128)(2,1)} %get-tuple-element.104, bf16[512,2048]{1,0:T(8,128)(2,1)} %bitcast.405), kind=kOutput, calls=%fused_computation.20 | convolution fusion | flops 4299161600 | bytes 12582912 | tf_op jit(solution)/shard_map/dot_general | solution.py:63
  570.4 35.6 %all-to-all-done.7 = bf16[4,128,2048]{2,1,0:T(8,128)(2,1)} async-done(((bf16[4,128,2048]{2,1,0:T(8,128)(2,1)}), bf16[4,128,2048]{2,1,0:T(8,128)(2,1)}, u32[]{:S(2)}, u32[]{:S(2)}) %all-to-all-start.7) | async-done | bytes 2097184 | tf_op jit(solution)/shard_map/all_to_all | solution.py:79
  609.2 5.3 fusion.6
  621.2 37.4 %reduce-scatter.2.cloned.1.call-done = bf16[512,2048]{1,0:T(8,128)(2,1)} async-done(((bf16[4096,2048]{1,0:T(8,128)(2,1)}), bf16[512,2048]{1,0:T(8,128)(2,1)}) %reduce-scatter.2.cloned.1.call-update) | async-done | bytes 2097168 | tf_op jit(solution)/shard_map/reduce_scatter | solution.py:688
  674.8 4.5 all-to-all-start.8
  695.1 5.0 collective-permute-done.24
  701.4 51.9 %collective-permute-done.23 = bf16[512,640]{1,0:T(8,128)(2,1)S(1)} collective-permute-done((bf16[512,640]{1,0:T(8,128)(2,1)S(1)}, bf16[512,640]{1,0:T(8,128)(2,1)S(1)}, u32[]{:S(2)}, u32[]{:S(2)}) %collective-permute-start.23) | collective-permute-done | bytes 655392 | tf_op jit(solution)/shard_map/ppermute | solution.py:352
  755.2 4.5 gather_fusion.3
  763.2 22.7 %collective-permute-done.19 = bf16[2,512,256]{1,2,0:T(8,128)(2,1)} collective-permute-done((bf16[2,512,256]{1,2,0:T(8,128)(2,1)}, bf16[2,512,256]{1,2,0:T(8,128)(2,1)}, u32[]{:S(2)}, u32[]{:S(2)}) %collective-permute-start.19) | collective-permute-done | bytes 524320 | tf_op jit(solution)/shard_map/ppermute | solution.py:352
  822.1 4.7 convolution_convert_fusion.2
  842.3 6.1 convolution_convert_fusion.3
  851.2 4.7 all-to-all-start.9
  864.9 9.8 collective-permute-done.33
  875.7 21.6 %collective-permute-done.38 = bf16[512,256]{1,0:T(8,128)(2,1)S(1)} collective-permute-done((bf16[512,256]{1,0:T(8,128)(2,1)S(1)}, bf16[512,256]{1,0:T(8,128)(2,1)S(1)}, u32[]{:S(2)}, u32[]{:S(2)}) %collective-permute-start.38) | collective-permute-done | bytes 262176 | tf_op jit(solution)/shard_map/ppermute | solution.py:97
  898.6 26.7 %collective-permute-done.60 = bf16[512,640]{1,0:T(8,128)(2,1)S(1)} collective-permute-done((bf16[512,640]{1,0:T(8,128)(2,1)S(1)}, bf16[512,640]{1,0:T(8,128)(2,1)S(1)}, u32[]{:S(2)}, u32[]{:S(2)}) %collective-permute-start.60) | collective-permute-done | bytes 655392 | tf_op jit(solution)/shard_map/ppermute | solution.py:97
  928.1 11.8 %convert_element_type.449 = f32[2048,2048]{1,0:T(8,128)} convert(bf16[2048,2048]{1,0:T(8,128)(2,1)} %all-reduce.10.cloned.1.call-done) | non-fusion elementwise | flops 4194304 | bytes 25165824 | tf_op jit(solution)/shard_map/convert_element_type | solution.py:836
  941.9 4.8 collective-permute-done.32
  951.8 24.5 %fusion.8 = f32[4096,256]{1,0:T(8,128)} fusion(s32[4096]{0:T(1024)S(1)} %copy-done.112, bf16[2048,256]{1,0:T(8,128)(2,1)} %collective-permute-done.40, bf16[1024,256]{1,0:T(8,128)(2,1)S(1)} %copy-done.63, bf16[512,256]{1,0:T(8,128)(2,1)S(1)} %collective-permute-done.38, bf16[512,256]{1,0:T(8,128)(2,1)S(1)} %bitcast.398), kind=kOutput, calls=%fused_computation.22 | convolution fusion | flops 8616148992 | bytes 6307840 | tf_op jit(solution)/shard_map/dot_general | solution.py:63
  990.0 6.4 collective-permute-done.63
  1008.6 6.7 collective-permute-done.66
  1023.1 7.6 collective-permute-done.45.refs_2_
  1036.6 5.3 collective-permute-done.47
  1046.6 5.1 shard_map.327
  1052.9 6.2 shard_map.326
  1059.1 25.9 %shard_map.328 = (f32[512,8192]{1,0:T(8,128)}, f32[512,8192]{1,0:T(8,128)}) custom-call(s32[4]{0:T(128)} %and_select_fusion.1.places, bf16[8,4,2,512,256]{4,3,2,1,0:T(8,128)(2,1)} %bitcast.380), custom_call_target="tpu_custom_call" | custom-call | bytes 50331648 | tf_op jit(solution)/shard_map/pallas_call | solution.py:332
  (695 shorter events, 328.5 us)
Async XLA Ops:
  7.2 115.1 %all-gather.8.cloned.1.call-start = ((), (), s32[]{:S(2)}) async-start(), calls=%async_computation.14 | async-start | bytes 7667712 | tf_op jit(solution)/shard_map/all_gather | solution.py:527
  23.8 23.4 %collective-permute-start.4 = (bf16[80,1664]{1,0:T(8,128)(2,1)S(1)}, bf16[80,1664]{1,0:T(8,128)(2,1)S(1)}, u32[]{:S(2)}, u32[]{:S(2)}) collective-permute-start(bf16[80,1664]{1,0:T(8,128)(2,1)S(1)} %get-tuple-element.346), channel_id=1, source_target_pairs={{0,2},{1,3},{2,0},{3,1},{4,6},{5,7},{6,4},{7,5},{8,10},{9,11},{10,... | collective-permute-start | bytes 798728 | tf_op jit(solution)/shard_map/ppermute | solution.py:352
  25.0 22.3 %collective-permute-start.3 = (bf16[80,1664]{1,0:T(8,128)(2,1)S(1)}, bf16[80,1664]{1,0:T(8,128)(2,1)S(1)}, u32[]{:S(2)}, u32[]{:S(2)}) collective-permute-start(bf16[80,1664]{1,0:T(8,128)(2,1)S(1)} %get-tuple-element.345), channel_id=1, source_target_pairs={{0,1},{1,2},{2,3},{3,0},{4,5},{5,6},{6,7},{7,4},{8,9},{9,10},{10,1... | collective-permute-start | bytes 798728 | tf_op jit(solution)/shard_map/ppermute | solution.py:352
  56.2 51.6 %all-to-all-start = ((bf16[4,128,2048]{2,1,0:T(8,128)(2,1)}), bf16[4,128,2048]{2,1,0:T(8,128)(2,1)}, u32[]{:S(2)}, u32[]{:S(2)}) async-start(bf16[4,128,2048]{2,1,0:T(8,128)(2,1)} %broadcast_in_dim.129), calls=%async_computation | async-start | bytes 4194304 | tf_op jit(solution)/shard_map/all_to_all | solution.py:79
  109.8 43.8 %collective-permute-start.9 = (bf16[512,512]{1,0:T(8,128)(2,1)}, bf16[512,512]{1,0:T(8,128)(2,1)}, u32[]{:S(2)}, u32[]{:S(2)}) collective-permute-start(bf16[512,512]{1,0:T(8,128)(2,1)} %pad_maximum_fusion.10), channel_id=1, source_target_pairs={{0,1},{1,2},{2,3},{3,0},{4,5},{5,6},{6,7},{7,4},{8,9},{9,10},{10,1... | collective-permute-start | bytes 1572872 | tf_op jit(solution)/shard_map/ppermute | solution.py:352
  111.5 42.1 %collective-permute-start.10 = (bf16[512,512]{1,0:T(8,128)(2,1)}, bf16[512,512]{1,0:T(8,128)(2,1)}, u32[]{:S(2)}, u32[]{:S(2)}) collective-permute-start(bf16[512,512]{1,0:T(8,128)(2,1)} %pad_maximum_fusion.11), channel_id=1, source_target_pairs={{0,2},{1,3},{2,0},{3,1},{4,6},{5,7},{6,4},{7,5},{8,10},{9,11},{10,... | collective-permute-start | bytes 1572872 | tf_op jit(solution)/shard_map/ppermute | solution.py:352
  114.0 39.7 %collective-permute-start.11 = (bf16[512,512]{1,0:T(8,128)(2,1)}, bf16[512,512]{1,0:T(8,128)(2,1)}, u32[]{:S(2)}, u32[]{:S(2)}) collective-permute-start(bf16[512,512]{1,0:T(8,128)(2,1)} %pad_maximum_fusion.12), channel_id=1, source_target_pairs={{0,3},{1,0},{2,1},{3,2},{4,7},{5,4},{6,5},{7,6},{8,11},{9,8},{10,9... | collective-permute-start | bytes 1572872 | tf_op jit(solution)/shard_map/ppermute | solution.py:352
  133.2 28.9 %all-to-all-start.1 = ((bf16[4,512,512]{2,1,0:T(8,128)(2,1)}), bf16[4,512,512]{2,1,0:T(8,128)(2,1)}, u32[]{:S(2)}, u32[]{:S(2)}) async-start(bf16[4,512,512]{2,1,0:T(8,128)(2,1)} %broadcast_in_dim.234), calls=%async_computation.1 | async-start | bytes 4194304 | tf_op jit(solution)/shard_map/all_to_all | solution.py:79
  137.8 176.9 %all-gather.6.cloned.1.call-start = ((), (), s32[]{:S(2)}) async-start(), calls=%async_computation.11 | async-start | bytes 18874368 | tf_op jit(solution)/shard_map/all_gather | solution.py:597
  206.7 52.4 %all-to-all-start.2 = ((bf16[4,128,2048]{2,1,0:T(8,128)(2,1)}), bf16[4,128,2048]{2,1,0:T(8,128)(2,1)}, u32[]{:S(2)}, u32[]{:S(2)}) async-start(bf16[4,128,2048]{2,1,0:T(8,128)(2,1)} %bitcast.406), calls=%async_computation.2 | async-start | bytes 4194304 | tf_op jit(solution)/shard_map/all_to_all | solution.py:79
  215.9 25.8 %collective-permute-start.13 = (bf16[1024,256]{1,0:T(8,128)(2,1)S(1)}, bf16[1024,256]{1,0:T(8,128)(2,1)S(1)}, u32[]{:S(2)}, u32[]{:S(2)}) collective-permute-start(bf16[1024,256]{1,0:T(8,128)(2,1)S(1)} %slice.327), channel_id=1, source_target_pairs={{0,8},{4,12},{8,0},{12,4},{1,9},{5,13},{9,1},{13,5},{2,10},{6,14},... | collective-permute-start | bytes 1572872 | tf_op jit(solution)/shard_map/ppermute | solution.py:97
  338.5 62.2 %all-to-all-start.4 = ((bf16[4,128,2048]{2,1,0:T(8,128)(2,1)}), bf16[4,128,2048]{2,1,0:T(8,128)(2,1)}, u32[]{:S(2)}, u32[]{:S(2)}) async-start(bf16[4,128,2048]{2,1,0:T(8,128)(2,1)} %bitcast.403), calls=%async_computation.4 | async-start | bytes 4194304 | tf_op jit(solution)/shard_map/all_to_all | solution.py:79
  344.2 34.7 %collective-permute-start.17 = (bf16[128,256]{1,0:T(8,128)(2,1)S(1)}, bf16[128,256]{1,0:T(8,128)(2,1)S(1)}, u32[]{:S(2)}, u32[]{:S(2)}) collective-permute-start(bf16[128,256]{1,0:T(8,128)(2,1)S(1)} %get-tuple-element.337), channel_id=1, source_target_pairs={{0,3},{1,0},{2,1},{3,2},{4,7},{5,4},{6,5},{7,6},{8,11},{9,8},{10,9... | collective-permute-start | bytes 196616 | tf_op jit(solution)/shard_map/ppermute | solution.py:352
  348.0 48.0 %collective-permute-start.16 = (bf16[128,256]{1,0:T(8,128)(2,1)S(1)}, bf16[128,256]{1,0:T(8,128)(2,1)S(1)}, u32[]{:S(2)}, u32[]{:S(2)}) collective-permute-start(bf16[128,256]{1,0:T(8,128)(2,1)S(1)} %get-tuple-element.338), channel_id=1, source_target_pairs={{0,2},{1,3},{2,0},{3,1},{4,6},{5,7},{6,4},{7,5},{8,10},{9,11},{10,... | collective-permute-start | bytes 196616 | tf_op jit(solution)/shard_map/ppermute | solution.py:352
  348.0 48.0 %collective-permute-start.15 = (bf16[128,256]{1,0:T(8,128)(2,1)S(1)}, bf16[128,256]{1,0:T(8,128)(2,1)S(1)}, u32[]{:S(2)}, u32[]{:S(2)}) collective-permute-start(bf16[128,256]{1,0:T(8,128)(2,1)S(1)} %get-tuple-element.339), channel_id=1, source_target_pairs={{0,1},{1,2},{2,3},{3,0},{4,5},{5,6},{6,7},{7,4},{8,9},{9,10},{10,1... | collective-permute-start | bytes 196616 | tf_op jit(solution)/shard_map/ppermute | solution.py:352
  488.3 51.8 %all-to-all-start.6 = ((bf16[4,128,2048]{2,1,0:T(8,128)(2,1)}), bf16[4,128,2048]{2,1,0:T(8,128)(2,1)}, u32[]{:S(2)}, u32[]{:S(2)}) async-start(bf16[4,128,2048]{2,1,0:T(8,128)(2,1)} %bitcast.407), calls=%async_computation.6 | async-start | bytes 4194304 | tf_op jit(solution)/shard_map/all_to_all | solution.py:79
  492.7 165.9 %reduce-scatter.2.cloned.1.call-start = ((), (), s32[]{:S(2)}) async-start(), calls=%async_computation.12 | async-start | bytes 18874368 | tf_op jit(solution)/shard_map/reduce_scatter | solution.py:688
  554.2 51.8 %all-to-all-start.7 = ((bf16[4,128,2048]{2,1,0:T(8,128)(2,1)}), bf16[4,128,2048]{2,1,0:T(8,128)(2,1)}, u32[]{:S(2)}, u32[]{:S(2)}) async-start(bf16[4,128,2048]{2,1,0:T(8,128)(2,1)} %broadcast_in_dim.245), calls=%async_computation.7 | async-start | bytes 4194304 | tf_op jit(solution)/shard_map/all_to_all | solution.py:79
  558.7 369.4 %all-reduce.10.cloned.1.call-start = ((), (), s32[]{:S(2)}) async-start(), calls=%async_computation.13 | async-start | bytes 16777216 | tf_op jit(solution)/shard_map/psum | solution.py:731
  674.8 114.1 %all-to-all-start.8 = ((bf16[4,512,512]{1,2,0:T(8,128)(2,1)}), bf16[4,512,512]{1,2,0:T(8,128)(2,1)}, u32[]{:S(2)}, u32[]{:S(2)}) async-start(bf16[4,512,512]{1,2,0:T(8,128)(2,1)} %bitcast.382), calls=%async_computation.9 | async-start | bytes 4194304 | tf_op jit(solution)/shard_map/all_to_all | solution.py:79
  679.3 379.8 %all-gather.10.cloned.1.call-start = ((), (), s32[]{:S(2)}) async-start(), calls=%async_computation.15 | async-start | bytes 18874368 | tf_op jit(solution)/shard_map/all_gather | solution.py:737
  681.6 18.6 %collective-permute-start.24 = (bf16[512,640]{1,0:T(8,128)(2,1)S(1)}, bf16[512,640]{1,0:T(8,128)(2,1)S(1)}, u32[]{:S(2)}, u32[]{:S(2)}) collective-permute-start(bf16[512,640]{1,0:T(8,128)(2,1)S(1)} %get-tuple-element.291), channel_id=1, source_target_pairs={{0,3},{1,0},{2,1},{3,2},{4,7},{5,4},{6,5},{7,6},{8,11},{9,8},{10,9... | collective-permute-start | bytes 1966088 | tf_op jit(solution)/shard_map/ppermute | solution.py:352
  684.7 68.6 %collective-permute-start.23 = (bf16[512,640]{1,0:T(8,128)(2,1)S(1)}, bf16[512,640]{1,0:T(8,128)(2,1)S(1)}, u32[]{:S(2)}, u32[]{:S(2)}) collective-permute-start(bf16[512,640]{1,0:T(8,128)(2,1)S(1)} %get-tuple-element.292), channel_id=1, source_target_pairs={{0,2},{1,3},{2,0},{3,1},{4,6},{5,7},{6,4},{7,5},{8,10},{9,11},{10,... | collective-permute-start | bytes 1966088 | tf_op jit(solution)/shard_map/ppermute | solution.py:352
  684.7 68.6 %collective-permute-start.22 = (bf16[512,640]{1,0:T(8,128)(2,1)S(1)}, bf16[512,640]{1,0:T(8,128)(2,1)S(1)}, u32[]{:S(2)}, u32[]{:S(2)}) collective-permute-start(bf16[512,640]{1,0:T(8,128)(2,1)S(1)} %get-tuple-element.293), channel_id=1, source_target_pairs={{0,1},{1,2},{2,3},{3,0},{4,5},{5,6},{6,7},{7,4},{8,9},{9,10},{10,1... | collective-permute-start | bytes 1966088 | tf_op jit(solution)/shard_map/ppermute | solution.py:352
  690.1 101.8 %collective-permute-start.21 = (bf16[4,64,2048]{2,1,0:T(8,128)(2,1)}, bf16[4,64,2048]{2,1,0:T(8,128)(2,1)}, u32[]{:S(2)}, u32[]{:S(2)}) collective-permute-start(bf16[4,64,2048]{2,1,0:T(8,128)(2,1)} %get-tuple-element.298), channel_id=1, source_target_pairs={{0,16},{16,0},{1,17},{17,1},{2,18},{18,2},{3,19},{19,3},{4,20},{20... | collective-permute-start | bytes 3145736 | tf_op jit(solution)/shard_map/ppermute | solution.py:97
  692.4 70.8 %collective-permute-start.20 = (bf16[2,512,256]{1,2,0:T(8,128)(2,1)}, bf16[2,512,256]{1,2,0:T(8,128)(2,1)}, u32[]{:S(2)}, u32[]{:S(2)}) collective-permute-start(bf16[2,512,256]{1,2,0:T(8,128)(2,1)} %bitcast.85), channel_id=1, source_target_pairs={{0,3},{1,0},{2,1},{3,2},{4,7},{5,4},{6,5},{7,6},{8,11},{9,8},{10,9... | collective-permute-start | bytes 1572872 | tf_op jit(solution)/shard_map/ppermute | solution.py:352
  700.2 85.8 %collective-permute-start.19 = (bf16[2,512,256]{1,2,0:T(8,128)(2,1)}, bf16[2,512,256]{1,2,0:T(8,128)(2,1)}, u32[]{:S(2)}, u32[]{:S(2)}) collective-permute-start(bf16[2,512,256]{1,2,0:T(8,128)(2,1)} %bitcast.82), channel_id=1, source_target_pairs={{0,2},{1,3},{2,0},{3,1},{4,6},{5,7},{6,4},{7,5},{8,10},{9,11},{10,... | collective-permute-start | bytes 1572872 | tf_op jit(solution)/shard_map/ppermute | solution.py:352
  753.3 32.7 %collective-permute-start.18 = (bf16[2,512,256]{1,2,0:T(8,128)(2,1)}, bf16[2,512,256]{1,2,0:T(8,128)(2,1)}, u32[]{:S(2)}, u32[]{:S(2)}) collective-permute-start(bf16[2,512,256]{1,2,0:T(8,128)(2,1)} %bitcast.79), channel_id=1, source_target_pairs={{0,1},{1,2},{2,3},{3,0},{4,5},{5,6},{6,7},{7,4},{8,9},{9,10},{10,1... | collective-permute-start | bytes 1572872 | tf_op jit(solution)/shard_map/ppermute | solution.py:352
  797.4 35.0 %collective-permute-start.37 = (bf16[128,256]{1,0:T(8,128)(2,1)S(1)}, bf16[128,256]{1,0:T(8,128)(2,1)}, u32[]{:S(2)}, u32[]{:S(2)}) collective-permute-start(bf16[128,256]{1,0:T(8,128)(2,1)S(1)} %copy-done.82), channel_id=1, source_target_pairs={{0,3},{1,0},{2,1},{3,2},{4,7},{5,4},{6,5},{7,6},{8,11},{9,8},{10,9... | collective-permute-start | bytes 196616 | tf_op jit(solution)/shard_map/ppermute | solution.py:352
  797.4 35.0 %collective-permute-start.36 = (bf16[128,256]{1,0:T(8,128)(2,1)S(1)}, bf16[128,256]{1,0:T(8,128)(2,1)}, u32[]{:S(2)}, u32[]{:S(2)}) collective-permute-start(bf16[128,256]{1,0:T(8,128)(2,1)S(1)} %copy-done.82), channel_id=1, source_target_pairs={{0,2},{1,3},{2,0},{3,1},{4,6},{5,7},{6,4},{7,5},{8,10},{9,11},{10,... | collective-permute-start | bytes 196616 | tf_op jit(solution)/shard_map/ppermute | solution.py:352
  800.3 32.2 %collective-permute-start.35 = (bf16[128,256]{1,0:T(8,128)(2,1)S(1)}, bf16[128,256]{1,0:T(8,128)(2,1)}, u32[]{:S(2)}, u32[]{:S(2)}) collective-permute-start(bf16[128,256]{1,0:T(8,128)(2,1)S(1)} %copy-done.82), channel_id=1, source_target_pairs={{0,1},{1,2},{2,3},{3,0},{4,5},{5,6},{6,7},{7,4},{8,9},{9,10},{10,1... | collective-permute-start | bytes 196616 | tf_op jit(solution)/shard_map/ppermute | solution.py:352
  829.3 21.2 %collective-permute-start.27 = (bf16[4,4,64,1024]{3,2,0,1:T(8,128)(2,1)}, bf16[4,4,64,1024]{3,2,0,1:T(8,128)(2,1)}, u32[]{:S(2)}, u32[]{:S(2)}) collective-permute-start(bf16[4,4,64,1024]{3,2,0,1:T(8,128)(2,1)} %get-tuple-element.288), channel_id=1, source_target_pairs={{0,16},{16,0},{1,17},{17,1},{2,18},{18,2},{3,19},{19,3},{4,20},{20... | collective-permute-start | bytes 6291464 | tf_op jit(solution)/shard_map/ppermute | solution.py:97
  851.2 125.2 %all-to-all-start.9 = ((bf16[4,128,2048]{2,1,0:T(8,128)(2,1)}), bf16[4,128,2048]{2,1,0:T(8,128)(2,1)}, u32[]{:S(2)}, u32[]{:S(2)}) async-start(bf16[4,128,2048]{2,1,0:T(8,128)(2,1)} %bitcast.400), calls=%async_computation.10 | async-start | bytes 4194304 | tf_op jit(solution)/shard_map/all_to_all | solution.py:79
  861.9 116.8 %collective-permute-start.29 = (bf16[64,2048]{1,0:T(8,128)(2,1)}, bf16[64,2048]{1,0:T(8,128)(2,1)}, u32[]{:S(2)}, u32[]{:S(2)}) collective-permute-start(bf16[64,2048]{1,0:T(8,128)(2,1)} %pad_maximum_fusion.31), channel_id=1, source_target_pairs={{0,4},{4,0},{8,12},{12,8},{1,5},{5,1},{9,13},{13,9},{2,6},{6,2},{1... | collective-permute-start | bytes 786440 | tf_op jit(solution)/shard_map/ppermute | solution.py:97
  862.8 34.5 %collective-permute-start.31 = (bf16[2,64,1024]{2,1,0:T(8,128)(2,1)S(1)}, bf16[2,64,1024]{2,1,0:T(8,128)(2,1)S(1)}, u32[]{:S(2)}, u32[]{:S(2)}) collective-permute-start(bf16[2,64,1024]{2,1,0:T(8,128)(2,1)S(1)} %get-tuple-element.296), channel_id=1, source_target_pairs={{0,8},{4,12},{8,0},{12,4},{1,9},{5,13},{9,1},{13,5},{2,10},{6,14},... | collective-permute-start | bytes 786440 | tf_op jit(solution)/shard_map/ppermute | solution.py:97
  862.8 34.4 %collective-permute-start.38 = (bf16[512,256]{1,0:T(8,128)(2,1)S(1)}, bf16[512,256]{1,0:T(8,128)(2,1)S(1)}, u32[]{:S(2)}, u32[]{:S(2)}) collective-permute-start(bf16[512,256]{1,0:T(8,128)(2,1)S(1)} %bitcast.395), channel_id=1, source_target_pairs={{0,4},{4,0},{8,12},{12,8},{1,5},{5,1},{9,13},{13,9},{2,6},{6,2},{1... | collective-permute-start | bytes 786440 | tf_op jit(solution)/shard_map/ppermute | solution.py:97
  863.9 61.4 %collective-permute-start.60 = (bf16[512,640]{1,0:T(8,128)(2,1)S(1)}, bf16[512,640]{1,0:T(8,128)(2,1)S(1)}, u32[]{:S(2)}, u32[]{:S(2)}) collective-permute-start(bf16[512,640]{1,0:T(8,128)(2,1)S(1)} %copy-done.36), channel_id=1, source_target_pairs={{0,4},{4,0},{8,12},{12,8},{1,5},{5,1},{9,13},{13,9},{2,6},{6,2},{1... | collective-permute-start | bytes 1966088 | tf_op jit(solution)/shard_map/ppermute | solution.py:97
  875.7 64.2 %collective-permute-start.34 = (bf16[4,64,1024]{2,1,0:T(8,128)(2,1)}, bf16[4,64,1024]{2,1,0:T(8,128)(2,1)}, u32[]{:S(2)}, u32[]{:S(2)}) collective-permute-start(bf16[4,64,1024]{2,1,0:T(8,128)(2,1)} %pad_maximum_fusion.15), channel_id=1, source_target_pairs={{0,8},{4,12},{8,0},{12,4},{1,9},{5,13},{9,1},{13,5},{2,10},{6,14},... | collective-permute-start | bytes 1572872 | tf_op jit(solution)/shard_map/ppermute | solution.py:97
  897.3 28.3 %collective-permute-start.39 = (bf16[1024,256]{1,0:T(8,128)(2,1)S(1)}, bf16[1024,256]{1,0:T(8,128)(2,1)S(1)}, u32[]{:S(2)}, u32[]{:S(2)}) collective-permute-start(bf16[1024,256]{1,0:T(8,128)(2,1)S(1)} %pad_maximum_fusion.16), channel_id=1, source_target_pairs={{0,8},{4,12},{8,0},{12,4},{1,9},{5,13},{9,1},{13,5},{2,10},{6,14},... | collective-permute-start | bytes 1572872 | tf_op jit(solution)/shard_map/ppermute | solution.py:97
  898.3 48.3 %collective-permute-start.32 = (bf16[4,64,1024]{2,1,0:T(8,128)(2,1)}, bf16[4,64,1024]{2,1,0:T(8,128)(2,1)}, u32[]{:S(2)}, u32[]{:S(2)}) collective-permute-start(bf16[4,64,1024]{2,1,0:T(8,128)(2,1)} %pad_maximum_fusion.14), channel_id=1, source_target_pairs={{0,4},{4,0},{8,12},{12,8},{1,5},{5,1},{9,13},{13,9},{2,6},{6,2},{1... | collective-permute-start | bytes 1572872 | tf_op jit(solution)/shard_map/ppermute | solution.py:97
  925.5 23.7 %collective-permute-start.61 = (bf16[512,640]{1,0:T(8,128)(2,1)S(1)}, bf16[512,640]{1,0:T(8,128)(2,1)}, u32[]{:S(2)}, u32[]{:S(2)}) collective-permute-start(bf16[512,640]{1,0:T(8,128)(2,1)S(1)} %add_convert_fusion.4), channel_id=1, source_target_pairs={{0,8},{4,12},{8,0},{12,4},{1,9},{5,13},{9,1},{13,5},{2,10},{6,14},... | collective-permute-start | bytes 1966088 | tf_op jit(solution)/shard_map/ppermute | solution.py:97
  927.4 24.2 %collective-permute-start.40 = (bf16[2048,256]{1,0:T(8,128)(2,1)}, bf16[2048,256]{1,0:T(8,128)(2,1)}, u32[]{:S(2)}, u32[]{:S(2)}) collective-permute-start(bf16[2048,256]{1,0:T(8,128)(2,1)} %pad_maximum_fusion.7), channel_id=1, source_target_pairs={{0,16},{16,0},{1,17},{17,1},{2,18},{18,2},{3,19},{19,3},{4,20},{20... | collective-permute-start | bytes 3145736 | tf_op jit(solution)/shard_map/ppermute | solution.py:97
  939.9 38.8 %collective-permute-start.30 = (bf16[64,2048]{1,0:T(8,128)(2,1)}, bf16[64,2048]{1,0:T(8,128)(2,1)}, u32[]{:S(2)}, u32[]{:S(2)}) collective-permute-start(bf16[64,2048]{1,0:T(8,128)(2,1)} %pad_maximum_fusion.32), channel_id=1, source_target_pairs={{0,8},{4,12},{8,0},{12,4},{1,9},{5,13},{9,1},{13,5},{2,10},{6,14},... | collective-permute-start | bytes 786440 | tf_op jit(solution)/shard_map/ppermute | solution.py:97
  996.4 20.9 %collective-permute-start.52 = (bf16[64,2048]{1,0:T(8,128)(2,1)S(1)}, bf16[64,2048]{1,0:T(8,128)(2,1)}, u32[]{:S(2)}, u32[]{:S(2)}) collective-permute-start(bf16[64,2048]{1,0:T(8,128)(2,1)S(1)} %fusion.71), channel_id=1, source_target_pairs={{0,4},{4,0},{8,12},{12,8},{1,5},{5,1},{9,13},{13,9},{2,6},{6,2},{1... | collective-permute-start | bytes 786440 | tf_op jit(solution)/shard_map/ppermute | solution.py:97
  998.4 20.3 %collective-permute-start.44 = (bf16[4,64,1024]{2,1,0:T(8,128)(2,1)S(1)}, bf16[4,64,1024]{2,1,0:T(8,128)(2,1)}, u32[]{:S(2)}, u32[]{:S(2)}) collective-permute-start(bf16[4,64,1024]{2,1,0:T(8,128)(2,1)S(1)} %broadcast_select_fusion.1.refs_0_), channel_id=1, source_target_pairs={{0,4},{4,0},{8,12},{12,8},{1,5},{5,1},{9,13},{13,9},{2,6},{6,2},{1... | collective-permute-start | bytes 1572872 | tf_op jit(solution)/shard_map/ppermute | solution.py:97
  1019.7 16.5 %collective-permute-start.46 = (bf16[2,64,1024]{2,1,0:T(8,128)(2,1)S(1)}, bf16[2,64,1024]{2,1,0:T(8,128)(2,1)S(1)}, u32[]{:S(2)}, u32[]{:S(2)}) collective-permute-start(bf16[2,64,1024]{2,1,0:T(8,128)(2,1)S(1)} %slice.343), channel_id=1, source_target_pairs={{0,8},{4,12},{8,0},{12,4},{1,9},{5,13},{9,1},{13,5},{2,10},{6,14},... | collective-permute-start | bytes 786440 | tf_op jit(solution)/shard_map/ppermute | solution.py:97
  1022.5 19.4 %collective-permute-start.56 = (bf16[64,2048]{1,0:T(8,128)(2,1)S(1)}, bf16[64,2048]{1,0:T(8,128)(2,1)S(1)}, u32[]{:S(2)}, u32[]{:S(2)}) collective-permute-start(bf16[64,2048]{1,0:T(8,128)(2,1)S(1)} %fusion.71), channel_id=1, source_target_pairs={{0,16},{16,0},{1,17},{17,1},{2,18},{18,2},{3,19},{19,3},{4,20},{20... | collective-permute-start | bytes 786440 | tf_op jit(solution)/shard_map/ppermute | solution.py:97
  1022.6 29.1 %collective-permute-start.48 = (bf16[4,64,1024]{2,1,0:T(8,128)(2,1)S(1)}, bf16[4,64,1024]{2,1,0:T(8,128)(2,1)S(1)}, u32[]{:S(2)}, u32[]{:S(2)}) collective-permute-start(bf16[4,64,1024]{2,1,0:T(8,128)(2,1)S(1)} %broadcast_select_fusion.1.refs_0_), channel_id=1, source_target_pairs={{0,16},{16,0},{1,17},{17,1},{2,18},{18,2},{3,19},{19,3},{4,20},{20... | collective-permute-start | bytes 1572872 | tf_op jit(solution)/shard_map/ppermute | solution.py:97
  (182 other events, 2685.4 us)
Sparse Core Ops, SparseCore 0:
  54.8 47.1 all-gather.7
  162.2 100.1 all-gather.5
  543.2 115.3 reduce-scatter.1
  662.5 149.0 all-reduce.9
  814.1 134.0 all-gather.9

commit v3 on v2

--- a/solution.py
+++ b/solution.py
@@ -322,6 +322,160 @@
     )(grad, down, both, pair)
 
 
+def attention_kernel(
+    raw_ref, gain_ref, cos_ref, sin_ref, places_ref, limit_ref, kv_ref,
+    q_ref, probs_ref, wide_ref, low_ref,
+):
+    raw = raw_ref[...]
+    scale = lax.rsqrt(jnp.mean(raw * raw, axis=-1, keepdims=True) + EPSILON)
+    raw = raw * scale * gain_ref[...]
+    half = raw.shape[1] // 2
+    front, behind = raw[:, :half], raw[:, half:]
+    cosine, sine = cos_ref[...], sin_ref[...]
+    q_ref[:, :half] = (front * cosine - behind * sine).astype(LOW)
+    q_ref[:, half:] = (behind * cosine + front * sine).astype(LOW)
+    scores = contract_last(q_ref[...], kv_ref[:, :HEAD_DIM])
+    scores = jnp.where(limit_ref[...] <= places_ref[...], scores, NEGATIVE)
+    raised = jnp.exp(scores - jnp.max(scores, axis=-1, keepdims=True))
+    probs = raised * (1.0 / jnp.sum(raised, axis=-1, keepdims=True))
+    probs_ref[0] = probs
+    attended = jnp.dot(probs.astype(LOW), kv_ref[:, HEAD_DIM:], preferred_element_type=WIDE)
+    wide_ref[...] = attended
+    low_ref[...] = attended.astype(LOW)
+
+
+def attention_forward(projected, gain, cosine, sine, query_places, key_limit, keys_values, heads):
+    rows = projected.shape[0]
+    keys = keys_values.shape[0]
+    block = min(rows, 256, (1 << 19) // keys)
+    return pl.pallas_call(
+        attention_kernel,
+        grid=(heads, rows // block),
+        in_specs=[
+            pl.BlockSpec((block, HEAD_DIM), lambda h, i: (i, h)),
+            pl.BlockSpec((1, HEAD_DIM), lambda h, i: (0, 0)),
+            pl.BlockSpec((block, HEAD_DIM // 2), lambda h, i: (i, 0)),
+            pl.BlockSpec((block, HEAD_DIM // 2), lambda h, i: (i, 0)),
+            pl.BlockSpec((block, 1), lambda h, i: (i, 0)),
+            pl.BlockSpec((1, keys), lambda h, i: (0, 0)),
+            pl.BlockSpec((keys, 2 * HEAD_DIM), lambda h, i: (0, 0)),
+        ],
+        out_specs=[
+            pl.BlockSpec((block, HEAD_DIM), lambda h, i: (i, h)),
+            pl.BlockSpec((1, block, keys), lambda h, i: (h, i, 0)),
+            pl.BlockSpec((block, HEAD_DIM), lambda h, i: (i, h)),
+            pl.BlockSpec((block, HEAD_DIM), lambda h, i: (i, h)),
+        ],
+        out_shape=[
+            jax.ShapeDtypeStruct((rows, heads * HEAD_DIM), LOW),
+            jax.ShapeDtypeStruct((heads, rows, keys), WIDE),
+            jax.ShapeDtypeStruct((rows, heads * HEAD_DIM), WIDE),
+            jax.ShapeDtypeStruct((rows, heads * HEAD_DIM), LOW),
+        ],
+        cost_estimate=pl.CostEstimate(
+            flops=4 * heads * rows * keys * HEAD_DIM,
+            bytes_accessed=4 * heads * rows * keys + 4 * keys * HEAD_DIM + 14 * rows * heads * HEAD_DIM,
+            transcendentals=heads * rows * keys,
+        ),
+    )(projected, gain, cosine, sine, query_places, key_limit, keys_values)
+
+
+def attention_back_kernel(
+    grad_ref, wide_ref, probs_ref, q_ref, raw_ref, gain_ref, cos_ref, sin_ref, kv_ref,
+    grad_raw_ref, grad_gain_ref, grad_kv_ref, total,
+):
+    head, step = pl.program_id(0), pl.program_id(1)
+    first = jnp.logical_and(head == 0, step == 0)
+    last = jnp.logical_and(head == pl.num_programs(0) - 1, step == pl.num_programs(1) - 1)
+    grad = grad_ref[...]
+    delta = jnp.sum(grad.astype(WIDE) * wide_ref[...], axis=-1, keepdims=True)
+    probs = probs_ref[0]
+    grad_probs = contract_last(grad, kv_ref[:, HEAD_DIM:])
+    grad_scores = (probs * (grad_probs - delta)).astype(LOW)
+    rotated = jnp.dot(grad_scores, kv_ref[:, :HEAD_DIM], preferred_element_type=WIDE)
+    key_part = over_rows(grad_scores, q_ref[...])
+    value_part = over_rows(probs.astype(LOW), grad)
+
+    @pl.when(first)
+    def _():
+        total[:, :HEAD_DIM] = key_part
+        total[:, HEAD_DIM:] = value_part
+
+    @pl.when(jnp.logical_not(first))
+    def _():
+        total[:, :HEAD_DIM] += key_part
+        total[:, HEAD_DIM:] += value_part
+
+    @pl.when(last)
+    def _():
+        grad_kv_ref[...] = total[...].astype(LOW)
+
+    half = rotated.shape[1] // 2
+    front, behind = rotated[:, :half], rotated[:, half:]
+    cosine, sine = cos_ref[...], sin_ref[...]
+    back = jnp.concatenate([front * cosine + behind * sine, behind * cosine - front * sine], axis=1)
+    raw = raw_ref[...]
+    scale = lax.rsqrt(jnp.mean(raw * raw, axis=-1, keepdims=True) + EPSILON)
+    normed = raw * scale
+    gain_part = jnp.sum(back * normed, axis=0, keepdims=True)
+
+    @pl.when(first)
+    def _():
+        grad_gain_ref[...] = gain_part
+
+    @pl.when(jnp.logical_not(first))
+    def _():
+        grad_gain_ref[...] += gain_part
+
+    back = back * gain_ref[...]
+    grad_raw_ref[...] = (
+        scale * (back - normed * jnp.mean(back * normed, axis=-1, keepdims=True))
+    ).astype(LOW)
+
+
+def attention_backward(grad, wide, probs, q_low, projected, gain, cosine, sine, keys_values):
+    heads, rows, keys = probs.shape
+    block = min(rows, 256, (1 << 19) // keys)
+
+    def tile(h, i):
+        return (i, h)
+
+    def whole(h, i):
+        return (0, 0)
+
+    return pl.pallas_call(
+        attention_back_kernel,
+        grid=(heads, rows // block),
+        in_specs=[
+            pl.BlockSpec((block, HEAD_DIM), tile),
+            pl.BlockSpec((block, HEAD_DIM), tile),
+            pl.BlockSpec((1, block, keys), lambda h, i: (h, i, 0)),
+            pl.BlockSpec((block, HEAD_DIM), tile),
+            pl.BlockSpec((block, HEAD_DIM), tile),
+            pl.BlockSpec((1, HEAD_DIM), whole),
+            pl.BlockSpec((block, HEAD_DIM // 2), lambda h, i: (i, 0)),
+            pl.BlockSpec((block, HEAD_DIM // 2), lambda h, i: (i, 0)),
+            pl.BlockSpec((keys, 2 * HEAD_DIM), whole),
+        ],
+        out_specs=[
+            pl.BlockSpec((block, HEAD_DIM), tile),
+            pl.BlockSpec((1, HEAD_DIM), whole),
+            pl.BlockSpec((keys, 2 * HEAD_DIM), whole),
+        ],
+        out_shape=[
+            jax.ShapeDtypeStruct((rows, heads * HEAD_DIM), LOW),
+            jax.ShapeDtypeStruct((1, HEAD_DIM), WIDE),
+            jax.ShapeDtypeStruct((keys, 2 * HEAD_DIM), LOW),
+        ],
+        scratch_shapes=[pltpu.VMEM((keys, 2 * HEAD_DIM), WIDE)],
+        cost_estimate=pl.CostEstimate(
+            flops=8 * heads * rows * keys * HEAD_DIM,
+            bytes_accessed=4 * heads * rows * keys + 8 * keys * HEAD_DIM + 14 * rows * heads * HEAD_DIM,
+            transcendentals=0,
+        ),
+    )(grad, wide, probs, q_low, projected, gain, cosine, sine, keys_values)
+
+
 def widen_kernel(places, source, gate, up):
     gate[...] = source[0, 0, 0].astype(WIDE)
     up[...] = source[0, 0, 1].astype(WIDE)
@@ -390,47 +544,6 @@
 
 def entry(stacked):
     return lambda index: lax.dynamic_index_in_dim(stacked, index, 0, False)
-
-
-def widen_heads_kernel(run, query_width, own, *refs):
-    step = pl.program_id(0)
-    sources, (query, key, value) = refs[:-3], refs[-3:]
-    group = run // KV_HEADS
-    for place, source in enumerate(sources):
-
-        @pl.when(step == place)
-        def _(source=source):
-            for k in range(run):
-                begin = k * query_width
-                query[:, begin : begin + query_width] = source[k, :, :query_width].astype(WIDE)
-            for number, out in enumerate((key, value)):
-                begin = query_width + number * HEAD_DIM
-                for head in range(KV_HEADS):
-                    total = source[head * group, :, begin : begin + HEAD_DIM].astype(WIDE)
-                    for k in range(1, group):
-                        total += source[head * group + k, :, begin : begin + HEAD_DIM].astype(WIDE)
-                    out[:, head * HEAD_DIM : (head + 1) * HEAD_DIM] = total
-
-
-def widen_heads(pieces, own, query_width):
-    parts = len(pieces)
-    run, rows, columns = pieces[0].shape
-    widths = (HEADS * HEAD_DIM, KV_HEADS * HEAD_DIM, KV_HEADS * HEAD_DIM)
-    return pl.pallas_call(
-        functools.partial(widen_heads_kernel, run, query_width),
-        grid_spec=pltpu.PrefetchScalarGridSpec(
-            num_scalar_prefetch=1,
-            grid=(parts,),
-            in_specs=[pl.BlockSpec((run, rows, columns), lambda r, o: (0, 0, 0))] * parts,
-            out_specs=[
-                pl.BlockSpec((rows, w), lambda r, o: (lax.bitwise_xor(r, o[0]), 0)) for w in widths
-            ],
-        ),
-        out_shape=[jax.ShapeDtypeStruct((rows * parts, w), WIDE) for w in widths],
-        cost_estimate=pl.CostEstimate(
-            flops=0, bytes_accessed=6 * parts * pieces[0].size, transcendentals=0
-        ),
-    )(own, *pieces)
 
 
 def shards(
@@ -472,9 +585,6 @@
     places = ((lax.axis_index("wsh") - jnp.arange(run)) % run).astype(jnp.int32)
     gain_cut = query_gain.shape[0]
 
-    def joined(make):
-        return place_columns(shift_blocks(make), places)
-
     def share(weight):
         return lax.dynamic_slice_in_dim(weight, chip * head_piece, head_piece, 0)
 
@@ -561,26 +671,23 @@
         return ((all_ids - vocab_first)[:, None] == vocab_range[None, :]).astype(LOW)
 
     table_rows = matmul(one_hot(), per_layer_table).astype(LOW)
+    tokens_run, table_rows = lax.optimization_barrier((tokens_run, table_rows))
     def pair_block(index):
         first = index * hidden_width + chip * piece
         gate_cut = lax.dynamic_slice_in_dim(w_gate, first, piece, 1)
         up_cut = lax.dynamic_slice_in_dim(w_up, first, piece, 1)
-        gate_cut, up_cut = after((gate_cut, up_cut), tokens_run)
+        gate_cut, up_cut = after((gate_cut, up_cut), head_share)
         return jnp.concatenate([gate_cut.T, up_cut.T], axis=0)
 
-    pair_share = joined(pair_block)
+    pair_received = shift_blocks(pair_block)
     normed_run = rms_norm(tokens_run.astype(WIDE), gains_full[0]).astype(LOW)
     tokens_f = tokens[0].astype(WIDE)
     normed = rms_norm(tokens_f, gains_full[0])
     normed_low = normed.astype(LOW)
     total_rows = run * rows_dev
     projected = matmul(normed_run, w_heads)
-    query = projected[:, :query_width]
     key = projected[:, query_width : query_width + HEAD_DIM]
     value = projected[:, query_width + HEAD_DIM :]
-
-    def query_path(raw, gain):
-        return rotate(rms_norm(raw.reshape(total_rows, heads_here, HEAD_DIM), gain), run_places)
 
     def key_path(raw, gain):
         return rotate(rms_norm(raw.reshape(total_rows, 1, HEAD_DIM), gain), run_places)[:, 0]
@@ -591,10 +698,6 @@
     k_low = key_path(key, key_gain_full).astype(LOW)
     v_low = value_path(value).astype(LOW)
     keys_values = spread(jnp.concatenate([k_low, v_low], axis=1), "ctx")
-    keys_values, table_rows, pair_share = lax.optimization_barrier(
-        (keys_values, table_rows, pair_share)
-    )
-    pair_weight = lax.all_gather(pair_share, COPIES, axis=0, tiled=True)
     half = table_rows.shape[0] // 2
     looked_up = add_low(table_rows[:half], swap(table_rows[half:], "slot", 1))
     bit = contexts // 2
@@ -603,19 +706,26 @@
         looked_up = add_low(looked_up[:half], swap(looked_up[half:], "ctx", bit))
         bit //= 2
     looked_up = looked_up.reshape(run, rows_dev, -1)
-    q_low = query_path(query, query_gain_full).astype(LOW)
-    keys_all = keys_values[:, :HEAD_DIM]
-    values_all = keys_values[:, HEAD_DIM:]
-    allowed = (key_places[None, :] <= run_places[:, None]) & (key_places < length)[None, :]
-    scores = jnp.einsum("qhd,td->hqt", q_low, keys_all, preferred_element_type=WIDE)
-    scores = jnp.where(allowed[None], scores, NEGATIVE)
-    top = jnp.max(scores, axis=-1, keepdims=True)
-    raised = jnp.exp(scores - top)
-    probs = raised / jnp.sum(raised, axis=-1, keepdims=True)
-    attended = jnp.einsum(
-        "hqt,td->qhd", probs.astype(LOW), values_all, preferred_element_type=WIDE
-    )
-    attended_low = attended.astype(LOW).reshape(total_rows, query_width)
+    inverse = jnp.exp(
+        -math.log(ROPE_BASE)
+        * (2.0 * jnp.arange(HEAD_DIM // 2, dtype=jnp.float32) / HEAD_DIM)
+    )
+    angles = run_places.astype(WIDE)[:, None] * inverse[None, :]
+    cosine, sine = jnp.cos(angles), jnp.sin(angles)
+    key_limit = jnp.where(key_places < length, key_places, jnp.int32(1 << 30))
+    q_low, probs, attended, attended_low = attention_forward(
+        projected,
+        query_gain_full[None],
+        cosine,
+        sine,
+        run_places[:, None],
+        key_limit[None],
+        keys_values,
+        heads_here,
+    )
+    attended_low, pair_received = lax.optimization_barrier((attended_low, pair_received))
+    pair_share = place_columns(pair_received, places)
+    pair_weight = lax.all_gather(pair_share, COPIES, axis=0, tiled=True)
     attn_proj = collect(matmul(attended_low, w_output).astype(LOW), "wsh")
     attn_proj, looked_up = lax.optimization_barrier((attn_proj, looked_up))
     layer_input = EMBED_SCALE * jnp.sum(shift_exchange(entry(looked_up)).astype(WIDE), axis=0)
@@ -638,8 +748,8 @@
         upward = both_parts[:, :, 1].reshape(total_rows, hidden_width)
         hidden_low = gated_product(gate, upward).astype(LOW)
         ff_part = matmul(hidden_low, w_down).astype(LOW)
+    ff_part, layer_input = lax.optimization_barrier((ff_part, layer_input))
     ff_out = collect(ff_part, "wsh")
-    ff_out, layer_input = lax.optimization_barrier((ff_out, layer_input))
     third_sum = mixed + rms_norm(ff_out, gains_full[4])
     third_low = third_sum.astype(LOW)
 
@@ -665,6 +775,18 @@
     grad_ff_low = grad_ff.astype(LOW)
 
     grad_ff_run = spread(grad_ff_low, "wsh")
+    every_grad = shift_exchange(lambda k: grad_input_low).reshape(total_rows, -1)
+    down_part = over_rows(hidden_low, grad_ff_run).astype(LOW)
+    grad_ff_run, every_grad, down_part = lax.optimization_barrier(
+        (grad_ff_run, every_grad, down_part)
+    )
+    down_own = lax.psum_scatter(down_part, COPIES, scatter_dimension=0, tiled=True)
+
+    def wider(rows, axis, bit):
+        return jnp.concatenate([rows, swap(rows, axis, bit)], axis=0)
+
+    hops = [1 << power for power in range(contexts.bit_length() - 1)]
+    every_grad = wider(every_grad, "ctx", hops[0])
     if aligned:
         grad_both, ff_part = ff_backward(grad_ff_run, pair_weight, w_down, both, piece)
     else:
@@ -680,11 +802,13 @@
         )
         grad_both = grad_both.reshape(total_rows, 2 * hidden_width).astype(LOW)
         ff_part = matmul(grad_both, pair_weight).astype(LOW)
+    ff_part, every_grad = lax.optimization_barrier((ff_part, every_grad))
+    for bit in hops[1:]:
+        every_grad = wider(every_grad, "ctx", bit)
     grad_ff_in = collect(ff_part, "wsh")
     pair_part = over_rows(after(grad_both, ff_part), ff_run).astype(LOW)
-    grad_ff_in, pair_part = lax.optimization_barrier((grad_ff_in, pair_part))
-    grad_input_low = after(grad_input_low, pair_part)
-    every_grad = shift_exchange(lambda k: grad_input_low).reshape(total_rows, -1)
+    grad_ff_in, pair_part, every_grad = lax.optimization_barrier((grad_ff_in, pair_part, every_grad))
+    every_grad = wider(every_grad, "slot", 1)
     pair_own = lax.psum_scatter(pair_part, COPIES, scatter_dimension=0, tiled=True)
     _, pullback = jax.vjp(rms_norm, mixed, gains_full[3])
     grad_mixed_norm, grad_gain_three = pullback(grad_ff_in)
@@ -693,8 +817,10 @@
     grad_attn, grad_gain_one = pullback(grad_branch)
     grad_attn_low = grad_attn.astype(LOW)
     grad_attn_run = spread(grad_attn_low, "wsh")
-    down_part = over_rows(after(hidden_low, grad_attn_low), grad_ff_run).astype(LOW)
-    grad_attn_run, down_part = lax.optimization_barrier((grad_attn_run, down_part))
+    grad_attn_run, down_own, every_grad = lax.optimization_barrier(
+        (grad_attn_run, down_own, every_grad)
+    )
+    down_grad = lax.all_gather(down_own, COPIES, axis=0, tiled=True)
 
     def pair_back(index):
         block = lax.dynamic_slice_in_dim(pair_own, index * shard_rows, shard_rows, 1)
@@ -710,79 +836,85 @@
     layer_gate_grad = over_rows(third_low, grad_lgate_low)
     layer_proj_grad = over_rows(gated_low, grad_proj_low)
 
-    narrow = jnp.concatenate([left_grad, right_grad, layer_gate_grad], axis=1)
-    narrow = narrow.reshape(run, shard_rows, -1)
-    narrow_columns = narrow.shape[2]
-    layer_proj_grad = layer_proj_grad.reshape(run, shard_rows, -1)
-    sums = jnp.concatenate([narrow, layer_proj_grad], axis=2).astype(LOW)
-    sums = jnp.sum(shift_exchange(entry(after(sums, grad_attn_run))).astype(WIDE), axis=0).astype(LOW)
+    narrow = jnp.concatenate([left_grad, right_grad, layer_gate_grad], axis=1).astype(LOW)
+    narrow_columns = narrow.shape[1]
+    proj_back = layer_proj_grad.astype(LOW).reshape(run, proj_rows, parts, width // parts)
+    proj_back = proj_back.transpose(0, 2, 1, 3).reshape(run, parts, head_piece, -1)
+    narrow = jnp.concatenate(
+        [narrow.reshape(run, parts, head_piece, narrow_columns), proj_back], axis=3
+    )
 
     grad_att_low = times_transposed(grad_attn_run, w_output).astype(LOW)
-    grad_att = grad_att_low.reshape(total_rows, heads_here, HEAD_DIM)
-    row_delta = jnp.sum(grad_att.astype(WIDE) * attended, axis=-1)
-    grad_probs = jnp.einsum("qhd,td->hqt", grad_att, values_all, preferred_element_type=WIDE)
-    grad_scores = (probs * (grad_probs - row_delta.T[:, :, None])).astype(LOW)
-    key_part = jnp.einsum("hqt,qhd->td", grad_scores, q_low, preferred_element_type=WIDE)
-    value_part = jnp.einsum("hqt,qhd->td", probs.astype(LOW), grad_att, preferred_element_type=WIDE)
-    kv_part = jnp.concatenate([key_part, value_part], axis=1).astype(LOW)
-    kv_part, pair_own = lax.optimization_barrier((kv_part, pair_own))
+    grad_query, grad_query_gain, kv_part = attention_backward(
+        grad_att_low,
+        attended,
+        probs,
+        q_low,
+        projected,
+        query_gain_full[None],
+        cosine,
+        sine,
+        keys_values,
+    )
+    grad_query_gain = grad_query_gain[0]
     kv_sum = collect(kv_part, "ctx")
-    pair_blocks = jnp.stack(shift_blocks(pair_back))
-    down_grad = lax.psum(after(down_part, pair_own), COPIES)
     output_part = over_rows(attended_low, grad_attn_run).astype(LOW)
     output_kept, output_given = halves(output_part.reshape(parts, -1, width))
-    kv_sum, pair_blocks, output_kept, output_given, sums = lax.optimization_barrier(
-        (kv_sum, pair_blocks, output_kept, output_given, sums)
-    )
-    pair_all = lax.all_gather(pair_blocks, COPIES, axis=0)
+    kv_sum, pair_own, output_kept, output_given, narrow = lax.optimization_barrier(
+        (kv_sum, pair_own, output_kept, output_given, narrow)
+    )
+    pair_blocks = jnp.stack(shift_blocks(pair_back))
     output_pieces = nearest(add_low(output_kept, output_given))
     output_first = reduce_first(output_pieces)
-    sums = add_low(sums, swap(sums, "slot", 1))
-    grad_q_rot = jnp.einsum("hqt,td->qhd", grad_scores, keys_all, preferred_element_type=WIDE)
-    _, pullback = jax.vjp(query_path, query, query_gain_full)
-    grad_query, grad_query_gain = pullback(grad_q_rot)
     _, pullback = jax.vjp(key_path, key, key_gain_full)
     grad_key, grad_key_gain = pullback(kv_sum[:, :HEAD_DIM])
     _, pullback = jax.vjp(value_path, value)
     (grad_value,) = pullback(kv_sum[:, HEAD_DIM:])
-    grad_heads = jnp.concatenate([grad_query, grad_key, grad_value], axis=1).astype(LOW)
+    grad_heads = jnp.concatenate(
+        [grad_query, grad_key.astype(LOW), grad_value.astype(LOW)], axis=1
+    )
     heads_part = over_rows(normed_run, grad_heads).astype(LOW)
-    heads_part = heads_part.reshape(run, parts, head_piece, head_width).transpose(1, 0, 2, 3)
+    heads_part = heads_part.reshape(run, parts, head_piece, head_width)
+    heads_part = jnp.concatenate([heads_part, narrow], axis=3).transpose(1, 0, 2, 3)
     heads_kept, heads_given = halves(heads_part)
     normed_part = times_transposed(grad_heads, w_heads).astype(LOW)
-    normed_part, output_first, heads_kept, heads_given, sums = lax.optimization_barrier(
-        (normed_part, output_first, heads_kept, heads_given, sums)
-    )
+    normed_part, output_first, heads_kept, heads_given, pair_blocks = lax.optimization_barrier(
+        (normed_part, output_first, heads_kept, heads_given, pair_blocks)
+    )
+    pair_all = lax.all_gather(pair_blocks, COPIES, axis=0)
+    table_grad = EMBED_SCALE * over_rows(one_hot(), after(every_grad, normed_part))
+    heads_pieces = nearest(add_low(heads_kept, heads_given))
+    heads_first = reduce_first(heads_pieces)
+    heads_second = reduce_second(heads_pieces, heads_first)
+    output_second = reduce_second(output_pieces, output_first)
     grad_run = collect(normed_part, "wsh")
-    output_second = reduce_second(output_pieces, output_first)
-    heads_pieces = nearest(add_low(heads_kept, heads_given))
-    heads_second = reduce_second(heads_pieces, reduce_first(heads_pieces))
+    grad_run, heads_second, output_second, table_grad = lax.optimization_barrier(
+        (grad_run, heads_second, output_second, table_grad)
+    )
     heads_own = reduce_last(heads_pieces, heads_second)
-    every_grad = after(every_grad, normed_part)
-    bit = 1
-    while bit < contexts:
-        every_grad = jnp.concatenate([every_grad, swap(every_grad, "ctx", bit)], axis=0)
-        bit *= 2
-    every_grad = jnp.concatenate([every_grad, swap(every_grad, "slot", 1)], axis=0)
-    table_grad = EMBED_SCALE * over_rows(one_hot(), every_grad)
-    grad_run, output_second, heads_own, table_grad = lax.optimization_barrier(
-        (grad_run, output_second, heads_own, table_grad)
-    )
+    heads_own = shift_exchange(entry(heads_own)).astype(WIDE)
+    pieces = [heads_own[:, :, :query_width].transpose(1, 0, 2).reshape(head_piece, -1)]
+    for begin in (query_width, query_width + HEAD_DIM):
+        one = heads_own[:, :, begin : begin + HEAD_DIM]
+        one = one.reshape(KV_HEADS, run // KV_HEADS, head_piece, HEAD_DIM).sum(axis=1)
+        pieces.append(one.transpose(1, 0, 2).reshape(head_piece, -1))
+    pieces.append(heads_own[:, :, head_width : head_width + narrow_columns].sum(axis=0))
+    pieces.append(heads_own[:, :, head_width + narrow_columns :].sum(axis=0))
+    cuts = []
+    for one in pieces:
+        cuts.append((sum(w for _, w in cuts), one.shape[1]))
+    heads_piece = jnp.concatenate(pieces, axis=1).astype(LOW)
+    heads_near = gather_second(heads_piece, gather_first(heads_piece))
+    output_own = reduce_last(output_pieces, output_second)
+    output_near = gather_first(output_own)
+    down_grad = after(down_grad, grad_run).astype(WIDE)
+    own = jnp.full((1,), chip, jnp.int32)
     if aligned:
         gate_grad, up_grad = widen_pair(pair_all, places)
     else:
         pair_all = jnp.take(pair_all, places, axis=1)
         pair_all = pair_all.transpose(2, 3, 1, 0, 4).reshape(2, shard_rows, -1).astype(WIDE)
         gate_grad, up_grad = pair_all[0], pair_all[1]
-    output_own = reduce_last(output_pieces, output_second)
-    own = jnp.full((1,), chip, jnp.int32)
-    bit = 1
-    while bit < contexts:
-        sums = add_low(sums, swap(sums, "ctx", bit))
-        bit *= 2
-    sums = sums.astype(WIDE)
-    narrow = sums[:, :narrow_columns]
-    layer_proj_grad = sums[:, narrow_columns:].reshape(proj_rows, width)
     grad_normed = (
         grad_run
         + times_transposed(grad_rank_low, left_full)
@@ -792,11 +924,14 @@
     grad_tokens, grad_gain_zero = pullback(grad_normed)
     tokens_grad = (grad_tokens + grad_branch).astype(LOW)[None]
 
-    output_all = last_gather(gather_second(output_own, gather_first(output_own)))
+    output_all = last_gather(gather_second(output_own, output_near))
     (output_grad,) = assemble([p[None] for p in output_all], own, WIDE)
-    heads_own = shift_exchange(entry(heads_own))
-    heads_all = last_gather(gather_second(heads_own, gather_first(heads_own)))
-    query_grad, key_grad, value_grad = widen_heads(heads_all, own, query_width)
+    query_grad, key_grad, value_grad, narrow, layer_proj_grad = assemble(
+        [p[None] for p in last_gather(heads_near)], own, WIDE, cuts
+    )
+    narrow = narrow.reshape(shard_rows, -1)
+    layer_proj_grad = layer_proj_grad.reshape(parts, proj_rows, width // parts)
+    layer_proj_grad = layer_proj_grad.transpose(1, 0, 2).reshape(proj_rows, width)
 
     vector = jnp.concatenate(
         [grad_query_gain.reshape(run, gain_cut), grad_key_gain.reshape(run, gain_cut)], axis=1
@@ -814,26 +949,22 @@
             jnp.zeros_like(vector),
         ]
     )
-    gain_sums = gain_sums.reshape(8, run, shard_rows).transpose(1, 0, 2)
-    gain_sums = jnp.sum(shift_exchange(entry(gain_sums)), axis=0)
-    gain_sums = gain_sums + swap(gain_sums, "slot", 1)
-    bit = 1
-    while bit < contexts:
-        gain_sums = gain_sums + swap(gain_sums, "ctx", bit)
-        bit *= 2
+    gain_sums = gain_sums.reshape(8, run, shard_rows).transpose(1, 0, 2).reshape(8 * run, shard_rows)
+    gain_sums = collect(gain_sums, "wsh")
+    gain_sums = jnp.sum(spread(gain_sums[None], COPIES), axis=0)
     return (
         layer_out,
         tokens_grad,
         table_grad,
-        query_grad,
-        key_grad,
-        value_grad,
+        query_grad.reshape(shard_rows, -1),
+        key_grad.reshape(shard_rows, -1),
+        value_grad.reshape(shard_rows, -1),
         output_grad.reshape(query_width, width),
         narrow[:, :rank],
         narrow[:, rank : 2 * rank],
         gate_grad,
         up_grad,
-        down_grad.astype(WIDE),
+        down_grad,
         narrow[:, 2 * rank :],
         layer_proj_grad,
         gain_sums[:6].T,

time: 1100 us -> 992 us (0.902)
  blocking collectives: 102 us -> 0 us
  other arithmetic: 135 us -> 94.3 us
  Pallas kernels: 90.4 us -> 117 us
  matrix products: 121 us -> 98 us
  starting transfers between devices: 103 us -> 123 us
    all_to_all x2 -> x0, blocking collectives: 102 us -> none  [exchange(): return lax.all_to_all(value, axis, 0, 0, tiled=True)]
    all_to_all x8 -> x12, waiting for transfers between devices: 104 us -> 168 us  [exchange(): return lax.all_to_all(value, axis, 0, 0, tiled=True)]
    ppermute x41 -> x35, waiting for transfers between devices: 124 us -> 81.7 us  [swap(): return lax.ppermute(value, axis, [(i, i ^ bit) for i in range(size)])]
    reduce_scatter x1, waiting for transfers between devices: 37.4 us -> 0.02 us  [shards(): lax.psum_scatter(pair_part, COPIES, scatter_dimension=0, tiled=True)]
    all_to_all x8 -> x12, starting transfers between devices: 36.4 us -> 62.9 us  [exchange(): return lax.all_to_all(value, axis, 0, 0, tiled=True)]
    ppermute x27 -> x21, waiting for transfers between devices: 152 us -> 176 us  [shift_blocks(): block = lax.ppermute(block, 'wsh', [(i, (i + k) % run) for i in range(run)])]
    dot_general x6 -> x0, matrix products: 22.7 us -> none  [the longest x1 6.12 us: shards(): jnp.einsum('qhd,td->hqt', q_low, keys_all, preferred_element_type=WIDE)]
    pallas_call x1 -> x2, Pallas kernels: 6.15 us -> 23.8 us  [the longest x1 12.6 us: attention_backward(): pl.pallas_call(attention_back_kernel, grid=(heads, rows // block), in_spe...]
  transfers between devices with their start and end apart: 81 -> 74, of which waited for: 29 -> 30; matrix products, arithmetic and copies ran while one was open for 30% -> 25% of each run, Pallas kernels for 1% -> 6%
where the time goes in v3:
time: 992 us; the launch traced here: 979 us
  waiting for transfers between devices  425 us (43%)
  starting transfers between devices  123 us (12%)
  Pallas kernels  117 us (12%)
  local copies, waits for them, and re-layouts  104 us (10%)
  matrix products  98 us (10%)
  other arithmetic  94.3 us (10%)
  between operations  17.3 us (2%)
    ppermute x21, waiting for transfers between devices, shift_blocks(): block = lax.ppermute(block, 'wsh', [(i, (i + k) % run) for i in range(run)])  176 us
    all_to_all x12, waiting for transfers between devices, exchange(): return lax.all_to_all(value, axis, 0, 0, tiled=True)  168 us
    ppermute x35, waiting for transfers between devices, swap(): return lax.ppermute(value, axis, [(i, i ^ bit) for i in range(size)])  81.7 us
    all_to_all x12, starting transfers between devices, exchange(): return lax.all_to_all(value, axis, 0, 0, tiled=True)  62.9 us
    dot_general x9, matrix products, over_rows(): lax.dot_general(left, right, (((0,), (0,)), ((), ())), preferred_element_...  59 us
    ppermute x21, starting transfers between devices, shift_blocks(): block = lax.ppermute(block, 'wsh', [(i, (i + k) % run) for i in range(run)])  30.6 us
    ppermute x35, starting transfers between devices, swap(): return lax.ppermute(value, axis, [(i, i ^ bit) for i in range(size)])  28.8 us
    pallas_call x1, Pallas kernels, ff_backward(): pl.pallas_call(functools.partial(ff_backward_kernel, piece, count), grid=...  27.8 us
  transfers between devices with their start and end apart: 74, of which 30 were waited for; matrix products, arithmetic and copies ran while one was open for 25% of the time, Pallas kernels for 6%

profile of v3, /device:TPU:0, one launch (start us, length us, event | category | flops | bytes accessed | tf_op | source)
XLA Modules:
  0.0 979.0 jit_solution(14785283561239190938)
XLA Ops:
  8.1 5.0 collective-permute-start.2
  24.6 5.6 collective-permute-done.8
  30.3 16.6 %collective-permute-done.7 = bf16[80,1664]{1,0:T(8,128)(2,1)S(1)} collective-permute-done((bf16[80,1664]{1,0:T(8,128)(2,1)S(1)}, bf16[80,1664]{1,0:T(8,128)(2,1)S(1)}, u32[]{:S(2)}, u32[]{:S(2)}) %collective-permute-start.7) | collective-permute-done | bytes 266272 | tf_op jit(solution)/shard_map/ppermute | solution.py:506
  53.7 4.4 all-to-all-start
  69.9 14.7 %fusion.5 = bf16[4096,256]{1,0:T(8,128)(2,1)} fusion(bf16[4096,256]{1,0:T(8,128)(2,1)} %param.27, s32[4096]{0:T(1024)S(1)} %add_subtract_fusion), kind=kOutput, calls=%fused_computation.17 | convolution fusion | flops 8607760384 | bytes 4210688 | tf_op jit(solution)/shard_map/dot_general | solution.py:53
  86.5 18.9 %all-to-all-done = bf16[4,128,2048]{2,1,0:T(8,128)(2,1)} async-done(((bf16[4,128,2048]{2,1,0:T(8,128)(2,1)}), bf16[4,128,2048]{2,1,0:T(8,128)(2,1)}, u32[]{:S(2)}, u32[]{:S(2)}) %all-to-all-start) | async-done | bytes 2097184 | tf_op jit(solution)/shard_map/all_to_all | solution.py:79
  110.9 5.5 fusion.39.raw_ref
  120.7 4.7 all-to-all-start.1
  150.7 11.2 %shard_map.323 = (bf16[512,512]{1,0:T(8,128)(2,1)}, f32[2,512,2048]{2,1,0:T(8,128)}, f32[512,512]{1,0:T(8,128)}, bf16[512,512]{1,0:T(8,128)(2,1)}) custom-call(f32[512,1024]{1,0:T(8,128)} %copy-done.18, f32[1,256]{1,0:T(1,128)} %reshape.781.gain_ref, f32[512,128]{1,0:T(8,128)} %get-tuple-element.361.cos_ref, f32[512,128]{1,0:T(8,128)} %get-tuple-element.360.sin_ref, ...), custom_call_target="tpu_custom_call" | custom-call | flops 2147483648 | bytes 14155776 | tf_op jit(solution)/shard_map/pallas_call | solution.py:351
  161.9 18.2 %collective-permute-done.10.refs_2_ = bf16[512,512]{1,0:T(8,128)(2,1)} collective-permute-done((bf16[512,512]{1,0:T(8,128)(2,1)}, bf16[512,512]{1,0:T(8,128)(2,1)}, u32[]{:S(2)}, u32[]{:S(2)}) %collective-permute-start.10) | collective-permute-done | bytes 524320 | tf_op jit(solution)/shard_map/ppermute | solution.py:506
  189.1 13.0 %all-to-all-start.2 = ((bf16[4,128,2048]{2,1,0:T(8,128)(2,1)}), bf16[4,128,2048]{2,1,0:T(8,128)(2,1)}, u32[]{:S(2)}, u32[]{:S(2)}) async-start(bf16[4,128,2048]{2,1,0:T(8,128)(2,1)} %bitcast.357), calls=%async_computation.2 | async-start | bytes 4194304 | tf_op jit(solution)/shard_map/all_to_all | solution.py:79
  205.9 23.9 %collective-permute-done.13 = bf16[1024,256]{1,0:T(8,128)(2,1)S(1)} collective-permute-done((bf16[1024,256]{1,0:T(8,128)(2,1)S(1)}, bf16[1024,256]{1,0:T(8,128)(2,1)S(1)}, u32[]{:S(2)}, u32[]{:S(2)}) %collective-permute-start.13) | collective-permute-done | bytes 524320 | tf_op jit(solution)/shard_map/ppermute | solution.py:97
  232.6 5.1 collective-permute-done.14
  242.1 8.9 all-to-all-done.2
  257.5 4.6 all-to-all-start.3
  267.7 30.8 %collective-permute-done.17 = bf16[128,256]{1,0:T(8,128)(2,1)S(1)} collective-permute-done((bf16[128,256]{1,0:T(8,128)(2,1)S(1)}, bf16[128,256]{1,0:T(8,128)(2,1)S(1)}, u32[]{:S(2)}, u32[]{:S(2)}) %collective-permute-start.17) | collective-permute-done | bytes 65568 | tf_op jit(solution)/shard_map/ppermute | solution.py:506
  298.5 17.5 %collective-permute-done.16 = bf16[128,256]{1,0:T(8,128)(2,1)S(1)} collective-permute-done((bf16[128,256]{1,0:T(8,128)(2,1)S(1)}, bf16[128,256]{1,0:T(8,128)(2,1)S(1)}, u32[]{:S(2)}, u32[]{:S(2)}) %collective-permute-start.16) | collective-permute-done | bytes 65568 | tf_op jit(solution)/shard_map/ppermute | solution.py:506
  319.3 23.8 %shard_map.325 = (f32[512,4096]{1,0:T(8,128)}, bf16[512,2048]{1,0:T(8,128)(2,1)}, bf16[512,2048]{1,0:T(8,128)(2,1)}) custom-call(bf16[512,2048]{1,0:T(8,128)(2,1)} %bitcast.41.x_ref, bf16[4096,2048]{1,0:T(8,128)(2,1)} %all-gather.7.cloned.1.call-done.pair_ref, bf16[2048,2048]{1,0:T(8,128)(2,1)} %down_ref.3), custom_call_target="tpu_custom_call" | custom-call | flops 12884901888 | bytes 35651584 | tf_op jit(solution)/shard_map/pallas_call | solution.py:243
  343.1 5.0 all-to-all-start.4
  351.3 44.2 %all-to-all-done.4 = bf16[4,128,2048]{2,1,0:T(8,128)(2,1)} async-done(((bf16[4,128,2048]{2,1,0:T(8,128)(2,1)}), bf16[4,128,2048]{2,1,0:T(8,128)(2,1)}, u32[]{:S(2)}, u32[]{:S(2)}) %all-to-all-start.4) | async-done | bytes 2097184 | tf_op jit(solution)/shard_map/all_to_all | solution.py:79
  407.5 4.4 all-to-all-start.5
  416.9 31.3 %collective-permute-done.20 = bf16[128,256]{1,0:T(8,128)(2,1)S(1)} collective-permute-done((bf16[128,256]{1,0:T(8,128)(2,1)S(1)}, bf16[128,256]{1,0:T(8,128)(2,1)S(1)}, u32[]{:S(2)}, u32[]{:S(2)}) %collective-permute-start.20) | collective-permute-done | bytes 65568 | tf_op jit(solution)/shard_map/ppermute | solution.py:506
  448.2 17.1 %collective-permute-done.19 = bf16[128,256]{1,0:T(8,128)(2,1)S(1)} collective-permute-done((bf16[128,256]{1,0:T(8,128)(2,1)S(1)}, bf16[128,256]{1,0:T(8,128)(2,1)S(1)}, u32[]{:S(2)}, u32[]{:S(2)}) %collective-permute-start.19) | collective-permute-done | bytes 65568 | tf_op jit(solution)/shard_map/ppermute | solution.py:506
  469.1 10.2 %convolution_convert_fusion.1 = bf16[2048,2048]{1,0:T(8,128)(2,1)} fusion(bf16[512,2048]{1,0:T(8,128)(2,1)} %get-tuple-element.120, bf16[512,2048]{1,0:T(8,128)(2,1)} %bitcast.53.grad_ref), kind=kOutput, calls=%fused_computation.12 | convolution fusion | flops 4299161600 | bytes 12582912 | tf_op jit(solution)/shard_map/dot_general | solution.py:63
  481.8 27.8 %shard_map.326 = (bf16[512,4096]{1,0:T(8,128)(2,1)}, bf16[512,2048]{1,0:T(8,128)(2,1)}) custom-call(bf16[512,2048]{1,0:T(8,128)(2,1)} %bitcast.53.grad_ref, bf16[2048,2048]{1,0:T(8,128)(2,1)} %down_ref.3, f32[512,4096]{1,0:T(8,128)} %get-tuple-element.122.both_ref, bf16[4096,2048]{1,0:T(8,128)(2,1)} %all-gather.7.cloned.1.call-done.pair_ref), custom_call_target="tpu_custom_call" | custom-call | flops 12884901888 | bytes 37748736 | tf_op jit(solution)/shard_map/pallas_call | solution.py:300
  511.4 4.4 all-to-all-start.6
  517.8 15.1 %convolution_convert_fusion = bf16[4096,2048]{1,0:T(8,128)(2,1)} fusion(bf16[512,4096]{1,0:T(8,128)(2,1)} %get-tuple-element.127, bf16[512,2048]{1,0:T(8,128)(2,1)} %bitcast.41.x_ref), kind=kOutput, calls=%fused_computation.11 | convolution fusion | flops 8598323200 | bytes 23068672 | tf_op jit(solution)/shard_map/dot_general | solution.py:63
  532.9 5.9 collective-permute-done.22
  541.1 21.1 %all-to-all-done.6 = bf16[4,128,2048]{2,1,0:T(8,128)(2,1)} async-done(((bf16[4,128,2048]{2,1,0:T(8,128)(2,1)}), bf16[4,128,2048]{2,1,0:T(8,128)(2,1)}, u32[]{:S(2)}, u32[]{:S(2)}) %all-to-all-start.6) | async-done | bytes 2097184 | tf_op jit(solution)/shard_map/all_to_all | solution.py:79
  575.0 4.6 all-to-all-start.7
  585.3 41.6 %all-to-all-done.7 = bf16[4,128,2048]{2,1,0:T(8,128)(2,1)} async-done(((bf16[4,128,2048]{2,1,0:T(8,128)(2,1)}), bf16[4,128,2048]{2,1,0:T(8,128)(2,1)}, u32[]{:S(2)}, u32[]{:S(2)}) %all-to-all-start.7) | async-done | bytes 2097184 | tf_op jit(solution)/shard_map/all_to_all | solution.py:79
  635.5 12.6 %shard_map.327 = (bf16[512,512]{1,0:T(8,128)(2,1)}, f32[1,256]{1,0:T(1,128)}, bf16[2048,512]{1,0:T(8,128)(2,1)}) custom-call(bf16[512,512]{1,0:T(8,128)(2,1)} %convolution_convert_fusion.9.grad_ref, f32[512,512]{1,0:T(8,128)} %get-tuple-element.133.wide_ref, f32[2,512,2048]{2,1,0:T(8,128)} %get-tuple-element.134.probs_ref, ...), custom_call_target="tpu_custom_call" | custom-call | flops 4294967296 | bytes 16252928 | tf_op jit(solution)/shard_map/pallas_call | solution.py:446
  648.1 4.6 all-to-all-start.8
  665.8 33.2 %all-to-all-done.8 = bf16[4,512,512]{2,1,0:T(8,128)(2,1)} async-done(((bf16[4,512,512]{2,1,0:T(8,128)(2,1)}), bf16[4,512,512]{2,1,0:T(8,128)(2,1)}, u32[]{:S(2)}, u32[]{:S(2)}) %all-to-all-start.8) | async-done | bytes 2097184 | tf_op jit(solution)/shard_map/all_to_all | solution.py:79
  705.0 4.2 convolution_convert_fusion.2
  725.2 9.2 collective-permute-done.30
  735.2 29.3 %collective-permute-done.29 = bf16[2,512,256]{1,2,0:T(8,128)(2,1)S(1)} collective-permute-done((bf16[2,512,256]{1,2,0:T(8,128)(2,1)S(1)}, bf16[2,512,256]{1,2,0:T(8,128)(2,1)S(1)}, u32[]{:S(2)}, u32[]{:S(2)}) %collective-permute-start.29) | collective-permute-done | bytes 524320 | tf_op jit(solution)/shard_map/ppermute | solution.py:506
  772.4 4.8 all-to-all-start.9
  777.2 5.1 add_convert_fusion
  788.3 15.9 %collective-permute-done.33 = bf16[2,64,1664]{2,1,0:T(8,128)(2,1)S(1)} collective-permute-done((bf16[2,64,1664]{2,1,0:T(8,128)(2,1)S(1)}, bf16[2,64,1664]{2,1,0:T(8,128)(2,1)S(1)}, u32[]{:S(2)}, u32[]{:S(2)}) %collective-permute-start.33) | collective-permute-done | bytes 426016 | tf_op jit(solution)/shard_map/ppermute | solution.py:97
  809.4 24.0 %fusion.4 = f32[4096,256]{1,0:T(8,128)} fusion(bf16[4096,256]{1,0:T(8,128)(2,1)S(1)} %copy-done.32, s32[4096]{0:T(1024)S(1)} %copy-done.82), kind=kOutput, calls=%fused_computation.14 | convolution fusion | flops 8607760384 | bytes 6307840 | tf_op jit(solution)/shard_map/dot_general | solution.py:63
  836.0 7.4 collective-permute-done.32
  859.2 4.3 all-to-all-start.10
  866.1 11.9 %convert_element_type.410 = f32[2048,2048]{1,0:T(8,128)} convert(bf16[2048,2048]{1,0:T(8,128)(2,1)} %all-gather.9.cloned.1.call-done) | non-fusion elementwise | flops 4194304 | bytes 25165824 | tf_op jit(solution)/shard_map/convert_element_type | solution.py:910
  918.7 5.3 collective-permute-done.43
  929.2 5.1 shard_map.329
  934.3 6.4 shard_map.328
  946.2 25.8 %shard_map.330 = (f32[512,8192]{1,0:T(8,128)}, f32[512,8192]{1,0:T(8,128)}) custom-call(s32[4]{0:T(128)} %and_select_fusion.1.places, bf16[8,4,2,512,256]{4,3,2,1,0:T(8,128)(2,1)} %bitcast.339), custom_call_target="tpu_custom_call" | custom-call | bytes 50331648 | tf_op jit(solution)/shard_map/pallas_call | solution.py:486
  (591 shorter events, 287.2 us)
Async XLA Ops:
  7.2 100.3 %all-gather.11.cloned.1.call-start = ((), (), s32[]{:S(2)}) async-start(), calls=%async_computation.18 | async-start | bytes 7667712 | tf_op jit(solution)/shard_map/all_gather | solution.py:637
  23.4 23.4 %collective-permute-start.7 = (bf16[80,1664]{1,0:T(8,128)(2,1)S(1)}, bf16[80,1664]{1,0:T(8,128)(2,1)S(1)}, u32[]{:S(2)}, u32[]{:S(2)}) collective-permute-start(bf16[80,1664]{1,0:T(8,128)(2,1)S(1)} %get-tuple-element.337), channel_id=1, source_target_pairs={{0,2},{1,3},{2,0},{3,1},{4,6},{5,7},{6,4},{7,5},{8,10},{9,11},{10,... | collective-permute-start | bytes 798728 | tf_op jit(solution)/shard_map/ppermute | solution.py:506
  24.6 22.3 %collective-permute-start.6 = (bf16[80,1664]{1,0:T(8,128)(2,1)S(1)}, bf16[80,1664]{1,0:T(8,128)(2,1)S(1)}, u32[]{:S(2)}, u32[]{:S(2)}) collective-permute-start(bf16[80,1664]{1,0:T(8,128)(2,1)S(1)} %get-tuple-element.336), channel_id=1, source_target_pairs={{0,1},{1,2},{2,3},{3,0},{4,5},{5,6},{6,7},{7,4},{8,9},{9,10},{10,1... | collective-permute-start | bytes 798728 | tf_op jit(solution)/shard_map/ppermute | solution.py:506
  53.7 51.6 %all-to-all-start = ((bf16[4,128,2048]{2,1,0:T(8,128)(2,1)}), bf16[4,128,2048]{2,1,0:T(8,128)(2,1)}, u32[]{:S(2)}, u32[]{:S(2)}) async-start(bf16[4,128,2048]{2,1,0:T(8,128)(2,1)} %broadcast_in_dim.119), calls=%async_computation | async-start | bytes 4194304 | tf_op jit(solution)/shard_map/all_to_all | solution.py:79
  120.7 30.0 %all-to-all-start.1 = ((bf16[4,512,512]{2,1,0:T(8,128)(2,1)}), bf16[4,512,512]{2,1,0:T(8,128)(2,1)}, u32[]{:S(2)}, u32[]{:S(2)}) async-start(bf16[4,512,512]{2,1,0:T(8,128)(2,1)} %broadcast_in_dim.219), calls=%async_computation.1 | async-start | bytes 4194304 | tf_op jit(solution)/shard_map/all_to_all | solution.py:79
  125.4 193.9 %all-gather.7.cloned.1.call-start = ((), (), s32[]{:S(2)}) async-start(), calls=%async_computation.14 | async-start | bytes 18874368 | tf_op jit(solution)/shard_map/all_gather | solution.py:728
  143.9 36.1 %collective-permute-start.10 = (bf16[512,512]{1,0:T(8,128)(2,1)}, bf16[512,512]{1,0:T(8,128)(2,1)}, u32[]{:S(2)}, u32[]{:S(2)}) collective-permute-start(bf16[512,512]{1,0:T(8,128)(2,1)} %pad_maximum_fusion.12), channel_id=1, source_target_pairs={{0,2},{1,3},{2,0},{3,1},{4,6},{5,7},{6,4},{7,5},{8,10},{9,11},{10,... | collective-permute-start | bytes 1572872 | tf_op jit(solution)/shard_map/ppermute | solution.py:506
  146.4 33.7 %collective-permute-start.11 = (bf16[512,512]{1,0:T(8,128)(2,1)}, bf16[512,512]{1,0:T(8,128)(2,1)}, u32[]{:S(2)}, u32[]{:S(2)}) collective-permute-start(bf16[512,512]{1,0:T(8,128)(2,1)} %pad_maximum_fusion.13), channel_id=1, source_target_pairs={{0,3},{1,0},{2,1},{3,2},{4,7},{5,4},{6,5},{7,6},{8,11},{9,8},{10,9... | collective-permute-start | bytes 1572872 | tf_op jit(solution)/shard_map/ppermute | solution.py:506
  189.1 61.9 %all-to-all-start.2 = ((bf16[4,128,2048]{2,1,0:T(8,128)(2,1)}), bf16[4,128,2048]{2,1,0:T(8,128)(2,1)}, u32[]{:S(2)}, u32[]{:S(2)}) async-start(bf16[4,128,2048]{2,1,0:T(8,128)(2,1)} %bitcast.357), calls=%async_computation.2 | async-start | bytes 4194304 | tf_op jit(solution)/shard_map/all_to_all | solution.py:79
  204.2 25.7 %collective-permute-start.13 = (bf16[1024,256]{1,0:T(8,128)(2,1)S(1)}, bf16[1024,256]{1,0:T(8,128)(2,1)S(1)}, u32[]{:S(2)}, u32[]{:S(2)}) collective-permute-start(bf16[1024,256]{1,0:T(8,128)(2,1)S(1)} %slice.312), channel_id=1, source_target_pairs={{0,8},{4,12},{8,0},{12,4},{1,9},{5,13},{9,1},{13,5},{2,10},{6,14},... | collective-permute-start | bytes 1572872 | tf_op jit(solution)/shard_map/ppermute | solution.py:97
  257.5 61.7 %all-to-all-start.3 = ((bf16[4,128,2048]{2,1,0:T(8,128)(2,1)}), bf16[4,128,2048]{2,1,0:T(8,128)(2,1)}, u32[]{:S(2)}, u32[]{:S(2)}) async-start(bf16[4,128,2048]{2,1,0:T(8,128)(2,1)} %broadcast_in_dim.220), calls=%async_computation.3 | async-start | bytes 4194304 | tf_op jit(solution)/shard_map/all_to_all | solution.py:79
  262.2 36.4 %collective-permute-start.17 = (bf16[128,256]{1,0:T(8,128)(2,1)S(1)}, bf16[128,256]{1,0:T(8,128)(2,1)S(1)}, u32[]{:S(2)}, u32[]{:S(2)}) collective-permute-start(bf16[128,256]{1,0:T(8,128)(2,1)S(1)} %get-tuple-element.328), channel_id=1, source_target_pairs={{0,3},{1,0},{2,1},{3,2},{4,7},{5,4},{6,5},{7,6},{8,11},{9,8},{10,9... | collective-permute-start | bytes 196616 | tf_op jit(solution)/shard_map/ppermute | solution.py:506
  266.0 50.0 %collective-permute-start.16 = (bf16[128,256]{1,0:T(8,128)(2,1)S(1)}, bf16[128,256]{1,0:T(8,128)(2,1)S(1)}, u32[]{:S(2)}, u32[]{:S(2)}) collective-permute-start(bf16[128,256]{1,0:T(8,128)(2,1)S(1)} %get-tuple-element.329), channel_id=1, source_target_pairs={{0,2},{1,3},{2,0},{3,1},{4,6},{5,7},{6,4},{7,5},{8,10},{9,11},{10,... | collective-permute-start | bytes 196616 | tf_op jit(solution)/shard_map/ppermute | solution.py:506
  266.0 50.0 %collective-permute-start.15 = (bf16[128,256]{1,0:T(8,128)(2,1)S(1)}, bf16[128,256]{1,0:T(8,128)(2,1)S(1)}, u32[]{:S(2)}, u32[]{:S(2)}) collective-permute-start(bf16[128,256]{1,0:T(8,128)(2,1)S(1)} %get-tuple-element.330), channel_id=1, source_target_pairs={{0,1},{1,2},{2,3},{3,0},{4,5},{5,6},{6,7},{7,4},{8,9},{9,10},{10,1... | collective-permute-start | bytes 196616 | tf_op jit(solution)/shard_map/ppermute | solution.py:506
  343.1 52.5 %all-to-all-start.4 = ((bf16[4,128,2048]{2,1,0:T(8,128)(2,1)}), bf16[4,128,2048]{2,1,0:T(8,128)(2,1)}, u32[]{:S(2)}, u32[]{:S(2)}) async-start(bf16[4,128,2048]{2,1,0:T(8,128)(2,1)} %bitcast.360), calls=%async_computation.4 | async-start | bytes 4194304 | tf_op jit(solution)/shard_map/all_to_all | solution.py:79
  407.5 61.6 %all-to-all-start.5 = ((bf16[4,128,2048]{2,1,0:T(8,128)(2,1)}), bf16[4,128,2048]{2,1,0:T(8,128)(2,1)}, u32[]{:S(2)}, u32[]{:S(2)}) async-start(bf16[4,128,2048]{2,1,0:T(8,128)(2,1)} %broadcast_in_dim.224), calls=%async_computation.5 | async-start | bytes 4194304 | tf_op jit(solution)/shard_map/all_to_all | solution.py:79
  412.0 215.0 %reduce-scatter.3.cloned.1.call-start = ((), (), s32[]{:S(2)}) async-start(), calls=%async_computation.15 | async-start | bytes 9437184 | tf_op jit(solution)/shard_map/reduce_scatter | solution.py:783
  412.0 36.1 %collective-permute-start.20 = (bf16[128,256]{1,0:T(8,128)(2,1)S(1)}, bf16[128,256]{1,0:T(8,128)(2,1)S(1)}, u32[]{:S(2)}, u32[]{:S(2)}) collective-permute-start(bf16[128,256]{1,0:T(8,128)(2,1)S(1)} %get-tuple-element.325), channel_id=1, source_target_pairs={{0,3},{1,0},{2,1},{3,2},{4,7},{5,4},{6,5},{7,6},{8,11},{9,8},{10,9... | collective-permute-start | bytes 196616 | tf_op jit(solution)/shard_map/ppermute | solution.py:506
  415.7 49.5 %collective-permute-start.19 = (bf16[128,256]{1,0:T(8,128)(2,1)S(1)}, bf16[128,256]{1,0:T(8,128)(2,1)S(1)}, u32[]{:S(2)}, u32[]{:S(2)}) collective-permute-start(bf16[128,256]{1,0:T(8,128)(2,1)S(1)} %get-tuple-element.325), channel_id=1, source_target_pairs={{0,2},{1,3},{2,0},{3,1},{4,6},{5,7},{6,4},{7,5},{8,10},{9,11},{10,... | collective-permute-start | bytes 196616 | tf_op jit(solution)/shard_map/ppermute | solution.py:506
  415.7 49.5 %collective-permute-start.18 = (bf16[128,256]{1,0:T(8,128)(2,1)S(1)}, bf16[128,256]{1,0:T(8,128)(2,1)S(1)}, u32[]{:S(2)}, u32[]{:S(2)}) collective-permute-start(bf16[128,256]{1,0:T(8,128)(2,1)S(1)} %get-tuple-element.325), channel_id=1, source_target_pairs={{0,1},{1,2},{2,3},{3,0},{4,5},{5,6},{6,7},{7,4},{8,9},{9,10},{10,1... | collective-permute-start | bytes 196616 | tf_op jit(solution)/shard_map/ppermute | solution.py:506
  480.2 29.4 %collective-permute-start.21 = (bf16[512,256]{1,0:T(8,128)(2,1)S(1)}, bf16[512,256]{1,0:T(8,128)(2,1)}, u32[]{:S(2)}, u32[]{:S(2)}) collective-permute-start(bf16[512,256]{1,0:T(8,128)(2,1)S(1)} %bitcast.369), channel_id=1, source_target_pairs={{0,4},{4,0},{8,12},{12,8},{1,5},{5,1},{9,13},{13,9},{2,6},{6,2},{1... | collective-permute-start | bytes 786440 | tf_op jit(solution)/shard_map/ppermute | solution.py:97
  511.4 50.8 %all-to-all-start.6 = ((bf16[4,128,2048]{2,1,0:T(8,128)(2,1)}), bf16[4,128,2048]{2,1,0:T(8,128)(2,1)}, u32[]{:S(2)}, u32[]{:S(2)}) async-start(bf16[4,128,2048]{2,1,0:T(8,128)(2,1)} %bitcast.359), calls=%async_computation.6 | async-start | bytes 4194304 | tf_op jit(solution)/shard_map/all_to_all | solution.py:79
  515.9 185.2 %reduce-scatter.5.cloned.1.call-start = ((), (), s32[]{:S(2)}) async-start(), calls=%async_computation.16 | async-start | bytes 18874368 | tf_op jit(solution)/shard_map/reduce_scatter | solution.py:812
  516.1 22.7 %collective-permute-start.22 = (bf16[1024,256]{1,0:T(8,128)(2,1)}, bf16[1024,256]{1,0:T(8,128)(2,1)}, u32[]{:S(2)}, u32[]{:S(2)}) collective-permute-start(bf16[1024,256]{1,0:T(8,128)(2,1)} %pad_maximum_fusion.14), channel_id=1, source_target_pairs={{0,8},{4,12},{8,0},{12,4},{1,9},{5,13},{9,1},{13,5},{2,10},{6,14},... | collective-permute-start | bytes 1572872 | tf_op jit(solution)/shard_map/ppermute | solution.py:97
  575.0 51.9 %all-to-all-start.7 = ((bf16[4,128,2048]{2,1,0:T(8,128)(2,1)}), bf16[4,128,2048]{2,1,0:T(8,128)(2,1)}, u32[]{:S(2)}, u32[]{:S(2)}) async-start(bf16[4,128,2048]{2,1,0:T(8,128)(2,1)} %broadcast_in_dim.226), calls=%async_computation.7 | async-start | bytes 4194304 | tf_op jit(solution)/shard_map/all_to_all | solution.py:79
  579.6 286.4 %all-gather.9.cloned.1.call-start = ((), (), s32[]{:S(2)}) async-start(), calls=%async_computation.17 | async-start | bytes 9437184 | tf_op jit(solution)/shard_map/all_gather | solution.py:823
  648.1 50.9 %all-to-all-start.8 = ((bf16[4,512,512]{2,1,0:T(8,128)(2,1)}), bf16[4,512,512]{2,1,0:T(8,128)(2,1)}, u32[]{:S(2)}, u32[]{:S(2)}) async-start(bf16[4,512,512]{2,1,0:T(8,128)(2,1)} %bitcast.358), calls=%async_computation.9 | async-start | bytes 4194304 | tf_op jit(solution)/shard_map/all_to_all | solution.py:79
  652.8 293.4 %all-gather.13.cloned.1.call-start = ((), (), s32[]{:S(2)}) async-start(), calls=%async_computation.19 | async-start | bytes 18874368 | tf_op jit(solution)/shard_map/all_gather | solution.py:884
  661.6 39.5 %collective-permute-start.24 = (bf16[4,64,2048]{2,1,0:T(8,128)(2,1)}, bf16[4,64,2048]{2,1,0:T(8,128)(2,1)}, u32[]{:S(2)}, u32[]{:S(2)}) collective-permute-start(bf16[4,64,2048]{2,1,0:T(8,128)(2,1)} %get-tuple-element.296), channel_id=1, source_target_pairs={{0,16},{16,0},{1,17},{17,1},{2,18},{18,2},{3,19},{19,3},{4,20},{20... | collective-permute-start | bytes 3145736 | tf_op jit(solution)/shard_map/ppermute | solution.py:97
  715.2 50.9 %collective-permute-start.27 = (bf16[4,4,64,1664]{3,2,1,0:T(8,128)(2,1)}, bf16[4,4,64,1664]{3,2,1,0:T(8,128)(2,1)}, u32[]{:S(2)}, u32[]{:S(2)}) collective-permute-start(bf16[4,4,64,1664]{3,2,1,0:T(8,128)(2,1)} %get-tuple-element.284), channel_id=1, source_target_pairs={{0,16},{16,0},{1,17},{17,1},{2,18},{18,2},{3,19},{19,3},{4,20},{20... | collective-permute-start | bytes 10223624 | tf_op jit(solution)/shard_map/ppermute | solution.py:97
  717.2 48.9 %collective-permute-start.25 = (bf16[32,2048]{1,0:T(8,128)(2,1)S(1)}, bf16[32,2048]{1,0:T(8,128)(2,1)S(1)}, u32[]{:S(2)}, u32[]{:S(2)}) collective-permute-start(bf16[32,2048]{1,0:T(8,128)(2,1)S(1)} %get-tuple-element.308), channel_id=1, source_target_pairs={{0,4},{4,0},{8,12},{12,8},{1,5},{5,1},{9,13},{13,9},{2,6},{6,2},{1... | collective-permute-start | bytes 393224 | tf_op jit(solution)/shard_map/ppermute | solution.py:97
  719.1 45.4 %collective-permute-start.29 = (bf16[2,512,256]{1,2,0:T(8,128)(2,1)S(1)}, bf16[2,512,256]{1,2,0:T(8,128)(2,1)S(1)}, u32[]{:S(2)}, u32[]{:S(2)}) collective-permute-start(bf16[2,512,256]{1,2,0:T(8,128)(2,1)S(1)} %bitcast.387), channel_id=1, source_target_pairs={{0,2},{1,3},{2,0},{3,1},{4,6},{5,7},{6,4},{7,5},{8,10},{9,11},{10,... | collective-permute-start | bytes 1572872 | tf_op jit(solution)/shard_map/ppermute | solution.py:506
  719.2 45.4 %collective-permute-start.28 = (bf16[2,512,256]{1,2,0:T(8,128)(2,1)S(1)}, bf16[2,512,256]{1,2,0:T(8,128)(2,1)S(1)}, u32[]{:S(2)}, u32[]{:S(2)}) collective-permute-start(bf16[2,512,256]{1,2,0:T(8,128)(2,1)S(1)} %bitcast.386), channel_id=1, source_target_pairs={{0,1},{1,2},{2,3},{3,0},{4,5},{5,6},{6,7},{7,4},{8,9},{9,10},{10,1... | collective-permute-start | bytes 1572872 | tf_op jit(solution)/shard_map/ppermute | solution.py:506
  734.4 31.7 %collective-permute-start.26 = (bf16[32,2048]{1,0:T(8,128)(2,1)S(1)}, bf16[32,2048]{1,0:T(8,128)(2,1)}, u32[]{:S(2)}, u32[]{:S(2)}) collective-permute-start(bf16[32,2048]{1,0:T(8,128)(2,1)S(1)} %get-tuple-element.309), channel_id=1, source_target_pairs={{0,8},{4,12},{8,0},{12,4},{1,9},{5,13},{9,1},{13,5},{2,10},{6,14},... | collective-permute-start | bytes 393224 | tf_op jit(solution)/shard_map/ppermute | solution.py:97
  772.4 61.1 %all-to-all-start.9 = ((bf16[4,128,2048]{2,1,0:T(8,128)(2,1)}), bf16[4,128,2048]{2,1,0:T(8,128)(2,1)}, u32[]{:S(2)}, u32[]{:S(2)}) async-start(bf16[4,128,2048]{2,1,0:T(8,128)(2,1)} %bitcast.356), calls=%async_computation.11 | async-start | bytes 4194304 | tf_op jit(solution)/shard_map/all_to_all | solution.py:79
  782.4 21.8 %collective-permute-start.33 = (bf16[2,64,1664]{2,1,0:T(8,128)(2,1)S(1)}, bf16[2,64,1664]{2,1,0:T(8,128)(2,1)S(1)}, u32[]{:S(2)}, u32[]{:S(2)}) collective-permute-start(bf16[2,64,1664]{2,1,0:T(8,128)(2,1)S(1)} %get-tuple-element.288), channel_id=1, source_target_pairs={{0,4},{4,0},{8,12},{12,8},{1,5},{5,1},{9,13},{13,9},{2,6},{6,2},{1... | collective-permute-start | bytes 1277960 | tf_op jit(solution)/shard_map/ppermute | solution.py:97
  786.3 49.7 %collective-permute-start.35 = (bf16[64,2048]{1,0:T(8,128)(2,1)}, bf16[64,2048]{1,0:T(8,128)(2,1)}, u32[]{:S(2)}, u32[]{:S(2)}) collective-permute-start(bf16[64,2048]{1,0:T(8,128)(2,1)} %pad_maximum_fusion.27), channel_id=1, source_target_pairs={{0,4},{4,0},{8,12},{12,8},{1,5},{5,1},{9,13},{13,9},{2,6},{6,2},{1... | collective-permute-start | bytes 786440 | tf_op jit(solution)/shard_map/ppermute | solution.py:97
  787.1 48.9 %collective-permute-start.36 = (bf16[64,2048]{1,0:T(8,128)(2,1)S(1)}, bf16[64,2048]{1,0:T(8,128)(2,1)}, u32[]{:S(2)}, u32[]{:S(2)}) collective-permute-start(bf16[64,2048]{1,0:T(8,128)(2,1)S(1)} %pad_maximum_fusion.28), channel_id=1, source_target_pairs={{0,8},{4,12},{8,0},{12,4},{1,9},{5,13},{9,1},{13,5},{2,10},{6,14},... | collective-permute-start | bytes 786440 | tf_op jit(solution)/shard_map/ppermute | solution.py:97
  806.4 37.0 %collective-permute-start.32 = (bf16[4,64,1664]{2,1,0:T(8,128)(2,1)}, bf16[4,64,1664]{2,1,0:T(8,128)(2,1)}, u32[]{:S(2)}, u32[]{:S(2)}) collective-permute-start(bf16[4,64,1664]{2,1,0:T(8,128)(2,1)} %pad_maximum_fusion.6), channel_id=1, source_target_pairs={{0,4},{4,0},{8,12},{12,8},{1,5},{5,1},{9,13},{13,9},{2,6},{6,2},{1... | collective-permute-start | bytes 2555912 | tf_op jit(solution)/shard_map/ppermute | solution.py:97
  808.5 36.0 %collective-permute-start.34 = (bf16[4,64,1664]{2,1,0:T(8,128)(2,1)}, bf16[4,64,1664]{2,1,0:T(8,128)(2,1)}, u32[]{:S(2)}, u32[]{:S(2)}) collective-permute-start(bf16[4,64,1664]{2,1,0:T(8,128)(2,1)} %pad_maximum_fusion.7), channel_id=1, source_target_pairs={{0,8},{4,12},{8,0},{12,4},{1,9},{5,13},{9,1},{13,5},{2,10},{6,14},... | collective-permute-start | bytes 2555912 | tf_op jit(solution)/shard_map/ppermute | solution.py:97
  846.4 59.8 %collective-permute-start.48 = (bf16[64,2048]{1,0:T(8,128)(2,1)}, bf16[64,2048]{1,0:T(8,128)(2,1)}, u32[]{:S(2)}, u32[]{:S(2)}) collective-permute-start(bf16[64,2048]{1,0:T(8,128)(2,1)} %fusion.46), channel_id=1, source_target_pairs={{0,4},{4,0},{8,12},{12,8},{1,5},{5,1},{9,13},{13,9},{2,6},{6,2},{1... | collective-permute-start | bytes 786440 | tf_op jit(solution)/shard_map/ppermute | solution.py:97
  847.9 62.7 %collective-permute-start.49 = (bf16[64,2048]{1,0:T(8,128)(2,1)}, bf16[64,2048]{1,0:T(8,128)(2,1)}, u32[]{:S(2)}, u32[]{:S(2)}) collective-permute-start(bf16[64,2048]{1,0:T(8,128)(2,1)} %fusion.46), channel_id=1, source_target_pairs={{0,8},{4,12},{8,0},{12,4},{1,9},{5,13},{9,1},{13,5},{2,10},{6,14},... | collective-permute-start | bytes 786440 | tf_op jit(solution)/shard_map/ppermute | solution.py:97
  851.3 31.4 %collective-permute-start.39 = (bf16[64,1664]{1,0:T(8,128)(2,1)}, bf16[64,1664]{1,0:T(8,128)(2,1)}, u32[]{:S(2)}, u32[]{:S(2)}) collective-permute-start(bf16[64,1664]{1,0:T(8,128)(2,1)} %get-tuple-element.315), channel_id=1, source_target_pairs={{0,3},{1,0},{2,1},{3,2},{4,7},{5,4},{6,5},{7,6},{8,11},{9,8},{10,9... | collective-permute-start | bytes 638984 | tf_op jit(solution)/shard_map/ppermute | solution.py:506
  854.7 28.4 %collective-permute-start.38 = (bf16[64,1664]{1,0:T(8,128)(2,1)}, bf16[64,1664]{1,0:T(8,128)(2,1)}, u32[]{:S(2)}, u32[]{:S(2)}) collective-permute-start(bf16[64,1664]{1,0:T(8,128)(2,1)} %get-tuple-element.316), channel_id=1, source_target_pairs={{0,2},{1,3},{2,0},{3,1},{4,6},{5,7},{6,4},{7,5},{8,10},{9,11},{10,... | collective-permute-start | bytes 638984 | tf_op jit(solution)/shard_map/ppermute | solution.py:506
  854.8 28.3 %collective-permute-start.37 = (bf16[64,1664]{1,0:T(8,128)(2,1)}, bf16[64,1664]{1,0:T(8,128)(2,1)}, u32[]{:S(2)}, u32[]{:S(2)}) collective-permute-start(bf16[64,1664]{1,0:T(8,128)(2,1)} %get-tuple-element.317), channel_id=1, source_target_pairs={{0,1},{1,2},{2,3},{3,0},{4,5},{5,6},{6,7},{7,4},{8,9},{9,10},{10,1... | collective-permute-start | bytes 638984 | tf_op jit(solution)/shard_map/ppermute | solution.py:506
  878.7 26.0 %all-to-all-start.11 = ((f32[8,8,512]{2,1,0:T(8,128)}), f32[8,8,512]{2,1,0:T(8,128)}, u32[]{:S(2)}, u32[]{:S(2)}) async-start(f32[8,8,512]{2,1,0:T(8,128)} %reshape.780), calls=%async_computation.13 | async-start | bytes 262144 | tf_op jit(solution)/shard_map/all_to_all | solution.py:79
  882.7 42.1 %collective-permute-start.52 = (bf16[64,2048]{1,0:T(8,128)(2,1)}, bf16[64,2048]{1,0:T(8,128)(2,1)}, u32[]{:S(2)}, u32[]{:S(2)}) collective-permute-start(bf16[64,2048]{1,0:T(8,128)(2,1)} %fusion.46), channel_id=1, source_target_pairs={{0,16},{16,0},{1,17},{17,1},{2,18},{18,2},{3,19},{19,3},{4,20},{20... | collective-permute-start | bytes 786440 | tf_op jit(solution)/shard_map/ppermute | solution.py:97
  910.6 23.7 %collective-permute-start.44 = (bf16[64,3712]{1,0:T(8,128)(2,1)}, bf16[64,3712]{1,0:T(8,128)(2,1)}, u32[]{:S(2)}, u32[]{:S(2)}) collective-permute-start(bf16[64,3712]{1,0:T(8,128)(2,1)} %constant_dynamic-update-slice_fusion.5), channel_id=1, source_target_pairs={{0,16},{16,0},{1,17},{17,1},{2,18},{18,2},{3,19},{19,3},{4,20},{20... | collective-permute-start | bytes 1425416 | tf_op jit(solution)/shard_map/ppermute | solution.py:97
  (139 other events, 1435.6 us)
Sparse Core Ops, SparseCore 0:
  52.3 47.1 all-gather.10
  184.3 110.5 all-gather.6
  479.4 80.3 reduce-scatter.2
  565.4 135.5 reduce-scatter.4
  702.9 56.7 all-gather.8
  770.4 122.4 all-gather.12

commit v4 on v3

--- a/solution.py
+++ b/solution.py
@@ -728,7 +728,6 @@
     pair_weight = lax.all_gather(pair_share, COPIES, axis=0, tiled=True)
     attn_proj = collect(matmul(attended_low, w_output).astype(LOW), "wsh")
     attn_proj, looked_up = lax.optimization_barrier((attn_proj, looked_up))
-    layer_input = EMBED_SCALE * jnp.sum(shift_exchange(entry(looked_up)).astype(WIDE), axis=0)
 
     first_sum = tokens_f + rms_norm(attn_proj, gains_full[1])
     low_rank_low = matmul(normed_low, left_full).astype(LOW)
@@ -738,6 +737,8 @@
     ff_in_low = rms_norm(mixed, gains_full[3]).astype(LOW)
 
     ff_run = spread(ff_in_low, "wsh")
+    looked_up = after(looked_up, ff_run)
+    layer_input = EMBED_SCALE * jnp.sum(shift_exchange(entry(looked_up)).astype(WIDE), axis=0)
     aligned = piece % 128 == 0
     if aligned:
         both, hidden_low, ff_part = ff_forward(ff_run, pair_weight, w_down, piece)
@@ -775,18 +776,16 @@
     grad_ff_low = grad_ff.astype(LOW)
 
     grad_ff_run = spread(grad_ff_low, "wsh")
+    down_part = over_rows(hidden_low, grad_ff_run).astype(LOW)
+    grad_ff_run, down_part = lax.optimization_barrier((grad_ff_run, down_part))
+    down_own = lax.psum_scatter(down_part, COPIES, scatter_dimension=0, tiled=True)
+    grad_input_low = after(grad_input_low, grad_ff_run)
     every_grad = shift_exchange(lambda k: grad_input_low).reshape(total_rows, -1)
-    down_part = over_rows(hidden_low, grad_ff_run).astype(LOW)
-    grad_ff_run, every_grad, down_part = lax.optimization_barrier(
-        (grad_ff_run, every_grad, down_part)
-    )
-    down_own = lax.psum_scatter(down_part, COPIES, scatter_dimension=0, tiled=True)
 
     def wider(rows, axis, bit):
         return jnp.concatenate([rows, swap(rows, axis, bit)], axis=0)
 
     hops = [1 << power for power in range(contexts.bit_length() - 1)]
-    every_grad = wider(every_grad, "ctx", hops[0])
     if aligned:
         grad_both, ff_part = ff_backward(grad_ff_run, pair_weight, w_down, both, piece)
     else:
@@ -803,12 +802,12 @@
         grad_both = grad_both.reshape(total_rows, 2 * hidden_width).astype(LOW)
         ff_part = matmul(grad_both, pair_weight).astype(LOW)
     ff_part, every_grad = lax.optimization_barrier((ff_part, every_grad))
-    for bit in hops[1:]:
-        every_grad = wider(every_grad, "ctx", bit)
+    every_grad = wider(every_grad, "ctx", hops[0])
     grad_ff_in = collect(ff_part, "wsh")
     pair_part = over_rows(after(grad_both, ff_part), ff_run).astype(LOW)
     grad_ff_in, pair_part, every_grad = lax.optimization_barrier((grad_ff_in, pair_part, every_grad))
-    every_grad = wider(every_grad, "slot", 1)
+    for bit in hops[1:]:
+        every_grad = wider(every_grad, "ctx", bit)
     pair_own = lax.psum_scatter(pair_part, COPIES, scatter_dimension=0, tiled=True)
     _, pullback = jax.vjp(rms_norm, mixed, gains_full[3])
     grad_mixed_norm, grad_gain_three = pullback(grad_ff_in)
@@ -820,6 +819,7 @@
     grad_attn_run, down_own, every_grad = lax.optimization_barrier(
         (grad_attn_run, down_own, every_grad)
     )
+    every_grad = wider(every_grad, "slot", 1)
     down_grad = lax.all_gather(down_own, COPIES, axis=0, tiled=True)
 
     def pair_back(index):
@@ -859,13 +859,10 @@
     grad_query_gain = grad_query_gain[0]
     kv_sum = collect(kv_part, "ctx")
     output_part = over_rows(attended_low, grad_attn_run).astype(LOW)
-    output_kept, output_given = halves(output_part.reshape(parts, -1, width))
-    kv_sum, pair_own, output_kept, output_given, narrow = lax.optimization_barrier(
-        (kv_sum, pair_own, output_kept, output_given, narrow)
+    kv_sum, pair_own, output_part, narrow, every_grad = lax.optimization_barrier(
+        (kv_sum, pair_own, output_part, narrow, every_grad)
     )
     pair_blocks = jnp.stack(shift_blocks(pair_back))
-    output_pieces = nearest(add_low(output_kept, output_given))
-    output_first = reduce_first(output_pieces)
     _, pullback = jax.vjp(key_path, key, key_gain_full)
     grad_key, grad_key_gain = pullback(kv_sum[:, :HEAD_DIM])
     _, pullback = jax.vjp(value_path, value)
@@ -875,46 +872,33 @@
     )
     heads_part = over_rows(normed_run, grad_heads).astype(LOW)
     heads_part = heads_part.reshape(run, parts, head_piece, head_width)
-    heads_part = jnp.concatenate([heads_part, narrow], axis=3).transpose(1, 0, 2, 3)
+    heads_part = jnp.concatenate(
+        [one[index] for index in range(run) for one in (heads_part, narrow)]
+        + [output_part.reshape(parts, head_piece, width)],
+        axis=2,
+    )
+    fetch_back = head_width + narrow.shape[3]
     heads_kept, heads_given = halves(heads_part)
     normed_part = times_transposed(grad_heads, w_heads).astype(LOW)
-    normed_part, output_first, heads_kept, heads_given, pair_blocks = lax.optimization_barrier(
-        (normed_part, output_first, heads_kept, heads_given, pair_blocks)
+    heads_pieces = [add_low(a, b) for a, b in zip(nearest(heads_kept), nearest(heads_given))]
+    heads_first = reduce_first(heads_pieces)
+    normed_part, heads_first, pair_blocks, down_grad = lax.optimization_barrier(
+        (normed_part, heads_first, pair_blocks, down_grad)
     )
     pair_all = lax.all_gather(pair_blocks, COPIES, axis=0)
     table_grad = EMBED_SCALE * over_rows(one_hot(), after(every_grad, normed_part))
-    heads_pieces = nearest(add_low(heads_kept, heads_given))
-    heads_first = reduce_first(heads_pieces)
     heads_second = reduce_second(heads_pieces, heads_first)
-    output_second = reduce_second(output_pieces, output_first)
     grad_run = collect(normed_part, "wsh")
-    grad_run, heads_second, output_second, table_grad = lax.optimization_barrier(
-        (grad_run, heads_second, output_second, table_grad)
+    grad_run, heads_second, table_grad = lax.optimization_barrier(
+        (grad_run, heads_second, table_grad)
     )
     heads_own = reduce_last(heads_pieces, heads_second)
-    heads_own = shift_exchange(entry(heads_own)).astype(WIDE)
-    pieces = [heads_own[:, :, :query_width].transpose(1, 0, 2).reshape(head_piece, -1)]
-    for begin in (query_width, query_width + HEAD_DIM):
-        one = heads_own[:, :, begin : begin + HEAD_DIM]
-        one = one.reshape(KV_HEADS, run // KV_HEADS, head_piece, HEAD_DIM).sum(axis=1)
-        pieces.append(one.transpose(1, 0, 2).reshape(head_piece, -1))
-    pieces.append(heads_own[:, :, head_width : head_width + narrow_columns].sum(axis=0))
-    pieces.append(heads_own[:, :, head_width + narrow_columns :].sum(axis=0))
-    cuts = []
-    for one in pieces:
-        cuts.append((sum(w for _, w in cuts), one.shape[1]))
-    heads_piece = jnp.concatenate(pieces, axis=1).astype(LOW)
-    heads_near = gather_second(heads_piece, gather_first(heads_piece))
-    output_own = reduce_last(output_pieces, output_second)
-    output_near = gather_first(output_own)
-    down_grad = after(down_grad, grad_run).astype(WIDE)
-    own = jnp.full((1,), chip, jnp.int32)
-    if aligned:
-        gate_grad, up_grad = widen_pair(pair_all, places)
-    else:
-        pair_all = jnp.take(pair_all, places, axis=1)
-        pair_all = pair_all.transpose(2, 3, 1, 0, 4).reshape(2, shard_rows, -1).astype(WIDE)
-        gate_grad, up_grad = pair_all[0], pair_all[1]
+    output_own = heads_own[:, run * fetch_back :]
+
+    def head_back(index):
+        return lax.dynamic_slice_in_dim(heads_own, index * fetch_back, fetch_back, 1)
+
+    heads_sent = shift_exchange(head_back).astype(WIDE)
     grad_normed = (
         grad_run
         + times_transposed(grad_rank_low, left_full)
@@ -923,15 +907,6 @@
     _, pullback = jax.vjp(rms_norm, tokens_f, gains_full[0])
     grad_tokens, grad_gain_zero = pullback(grad_normed)
     tokens_grad = (grad_tokens + grad_branch).astype(LOW)[None]
-
-    output_all = last_gather(gather_second(output_own, output_near))
-    (output_grad,) = assemble([p[None] for p in output_all], own, WIDE)
-    query_grad, key_grad, value_grad, narrow, layer_proj_grad = assemble(
-        [p[None] for p in last_gather(heads_near)], own, WIDE, cuts
-    )
-    narrow = narrow.reshape(shard_rows, -1)
-    layer_proj_grad = layer_proj_grad.reshape(parts, proj_rows, width // parts)
-    layer_proj_grad = layer_proj_grad.transpose(1, 0, 2).reshape(proj_rows, width)
 
     vector = jnp.concatenate(
         [grad_query_gain.reshape(run, gain_cut), grad_key_gain.reshape(run, gain_cut)], axis=1
@@ -951,7 +926,51 @@
     )
     gain_sums = gain_sums.reshape(8, run, shard_rows).transpose(1, 0, 2).reshape(8 * run, shard_rows)
     gain_sums = collect(gain_sums, "wsh")
+    pieces = [heads_sent[:, :, :query_width].transpose(1, 0, 2).reshape(head_piece, -1)]
+    for begin in (query_width, query_width + HEAD_DIM):
+        one = heads_sent[:, :, begin : begin + HEAD_DIM]
+        one = one.reshape(KV_HEADS, run // KV_HEADS, head_piece, HEAD_DIM).sum(axis=1)
+        pieces.append(one.transpose(1, 0, 2).reshape(head_piece, -1))
+    begin = head_width
+    for size in (rank, rank, w_layer_gate.shape[1]):
+        pieces.append(heads_sent[:, :, begin : begin + size].sum(axis=0))
+        begin += size
+    pieces.append(heads_sent[:, :, head_width + narrow_columns :].sum(axis=0))
+    pieces.append(output_own.astype(WIDE))
+    cuts = []
+    for one in pieces:
+        cuts.append((sum(w for _, w in cuts), one.shape[1]))
+    heads_piece = jnp.concatenate(pieces, axis=1).astype(LOW)
+    heads_piece, gain_sums = lax.optimization_barrier((heads_piece, gain_sums))
+    heads_near = gather_first(heads_piece)
     gain_sums = jnp.sum(spread(gain_sums[None], COPIES), axis=0)
+    own = jnp.full((1,), chip, jnp.int32)
+    if aligned:
+        gate_grad, up_grad = widen_pair(pair_all, places)
+    else:
+        pair_all = jnp.take(pair_all, places, axis=1)
+        pair_all = pair_all.transpose(2, 3, 1, 0, 4).reshape(2, shard_rows, -1).astype(WIDE)
+        gate_grad, up_grad = pair_all[0], pair_all[1]
+    down_grad = after(down_grad, heads_piece).astype(WIDE)
+    heads_near, down_grad, gain_sums = lax.optimization_barrier((heads_near, down_grad, gain_sums))
+    heads_near = gather_second(heads_piece, heads_near)
+    heads_near, gate_grad, up_grad = lax.optimization_barrier((heads_near, gate_grad, up_grad))
+    heads_all = last_gather(heads_near)
+    (
+        query_grad,
+        key_grad,
+        value_grad,
+        left_grad,
+        right_grad,
+        layer_gate_grad,
+        layer_proj_grad,
+        output_grad,
+    ) = assemble(
+        [p[None] for p in heads_all], own, WIDE, cuts
+    )
+    layer_proj_grad = layer_proj_grad.reshape(parts, proj_rows, width // parts)
+    layer_proj_grad = layer_proj_grad.transpose(1, 0, 2).reshape(proj_rows, width)
+
     return (
         layer_out,
         tokens_grad,
@@ -960,12 +979,12 @@
         key_grad.reshape(shard_rows, -1),
         value_grad.reshape(shard_rows, -1),
         output_grad.reshape(query_width, width),
-        narrow[:, :rank],
-        narrow[:, rank : 2 * rank],
+        left_grad.reshape(shard_rows, -1),
+        right_grad.reshape(shard_rows, -1),
         gate_grad,
         up_grad,
         down_grad,
-        narrow[:, 2 * rank :],
+        layer_gate_grad.reshape(shard_rows, -1),
         layer_proj_grad,
         gain_sums[:6].T,
         gain_sums[6, :gain_cut],

time: 992 us -> 958 us (0.966)
  waiting for transfers between devices: 425 us -> 374 us
  blocking collectives: 0 us -> 50.3 us
  starting transfers between devices: 123 us -> 103 us
  local copies, waits for them, and re-layouts: 104 us -> 93.2 us
    ppermute x21, waiting for transfers between devices: 176 us -> 75.2 us  [shift_blocks(): block = lax.ppermute(block, 'wsh', [(i, (i + k) % run) for i in range(run)])]
    all_to_all x12 -> x11, waiting for transfers between devices: 168 us -> 226 us  [exchange(): return lax.all_to_all(value, axis, 0, 0, tiled=True)]
    all_to_all x0 -> x1, blocking collectives: none -> 50.3 us  [exchange(): return lax.all_to_all(value, axis, 0, 0, tiled=True)]
    ppermute x35 -> x22, waiting for transfers between devices: 81.7 us -> 54.9 us  [swap(): return lax.ppermute(value, axis, [(i, i ^ bit) for i in range(size)])]
    reduce_scatter x1, waiting for transfers between devices: 0.02 us -> 16.8 us  [shards(): lax.psum_scatter(pair_part, COPIES, scatter_dimension=0, tiled=True)]
    ppermute x35 -> x22, starting transfers between devices: 28.8 us -> 20.1 us  [swap(): return lax.ppermute(value, axis, [(i, i ^ bit) for i in range(size)])]
    all_to_all x12 -> x11, starting transfers between devices: 62.9 us -> 58.1 us  [exchange(): return lax.all_to_all(value, axis, 0, 0, tiled=True)]
    unnamed x254 -> x221, local copies, waits for them, and re-layouts: 22.8 us -> 21 us
  transfers between devices with their start and end apart: 74 -> 60, of which waited for: 30 -> 27; matrix products, arithmetic and copies ran while one was open for 25% -> 25% of each run, Pallas kernels for 6% -> 5%
where the time goes in v4:
time: 958 us; the launch traced here: 945 us
  waiting for transfers between devices  374 us (39%)
  Pallas kernels  113 us (12%)
  starting transfers between devices  103 us (11%)
  other arithmetic  99.8 us (10%)
  matrix products  94.9 us (10%)
  local copies, waits for them, and re-layouts  93.2 us (10%)
  blocking collectives  50.3 us (5%)
  between operations  17.1 us (2%)
    all_to_all x11, waiting for transfers between devices, exchange(): return lax.all_to_all(value, axis, 0, 0, tiled=True)  226 us
    ppermute x21, waiting for transfers between devices, shift_blocks(): block = lax.ppermute(block, 'wsh', [(i, (i + k) % run) for i in range(run)])  75.2 us
    all_to_all x11, starting transfers between devices, exchange(): return lax.all_to_all(value, axis, 0, 0, tiled=True)  58.1 us
    dot_general x9, matrix products, over_rows(): lax.dot_general(left, right, (((0,), (0,)), ((), ())), preferred_element_...  56 us
    ppermute x22, waiting for transfers between devices, swap(): return lax.ppermute(value, axis, [(i, i ^ bit) for i in range(size)])  54.9 us
    all_to_all x1, blocking collectives, exchange(): return lax.all_to_all(value, axis, 0, 0, tiled=True)  50.3 us
    pallas_call x1, Pallas kernels, ff_backward(): pl.pallas_call(functools.partial(ff_backward_kernel, piece, count), grid=...  27.7 us
    pallas_call x1, Pallas kernels, widen_pair(): pl.pallas_call(widen_kernel, grid_spec=pltpu.PrefetchScalarGridSpec(num_s...  25.8 us
  transfers between devices with their start and end apart: 60, of which 27 were waited for; matrix products, arithmetic and copies ran while one was open for 25% of the time, Pallas kernels for 5%

profile of v4, /device:TPU:0, one launch (start us, length us, event | category | flops | bytes accessed | tf_op | source)
XLA Modules:
  0.0 945.0 jit_solution(7615607231812000715)
XLA Ops:
  8.1 5.0 collective-permute-start.2
  24.6 5.6 collective-permute-done.8
  30.3 16.6 %collective-permute-done.7 = bf16[80,1664]{1,0:T(8,128)(2,1)S(1)} collective-permute-done((bf16[80,1664]{1,0:T(8,128)(2,1)S(1)}, bf16[80,1664]{1,0:T(8,128)(2,1)S(1)}, u32[]{:S(2)}, u32[]{:S(2)}) %collective-permute-start.7) | collective-permute-done | bytes 266272 | tf_op jit(solution)/shard_map/ppermute | solution.py:506
  53.7 4.5 all-to-all-start
  69.9 14.7 %fusion.5 = bf16[4096,256]{1,0:T(8,128)(2,1)} fusion(bf16[4096,256]{1,0:T(8,128)(2,1)} %param.27, s32[4096]{0:T(1024)S(1)} %add_subtract_fusion), kind=kOutput, calls=%fused_computation.16 | convolution fusion | flops 8607760384 | bytes 4210688 | tf_op jit(solution)/shard_map/dot_general | solution.py:53
  86.5 18.9 %all-to-all-done = bf16[4,128,2048]{2,1,0:T(8,128)(2,1)} async-done(((bf16[4,128,2048]{2,1,0:T(8,128)(2,1)}), bf16[4,128,2048]{2,1,0:T(8,128)(2,1)}, u32[]{:S(2)}, u32[]{:S(2)}) %all-to-all-start) | async-done | bytes 2097184 | tf_op jit(solution)/shard_map/all_to_all | solution.py:79
  110.9 5.5 fusion.39.raw_ref
  120.4 4.9 all-to-all-start.1
  150.8 11.2 %shard_map.323 = (bf16[512,512]{1,0:T(8,128)(2,1)}, f32[2,512,2048]{2,1,0:T(8,128)}, f32[512,512]{1,0:T(8,128)}, bf16[512,512]{1,0:T(8,128)(2,1)}) custom-call(f32[512,1024]{1,0:T(8,128)} %copy-done.18, f32[1,256]{1,0:T(1,128)} %reshape.722.gain_ref, f32[512,128]{1,0:T(8,128)} %get-tuple-element.383.cos_ref, f32[512,128]{1,0:T(8,128)} %get-tuple-element.382.sin_ref, ...), custom_call_target="tpu_custom_call" | custom-call | flops 2147483648 | bytes 14155776 | tf_op jit(solution)/shard_map/pallas_call | solution.py:351
  162.0 18.2 %collective-permute-done.10.refs_2_ = bf16[512,512]{1,0:T(8,128)(2,1)} collective-permute-done((bf16[512,512]{1,0:T(8,128)(2,1)}, bf16[512,512]{1,0:T(8,128)(2,1)}, u32[]{:S(2)}, u32[]{:S(2)}) %collective-permute-start.10) | collective-permute-done | bytes 524320 | tf_op jit(solution)/shard_map/ppermute | solution.py:506
  180.2 4.1 shard_map.324
  189.2 13.0 %all-to-all-start.2 = ((bf16[4,128,2048]{2,1,0:T(8,128)(2,1)}), bf16[4,128,2048]{2,1,0:T(8,128)(2,1)}, u32[]{:S(2)}, u32[]{:S(2)}) async-start(bf16[4,128,2048]{2,1,0:T(8,128)(2,1)} %bitcast.330), calls=%async_computation.2 | async-start | bytes 4194304 | tf_op jit(solution)/shard_map/all_to_all | solution.py:79
  206.1 23.9 %collective-permute-done.13 = bf16[1024,256]{1,0:T(8,128)(2,1)S(1)} collective-permute-done((bf16[1024,256]{1,0:T(8,128)(2,1)S(1)}, bf16[1024,256]{1,0:T(8,128)(2,1)S(1)}, u32[]{:S(2)}, u32[]{:S(2)}) %collective-permute-start.13) | collective-permute-done | bytes 524320 | tf_op jit(solution)/shard_map/ppermute | solution.py:97
  232.2 5.5 collective-permute-done.14
  242.2 8.9 all-to-all-done.2
  257.8 4.5 all-to-all-start.3
  262.8 48.2 %all-to-all-done.3 = bf16[4,128,2048]{2,1,0:T(8,128)(2,1)} async-done(((bf16[4,128,2048]{2,1,0:T(8,128)(2,1)}), bf16[4,128,2048]{2,1,0:T(8,128)(2,1)}, u32[]{:S(2)}, u32[]{:S(2)}) %all-to-all-start.3) | async-done | bytes 2097184 | tf_op jit(solution)/shard_map/all_to_all | solution.py:79
  322.0 23.8 %shard_map.325 = (f32[512,4096]{1,0:T(8,128)}, bf16[512,2048]{1,0:T(8,128)(2,1)}, bf16[512,2048]{1,0:T(8,128)(2,1)}) custom-call(bf16[512,2048]{1,0:T(8,128)(2,1)} %bitcast.41.x_ref, bf16[4096,2048]{1,0:T(8,128)(2,1)} %all-gather.7.cloned.1.call-done.pair_ref, bf16[2048,2048]{1,0:T(8,128)(2,1)} %down_ref.3), custom_call_target="tpu_custom_call" | custom-call | flops 12884901888 | bytes 35651584 | tf_op jit(solution)/shard_map/pallas_call | solution.py:243
  345.9 4.6 all-to-all-start.4
  353.9 42.6 %all-to-all-done.4 = bf16[4,128,2048]{2,1,0:T(8,128)(2,1)} async-done(((bf16[4,128,2048]{2,1,0:T(8,128)(2,1)}), bf16[4,128,2048]{2,1,0:T(8,128)(2,1)}, u32[]{:S(2)}, u32[]{:S(2)}) %all-to-all-start.4) | async-done | bytes 2097184 | tf_op jit(solution)/shard_map/all_to_all | solution.py:79
  407.2 50.3 %all_to_all.99 = bf16[4,128,2048]{2,1,0:T(8,128)(2,1)S(1)} all-to-all(bf16[4,128,2048]{2,1,0:T(8,128)(2,1)S(1)} %broadcast_in_dim.202), channel_id=1, replica_groups=mesh['slot'=2,'ctx'=4,'wsh'=4] {'wsh'}, dimensions={0} | all-to-all | bytes 4194304 | tf_op jit(solution)/shard_map/all_to_all | solution.py:79
  458.8 6.8 convolution_convert_fusion.1
  467.9 27.7 %shard_map.326 = (bf16[512,4096]{1,0:T(8,128)(2,1)}, bf16[512,2048]{1,0:T(8,128)(2,1)}) custom-call(bf16[512,2048]{1,0:T(8,128)(2,1)} %bitcast.334, bf16[2048,2048]{1,0:T(8,128)(2,1)} %down_ref.3, f32[512,4096]{1,0:T(8,128)} %get-tuple-element.136.both_ref, bf16[4096,2048]{1,0:T(8,128)(2,1)} %all-gather.7.cloned.1.call-done.pair_ref), custom_call_target="tpu_custom_call" | custom-call | flops 12884901888 | bytes 37748736 | tf_op jit(solution)/shard_map/pallas_call | solution.py:300
  500.2 4.6 all-to-all-start.6
  506.6 15.2 %convolution_convert_fusion = bf16[4096,2048]{1,0:T(8,128)(2,1)} fusion(bf16[512,4096]{1,0:T(8,128)(2,1)} %get-tuple-element.141, bf16[512,2048]{1,0:T(8,128)(2,1)} %bitcast.41.x_ref), kind=kOutput, calls=%fused_computation.11 | convolution fusion | flops 8598323200 | bytes 23068672 | tf_op jit(solution)/shard_map/dot_general | solution.py:63
  523.6 27.6 %all-to-all-done.6 = bf16[4,128,2048]{2,1,0:T(8,128)(2,1)} async-done(((bf16[4,128,2048]{2,1,0:T(8,128)(2,1)}), bf16[4,128,2048]{2,1,0:T(8,128)(2,1)}, u32[]{:S(2)}, u32[]{:S(2)}) %all-to-all-start.6) | async-done | bytes 2097184 | tf_op jit(solution)/shard_map/all_to_all | solution.py:79
  563.7 4.9 all-to-all-start.7
  576.5 6.8 collective-permute-done.22
  585.5 30.8 %all-to-all-done.7 = bf16[4,128,2048]{2,1,0:T(8,128)(2,1)} async-done(((bf16[4,128,2048]{2,1,0:T(8,128)(2,1)}), bf16[4,128,2048]{2,1,0:T(8,128)(2,1)}, u32[]{:S(2)}, u32[]{:S(2)}) %all-to-all-start.7) | async-done | bytes 2097184 | tf_op jit(solution)/shard_map/all_to_all | solution.py:79
  620.3 12.5 %shard_map.327 = (bf16[512,512]{1,0:T(8,128)(2,1)}, f32[1,256]{1,0:T(1,128)}, bf16[2048,512]{1,0:T(8,128)(2,1)}) custom-call(bf16[512,512]{1,0:T(8,128)(2,1)} %convolution_convert_fusion.9.grad_ref, f32[512,512]{1,0:T(8,128)} %get-tuple-element.147.wide_ref, f32[2,512,2048]{2,1,0:T(8,128)} %get-tuple-element.148.probs_ref, ...), custom_call_target="tpu_custom_call" | custom-call | flops 4294967296 | bytes 16252928 | tf_op jit(solution)/shard_map/pallas_call | solution.py:446
  632.8 4.5 all-to-all-start.8
  643.1 4.4 convolution_convert_fusion.4
  650.1 16.6 %all-to-all-done.8 = bf16[4,512,512]{2,1,0:T(8,128)(2,1)} async-done(((bf16[4,512,512]{2,1,0:T(8,128)(2,1)}), bf16[4,512,512]{2,1,0:T(8,128)(2,1)}, u32[]{:S(2)}, u32[]{:S(2)}) %all-to-all-start.8) | async-done | bytes 2097184 | tf_op jit(solution)/shard_map/all_to_all | solution.py:79
  668.7 16.8 %reduce-scatter.5.cloned.1.call-done = bf16[512,2048]{1,0:T(8,128)(2,1)} async-done(((bf16[4096,2048]{1,0:T(8,128)(2,1)}), bf16[512,2048]{1,0:T(8,128)(2,1)}) %reduce-scatter.5.cloned.1.call-update) | async-done | bytes 2097168 | tf_op jit(solution)/shard_map/reduce_scatter | solution.py:811
  689.3 4.1 convolution_convert_fusion.2
  710.4 4.8 add_convert_fusion.1
  722.2 30.2 %collective-permute-done.28 = bf16[2,512,256]{1,2,0:T(8,128)(2,1)S(1)} collective-permute-done((bf16[2,512,256]{1,2,0:T(8,128)(2,1)S(1)}, bf16[2,512,256]{1,2,0:T(8,128)(2,1)S(1)}, u32[]{:S(2)}, u32[]{:S(2)}) %collective-permute-start.28) | collective-permute-done | bytes 524320 | tf_op jit(solution)/shard_map/ppermute | solution.py:506
  754.0 4.1 copy.137
  764.7 4.7 all-to-all-start.9
  777.4 23.2 %fusion.4 = f32[4096,256]{1,0:T(8,128)} fusion(bf16[4096,256]{1,0:T(8,128)(2,1)S(1)} %copy-done.32, s32[4096]{0:T(1024)S(1)} %copy-done.67), kind=kOutput, calls=%fused_computation.13 | convolution fusion | flops 8607760384 | bytes 6307840 | tf_op jit(solution)/shard_map/dot_general | solution.py:63
  800.7 17.2 %all-to-all-done.9 = bf16[4,128,2048]{2,1,0:T(8,128)(2,1)} async-done(((bf16[4,128,2048]{2,1,0:T(8,128)(2,1)}), bf16[4,128,2048]{2,1,0:T(8,128)(2,1)}, u32[]{:S(2)}, u32[]{:S(2)}) %all-to-all-start.9) | async-done | bytes 2097184 | tf_op jit(solution)/shard_map/all_to_all | solution.py:79
  827.7 4.6 all-to-all-start.10
  832.3 11.2 %all-to-all-done.10 = f32[4,8,512]{2,1,0:T(8,128)S(1)} async-done(((f32[4,8,512]{2,1,0:T(8,128)}), f32[4,8,512]{2,1,0:T(8,128)S(1)}, u32[]{:S(2)}, u32[]{:S(2)}) %all-to-all-start.10) | async-done | bytes 65568 | tf_op jit(solution)/shard_map/all_to_all | solution.py:79
  862.0 11.9 %convert_element_type.388 = f32[2048,2048]{1,0:T(8,128)} convert(bf16[2048,2048]{1,0:T(8,128)(2,1)} %all-gather.9.cloned.1.call-done) | non-fusion elementwise | flops 4194304 | bytes 25165824 | tf_op jit(solution)/shard_map/convert_element_type | solution.py:954
  874.0 4.5 all-to-all-done.11
  882.5 7.7 collective-permute-done.38
  893.0 25.8 %shard_map.328 = (f32[512,8192]{1,0:T(8,128)}, f32[512,8192]{1,0:T(8,128)}) custom-call(s32[4]{0:T(128)} %and_select_fusion.1.places, bf16[8,4,2,512,256]{4,3,2,1,0:T(8,128)(2,1)} %bitcast.308), custom_call_target="tpu_custom_call" | custom-call | bytes 50331648 | tf_op jit(solution)/shard_map/pallas_call | solution.py:486
  924.5 8.1 shard_map.329
  (517 shorter events, 252.1 us)
Async XLA Ops:
  7.2 100.3 %all-gather.11.cloned.1.call-start = ((), (), s32[]{:S(2)}) async-start(), calls=%async_computation.18 | async-start | bytes 7667712 | tf_op jit(solution)/shard_map/all_gather | solution.py:637
  8.1 11.6 %collective-permute-start.2 = (s32[2,128]{1,0:T(2,128)S(1)}, s32[2,128]{1,0:T(2,128)S(1)}, u32[]{:S(2)}, u32[]{:S(2)}) collective-permute-start(s32[2,128]{1,0:T(2,128)S(1)} %get-tuple-element.385), channel_id=1, source_target_pairs={{0,3},{1,0},{2,1},{3,2},{4,7},{5,4},{6,5},{7,6},{8,11},{9,8},{10,9... | collective-permute-start | bytes 3080 | tf_op jit(solution)/shard_map/ppermute | solution.py:506
  20.5 9.8 %collective-permute-start.8 = (bf16[80,1664]{1,0:T(8,128)(2,1)S(1)}, bf16[80,1664]{1,0:T(8,128)(2,1)S(1)}, u32[]{:S(2)}, u32[]{:S(2)}) collective-permute-start(bf16[80,1664]{1,0:T(8,128)(2,1)S(1)} %pad_maximum_fusion.16), channel_id=1, source_target_pairs={{0,3},{1,0},{2,1},{3,2},{4,7},{5,4},{6,5},{7,6},{8,11},{9,8},{10,9... | collective-permute-start | bytes 798728 | tf_op jit(solution)/shard_map/ppermute | solution.py:506
  23.4 23.4 %collective-permute-start.7 = (bf16[80,1664]{1,0:T(8,128)(2,1)S(1)}, bf16[80,1664]{1,0:T(8,128)(2,1)S(1)}, u32[]{:S(2)}, u32[]{:S(2)}) collective-permute-start(bf16[80,1664]{1,0:T(8,128)(2,1)S(1)} %get-tuple-element.359), channel_id=1, source_target_pairs={{0,2},{1,3},{2,0},{3,1},{4,6},{5,7},{6,4},{7,5},{8,10},{9,11},{10,... | collective-permute-start | bytes 798728 | tf_op jit(solution)/shard_map/ppermute | solution.py:506
  24.6 22.3 %collective-permute-start.6 = (bf16[80,1664]{1,0:T(8,128)(2,1)S(1)}, bf16[80,1664]{1,0:T(8,128)(2,1)S(1)}, u32[]{:S(2)}, u32[]{:S(2)}) collective-permute-start(bf16[80,1664]{1,0:T(8,128)(2,1)S(1)} %get-tuple-element.358), channel_id=1, source_target_pairs={{0,1},{1,2},{2,3},{3,0},{4,5},{5,6},{6,7},{7,4},{8,9},{9,10},{10,1... | collective-permute-start | bytes 798728 | tf_op jit(solution)/shard_map/ppermute | solution.py:506
  53.7 51.6 %all-to-all-start = ((bf16[4,128,2048]{2,1,0:T(8,128)(2,1)}), bf16[4,128,2048]{2,1,0:T(8,128)(2,1)}, u32[]{:S(2)}, u32[]{:S(2)}) async-start(bf16[4,128,2048]{2,1,0:T(8,128)(2,1)} %broadcast_in_dim.105), calls=%async_computation | async-start | bytes 4194304 | tf_op jit(solution)/shard_map/all_to_all | solution.py:79
  120.4 30.4 %all-to-all-start.1 = ((bf16[4,512,512]{2,1,0:T(8,128)(2,1)}), bf16[4,512,512]{2,1,0:T(8,128)(2,1)}, u32[]{:S(2)}, u32[]{:S(2)}) async-start(bf16[4,512,512]{2,1,0:T(8,128)(2,1)} %broadcast_in_dim.197), calls=%async_computation.1 | async-start | bytes 4194304 | tf_op jit(solution)/shard_map/all_to_all | solution.py:79
  125.3 196.7 %all-gather.7.cloned.1.call-start = ((), (), s32[]{:S(2)}) async-start(), calls=%async_computation.14 | async-start | bytes 18874368 | tf_op jit(solution)/shard_map/all_gather | solution.py:728
  142.2 19.8 %collective-permute-start.9 = (bf16[512,512]{1,0:T(8,128)(2,1)}, bf16[512,512]{1,0:T(8,128)(2,1)}, u32[]{:S(2)}, u32[]{:S(2)}) collective-permute-start(bf16[512,512]{1,0:T(8,128)(2,1)} %pad_maximum_fusion.12), channel_id=1, source_target_pairs={{0,1},{1,2},{2,3},{3,0},{4,5},{5,6},{6,7},{7,4},{8,9},{9,10},{10,1... | collective-permute-start | bytes 1572872 | tf_op jit(solution)/shard_map/ppermute | solution.py:506
  144.1 36.1 %collective-permute-start.10 = (bf16[512,512]{1,0:T(8,128)(2,1)}, bf16[512,512]{1,0:T(8,128)(2,1)}, u32[]{:S(2)}, u32[]{:S(2)}) collective-permute-start(bf16[512,512]{1,0:T(8,128)(2,1)} %pad_maximum_fusion.13), channel_id=1, source_target_pairs={{0,2},{1,3},{2,0},{3,1},{4,6},{5,7},{6,4},{7,5},{8,10},{9,11},{10,... | collective-permute-start | bytes 1572872 | tf_op jit(solution)/shard_map/ppermute | solution.py:506
  146.5 33.7 %collective-permute-start.11 = (bf16[512,512]{1,0:T(8,128)(2,1)}, bf16[512,512]{1,0:T(8,128)(2,1)}, u32[]{:S(2)}, u32[]{:S(2)}) collective-permute-start(bf16[512,512]{1,0:T(8,128)(2,1)} %pad_maximum_fusion.14), channel_id=1, source_target_pairs={{0,3},{1,0},{2,1},{3,2},{4,7},{5,4},{6,5},{7,6},{8,11},{9,8},{10,9... | collective-permute-start | bytes 1572872 | tf_op jit(solution)/shard_map/ppermute | solution.py:506
  186.6 15.6 %collective-permute-start.12 = (bf16[2048,256]{1,0:T(8,128)(2,1)}, bf16[2048,256]{1,0:T(8,128)(2,1)}, u32[]{:S(2)}, u32[]{:S(2)}) collective-permute-start(bf16[2048,256]{1,0:T(8,128)(2,1)} %slice.224), channel_id=1, source_target_pairs={{0,16},{16,0},{1,17},{17,1},{2,18},{18,2},{3,19},{19,3},{4,20},{20... | collective-permute-start | bytes 3145736 | tf_op jit(solution)/shard_map/ppermute | solution.py:97
  189.2 61.9 %all-to-all-start.2 = ((bf16[4,128,2048]{2,1,0:T(8,128)(2,1)}), bf16[4,128,2048]{2,1,0:T(8,128)(2,1)}, u32[]{:S(2)}, u32[]{:S(2)}) async-start(bf16[4,128,2048]{2,1,0:T(8,128)(2,1)} %bitcast.330), calls=%async_computation.2 | async-start | bytes 4194304 | tf_op jit(solution)/shard_map/all_to_all | solution.py:79
  204.3 25.7 %collective-permute-start.13 = (bf16[1024,256]{1,0:T(8,128)(2,1)S(1)}, bf16[1024,256]{1,0:T(8,128)(2,1)S(1)}, u32[]{:S(2)}, u32[]{:S(2)}) collective-permute-start(bf16[1024,256]{1,0:T(8,128)(2,1)S(1)} %slice.299), channel_id=1, source_target_pairs={{0,8},{4,12},{8,0},{12,4},{1,9},{5,13},{9,1},{13,5},{2,10},{6,14},... | collective-permute-start | bytes 1572872 | tf_op jit(solution)/shard_map/ppermute | solution.py:97
  230.2 7.6 collective-permute-start.14
  257.8 53.2 %all-to-all-start.3 = ((bf16[4,128,2048]{2,1,0:T(8,128)(2,1)}), bf16[4,128,2048]{2,1,0:T(8,128)(2,1)}, u32[]{:S(2)}, u32[]{:S(2)}) async-start(bf16[4,128,2048]{2,1,0:T(8,128)(2,1)} %broadcast_in_dim.198), calls=%async_computation.3 | async-start | bytes 4194304 | tf_op jit(solution)/shard_map/all_to_all | solution.py:79
  345.9 50.7 %all-to-all-start.4 = ((bf16[4,128,2048]{2,1,0:T(8,128)(2,1)}), bf16[4,128,2048]{2,1,0:T(8,128)(2,1)}, u32[]{:S(2)}, u32[]{:S(2)}) async-start(bf16[4,128,2048]{2,1,0:T(8,128)(2,1)} %bitcast.335), calls=%async_computation.4 | async-start | bytes 4194304 | tf_op jit(solution)/shard_map/all_to_all | solution.py:79
  350.5 265.9 %reduce-scatter.3.cloned.1.call-start = ((), (), s32[]{:S(2)}) async-start(), calls=%async_computation.15 | async-start | bytes 9437184 | tf_op jit(solution)/shard_map/reduce_scatter | solution.py:781
  465.6 29.9 %collective-permute-start.20 = (bf16[128,256]{1,0:T(8,128)(2,1)S(1)}, bf16[128,256]{1,0:T(8,128)(2,1)S(1)}, u32[]{:S(2)}, u32[]{:S(2)}) collective-permute-start(bf16[128,256]{1,0:T(8,128)(2,1)S(1)} %get-tuple-element.138), channel_id=1, source_target_pairs={{0,3},{1,0},{2,1},{3,2},{4,7},{5,4},{6,5},{7,6},{8,11},{9,8},{10,9... | collective-permute-start | bytes 196616 | tf_op jit(solution)/shard_map/ppermute | solution.py:506
  467.1 28.4 %collective-permute-start.19 = (bf16[128,256]{1,0:T(8,128)(2,1)S(1)}, bf16[128,256]{1,0:T(8,128)(2,1)S(1)}, u32[]{:S(2)}, u32[]{:S(2)}) collective-permute-start(bf16[128,256]{1,0:T(8,128)(2,1)S(1)} %get-tuple-element.138), channel_id=1, source_target_pairs={{0,2},{1,3},{2,0},{3,1},{4,6},{5,7},{6,4},{7,5},{8,10},{9,11},{10,... | collective-permute-start | bytes 196616 | tf_op jit(solution)/shard_map/ppermute | solution.py:506
  467.4 28.2 %collective-permute-start.18 = (bf16[128,256]{1,0:T(8,128)(2,1)S(1)}, bf16[128,256]{1,0:T(8,128)(2,1)}, u32[]{:S(2)}, u32[]{:S(2)}) collective-permute-start(bf16[128,256]{1,0:T(8,128)(2,1)S(1)} %get-tuple-element.138), channel_id=1, source_target_pairs={{0,1},{1,2},{2,3},{3,0},{4,5},{5,6},{6,7},{7,4},{8,9},{9,10},{10,1... | collective-permute-start | bytes 196616 | tf_op jit(solution)/shard_map/ppermute | solution.py:506
  500.2 50.9 %all-to-all-start.6 = ((bf16[4,128,2048]{2,1,0:T(8,128)(2,1)}), bf16[4,128,2048]{2,1,0:T(8,128)(2,1)}, u32[]{:S(2)}, u32[]{:S(2)}) async-start(bf16[4,128,2048]{2,1,0:T(8,128)(2,1)} %bitcast.332), calls=%async_computation.6 | async-start | bytes 4194304 | tf_op jit(solution)/shard_map/all_to_all | solution.py:79
  504.8 180.7 %reduce-scatter.5.cloned.1.call-start = ((), (), s32[]{:S(2)}) async-start(), calls=%async_computation.16 | async-start | bytes 18874368 | tf_op jit(solution)/shard_map/reduce_scatter | solution.py:811
  505.1 16.7 %collective-permute-start.21 = (bf16[512,256]{1,0:T(8,128)(2,1)S(1)}, bf16[512,256]{1,0:T(8,128)(2,1)}, u32[]{:S(2)}, u32[]{:S(2)}) collective-permute-start(bf16[512,256]{1,0:T(8,128)(2,1)S(1)} %bitcast.340), channel_id=1, source_target_pairs={{0,4},{4,0},{8,12},{12,8},{1,5},{5,1},{9,13},{13,9},{2,6},{6,2},{1... | collective-permute-start | bytes 786440 | tf_op jit(solution)/shard_map/ppermute | solution.py:97
  563.7 52.7 %all-to-all-start.7 = ((bf16[4,128,2048]{2,1,0:T(8,128)(2,1)}), bf16[4,128,2048]{2,1,0:T(8,128)(2,1)}, u32[]{:S(2)}, u32[]{:S(2)}) async-start(bf16[4,128,2048]{2,1,0:T(8,128)(2,1)} %broadcast_in_dim.204), calls=%async_computation.7 | async-start | bytes 4194304 | tf_op jit(solution)/shard_map/all_to_all | solution.py:79
  570.0 13.3 %collective-permute-start.22 = (bf16[1024,256]{1,0:T(8,128)(2,1)}, bf16[1024,256]{1,0:T(8,128)(2,1)}, u32[]{:S(2)}, u32[]{:S(2)}) collective-permute-start(bf16[1024,256]{1,0:T(8,128)(2,1)} %pad_maximum_fusion.15), channel_id=1, source_target_pairs={{0,8},{4,12},{8,0},{12,4},{1,9},{5,13},{9,1},{13,5},{2,10},{6,14},... | collective-permute-start | bytes 1572872 | tf_op jit(solution)/shard_map/ppermute | solution.py:97
  632.8 33.9 %all-to-all-start.8 = ((bf16[4,512,512]{2,1,0:T(8,128)(2,1)}), bf16[4,512,512]{2,1,0:T(8,128)(2,1)}, u32[]{:S(2)}, u32[]{:S(2)}) async-start(bf16[4,512,512]{2,1,0:T(8,128)(2,1)} %bitcast.331), calls=%async_computation.9 | async-start | bytes 4194304 | tf_op jit(solution)/shard_map/all_to_all | solution.py:79
  637.3 116.7 %all-gather.9.cloned.1.call-start = ((), (), s32[]{:S(2)}) async-start(), calls=%async_computation.17 | async-start | bytes 9437184 | tf_op jit(solution)/shard_map/all_gather | solution.py:823
  637.3 10.1 %collective-permute-start.23 = (bf16[2048,256]{1,0:T(8,128)(2,1)}, bf16[2048,256]{1,0:T(8,128)(2,1)}, u32[]{:S(2)}, u32[]{:S(2)}) collective-permute-start(bf16[2048,256]{1,0:T(8,128)(2,1)} %pad_maximum_fusion.6), channel_id=1, source_target_pairs={{0,16},{16,0},{1,17},{17,1},{2,18},{18,2},{3,19},{19,3},{4,20},{20... | collective-permute-start | bytes 3145736 | tf_op jit(solution)/shard_map/ppermute | solution.py:97
  642.5 250.5 %all-gather.13.cloned.1.call-start = ((), (), s32[]{:S(2)}) async-start(), calls=%async_computation.19 | async-start | bytes 18874368 | tf_op jit(solution)/shard_map/all_gather | solution.py:888
  702.5 7.9 collective-permute-start.24
  704.3 17.9 %collective-permute-start.29 = (bf16[2,512,256]{1,2,0:T(8,128)(2,1)S(1)}, bf16[2,512,256]{1,2,0:T(8,128)(2,1)S(1)}, u32[]{:S(2)}, u32[]{:S(2)}) collective-permute-start(bf16[2,512,256]{1,2,0:T(8,128)(2,1)S(1)} %bitcast.356), channel_id=1, source_target_pairs={{0,3},{1,0},{2,1},{3,2},{4,7},{5,4},{6,5},{7,6},{8,11},{9,8},{10,9... | collective-permute-start | bytes 1572872 | tf_op jit(solution)/shard_map/ppermute | solution.py:506
  706.8 45.6 %collective-permute-start.28 = (bf16[2,512,256]{1,2,0:T(8,128)(2,1)S(1)}, bf16[2,512,256]{1,2,0:T(8,128)(2,1)S(1)}, u32[]{:S(2)}, u32[]{:S(2)}) collective-permute-start(bf16[2,512,256]{1,2,0:T(8,128)(2,1)S(1)} %bitcast.354), channel_id=1, source_target_pairs={{0,2},{1,3},{2,0},{3,1},{4,6},{5,7},{6,4},{7,5},{8,10},{9,11},{10,... | collective-permute-start | bytes 1572872 | tf_op jit(solution)/shard_map/ppermute | solution.py:506
  706.8 45.6 %collective-permute-start.27 = (bf16[2,512,256]{1,2,0:T(8,128)(2,1)S(1)}, bf16[2,512,256]{1,2,0:T(8,128)(2,1)S(1)}, u32[]{:S(2)}, u32[]{:S(2)}) collective-permute-start(bf16[2,512,256]{1,2,0:T(8,128)(2,1)S(1)} %bitcast.353), channel_id=1, source_target_pairs={{0,1},{1,2},{2,3},{3,0},{4,5},{5,6},{6,7},{7,4},{8,9},{9,10},{10,1... | collective-permute-start | bytes 1572872 | tf_op jit(solution)/shard_map/ppermute | solution.py:506
  716.3 37.7 %collective-permute-start.25 = (bf16[32,8704]{1,0:T(8,128)(2,1)}, bf16[32,8704]{1,0:T(8,128)(2,1)}, u32[]{:S(2)}, u32[]{:S(2)}) collective-permute-start(bf16[32,8704]{1,0:T(8,128)(2,1)} %get-tuple-element.335), channel_id=1, source_target_pairs={{0,4},{4,0},{8,12},{12,8},{1,5},{5,1},{9,13},{13,9},{2,6},{6,2},{1... | collective-permute-start | bytes 1671176 | tf_op jit(solution)/shard_map/ppermute | solution.py:97
  717.9 36.1 %collective-permute-start.26 = (bf16[32,8704]{1,0:T(8,128)(2,1)}, bf16[32,8704]{1,0:T(8,128)(2,1)}, u32[]{:S(2)}, u32[]{:S(2)}) collective-permute-start(bf16[32,8704]{1,0:T(8,128)(2,1)} %get-tuple-element.334), channel_id=1, source_target_pairs={{0,8},{4,12},{8,0},{12,4},{1,9},{5,13},{9,1},{13,5},{2,10},{6,14},... | collective-permute-start | bytes 1671176 | tf_op jit(solution)/shard_map/ppermute | solution.py:97
  764.7 53.1 %all-to-all-start.9 = ((bf16[4,128,2048]{2,1,0:T(8,128)(2,1)}), bf16[4,128,2048]{2,1,0:T(8,128)(2,1)}, u32[]{:S(2)}, u32[]{:S(2)}) async-start(bf16[4,128,2048]{2,1,0:T(8,128)(2,1)} %bitcast.328), calls=%async_computation.11 | async-start | bytes 4194304 | tf_op jit(solution)/shard_map/all_to_all | solution.py:79
  773.0 47.0 %collective-permute-start.30 = (bf16[64,8704]{1,0:T(8,128)(2,1)}, bf16[64,8704]{1,0:T(8,128)(2,1)}, u32[]{:S(2)}, u32[]{:S(2)}) collective-permute-start(bf16[64,8704]{1,0:T(8,128)(2,1)} %pad_maximum_fusion.3), channel_id=1, source_target_pairs={{0,4},{4,0},{8,12},{12,8},{1,5},{5,1},{9,13},{13,9},{2,6},{6,2},{1... | collective-permute-start | bytes 3342344 | tf_op jit(solution)/shard_map/ppermute | solution.py:97
  776.6 43.4 %collective-permute-start.31 = (bf16[64,8704]{1,0:T(8,128)(2,1)}, bf16[64,8704]{1,0:T(8,128)(2,1)S(1)}, u32[]{:S(2)}, u32[]{:S(2)}) collective-permute-start(bf16[64,8704]{1,0:T(8,128)(2,1)} %pad_maximum_fusion.4), channel_id=1, source_target_pairs={{0,8},{4,12},{8,0},{12,4},{1,9},{5,13},{9,1},{13,5},{2,10},{6,14},... | collective-permute-start | bytes 3342344 | tf_op jit(solution)/shard_map/ppermute | solution.py:97
  823.5 20.7 %collective-permute-start.34 = (bf16[64,1664]{1,0:T(8,128)(2,1)}, bf16[64,1664]{1,0:T(8,128)(2,1)}, u32[]{:S(2)}, u32[]{:S(2)}) collective-permute-start(bf16[64,1664]{1,0:T(8,128)(2,1)} %get-tuple-element.331), channel_id=1, source_target_pairs={{0,3},{1,0},{2,1},{3,2},{4,7},{5,4},{6,5},{7,6},{8,11},{9,8},{10,9... | collective-permute-start | bytes 638984 | tf_op jit(solution)/shard_map/ppermute | solution.py:506
  824.9 19.2 %collective-permute-start.33 = (bf16[64,1664]{1,0:T(8,128)(2,1)}, bf16[64,1664]{1,0:T(8,128)(2,1)}, u32[]{:S(2)}, u32[]{:S(2)}) collective-permute-start(bf16[64,1664]{1,0:T(8,128)(2,1)} %get-tuple-element.332), channel_id=1, source_target_pairs={{0,2},{1,3},{2,0},{3,1},{4,6},{5,7},{6,4},{7,5},{8,10},{9,11},{10,... | collective-permute-start | bytes 638984 | tf_op jit(solution)/shard_map/ppermute | solution.py:506
  825.0 19.2 %collective-permute-start.32 = (bf16[64,1664]{1,0:T(8,128)(2,1)}, bf16[64,1664]{1,0:T(8,128)(2,1)}, u32[]{:S(2)}, u32[]{:S(2)}) collective-permute-start(bf16[64,1664]{1,0:T(8,128)(2,1)} %get-tuple-element.333), channel_id=1, source_target_pairs={{0,1},{1,2},{2,3},{3,0},{4,5},{5,6},{6,7},{7,4},{8,9},{9,10},{10,1... | collective-permute-start | bytes 638984 | tf_op jit(solution)/shard_map/ppermute | solution.py:506
  827.7 15.8 %all-to-all-start.10 = ((f32[4,8,512]{2,1,0:T(8,128)}), f32[4,8,512]{2,1,0:T(8,128)S(1)}, u32[]{:S(2)}, u32[]{:S(2)}) async-start(f32[4,8,512]{2,1,0:T(8,128)} %bitcast.120), calls=%async_computation.12 | async-start | bytes 131072 | tf_op jit(solution)/shard_map/all_to_all | solution.py:79
  854.7 23.9 %collective-permute-start.35 = (bf16[64,5760]{1,0:T(8,128)(2,1)}, bf16[64,5760]{1,0:T(8,128)(2,1)}, u32[]{:S(2)}, u32[]{:S(2)}) collective-permute-start(bf16[64,5760]{1,0:T(8,128)(2,1)} %concatenate.149), channel_id=1, source_target_pairs={{0,4},{4,0},{8,12},{12,8},{1,5},{5,1},{9,13},{13,9},{2,6},{6,2},{1... | collective-permute-start | bytes 2211848 | tf_op jit(solution)/shard_map/ppermute | solution.py:97
  856.1 22.5 %collective-permute-start.36 = (bf16[64,5760]{1,0:T(8,128)(2,1)}, bf16[64,5760]{1,0:T(8,128)(2,1)}, u32[]{:S(2)}, u32[]{:S(2)}) collective-permute-start(bf16[64,5760]{1,0:T(8,128)(2,1)} %concatenate.149), channel_id=1, source_target_pairs={{0,8},{4,12},{8,0},{12,4},{1,9},{5,13},{9,1},{13,5},{2,10},{6,14},... | collective-permute-start | bytes 2211848 | tf_op jit(solution)/shard_map/ppermute | solution.py:97
  858.6 19.8 %all-to-all-start.11 = ((f32[8,8,512]{2,1,0:T(8,128)}), f32[8,8,512]{2,1,0:T(8,128)S(1)}, u32[]{:S(2)}, u32[]{:S(2)}) async-start(f32[8,8,512]{2,1,0:T(8,128)} %reshape.712), calls=%async_computation.13 | async-start | bytes 262144 | tf_op jit(solution)/shard_map/all_to_all | solution.py:79
  879.5 10.7 %collective-permute-start.38 = (bf16[32,5760]{1,0:T(8,128)(2,1)S(1)}, bf16[32,5760]{1,0:T(8,128)(2,1)S(1)}, u32[]{:S(2)}, u32[]{:S(2)}) collective-permute-start(bf16[32,5760]{1,0:T(8,128)(2,1)S(1)} %slice.268), channel_id=1, source_target_pairs={{0,4},{4,0},{8,12},{12,8},{1,5},{5,1},{9,13},{13,9},{2,6},{6,2},{1... | collective-permute-start | bytes 1105928 | tf_op jit(solution)/shard_map/ppermute | solution.py:97
  881.7 10.4 %collective-permute-start.37 = (bf16[32,5760]{1,0:T(8,128)(2,1)S(1)}, bf16[32,5760]{1,0:T(8,128)(2,1)S(1)}, u32[]{:S(2)}, u32[]{:S(2)}) collective-permute-start(bf16[32,5760]{1,0:T(8,128)(2,1)S(1)} %slice.267), channel_id=1, source_target_pairs={{0,8},{4,12},{8,0},{12,4},{1,9},{5,13},{9,1},{13,5},{2,10},{6,14},... | collective-permute-start | bytes 1105928 | tf_op jit(solution)/shard_map/ppermute | solution.py:97
  (111 other events, 1056.2 us)
Sparse Core Ops, SparseCore 0:
  52.3 47.1 all-gather.10
  184.4 110.5 all-gather.6
  465.8 75.9 reduce-scatter.2
  554.4 131.0 reduce-scatter.4
  687.4 65.3 all-gather.8
  758.3 107.7 all-gather.12

commit v5 on v4

--- a/solution.py
+++ b/solution.py
@@ -211,15 +211,19 @@
     return 0.5 * value * (1.0 + inner), slope
 
 
-def ff_forward_kernel(piece, count, x_ref, pair_ref, down_ref, both_ref, hidden_ref, out_ref):
+def ff_forward_kernel(piece, many, count, x_ref, pair_ref, down_ref, both_ref, hidden_ref, out_ref):
     step = pl.program_id(0)
 
     @pl.when(step < count)
     def _():
         both = contract_last(x_ref[...], pair_ref[...])
         both_ref[...] = both
-        hidden = (gelu_tanh(both[:, :piece]) * both[:, piece:]).astype(LOW)
-        hidden_ref[:, pl.ds(pl.multiple_of(step * piece, piece), piece)] = hidden
+        for part in range(many):
+            begin = 2 * part * piece
+            gate = both[:, begin : begin + piece]
+            upward = both[:, begin + piece : begin + 2 * piece]
+            start = pl.multiple_of((step * many + part) * piece, piece)
+            hidden_ref[:, pl.ds(start, piece)] = (gelu_tanh(gate) * upward).astype(LOW)
 
     @pl.when(step >= count)
     def _():
@@ -231,8 +235,9 @@
 def ff_forward(x, pair, down, piece):
     rows, width = x.shape
     hidden = down.shape[0]
-    count = hidden // piece
-    cut = math.gcd(width, 512)
+    many = math.gcd(hidden // piece, 2)
+    count = hidden // piece // many
+    cut = math.gcd(width, 1024)
 
     def now(i):
         return jnp.minimum(i, count - 1)
@@ -241,15 +246,15 @@
         return jnp.maximum(i - count, 0)
 
     return pl.pallas_call(
-        functools.partial(ff_forward_kernel, piece, count),
+        functools.partial(ff_forward_kernel, piece, many, count),
         grid=(count + width // cut,),
         in_specs=[
             pl.BlockSpec((rows, width), lambda i: (0, 0)),
-            pl.BlockSpec((2 * piece, width), lambda i: (now(i), 0)),
+            pl.BlockSpec((2 * many * piece, width), lambda i: (now(i), 0)),
             pl.BlockSpec((hidden, cut), lambda i: (0, then(i))),
         ],
         out_specs=[
-            pl.BlockSpec((rows, 2 * piece), lambda i: (0, now(i))),
+            pl.BlockSpec((rows, 2 * many * piece), lambda i: (0, now(i))),
             pl.BlockSpec((rows, hidden), lambda i: (0, 0)),
             pl.BlockSpec((rows, cut), lambda i: (0, then(i))),
         ],
@@ -266,17 +271,23 @@
     )(x, pair, down)
 
 
-def ff_backward_kernel(piece, count, grad_ref, down_ref, both_ref, pair_ref, grad_both_ref, out_ref):
+def ff_backward_kernel(
+    piece, many, count, grad_ref, down_ref, both_ref, pair_ref, grad_both_ref, out_ref
+):
     step = pl.program_id(0)
 
     @pl.when(step < count)
     def _():
         grad_hidden = contract_last(grad_ref[...], down_ref[...])
-        value, slope = gelu_and_slope(both_ref[:, :piece])
-        start = pl.multiple_of(step * 2 * piece, piece)
-        grad_both_ref[:, pl.ds(start, piece)] = (grad_hidden * both_ref[:, piece:] * slope).astype(LOW)
-        start = pl.multiple_of(step * 2 * piece + piece, piece)
-        grad_both_ref[:, pl.ds(start, piece)] = (grad_hidden * value).astype(LOW)
+        for part in range(many):
+            grad = grad_hidden[:, part * piece : (part + 1) * piece]
+            begin = 2 * part * piece
+            value, slope = gelu_and_slope(both_ref[:, begin : begin + piece])
+            upward = both_ref[:, begin + piece : begin + 2 * piece]
+            start = pl.multiple_of((step * many + part) * 2 * piece, piece)
+            grad_both_ref[:, pl.ds(start, piece)] = (grad * upward * slope).astype(LOW)
+            start = pl.multiple_of((step * many + part) * 2 * piece + piece, piece)
+            grad_both_ref[:, pl.ds(start, piece)] = (grad * value).astype(LOW)
 
     @pl.when(step >= count)
     def _():
@@ -288,7 +299,8 @@
 def ff_backward(grad, pair, down, both, piece):
     rows, width = grad.shape
     hidden = down.shape[0]
-    count = hidden // piece
+    many = math.gcd(hidden // piece, 2)
+    count = hidden // piece // many
     cut = math.gcd(width, 512)
 
     def now(i):
@@ -298,12 +310,12 @@
         return jnp.maximum(i - count, 0)
 
     return pl.pallas_call(
-        functools.partial(ff_backward_kernel, piece, count),
+        functools.partial(ff_backward_kernel, piece, many, count),
         grid=(count + width // cut,),
         in_specs=[
             pl.BlockSpec((rows, width), lambda i: (0, 0)),
-            pl.BlockSpec((piece, width), lambda i: (now(i), 0)),
-            pl.BlockSpec((rows, 2 * piece), lambda i: (0, now(i))),
+            pl.BlockSpec((many * piece, width), lambda i: (now(i), 0)),
+            pl.BlockSpec((rows, 2 * many * piece), lambda i: (0, now(i))),
             pl.BlockSpec((2 * hidden, cut), lambda i: (0, then(i))),
         ],
         out_specs=[
@@ -506,6 +518,57 @@
             block = lax.ppermute(block, "wsh", [(i, (i + k) % run) for i in range(run)])
         received.append(block)
     return received
+
+
+def head_piece_kernel(run, query_width, places, *refs):
+    sources, (own_ref, out_ref, total) = refs[:run], refs[run:]
+    kv_width = KV_HEADS * HEAD_DIM
+    query_all = run * query_width
+    head_width = query_width + 2 * HEAD_DIM
+    total[...] = jnp.zeros_like(total)
+    rest = jnp.zeros((out_ref.shape[0], sources[0].shape[1] - head_width), WIDE)
+    for k, source in enumerate(sources):
+        place = places[k]
+        out_ref[:, pl.ds(pl.multiple_of(place * query_width, query_width), query_width)] = source[
+            :, :query_width
+        ]
+        head = place * KV_HEADS // run
+        for number in range(2):
+            begin = query_width + number * HEAD_DIM
+            at = pl.multiple_of(head * HEAD_DIM + number * kv_width, HEAD_DIM)
+            total[:, pl.ds(at, HEAD_DIM)] += source[:, begin : begin + HEAD_DIM].astype(WIDE)
+        rest += source[:, head_width:].astype(WIDE)
+    begin = query_all + 2 * kv_width
+    out_ref[:, query_all:begin] = total[...].astype(LOW)
+    out_ref[:, begin : begin + rest.shape[1]] = rest.astype(LOW)
+    out_ref[:, begin + rest.shape[1] :] = own_ref[:, run * sources[0].shape[1] :]
+
+
+def head_piece_sum(sources, own, places, query_width):
+    run = len(sources)
+    rows, columns = sources[0].shape
+    kv_width = KV_HEADS * HEAD_DIM
+    rest = columns - query_width - 2 * HEAD_DIM
+    width = run * query_width + 2 * kv_width + rest + own.shape[1] - run * columns
+
+    def whole(i, p):
+        return (0, 0)
+
+    return pl.pallas_call(
+        functools.partial(head_piece_kernel, run, query_width),
+        grid_spec=pltpu.PrefetchScalarGridSpec(
+            num_scalar_prefetch=1,
+            grid=(1,),
+            in_specs=[pl.BlockSpec((rows, columns), whole)] * run
+            + [pl.BlockSpec(own.shape, whole)],
+            out_specs=pl.BlockSpec((rows, width), whole),
+            scratch_shapes=[pltpu.VMEM((rows, 2 * kv_width), WIDE)],
+        ),
+        out_shape=jax.ShapeDtypeStruct((rows, width), LOW),
+        cost_estimate=pl.CostEstimate(
+            flops=0, bytes_accessed=2 * (own.size + 2 * rows * width), transcendentals=0
+        ),
+    )(places, *sources, own)
 
 
 def shift_exchange(make):
@@ -889,16 +952,16 @@
     table_grad = EMBED_SCALE * over_rows(one_hot(), after(every_grad, normed_part))
     heads_second = reduce_second(heads_pieces, heads_first)
     grad_run = collect(normed_part, "wsh")
-    grad_run, heads_second, table_grad = lax.optimization_barrier(
-        (grad_run, heads_second, table_grad)
+    down_grad = after(down_grad, table_grad).astype(WIDE)
+    grad_run, heads_second, table_grad, down_grad = lax.optimization_barrier(
+        (grad_run, heads_second, table_grad, down_grad)
     )
     heads_own = reduce_last(heads_pieces, heads_second)
-    output_own = heads_own[:, run * fetch_back :]
 
     def head_back(index):
         return lax.dynamic_slice_in_dim(heads_own, index * fetch_back, fetch_back, 1)
 
-    heads_sent = shift_exchange(head_back).astype(WIDE)
+    heads_sent = shift_blocks(head_back)
     grad_normed = (
         grad_run
         + times_transposed(grad_rank_low, left_full)
@@ -926,22 +989,21 @@
     )
     gain_sums = gain_sums.reshape(8, run, shard_rows).transpose(1, 0, 2).reshape(8 * run, shard_rows)
     gain_sums = collect(gain_sums, "wsh")
-    pieces = [heads_sent[:, :, :query_width].transpose(1, 0, 2).reshape(head_piece, -1)]
-    for begin in (query_width, query_width + HEAD_DIM):
-        one = heads_sent[:, :, begin : begin + HEAD_DIM]
-        one = one.reshape(KV_HEADS, run // KV_HEADS, head_piece, HEAD_DIM).sum(axis=1)
-        pieces.append(one.transpose(1, 0, 2).reshape(head_piece, -1))
-    begin = head_width
-    for size in (rank, rank, w_layer_gate.shape[1]):
-        pieces.append(heads_sent[:, :, begin : begin + size].sum(axis=0))
-        begin += size
-    pieces.append(heads_sent[:, :, head_width + narrow_columns :].sum(axis=0))
-    pieces.append(output_own.astype(WIDE))
+    heads_piece = head_piece_sum(heads_sent, heads_own, places, query_width)
+    kv_width = KV_HEADS * HEAD_DIM
     cuts = []
-    for one in pieces:
-        cuts.append((sum(w for _, w in cuts), one.shape[1]))
-    heads_piece = jnp.concatenate(pieces, axis=1).astype(LOW)
-    heads_piece, gain_sums = lax.optimization_barrier((heads_piece, gain_sums))
+    for size in (
+        HEADS * HEAD_DIM,
+        kv_width,
+        kv_width,
+        rank,
+        rank,
+        w_layer_gate.shape[1],
+        narrow.shape[3] - narrow_columns,
+        width,
+    ):
+        cuts.append((sum(w for _, w in cuts), size))
+    heads_piece, gain_sums = after((heads_piece, gain_sums), pair_all)
     heads_near = gather_first(heads_piece)
     gain_sums = jnp.sum(spread(gain_sums[None], COPIES), axis=0)
     own = jnp.full((1,), chip, jnp.int32)
@@ -951,10 +1013,11 @@
         pair_all = jnp.take(pair_all, places, axis=1)
         pair_all = pair_all.transpose(2, 3, 1, 0, 4).reshape(2, shard_rows, -1).astype(WIDE)
         gate_grad, up_grad = pair_all[0], pair_all[1]
-    down_grad = after(down_grad, heads_piece).astype(WIDE)
-    heads_near, down_grad, gain_sums = lax.optimization_barrier((heads_near, down_grad, gain_sums))
+
+    heads_near, gain_sums, gate_grad, up_grad = lax.optimization_barrier(
+        (heads_near, gain_sums, gate_grad, up_grad)
+    )
     heads_near = gather_second(heads_piece, heads_near)
-    heads_near, gate_grad, up_grad = lax.optimization_barrier((heads_near, gate_grad, up_grad))
     heads_all = last_gather(heads_near)
     (
         query_grad,

time: 958 us -> 948 us (0.990)
  blocking collectives: 50.3 us -> 66.9 us
  waiting for transfers between devices: 374 us -> 358 us
    all_to_all x11 -> x10, waiting for transfers between devices: 226 us -> 198 us  [exchange(): return lax.all_to_all(value, axis, 0, 0, tiled=True)]
    all_to_all x1 -> x2, blocking collectives: 50.3 us -> 66.9 us  [exchange(): return lax.all_to_all(value, axis, 0, 0, tiled=True)]
    all_gather x1, waiting for transfers between devices: 0.01 us -> 13.5 us  [shards(): pair_all = lax.all_gather(pair_blocks, COPIES, axis=0)]
    all_to_all x11 -> x10, starting transfers between devices: 58.1 us -> 53.3 us  [exchange(): return lax.all_to_all(value, axis, 0, 0, tiled=True)]
    unnamed x221 -> x237, local copies, waits for them, and re-layouts: 21 us -> 23.6 us
    pallas_call x2 -> x3, Pallas kernels: 51.5 us -> 53.4 us  [the longest x1 28.3 us: ff_backward(): pl.pallas_call(functools.partial(ff_backward_kernel, piece, many, count),...]
  transfers between devices with their start and end apart: 60 -> 59, of which waited for: 27 -> 25; matrix products, arithmetic and copies ran while one was open for 25% -> 23% of each run, Pallas kernels for 5% -> 9%
where the time goes in v5:
time: 948 us; the launch traced here: 935 us
  waiting for transfers between devices  358 us (38%)
  Pallas kernels  115 us (12%)
  starting transfers between devices  101 us (11%)
  matrix products  94.7 us (10%)
  other arithmetic  92.3 us (10%)
  local copies, waits for them, and re-layouts  89.1 us (9%)
  blocking collectives  66.9 us (7%)
  between operations  17.4 us (2%)
    all_to_all x10, waiting for transfers between devices, exchange(): return lax.all_to_all(value, axis, 0, 0, tiled=True)  198 us
    ppermute x21, waiting for transfers between devices, shift_blocks(): block = lax.ppermute(block, 'wsh', [(i, (i + k) % run) for i in range(run)])  75.4 us
    all_to_all x2, blocking collectives, exchange(): return lax.all_to_all(value, axis, 0, 0, tiled=True)  66.9 us
    dot_general x9, matrix products, over_rows(): lax.dot_general(left, right, (((0,), (0,)), ((), ())), preferred_element_...  56 us
    ppermute x22, waiting for transfers between devices, swap(): return lax.ppermute(value, axis, [(i, i ^ bit) for i in range(size)])  53.5 us
    all_to_all x10, starting transfers between devices, exchange(): return lax.all_to_all(value, axis, 0, 0, tiled=True)  53.3 us
    pallas_call x1, Pallas kernels, ff_backward(): pl.pallas_call(functools.partial(ff_backward_kernel, piece, many, count),...  28.3 us
    ppermute x21, starting transfers between devices, shift_blocks(): block = lax.ppermute(block, 'wsh', [(i, (i + k) % run) for i in range(run)])  26.4 us
  transfers between devices with their start and end apart: 59, of which 25 were waited for; matrix products, arithmetic and copies ran while one was open for 23% of the time, Pallas kernels for 9%

profile of v5, /device:TPU:0, one launch (start us, length us, event | category | flops | bytes accessed | tf_op | source)
XLA Modules:
  0.0 935.0 jit_solution(6451983238039965545)
XLA Ops:
  8.1 5.0 collective-permute-start.2
  24.6 5.6 collective-permute-done.8
  30.3 16.6 %collective-permute-done.7 = bf16[80,1664]{1,0:T(8,128)(2,1)S(1)} collective-permute-done((bf16[80,1664]{1,0:T(8,128)(2,1)S(1)}, bf16[80,1664]{1,0:T(8,128)(2,1)S(1)}, u32[]{:S(2)}, u32[]{:S(2)}) %collective-permute-start.7) | collective-permute-done | bytes 266272 | tf_op jit(solution)/shard_map/ppermute | solution.py:518
  53.7 4.5 all-to-all-start
  69.9 14.7 %fusion.5 = bf16[4096,256]{1,0:T(8,128)(2,1)} fusion(bf16[4096,256]{1,0:T(8,128)(2,1)} %param.27, s32[4096]{0:T(1024)S(1)} %add_subtract_fusion), kind=kOutput, calls=%fused_computation.15 | convolution fusion | flops 8607760384 | bytes 4210688 | tf_op jit(solution)/shard_map/dot_general | solution.py:53
  86.5 18.8 %all-to-all-done = bf16[4,128,2048]{2,1,0:T(8,128)(2,1)} async-done(((bf16[4,128,2048]{2,1,0:T(8,128)(2,1)}), bf16[4,128,2048]{2,1,0:T(8,128)(2,1)}, u32[]{:S(2)}, u32[]{:S(2)}) %all-to-all-start) | async-done | bytes 2097184 | tf_op jit(solution)/shard_map/all_to_all | solution.py:79
  110.8 5.5 fusion.39.raw_ref
  120.4 4.7 all-to-all-start.1
  150.5 11.2 %shard_map.323 = (bf16[512,512]{1,0:T(8,128)(2,1)}, f32[2,512,2048]{2,1,0:T(8,128)}, f32[512,512]{1,0:T(8,128)}, bf16[512,512]{1,0:T(8,128)(2,1)}) custom-call(f32[512,1024]{1,0:T(8,128)} %copy-done.20, f32[1,256]{1,0:T(1,128)} %reshape.699.gain_ref, f32[512,128]{1,0:T(8,128)} %get-tuple-element.367.cos_ref, f32[512,128]{1,0:T(8,128)} %get-tuple-element.366.sin_ref, ...), custom_call_target="tpu_custom_call" | custom-call | flops 2147483648 | bytes 14155776 | tf_op jit(solution)/shard_map/pallas_call | solution.py:363
  161.7 18.2 %collective-permute-done.10.refs_2_ = bf16[512,512]{1,0:T(8,128)(2,1)} collective-permute-done((bf16[512,512]{1,0:T(8,128)(2,1)}, bf16[512,512]{1,0:T(8,128)(2,1)}, u32[]{:S(2)}, u32[]{:S(2)}) %collective-permute-start.10) | collective-permute-done | bytes 524320 | tf_op jit(solution)/shard_map/ppermute | solution.py:518
  179.8 4.1 shard_map.324
  188.8 13.0 %all-to-all-start.2 = ((bf16[4,128,2048]{2,1,0:T(8,128)(2,1)}), bf16[4,128,2048]{2,1,0:T(8,128)(2,1)}, u32[]{:S(2)}, u32[]{:S(2)}) async-start(bf16[4,128,2048]{2,1,0:T(8,128)(2,1)} %bitcast.306), calls=%async_computation.2 | async-start | bytes 4194304 | tf_op jit(solution)/shard_map/all_to_all | solution.py:79
  205.7 23.9 %collective-permute-done.13 = bf16[1024,256]{1,0:T(8,128)(2,1)S(1)} collective-permute-done((bf16[1024,256]{1,0:T(8,128)(2,1)S(1)}, bf16[1024,256]{1,0:T(8,128)(2,1)S(1)}, u32[]{:S(2)}, u32[]{:S(2)}) %collective-permute-start.13) | collective-permute-done | bytes 524320 | tf_op jit(solution)/shard_map/ppermute | solution.py:97
  231.9 5.5 collective-permute-done.14
  241.9 8.9 all-to-all-done.2
  257.4 4.6 all-to-all-start.3
  262.5 48.1 %all-to-all-done.3 = bf16[4,128,2048]{2,1,0:T(8,128)(2,1)} async-done(((bf16[4,128,2048]{2,1,0:T(8,128)(2,1)}), bf16[4,128,2048]{2,1,0:T(8,128)(2,1)}, u32[]{:S(2)}, u32[]{:S(2)}) %all-to-all-start.3) | async-done | bytes 2097184 | tf_op jit(solution)/shard_map/all_to_all | solution.py:79
  321.7 21.8 %shard_map.325 = (f32[512,4096]{1,0:T(8,128)}, bf16[512,2048]{1,0:T(8,128)(2,1)}, bf16[512,2048]{1,0:T(8,128)(2,1)}) custom-call(bf16[512,2048]{1,0:T(8,128)(2,1)} %bitcast.41.x_ref, bf16[4096,2048]{1,0:T(8,128)(2,1)} %all-gather.7.cloned.1.call-done.pair_ref, bf16[2048,2048]{1,0:T(8,128)(2,1)} %down_ref.3), custom_call_target="tpu_custom_call" | custom-call | flops 12884901888 | bytes 35651584 | tf_op jit(solution)/shard_map/pallas_call | solution.py:248
  343.5 4.6 all-to-all-start.4
  351.4 42.7 %all-to-all-done.4 = bf16[4,128,2048]{2,1,0:T(8,128)(2,1)} async-done(((bf16[4,128,2048]{2,1,0:T(8,128)(2,1)}), bf16[4,128,2048]{2,1,0:T(8,128)(2,1)}, u32[]{:S(2)}, u32[]{:S(2)}) %all-to-all-start.4) | async-done | bytes 2097184 | tf_op jit(solution)/shard_map/all_to_all | solution.py:79
  404.8 50.3 %all_to_all.99 = bf16[4,128,2048]{2,1,0:T(8,128)(2,1)S(1)} all-to-all(bf16[4,128,2048]{2,1,0:T(8,128)(2,1)S(1)} %broadcast_in_dim.192), channel_id=1, replica_groups=mesh['slot'=2,'ctx'=4,'wsh'=4] {'wsh'}, dimensions={0} | all-to-all | bytes 4194304 | tf_op jit(solution)/shard_map/all_to_all | solution.py:79
  456.4 6.8 convolution_convert_fusion.1
  465.8 28.3 %shard_map.326 = (bf16[512,4096]{1,0:T(8,128)(2,1)}, bf16[512,2048]{1,0:T(8,128)(2,1)}) custom-call(bf16[512,2048]{1,0:T(8,128)(2,1)} %bitcast.310, bf16[2048,2048]{1,0:T(8,128)(2,1)} %down_ref.3, f32[512,4096]{1,0:T(8,128)} %get-tuple-element.132.both_ref, bf16[4096,2048]{1,0:T(8,128)(2,1)} %all-gather.7.cloned.1.call-done.pair_ref), custom_call_target="tpu_custom_call" | custom-call | flops 12884901888 | bytes 37748736 | tf_op jit(solution)/shard_map/pallas_call | solution.py:312
  498.8 4.6 all-to-all-start.6
  505.3 15.1 %convolution_convert_fusion = bf16[4096,2048]{1,0:T(8,128)(2,1)} fusion(bf16[512,4096]{1,0:T(8,128)(2,1)} %get-tuple-element.137, bf16[512,2048]{1,0:T(8,128)(2,1)} %bitcast.41.x_ref), kind=kOutput, calls=%fused_computation.10 | convolution fusion | flops 8598323200 | bytes 23068672 | tf_op jit(solution)/shard_map/dot_general | solution.py:63
  522.1 27.2 %all-to-all-done.6 = bf16[4,128,2048]{2,1,0:T(8,128)(2,1)} async-done(((bf16[4,128,2048]{2,1,0:T(8,128)(2,1)}), bf16[4,128,2048]{2,1,0:T(8,128)(2,1)}, u32[]{:S(2)}, u32[]{:S(2)}) %all-to-all-start.6) | async-done | bytes 2097184 | tf_op jit(solution)/shard_map/all_to_all | solution.py:79
  561.8 4.8 all-to-all-start.7
  574.6 6.7 collective-permute-done.22
  583.6 30.8 %all-to-all-done.7 = bf16[4,128,2048]{2,1,0:T(8,128)(2,1)} async-done(((bf16[4,128,2048]{2,1,0:T(8,128)(2,1)}), bf16[4,128,2048]{2,1,0:T(8,128)(2,1)}, u32[]{:S(2)}, u32[]{:S(2)}) %all-to-all-start.7) | async-done | bytes 2097184 | tf_op jit(solution)/shard_map/all_to_all | solution.py:79
  614.4 3.7 convolution_convert_fusion.9.grad_ref
  618.1 12.6 %shard_map.327 = (bf16[512,512]{1,0:T(8,128)(2,1)}, f32[1,256]{1,0:T(1,128)}, bf16[2048,512]{1,0:T(8,128)(2,1)}) custom-call(bf16[512,512]{1,0:T(8,128)(2,1)} %convolution_convert_fusion.9.grad_ref, f32[512,512]{1,0:T(8,128)} %get-tuple-element.143.wide_ref, f32[2,512,2048]{2,1,0:T(8,128)} %get-tuple-element.144.probs_ref, ...), custom_call_target="tpu_custom_call" | custom-call | flops 4294967296 | bytes 16252928 | tf_op jit(solution)/shard_map/pallas_call | solution.py:458
  630.7 4.5 all-to-all-start.8
  640.8 4.4 convolution_convert_fusion.4
  647.8 15.7 %all-to-all-done.8 = bf16[4,512,512]{2,1,0:T(8,128)(2,1)} async-done(((bf16[4,512,512]{2,1,0:T(8,128)(2,1)}), bf16[4,512,512]{2,1,0:T(8,128)(2,1)}, u32[]{:S(2)}, u32[]{:S(2)}) %all-to-all-start.8) | async-done | bytes 2097184 | tf_op jit(solution)/shard_map/all_to_all | solution.py:79
  665.6 18.0 %reduce-scatter.5.cloned.1.call-done = bf16[512,2048]{1,0:T(8,128)(2,1)} async-done(((bf16[4096,2048]{1,0:T(8,128)(2,1)}), bf16[512,2048]{1,0:T(8,128)(2,1)}) %reduce-scatter.5.cloned.1.call-update) | async-done | bytes 2097168 | tf_op jit(solution)/shard_map/reduce_scatter | solution.py:874
  687.4 4.1 convolution_convert_fusion.2
  708.6 4.8 add_convert_fusion.1
  720.2 30.6 %collective-permute-done.28 = bf16[2,512,256]{1,2,0:T(8,128)(2,1)S(1)} collective-permute-done((bf16[2,512,256]{1,2,0:T(8,128)(2,1)S(1)}, bf16[2,512,256]{1,2,0:T(8,128)(2,1)S(1)}, u32[]{:S(2)}, u32[]{:S(2)}) %collective-permute-start.28) | collective-permute-done | bytes 524320 | tf_op jit(solution)/shard_map/ppermute | solution.py:518
  752.4 4.1 copy.129
  763.1 4.7 all-to-all-start.9
  775.9 23.2 %fusion.4 = f32[4096,256]{1,0:T(8,128)} fusion(bf16[4096,256]{1,0:T(8,128)(2,1)S(1)} %copy-done.34, s32[4096]{0:T(1024)S(1)} %copy-done.73), kind=kOutput, calls=%fused_computation.12 | convolution fusion | flops 8607760384 | bytes 6307840 | tf_op jit(solution)/shard_map/dot_general | solution.py:63
  799.2 11.7 %convert_element_type.373 = f32[2048,2048]{1,0:T(8,128)} convert(bf16[2048,2048]{1,0:T(8,128)(2,1)} %all-gather.9.cloned.1.call-done) | non-fusion elementwise | flops 4194304 | bytes 25165824 | tf_op jit(solution)/shard_map/convert_element_type | solution.py:955
  810.8 5.4 all-to-all-done.9
  827.9 16.6 %all_to_all.100 = f32[4,8,512]{2,1,0:T(8,128)S(1)} all-to-all(f32[4,8,512]{2,1,0:T(8,128)S(1)} %bitcast.345), channel_id=1, replica_groups=mesh['slot'=2,'ctx'=4,'wsh'=4] {'wsh'}, dimensions={0} | all-to-all | bytes 131072 | tf_op jit(solution)/shard_map/all_to_all | solution.py:79
  848.5 13.5 %all-gather.13.cloned.1.call-done = bf16[32,2,512,256]{3,2,1,0:T(8,128)(2,1)} async-done(((bf16[4,2,512,256]{3,2,1,0:T(8,128)(2,1)}), bf16[32,2,512,256]{3,2,1,0:T(8,128)(2,1)}) %all-gather.13.cloned.1.call-update) | async-done | bytes 16777232 | tf_op jit(solution)/shard_map/all_gather | solution.py:951
  868.1 25.9 %shard_map.329 = (f32[512,8192]{1,0:T(8,128)}, f32[512,8192]{1,0:T(8,128)}) custom-call(s32[4]{0:T(128)} %and_select_fusion.1.places, bf16[8,4,2,512,256]{4,3,2,1,0:T(8,128)(2,1)} %bitcast.285), custom_call_target="tpu_custom_call" | custom-call | bytes 50331648 | tf_op jit(solution)/shard_map/pallas_call | solution.py:498
  900.4 5.8 collective-permute-done.37
  914.3 8.1 shard_map.330
  (521 shorter events, 243.4 us)
Async XLA Ops:
  7.2 100.2 %all-gather.11.cloned.1.call-start = ((), (), s32[]{:S(2)}) async-start(), calls=%async_computation.18 | async-start | bytes 7667712 | tf_op jit(solution)/shard_map/all_gather | solution.py:700
  8.1 11.6 %collective-permute-start.2 = (s32[2,128]{1,0:T(2,128)S(1)}, s32[2,128]{1,0:T(2,128)S(1)}, u32[]{:S(2)}, u32[]{:S(2)}) collective-permute-start(s32[2,128]{1,0:T(2,128)S(1)} %get-tuple-element.369), channel_id=1, source_target_pairs={{0,3},{1,0},{2,1},{3,2},{4,7},{5,4},{6,5},{7,6},{8,11},{9,8},{10,9... | collective-permute-start | bytes 3080 | tf_op jit(solution)/shard_map/ppermute | solution.py:518
  20.5 9.8 %collective-permute-start.8 = (bf16[80,1664]{1,0:T(8,128)(2,1)S(1)}, bf16[80,1664]{1,0:T(8,128)(2,1)S(1)}, u32[]{:S(2)}, u32[]{:S(2)}) collective-permute-start(bf16[80,1664]{1,0:T(8,128)(2,1)S(1)} %pad_maximum_fusion.14), channel_id=1, source_target_pairs={{0,3},{1,0},{2,1},{3,2},{4,7},{5,4},{6,5},{7,6},{8,11},{9,8},{10,9... | collective-permute-start | bytes 798728 | tf_op jit(solution)/shard_map/ppermute | solution.py:518
  23.4 23.4 %collective-permute-start.7 = (bf16[80,1664]{1,0:T(8,128)(2,1)S(1)}, bf16[80,1664]{1,0:T(8,128)(2,1)S(1)}, u32[]{:S(2)}, u32[]{:S(2)}) collective-permute-start(bf16[80,1664]{1,0:T(8,128)(2,1)S(1)} %get-tuple-element.343), channel_id=1, source_target_pairs={{0,2},{1,3},{2,0},{3,1},{4,6},{5,7},{6,4},{7,5},{8,10},{9,11},{10,... | collective-permute-start | bytes 798728 | tf_op jit(solution)/shard_map/ppermute | solution.py:518
  24.6 22.3 %collective-permute-start.6 = (bf16[80,1664]{1,0:T(8,128)(2,1)S(1)}, bf16[80,1664]{1,0:T(8,128)(2,1)S(1)}, u32[]{:S(2)}, u32[]{:S(2)}) collective-permute-start(bf16[80,1664]{1,0:T(8,128)(2,1)S(1)} %get-tuple-element.342), channel_id=1, source_target_pairs={{0,1},{1,2},{2,3},{3,0},{4,5},{5,6},{6,7},{7,4},{8,9},{9,10},{10,1... | collective-permute-start | bytes 798728 | tf_op jit(solution)/shard_map/ppermute | solution.py:518
  53.7 51.6 %all-to-all-start = ((bf16[4,128,2048]{2,1,0:T(8,128)(2,1)}), bf16[4,128,2048]{2,1,0:T(8,128)(2,1)}, u32[]{:S(2)}, u32[]{:S(2)}) async-start(bf16[4,128,2048]{2,1,0:T(8,128)(2,1)} %broadcast_in_dim.95), calls=%async_computation | async-start | bytes 4194304 | tf_op jit(solution)/shard_map/all_to_all | solution.py:79
  120.4 30.1 %all-to-all-start.1 = ((bf16[4,512,512]{2,1,0:T(8,128)(2,1)}), bf16[4,512,512]{2,1,0:T(8,128)(2,1)}, u32[]{:S(2)}, u32[]{:S(2)}) async-start(bf16[4,512,512]{2,1,0:T(8,128)(2,1)} %broadcast_in_dim.105), calls=%async_computation.1 | async-start | bytes 4194304 | tf_op jit(solution)/shard_map/all_to_all | solution.py:79
  125.1 196.6 %all-gather.7.cloned.1.call-start = ((), (), s32[]{:S(2)}) async-start(), calls=%async_computation.14 | async-start | bytes 18874368 | tf_op jit(solution)/shard_map/all_gather | solution.py:791
  141.9 19.8 %collective-permute-start.9 = (bf16[512,512]{1,0:T(8,128)(2,1)}, bf16[512,512]{1,0:T(8,128)(2,1)}, u32[]{:S(2)}, u32[]{:S(2)}) collective-permute-start(bf16[512,512]{1,0:T(8,128)(2,1)} %pad_maximum_fusion.10), channel_id=1, source_target_pairs={{0,1},{1,2},{2,3},{3,0},{4,5},{5,6},{6,7},{7,4},{8,9},{9,10},{10,1... | collective-permute-start | bytes 1572872 | tf_op jit(solution)/shard_map/ppermute | solution.py:518
  143.7 36.1 %collective-permute-start.10 = (bf16[512,512]{1,0:T(8,128)(2,1)}, bf16[512,512]{1,0:T(8,128)(2,1)}, u32[]{:S(2)}, u32[]{:S(2)}) collective-permute-start(bf16[512,512]{1,0:T(8,128)(2,1)} %pad_maximum_fusion.11), channel_id=1, source_target_pairs={{0,2},{1,3},{2,0},{3,1},{4,6},{5,7},{6,4},{7,5},{8,10},{9,11},{10,... | collective-permute-start | bytes 1572872 | tf_op jit(solution)/shard_map/ppermute | solution.py:518
  146.3 33.6 %collective-permute-start.11 = (bf16[512,512]{1,0:T(8,128)(2,1)}, bf16[512,512]{1,0:T(8,128)(2,1)}, u32[]{:S(2)}, u32[]{:S(2)}) collective-permute-start(bf16[512,512]{1,0:T(8,128)(2,1)} %pad_maximum_fusion.12), channel_id=1, source_target_pairs={{0,3},{1,0},{2,1},{3,2},{4,7},{5,4},{6,5},{7,6},{8,11},{9,8},{10,9... | collective-permute-start | bytes 1572872 | tf_op jit(solution)/shard_map/ppermute | solution.py:518
  186.2 15.6 %collective-permute-start.12 = (bf16[2048,256]{1,0:T(8,128)(2,1)}, bf16[2048,256]{1,0:T(8,128)(2,1)}, u32[]{:S(2)}, u32[]{:S(2)}) collective-permute-start(bf16[2048,256]{1,0:T(8,128)(2,1)} %slice.199), channel_id=1, source_target_pairs={{0,16},{16,0},{1,17},{17,1},{2,18},{18,2},{3,19},{19,3},{4,20},{20... | collective-permute-start | bytes 3145736 | tf_op jit(solution)/shard_map/ppermute | solution.py:97
  188.8 61.9 %all-to-all-start.2 = ((bf16[4,128,2048]{2,1,0:T(8,128)(2,1)}), bf16[4,128,2048]{2,1,0:T(8,128)(2,1)}, u32[]{:S(2)}, u32[]{:S(2)}) async-start(bf16[4,128,2048]{2,1,0:T(8,128)(2,1)} %bitcast.306), calls=%async_computation.2 | async-start | bytes 4194304 | tf_op jit(solution)/shard_map/all_to_all | solution.py:79
  204.0 25.7 %collective-permute-start.13 = (bf16[1024,256]{1,0:T(8,128)(2,1)S(1)}, bf16[1024,256]{1,0:T(8,128)(2,1)S(1)}, u32[]{:S(2)}, u32[]{:S(2)}) collective-permute-start(bf16[1024,256]{1,0:T(8,128)(2,1)S(1)} %slice.264), channel_id=1, source_target_pairs={{0,8},{4,12},{8,0},{12,4},{1,9},{5,13},{9,1},{13,5},{2,10},{6,14},... | collective-permute-start | bytes 1572872 | tf_op jit(solution)/shard_map/ppermute | solution.py:97
  257.4 53.2 %all-to-all-start.3 = ((bf16[4,128,2048]{2,1,0:T(8,128)(2,1)}), bf16[4,128,2048]{2,1,0:T(8,128)(2,1)}, u32[]{:S(2)}, u32[]{:S(2)}) async-start(bf16[4,128,2048]{2,1,0:T(8,128)(2,1)} %broadcast_in_dim.106), calls=%async_computation.3 | async-start | bytes 4194304 | tf_op jit(solution)/shard_map/all_to_all | solution.py:79
  343.5 50.7 %all-to-all-start.4 = ((bf16[4,128,2048]{2,1,0:T(8,128)(2,1)}), bf16[4,128,2048]{2,1,0:T(8,128)(2,1)}, u32[]{:S(2)}, u32[]{:S(2)}) async-start(bf16[4,128,2048]{2,1,0:T(8,128)(2,1)} %bitcast.311), calls=%async_computation.4 | async-start | bytes 4194304 | tf_op jit(solution)/shard_map/all_to_all | solution.py:79
  348.1 266.3 %reduce-scatter.3.cloned.1.call-start = ((), (), s32[]{:S(2)}) async-start(), calls=%async_computation.15 | async-start | bytes 9437184 | tf_op jit(solution)/shard_map/reduce_scatter | solution.py:844
  463.2 30.9 %collective-permute-start.20 = (bf16[128,256]{1,0:T(8,128)(2,1)S(1)}, bf16[128,256]{1,0:T(8,128)(2,1)S(1)}, u32[]{:S(2)}, u32[]{:S(2)}) collective-permute-start(bf16[128,256]{1,0:T(8,128)(2,1)S(1)} %get-tuple-element.134), channel_id=1, source_target_pairs={{0,3},{1,0},{2,1},{3,2},{4,7},{5,4},{6,5},{7,6},{8,11},{9,8},{10,9... | collective-permute-start | bytes 196616 | tf_op jit(solution)/shard_map/ppermute | solution.py:518
  464.7 29.5 %collective-permute-start.19 = (bf16[128,256]{1,0:T(8,128)(2,1)S(1)}, bf16[128,256]{1,0:T(8,128)(2,1)S(1)}, u32[]{:S(2)}, u32[]{:S(2)}) collective-permute-start(bf16[128,256]{1,0:T(8,128)(2,1)S(1)} %get-tuple-element.134), channel_id=1, source_target_pairs={{0,2},{1,3},{2,0},{3,1},{4,6},{5,7},{6,4},{7,5},{8,10},{9,11},{10,... | collective-permute-start | bytes 196616 | tf_op jit(solution)/shard_map/ppermute | solution.py:518
  464.9 29.2 %collective-permute-start.18 = (bf16[128,256]{1,0:T(8,128)(2,1)S(1)}, bf16[128,256]{1,0:T(8,128)(2,1)}, u32[]{:S(2)}, u32[]{:S(2)}) collective-permute-start(bf16[128,256]{1,0:T(8,128)(2,1)S(1)} %get-tuple-element.134), channel_id=1, source_target_pairs={{0,1},{1,2},{2,3},{3,0},{4,5},{5,6},{6,7},{7,4},{8,9},{9,10},{10,1... | collective-permute-start | bytes 196616 | tf_op jit(solution)/shard_map/ppermute | solution.py:518
  498.8 50.5 %all-to-all-start.6 = ((bf16[4,128,2048]{2,1,0:T(8,128)(2,1)}), bf16[4,128,2048]{2,1,0:T(8,128)(2,1)}, u32[]{:S(2)}, u32[]{:S(2)}) async-start(bf16[4,128,2048]{2,1,0:T(8,128)(2,1)} %bitcast.308), calls=%async_computation.6 | async-start | bytes 4194304 | tf_op jit(solution)/shard_map/all_to_all | solution.py:79
  503.5 180.1 %reduce-scatter.5.cloned.1.call-start = ((), (), s32[]{:S(2)}) async-start(), calls=%async_computation.16 | async-start | bytes 18874368 | tf_op jit(solution)/shard_map/reduce_scatter | solution.py:874
  503.5 16.9 %collective-permute-start.21 = (bf16[512,256]{1,0:T(8,128)(2,1)S(1)}, bf16[512,256]{1,0:T(8,128)(2,1)}, u32[]{:S(2)}, u32[]{:S(2)}) collective-permute-start(bf16[512,256]{1,0:T(8,128)(2,1)S(1)} %bitcast.317), channel_id=1, source_target_pairs={{0,4},{4,0},{8,12},{12,8},{1,5},{5,1},{9,13},{13,9},{2,6},{6,2},{1... | collective-permute-start | bytes 786440 | tf_op jit(solution)/shard_map/ppermute | solution.py:97
  561.8 52.6 %all-to-all-start.7 = ((bf16[4,128,2048]{2,1,0:T(8,128)(2,1)}), bf16[4,128,2048]{2,1,0:T(8,128)(2,1)}, u32[]{:S(2)}, u32[]{:S(2)}) async-start(bf16[4,128,2048]{2,1,0:T(8,128)(2,1)} %broadcast_in_dim.194), calls=%async_computation.7 | async-start | bytes 4194304 | tf_op jit(solution)/shard_map/all_to_all | solution.py:79
  568.1 13.2 %collective-permute-start.22 = (bf16[1024,256]{1,0:T(8,128)(2,1)}, bf16[1024,256]{1,0:T(8,128)(2,1)}, u32[]{:S(2)}, u32[]{:S(2)}) collective-permute-start(bf16[1024,256]{1,0:T(8,128)(2,1)} %pad_maximum_fusion.13), channel_id=1, source_target_pairs={{0,8},{4,12},{8,0},{12,4},{1,9},{5,13},{9,1},{13,5},{2,10},{6,14},... | collective-permute-start | bytes 1572872 | tf_op jit(solution)/shard_map/ppermute | solution.py:97
  630.7 32.9 %all-to-all-start.8 = ((bf16[4,512,512]{2,1,0:T(8,128)(2,1)}), bf16[4,512,512]{2,1,0:T(8,128)(2,1)}, u32[]{:S(2)}, u32[]{:S(2)}) async-start(bf16[4,512,512]{2,1,0:T(8,128)(2,1)} %bitcast.307), calls=%async_computation.9 | async-start | bytes 4194304 | tf_op jit(solution)/shard_map/all_to_all | solution.py:79
  635.2 117.2 %all-gather.9.cloned.1.call-start = ((), (), s32[]{:S(2)}) async-start(), calls=%async_computation.17 | async-start | bytes 9437184 | tf_op jit(solution)/shard_map/all_gather | solution.py:886
  635.3 9.9 %collective-permute-start.23 = (bf16[2048,256]{1,0:T(8,128)(2,1)}, bf16[2048,256]{1,0:T(8,128)(2,1)}, u32[]{:S(2)}, u32[]{:S(2)}) collective-permute-start(bf16[2048,256]{1,0:T(8,128)(2,1)} %pad_maximum_fusion.6), channel_id=1, source_target_pairs={{0,16},{16,0},{1,17},{17,1},{2,18},{18,2},{3,19},{19,3},{4,20},{20... | collective-permute-start | bytes 3145736 | tf_op jit(solution)/shard_map/ppermute | solution.py:97
  640.5 221.5 %all-gather.13.cloned.1.call-start = ((), (), s32[]{:S(2)}) async-start(), calls=%async_computation.19 | async-start | bytes 18874368 | tf_op jit(solution)/shard_map/all_gather | solution.py:951
  702.6 17.6 %collective-permute-start.29 = (bf16[2,512,256]{1,2,0:T(8,128)(2,1)S(1)}, bf16[2,512,256]{1,2,0:T(8,128)(2,1)S(1)}, u32[]{:S(2)}, u32[]{:S(2)}) collective-permute-start(bf16[2,512,256]{1,2,0:T(8,128)(2,1)S(1)} %bitcast.336), channel_id=1, source_target_pairs={{0,3},{1,0},{2,1},{3,2},{4,7},{5,4},{6,5},{7,6},{8,11},{9,8},{10,9... | collective-permute-start | bytes 1572872 | tf_op jit(solution)/shard_map/ppermute | solution.py:518
  705.2 45.6 %collective-permute-start.28 = (bf16[2,512,256]{1,2,0:T(8,128)(2,1)S(1)}, bf16[2,512,256]{1,2,0:T(8,128)(2,1)S(1)}, u32[]{:S(2)}, u32[]{:S(2)}) collective-permute-start(bf16[2,512,256]{1,2,0:T(8,128)(2,1)S(1)} %bitcast.334), channel_id=1, source_target_pairs={{0,2},{1,3},{2,0},{3,1},{4,6},{5,7},{6,4},{7,5},{8,10},{9,11},{10,... | collective-permute-start | bytes 1572872 | tf_op jit(solution)/shard_map/ppermute | solution.py:518
  705.2 45.6 %collective-permute-start.27 = (bf16[2,512,256]{1,2,0:T(8,128)(2,1)S(1)}, bf16[2,512,256]{1,2,0:T(8,128)(2,1)S(1)}, u32[]{:S(2)}, u32[]{:S(2)}) collective-permute-start(bf16[2,512,256]{1,2,0:T(8,128)(2,1)S(1)} %bitcast.333), channel_id=1, source_target_pairs={{0,1},{1,2},{2,3},{3,0},{4,5},{5,6},{6,7},{7,4},{8,9},{9,10},{10,1... | collective-permute-start | bytes 1572872 | tf_op jit(solution)/shard_map/ppermute | solution.py:518
  714.5 37.9 %collective-permute-start.25 = (bf16[32,8704]{1,0:T(8,128)(2,1)}, bf16[32,8704]{1,0:T(8,128)(2,1)}, u32[]{:S(2)}, u32[]{:S(2)}) collective-permute-start(bf16[32,8704]{1,0:T(8,128)(2,1)} %get-tuple-element.319), channel_id=1, source_target_pairs={{0,4},{4,0},{8,12},{12,8},{1,5},{5,1},{9,13},{13,9},{2,6},{6,2},{1... | collective-permute-start | bytes 1671176 | tf_op jit(solution)/shard_map/ppermute | solution.py:97
  716.1 36.3 %collective-permute-start.26 = (bf16[32,8704]{1,0:T(8,128)(2,1)}, bf16[32,8704]{1,0:T(8,128)(2,1)}, u32[]{:S(2)}, u32[]{:S(2)}) collective-permute-start(bf16[32,8704]{1,0:T(8,128)(2,1)} %get-tuple-element.318), channel_id=1, source_target_pairs={{0,8},{4,12},{8,0},{12,4},{1,9},{5,13},{9,1},{13,5},{2,10},{6,14},... | collective-permute-start | bytes 1671176 | tf_op jit(solution)/shard_map/ppermute | solution.py:97
  763.1 53.2 %all-to-all-start.9 = ((bf16[4,128,2048]{2,1,0:T(8,128)(2,1)}), bf16[4,128,2048]{2,1,0:T(8,128)(2,1)}, u32[]{:S(2)}, u32[]{:S(2)}) async-start(bf16[4,128,2048]{2,1,0:T(8,128)(2,1)} %bitcast.304), calls=%async_computation.11 | async-start | bytes 4194304 | tf_op jit(solution)/shard_map/all_to_all | solution.py:79
  771.5 46.9 %collective-permute-start.30 = (bf16[64,8704]{1,0:T(8,128)(2,1)}, bf16[64,8704]{1,0:T(8,128)(2,1)}, u32[]{:S(2)}, u32[]{:S(2)}) collective-permute-start(bf16[64,8704]{1,0:T(8,128)(2,1)} %pad_maximum_fusion.3), channel_id=1, source_target_pairs={{0,4},{4,0},{8,12},{12,8},{1,5},{5,1},{9,13},{13,9},{2,6},{6,2},{1... | collective-permute-start | bytes 3342344 | tf_op jit(solution)/shard_map/ppermute | solution.py:97
  775.1 43.3 %collective-permute-start.31 = (bf16[64,8704]{1,0:T(8,128)(2,1)}, bf16[64,8704]{1,0:T(8,128)(2,1)S(1)}, u32[]{:S(2)}, u32[]{:S(2)}) collective-permute-start(bf16[64,8704]{1,0:T(8,128)(2,1)} %pad_maximum_fusion.4), channel_id=1, source_target_pairs={{0,8},{4,12},{8,0},{12,4},{1,9},{5,13},{9,1},{13,5},{2,10},{6,14},... | collective-permute-start | bytes 3342344 | tf_op jit(solution)/shard_map/ppermute | solution.py:97
  822.0 22.5 %collective-permute-start.32 = (bf16[64,1664]{1,0:T(8,128)(2,1)}, bf16[64,1664]{1,0:T(8,128)(2,1)S(1)}, u32[]{:S(2)}, u32[]{:S(2)}) collective-permute-start(bf16[64,1664]{1,0:T(8,128)(2,1)} %get-tuple-element.316), channel_id=1, source_target_pairs={{0,1},{1,2},{2,3},{3,0},{4,5},{5,6},{6,7},{7,4},{8,9},{9,10},{10,1... | collective-permute-start | bytes 638984 | tf_op jit(solution)/shard_map/ppermute | solution.py:518
  822.0 22.5 %collective-permute-start.33 = (bf16[64,1664]{1,0:T(8,128)(2,1)}, bf16[64,1664]{1,0:T(8,128)(2,1)}, u32[]{:S(2)}, u32[]{:S(2)}) collective-permute-start(bf16[64,1664]{1,0:T(8,128)(2,1)} %get-tuple-element.315), channel_id=1, source_target_pairs={{0,2},{1,3},{2,0},{3,1},{4,6},{5,7},{6,4},{7,5},{8,10},{9,11},{10,... | collective-permute-start | bytes 638984 | tf_op jit(solution)/shard_map/ppermute | solution.py:518
  824.0 20.5 %collective-permute-start.34 = (bf16[64,1664]{1,0:T(8,128)(2,1)}, bf16[64,1664]{1,0:T(8,128)(2,1)}, u32[]{:S(2)}, u32[]{:S(2)}) collective-permute-start(bf16[64,1664]{1,0:T(8,128)(2,1)} %get-tuple-element.314), channel_id=1, source_target_pairs={{0,3},{1,0},{2,1},{3,2},{4,7},{5,4},{6,5},{7,6},{8,11},{9,8},{10,9... | collective-permute-start | bytes 638984 | tf_op jit(solution)/shard_map/ppermute | solution.py:518
  862.0 32.1 %collective-permute-start.35 = (bf16[64,5760]{1,0:T(8,128)(2,1)}, bf16[64,5760]{1,0:T(8,128)(2,1)}, u32[]{:S(2)}, u32[]{:S(2)}) collective-permute-start(bf16[64,5760]{1,0:T(8,128)(2,1)} %shard_map.328), channel_id=1, source_target_pairs={{0,4},{4,0},{8,12},{12,8},{1,5},{5,1},{9,13},{13,9},{2,6},{6,2},{1... | collective-permute-start | bytes 2211848 | tf_op jit(solution)/shard_map/ppermute | solution.py:97
  863.5 30.6 %collective-permute-start.36 = (bf16[64,5760]{1,0:T(8,128)(2,1)}, bf16[64,5760]{1,0:T(8,128)(2,1)}, u32[]{:S(2)}, u32[]{:S(2)}) collective-permute-start(bf16[64,5760]{1,0:T(8,128)(2,1)} %shard_map.328), channel_id=1, source_target_pairs={{0,8},{4,12},{8,0},{12,4},{1,9},{5,13},{9,1},{13,5},{2,10},{6,14},... | collective-permute-start | bytes 2211848 | tf_op jit(solution)/shard_map/ppermute | solution.py:97
  864.7 29.3 %all-to-all-start.11 = ((f32[8,8,512]{2,1,0:T(8,128)}), f32[8,8,512]{2,1,0:T(8,128)S(1)}, u32[]{:S(2)}, u32[]{:S(2)}) async-start(f32[8,8,512]{2,1,0:T(8,128)} %reshape.689), calls=%async_computation.13 | async-start | bytes 262144 | tf_op jit(solution)/shard_map/all_to_all | solution.py:79
  895.2 11.0 %collective-permute-start.37 = (bf16[32,5760]{1,0:T(8,128)(2,1)S(1)}, bf16[32,5760]{1,0:T(8,128)(2,1)S(1)}, u32[]{:S(2)}, u32[]{:S(2)}) collective-permute-start(bf16[32,5760]{1,0:T(8,128)(2,1)S(1)} %slice.234), channel_id=1, source_target_pairs={{0,8},{4,12},{8,0},{12,4},{1,9},{5,13},{9,1},{13,5},{2,10},{6,14},... | collective-permute-start | bytes 1105928 | tf_op jit(solution)/shard_map/ppermute | solution.py:97
  897.2 15.3 %collective-permute-start.39 = (bf16[64,5760]{1,0:T(8,128)(2,1)}, bf16[64,5760]{1,0:T(8,128)(2,1)S(1)}, u32[]{:S(2)}, u32[]{:S(2)}) collective-permute-start(bf16[64,5760]{1,0:T(8,128)(2,1)} %shard_map.328), channel_id=1, source_target_pairs={{0,16},{16,0},{1,17},{17,1},{2,18},{18,2},{3,19},{19,3},{4,20},{20... | collective-permute-start | bytes 2211848 | tf_op jit(solution)/shard_map/ppermute | solution.py:97
  897.3 15.2 %collective-permute-start.40 = (bf16[64,5760]{1,0:T(8,128)(2,1)}, bf16[64,5760]{1,0:T(8,128)(2,1)S(1)}, u32[]{:S(2)}, u32[]{:S(2)}) collective-permute-start(bf16[64,5760]{1,0:T(8,128)(2,1)} %collective-permute-done.35), channel_id=1, source_target_pairs={{0,16},{16,0},{1,17},{17,1},{2,18},{18,2},{3,19},{19,3},{4,20},{20... | collective-permute-start | bytes 2211848 | tf_op jit(solution)/shard_map/ppermute | solution.py:97
  898.8 13.7 %collective-permute-start.41 = (bf16[64,5760]{1,0:T(8,128)(2,1)}, bf16[64,5760]{1,0:T(8,128)(2,1)S(1)}, u32[]{:S(2)}, u32[]{:S(2)}) collective-permute-start(bf16[64,5760]{1,0:T(8,128)(2,1)} %collective-permute-done.36), channel_id=1, source_target_pairs={{0,16},{16,0},{1,17},{17,1},{2,18},{18,2},{3,19},{19,3},{4,20},{20... | collective-permute-start | bytes 2211848 | tf_op jit(solution)/shard_map/ppermute | solution.py:97
  899.0 10.9 %collective-permute-start.38 = (bf16[32,5760]{1,0:T(8,128)(2,1)S(1)}, bf16[32,5760]{1,0:T(8,128)(2,1)S(1)}, u32[]{:S(2)}, u32[]{:S(2)}) collective-permute-start(bf16[32,5760]{1,0:T(8,128)(2,1)S(1)} %slice.235), channel_id=1, source_target_pairs={{0,4},{4,0},{8,12},{12,8},{1,5},{5,1},{9,13},{13,9},{2,6},{6,2},{1... | collective-permute-start | bytes 1105928 | tf_op jit(solution)/shard_map/ppermute | solution.py:97
  (117 other events, 1114.4 us)
Sparse Core Ops, SparseCore 0:
  52.2 47.1 all-gather.10
  184.0 110.5 all-gather.6
  463.3 75.9 reduce-scatter.2
  552.5 131.0 reduce-scatter.4
  685.5 65.6 all-gather.8
  756.7 105.3 all-gather.12

commit v6 on v5

--- a/solution.py
+++ b/solution.py
@@ -488,23 +488,22 @@
     )(grad, wide, probs, q_low, projected, gain, cosine, sine, keys_values)
 
 
-def widen_kernel(places, source, gate, up):
-    gate[...] = source[0, 0, 0].astype(WIDE)
-    up[...] = source[0, 0, 1].astype(WIDE)
-
-
-def widen_pair(pieces, places):
+def widen_kernel(places, source, out):
+    out[...] = source[0, 0, 0].astype(WIDE)
+
+
+def widen_one(pieces, places, which):
     parts, run, _, rows, width = pieces.shape
     return pl.pallas_call(
         widen_kernel,
         grid_spec=pltpu.PrefetchScalarGridSpec(
             num_scalar_prefetch=1,
             grid=(run, parts),
-            in_specs=[pl.BlockSpec((1, 1, 2, rows, width), lambda k, r, p: (r, k, 0, 0, 0))],
-            out_specs=[pl.BlockSpec((rows, width), lambda k, r, p: (0, p[k] * parts + r))] * 2,
+            in_specs=[pl.BlockSpec((1, 1, 1, rows, width), lambda k, r, p: (r, k, which, 0, 0))],
+            out_specs=pl.BlockSpec((rows, width), lambda k, r, p: (0, p[k] * parts + r)),
         ),
-        out_shape=[jax.ShapeDtypeStruct((rows, width * parts * run), WIDE)] * 2,
-        cost_estimate=pl.CostEstimate(flops=0, bytes_accessed=6 * pieces.size, transcendentals=0),
+        out_shape=jax.ShapeDtypeStruct((rows, width * parts * run), WIDE),
+        cost_estimate=pl.CostEstimate(flops=0, bytes_accessed=3 * pieces.size, transcendentals=0),
     )(places, pieces)
 
 
@@ -1008,16 +1007,15 @@
     gain_sums = jnp.sum(spread(gain_sums[None], COPIES), axis=0)
     own = jnp.full((1,), chip, jnp.int32)
     if aligned:
-        gate_grad, up_grad = widen_pair(pair_all, places)
+        gate_grad, up_grad = widen_one(pair_all, places, 0), widen_one(pair_all, places, 1)
     else:
         pair_all = jnp.take(pair_all, places, axis=1)
         pair_all = pair_all.transpose(2, 3, 1, 0, 4).reshape(2, shard_rows, -1).astype(WIDE)
         gate_grad, up_grad = pair_all[0], pair_all[1]
 
-    heads_near, gain_sums, gate_grad, up_grad = lax.optimization_barrier(
-        (heads_near, gain_sums, gate_grad, up_grad)
-    )
+    heads_near, gain_sums, gate_grad = lax.optimization_barrier((heads_near, gain_sums, gate_grad))
     heads_near = gather_second(heads_piece, heads_near)
+    heads_near, up_grad = lax.optimization_barrier((heads_near, up_grad))
     heads_all = last_gather(heads_near)
     (
         query_grad,

time: 948 us -> 959 us (1.012)
  Pallas kernels: 115 us -> 131 us
    pallas_call x1 -> x2, Pallas kernels: 25.9 us -> 42.2 us  [widen_one(): pl.pallas_call(widen_kernel, grid_spec=pltpu.PrefetchScalarGridSpec(num_s...]
    unnamed x237 -> x246, local copies, waits for them, and re-layouts: 23.6 us -> 24.6 us
  transfers between devices with their start and end apart: 59 -> 59, of which waited for: 25 -> 26; matrix products, arithmetic and copies ran while one was open for 23% -> 22% of each run, Pallas kernels for 9% -> 10%
where the time goes in v6:
time: 959 us; the launch traced here: 946 us
  waiting for transfers between devices  361 us (38%)
  Pallas kernels  131 us (14%)
  starting transfers between devices  97.7 us (10%)
  matrix products  92.5 us (10%)
  other arithmetic  90.4 us (9%)
  local copies, waits for them, and re-layouts  88.8 us (9%)
  blocking collectives  67.7 us (7%)
  between operations  17.3 us (2%)
    all_to_all x10, waiting for transfers between devices, exchange(): return lax.all_to_all(value, axis, 0, 0, tiled=True)  203 us
    ppermute x21, waiting for transfers between devices, shift_blocks(): block = lax.ppermute(block, 'wsh', [(i, (i + k) % run) for i in range(run)])  78.1 us
    all_to_all x2, blocking collectives, exchange(): return lax.all_to_all(value, axis, 0, 0, tiled=True)  67.7 us
    dot_general x9, matrix products, over_rows(): lax.dot_general(left, right, (((0,), (0,)), ((), ())), preferred_element_...  56.1 us
    all_to_all x10, starting transfers between devices, exchange(): return lax.all_to_all(value, axis, 0, 0, tiled=True)  47.6 us
    ppermute x22, waiting for transfers between devices, swap(): return lax.ppermute(value, axis, [(i, i ^ bit) for i in range(size)])  45.8 us
    pallas_call x2, Pallas kernels, widen_one(): pl.pallas_call(widen_kernel, grid_spec=pltpu.PrefetchScalarGridSpec(num_s...  42.2 us
    ppermute x21, starting transfers between devices, shift_blocks(): block = lax.ppermute(block, 'wsh', [(i, (i + k) % run) for i in range(run)])  29.3 us
  transfers between devices with their start and end apart: 59, of which 26 were waited for; matrix products, arithmetic and copies ran while one was open for 22% of the time, Pallas kernels for 10%

profile of v6, /device:TPU:0, one launch (start us, length us, event | category | flops | bytes accessed | tf_op | source)
XLA Modules:
  0.0 946.4 jit_solution(5720134850157478303)
XLA Ops:
  8.1 4.0 collective-permute-start.1
  26.1 7.3 collective-permute-done.6
  33.5 9.5 %collective-permute-done.7 = bf16[80,1664]{1,0:T(8,128)(2,1)S(1)} collective-permute-done((bf16[80,1664]{1,0:T(8,128)(2,1)S(1)}, bf16[80,1664]{1,0:T(8,128)(2,1)S(1)}, u32[]{:S(2)}, u32[]{:S(2)}) %collective-permute-start.7) | collective-permute-done | bytes 266272 | tf_op jit(solution)/shard_map/ppermute | solution.py:517
  49.8 6.6 all-to-all-start
  67.7 14.7 %fusion.5 = bf16[4096,256]{1,0:T(8,128)(2,1)} fusion(bf16[4096,256]{1,0:T(8,128)(2,1)} %param.27, s32[4096]{0:T(1024)S(1)} %add_subtract_fusion), kind=kOutput, calls=%fused_computation.15 | convolution fusion | flops 8607760384 | bytes 4210688 | tf_op jit(solution)/shard_map/dot_general | solution.py:53
  84.3 19.7 %all-to-all-done = bf16[4,128,2048]{2,1,0:T(8,128)(2,1)} async-done(((bf16[4,128,2048]{2,1,0:T(8,128)(2,1)}), bf16[4,128,2048]{2,1,0:T(8,128)(2,1)}, u32[]{:S(2)}, u32[]{:S(2)}) %all-to-all-start) | async-done | bytes 2097184 | tf_op jit(solution)/shard_map/all_to_all | solution.py:79
  109.4 5.5 fusion.39.raw_ref
  119.0 4.6 all-to-all-start.1
  148.1 11.2 %shard_map.323 = (bf16[512,512]{1,0:T(8,128)(2,1)}, f32[2,512,2048]{2,1,0:T(8,128)}, f32[512,512]{1,0:T(8,128)}, bf16[512,512]{1,0:T(8,128)(2,1)}) custom-call(f32[512,1024]{1,0:T(8,128)} %copy-done.21, f32[1,256]{1,0:T(1,128)} %reshape.699.gain_ref, f32[512,128]{1,0:T(8,128)} %get-tuple-element.371.cos_ref, f32[512,128]{1,0:T(8,128)} %get-tuple-element.370.sin_ref, ...), custom_call_target="tpu_custom_call" | custom-call | flops 2147483648 | bytes 14155776 | tf_op jit(solution)/shard_map/pallas_call | solution.py:363
  159.3 25.8 %collective-permute-done.10.refs_2_ = bf16[512,512]{1,0:T(8,128)(2,1)} collective-permute-done((bf16[512,512]{1,0:T(8,128)(2,1)}, bf16[512,512]{1,0:T(8,128)(2,1)}, u32[]{:S(2)}, u32[]{:S(2)}) %collective-permute-start.10) | collective-permute-done | bytes 524320 | tf_op jit(solution)/shard_map/ppermute | solution.py:517
  185.1 4.1 shard_map.324
  194.1 5.6 all-to-all-start.2
  203.6 23.9 %collective-permute-done.13 = bf16[1024,256]{1,0:T(8,128)(2,1)S(1)} collective-permute-done((bf16[1024,256]{1,0:T(8,128)(2,1)S(1)}, bf16[1024,256]{1,0:T(8,128)(2,1)S(1)}, u32[]{:S(2)}, u32[]{:S(2)}) %collective-permute-start.13) | collective-permute-done | bytes 524320 | tf_op jit(solution)/shard_map/ppermute | solution.py:97
  229.8 5.5 collective-permute-done.14
  239.8 9.8 %all-to-all-done.2 = bf16[4,128,2048]{2,1,0:T(8,128)(2,1)} async-done(((bf16[4,128,2048]{2,1,0:T(8,128)(2,1)}), bf16[4,128,2048]{2,1,0:T(8,128)(2,1)}, u32[]{:S(2)}, u32[]{:S(2)}) %all-to-all-start.2) | async-done | bytes 2097184 | tf_op jit(solution)/shard_map/all_to_all | solution.py:79
  256.1 4.5 all-to-all-start.3
  261.1 48.1 %all-to-all-done.3 = bf16[4,128,2048]{2,1,0:T(8,128)(2,1)} async-done(((bf16[4,128,2048]{2,1,0:T(8,128)(2,1)}), bf16[4,128,2048]{2,1,0:T(8,128)(2,1)}, u32[]{:S(2)}, u32[]{:S(2)}) %all-to-all-start.3) | async-done | bytes 2097184 | tf_op jit(solution)/shard_map/all_to_all | solution.py:79
  320.6 21.8 %shard_map.325 = (f32[512,4096]{1,0:T(8,128)}, bf16[512,2048]{1,0:T(8,128)(2,1)}, bf16[512,2048]{1,0:T(8,128)(2,1)}) custom-call(bf16[512,2048]{1,0:T(8,128)(2,1)} %bitcast.41.x_ref, bf16[4096,2048]{1,0:T(8,128)(2,1)} %all-gather.7.cloned.1.call-done.pair_ref, bf16[2048,2048]{1,0:T(8,128)(2,1)} %down_ref.3), custom_call_target="tpu_custom_call" | custom-call | flops 12884901888 | bytes 35651584 | tf_op jit(solution)/shard_map/pallas_call | solution.py:248
  342.4 4.6 all-to-all-start.4
  350.3 43.2 %all-to-all-done.4 = bf16[4,128,2048]{2,1,0:T(8,128)(2,1)} async-done(((bf16[4,128,2048]{2,1,0:T(8,128)(2,1)}), bf16[4,128,2048]{2,1,0:T(8,128)(2,1)}, u32[]{:S(2)}, u32[]{:S(2)}) %all-to-all-start.4) | async-done | bytes 2097184 | tf_op jit(solution)/shard_map/all_to_all | solution.py:79
  404.2 50.4 %all_to_all.99 = bf16[4,128,2048]{2,1,0:T(8,128)(2,1)S(1)} all-to-all(bf16[4,128,2048]{2,1,0:T(8,128)(2,1)S(1)} %broadcast_in_dim.192), channel_id=1, replica_groups=mesh['slot'=2,'ctx'=4,'wsh'=4] {'wsh'}, dimensions={0} | all-to-all | bytes 4194304 | tf_op jit(solution)/shard_map/all_to_all | solution.py:79
  456.0 6.8 convolution_convert_fusion.1
  465.4 27.8 %shard_map.326 = (bf16[512,4096]{1,0:T(8,128)(2,1)}, bf16[512,2048]{1,0:T(8,128)(2,1)}) custom-call(bf16[512,2048]{1,0:T(8,128)(2,1)} %bitcast.312, bf16[2048,2048]{1,0:T(8,128)(2,1)} %down_ref.3, f32[512,4096]{1,0:T(8,128)} %get-tuple-element.134.both_ref, bf16[4096,2048]{1,0:T(8,128)(2,1)} %all-gather.7.cloned.1.call-done.pair_ref), custom_call_target="tpu_custom_call" | custom-call | flops 12884901888 | bytes 37748736 | tf_op jit(solution)/shard_map/pallas_call | solution.py:312
  498.0 4.6 all-to-all-start.6
  504.3 15.2 %convolution_convert_fusion = bf16[4096,2048]{1,0:T(8,128)(2,1)} fusion(bf16[512,4096]{1,0:T(8,128)(2,1)} %get-tuple-element.139, bf16[512,2048]{1,0:T(8,128)(2,1)} %bitcast.41.x_ref), kind=kOutput, calls=%fused_computation.10 | convolution fusion | flops 8598323200 | bytes 23068672 | tf_op jit(solution)/shard_map/dot_general | solution.py:63
  521.2 27.7 %all-to-all-done.6 = bf16[4,128,2048]{2,1,0:T(8,128)(2,1)} async-done(((bf16[4,128,2048]{2,1,0:T(8,128)(2,1)}), bf16[4,128,2048]{2,1,0:T(8,128)(2,1)}, u32[]{:S(2)}, u32[]{:S(2)}) %all-to-all-start.6) | async-done | bytes 2097184 | tf_op jit(solution)/shard_map/all_to_all | solution.py:79
  561.5 4.8 all-to-all-start.7
  574.2 6.9 collective-permute-done.22
  583.4 30.7 %all-to-all-done.7 = bf16[4,128,2048]{2,1,0:T(8,128)(2,1)} async-done(((bf16[4,128,2048]{2,1,0:T(8,128)(2,1)}), bf16[4,128,2048]{2,1,0:T(8,128)(2,1)}, u32[]{:S(2)}, u32[]{:S(2)}) %all-to-all-start.7) | async-done | bytes 2097184 | tf_op jit(solution)/shard_map/all_to_all | solution.py:79
  617.8 12.7 %shard_map.327 = (bf16[512,512]{1,0:T(8,128)(2,1)}, f32[1,256]{1,0:T(1,128)}, bf16[2048,512]{1,0:T(8,128)(2,1)}) custom-call(bf16[512,512]{1,0:T(8,128)(2,1)} %convolution_convert_fusion.9.grad_ref, f32[512,512]{1,0:T(8,128)} %get-tuple-element.145.wide_ref, f32[2,512,2048]{2,1,0:T(8,128)} %get-tuple-element.146.probs_ref, ...), custom_call_target="tpu_custom_call" | custom-call | flops 4294967296 | bytes 16252928 | tf_op jit(solution)/shard_map/pallas_call | solution.py:458
  630.5 4.6 all-to-all-start.8
  639.1 4.4 convolution_convert_fusion.4
  646.2 16.7 %all-to-all-done.8 = bf16[4,512,512]{2,1,0:T(8,128)(2,1)} async-done(((bf16[4,512,512]{2,1,0:T(8,128)(2,1)}), bf16[4,512,512]{2,1,0:T(8,128)(2,1)}, u32[]{:S(2)}, u32[]{:S(2)}) %all-to-all-start.8) | async-done | bytes 2097184 | tf_op jit(solution)/shard_map/all_to_all | solution.py:79
  665.1 18.4 %reduce-scatter.5.cloned.1.call-done = bf16[512,2048]{1,0:T(8,128)(2,1)} async-done(((bf16[4096,2048]{1,0:T(8,128)(2,1)}), bf16[512,2048]{1,0:T(8,128)(2,1)}) %reduce-scatter.5.cloned.1.call-update) | async-done | bytes 2097168 | tf_op jit(solution)/shard_map/reduce_scatter | solution.py:873
  687.3 4.1 convolution_convert_fusion.2
  708.6 4.8 add_convert_fusion.1
  720.1 30.9 %collective-permute-done.28 = bf16[2,512,256]{1,2,0:T(8,128)(2,1)S(1)} collective-permute-done((bf16[2,512,256]{1,2,0:T(8,128)(2,1)S(1)}, bf16[2,512,256]{1,2,0:T(8,128)(2,1)S(1)}, u32[]{:S(2)}, u32[]{:S(2)}) %collective-permute-start.28) | collective-permute-done | bytes 524320 | tf_op jit(solution)/shard_map/ppermute | solution.py:517
  752.6 4.1 copy.129
  762.3 4.3 all-to-all-start.9
  773.5 23.2 %fusion.4 = f32[4096,256]{1,0:T(8,128)} fusion(bf16[4096,256]{1,0:T(8,128)(2,1)S(1)} %copy-done.38, s32[4096]{0:T(1024)S(1)} %copy-done.80), kind=kOutput, calls=%fused_computation.12 | convolution fusion | flops 8607760384 | bytes 6307840 | tf_op jit(solution)/shard_map/dot_general | solution.py:63
  796.7 11.7 %convert_element_type.373 = f32[2048,2048]{1,0:T(8,128)} convert(bf16[2048,2048]{1,0:T(8,128)(2,1)} %all-gather.9.cloned.1.call-done) | non-fusion elementwise | flops 4194304 | bytes 25165824 | tf_op jit(solution)/shard_map/convert_element_type | solution.py:954
  808.4 6.2 all-to-all-done.9
  820.2 3.8 collective-permute-start.34
  826.6 17.3 %all_to_all.100 = f32[4,8,512]{2,1,0:T(8,128)S(1)} all-to-all(f32[4,8,512]{2,1,0:T(8,128)S(1)} %bitcast.347), channel_id=1, replica_groups=mesh['slot'=2,'ctx'=4,'wsh'=4] {'wsh'}, dimensions={0} | all-to-all | bytes 131072 | tf_op jit(solution)/shard_map/all_to_all | solution.py:79
  848.0 15.7 %all-gather.13.cloned.1.call-done = bf16[32,2,512,256]{3,2,1,0:T(8,128)(2,1)} async-done(((bf16[4,2,512,256]{3,2,1,0:T(8,128)(2,1)}), bf16[32,2,512,256]{3,2,1,0:T(8,128)(2,1)}) %all-gather.13.cloned.1.call-update) | async-done | bytes 16777232 | tf_op jit(solution)/shard_map/all_gather | solution.py:950
  869.8 21.1 %shard_map.329 = f32[512,8192]{1,0:T(8,128)} custom-call(s32[4]{0:T(128)} %and_select_fusion.1.places, bf16[8,4,2,512,256]{4,3,2,1,0:T(8,128)(2,1)} %bitcast.279), custom_call_target="tpu_custom_call" | custom-call | bytes 25165824 | tf_op jit(solution)/shard_map/pallas_call | solution.py:497
  896.5 21.2 %shard_map.330 = f32[512,8192]{1,0:T(8,128)} custom-call(s32[4]{0:T(128)} %and_select_fusion.1.places, bf16[8,4,2,512,256]{4,3,2,1,0:T(8,128)(2,1)} %bitcast.280), custom_call_target="tpu_custom_call" | custom-call | bytes 25165824 | tf_op jit(solution)/shard_map/pallas_call | solution.py:497
  925.6 8.2 shard_map.331
  (531 shorter events, 241.0 us)
Async XLA Ops:
  7.2 98.9 %all-gather.11.cloned.1.call-start = ((), (), s32[]{:S(2)}) async-start(), calls=%async_computation.18 | async-start | bytes 7667712 | tf_op jit(solution)/shard_map/all_gather | solution.py:699
  8.1 13.3 %collective-permute-start.1 = (s32[2,128]{1,0:T(2,128)S(1)}, s32[2,128]{1,0:T(2,128)S(1)}, u32[]{:S(2)}, u32[]{:S(2)}) collective-permute-start(s32[2,128]{1,0:T(2,128)S(1)} %get-tuple-element.373), channel_id=1, source_target_pairs={{0,2},{1,3},{2,0},{3,1},{4,6},{5,7},{6,4},{7,5},{8,10},{9,11},{10,... | collective-permute-start | bytes 3080 | tf_op jit(solution)/shard_map/ppermute | solution.py:517
  12.1 9.2 collective-permute-start
  13.7 7.7 collective-permute-start.2
  22.2 11.3 %collective-permute-start.6 = (bf16[80,1664]{1,0:T(8,128)(2,1)S(1)}, bf16[80,1664]{1,0:T(8,128)(2,1)S(1)}, u32[]{:S(2)}, u32[]{:S(2)}) collective-permute-start(bf16[80,1664]{1,0:T(8,128)(2,1)S(1)} %get-tuple-element.346), channel_id=1, source_target_pairs={{0,1},{1,2},{2,3},{3,0},{4,5},{5,6},{6,7},{7,4},{8,9},{9,10},{10,1... | collective-permute-start | bytes 798728 | tf_op jit(solution)/shard_map/ppermute | solution.py:517
  22.3 20.7 %collective-permute-start.7 = (bf16[80,1664]{1,0:T(8,128)(2,1)S(1)}, bf16[80,1664]{1,0:T(8,128)(2,1)S(1)}, u32[]{:S(2)}, u32[]{:S(2)}) collective-permute-start(bf16[80,1664]{1,0:T(8,128)(2,1)S(1)} %get-tuple-element.347), channel_id=1, source_target_pairs={{0,2},{1,3},{2,0},{3,1},{4,6},{5,7},{6,4},{7,5},{8,10},{9,11},{10,... | collective-permute-start | bytes 798728 | tf_op jit(solution)/shard_map/ppermute | solution.py:517
  22.8 20.1 %collective-permute-start.8 = (bf16[80,1664]{1,0:T(8,128)(2,1)S(1)}, bf16[80,1664]{1,0:T(8,128)(2,1)S(1)}, u32[]{:S(2)}, u32[]{:S(2)}) collective-permute-start(bf16[80,1664]{1,0:T(8,128)(2,1)S(1)} %pad_maximum_fusion.15), channel_id=1, source_target_pairs={{0,3},{1,0},{2,1},{3,2},{4,7},{5,4},{6,5},{7,6},{8,11},{9,8},{10,9... | collective-permute-start | bytes 798728 | tf_op jit(solution)/shard_map/ppermute | solution.py:517
  49.8 54.1 %all-to-all-start = ((bf16[4,128,2048]{2,1,0:T(8,128)(2,1)}), bf16[4,128,2048]{2,1,0:T(8,128)(2,1)}, u32[]{:S(2)}, u32[]{:S(2)}) async-start(bf16[4,128,2048]{2,1,0:T(8,128)(2,1)} %broadcast_in_dim.95), calls=%async_computation | async-start | bytes 4194304 | tf_op jit(solution)/shard_map/all_to_all | solution.py:79
  119.0 29.1 %all-to-all-start.1 = ((bf16[4,512,512]{2,1,0:T(8,128)(2,1)}), bf16[4,512,512]{2,1,0:T(8,128)(2,1)}, u32[]{:S(2)}, u32[]{:S(2)}) async-start(bf16[4,512,512]{2,1,0:T(8,128)(2,1)} %broadcast_in_dim.105), calls=%async_computation.1 | async-start | bytes 4194304 | tf_op jit(solution)/shard_map/all_to_all | solution.py:79
  123.7 196.9 %all-gather.7.cloned.1.call-start = ((), (), s32[]{:S(2)}) async-start(), calls=%async_computation.14 | async-start | bytes 18874368 | tf_op jit(solution)/shard_map/all_gather | solution.py:790
  139.0 20.3 %collective-permute-start.11 = (bf16[512,512]{1,0:T(8,128)(2,1)}, bf16[512,512]{1,0:T(8,128)(2,1)}, u32[]{:S(2)}, u32[]{:S(2)}) collective-permute-start(bf16[512,512]{1,0:T(8,128)(2,1)} %pad_maximum_fusion.13), channel_id=1, source_target_pairs={{0,3},{1,0},{2,1},{3,2},{4,7},{5,4},{6,5},{7,6},{8,11},{9,8},{10,9... | collective-permute-start | bytes 1572872 | tf_op jit(solution)/shard_map/ppermute | solution.py:517
  144.0 41.1 %collective-permute-start.10 = (bf16[512,512]{1,0:T(8,128)(2,1)}, bf16[512,512]{1,0:T(8,128)(2,1)}, u32[]{:S(2)}, u32[]{:S(2)}) collective-permute-start(bf16[512,512]{1,0:T(8,128)(2,1)} %pad_maximum_fusion.12), channel_id=1, source_target_pairs={{0,2},{1,3},{2,0},{3,1},{4,6},{5,7},{6,4},{7,5},{8,10},{9,11},{10,... | collective-permute-start | bytes 1572872 | tf_op jit(solution)/shard_map/ppermute | solution.py:517
  144.8 40.3 %collective-permute-start.9 = (bf16[512,512]{1,0:T(8,128)(2,1)}, bf16[512,512]{1,0:T(8,128)(2,1)}, u32[]{:S(2)}, u32[]{:S(2)}) collective-permute-start(bf16[512,512]{1,0:T(8,128)(2,1)} %pad_maximum_fusion.11), channel_id=1, source_target_pairs={{0,1},{1,2},{2,3},{3,0},{4,5},{5,6},{6,7},{7,4},{8,9},{9,10},{10,1... | collective-permute-start | bytes 1572872 | tf_op jit(solution)/shard_map/ppermute | solution.py:517
  191.5 8.2 collective-permute-start.12
  194.1 55.4 %all-to-all-start.2 = ((bf16[4,128,2048]{2,1,0:T(8,128)(2,1)}), bf16[4,128,2048]{2,1,0:T(8,128)(2,1)}, u32[]{:S(2)}, u32[]{:S(2)}) async-start(bf16[4,128,2048]{2,1,0:T(8,128)(2,1)} %bitcast.308), calls=%async_computation.2 | async-start | bytes 4194304 | tf_op jit(solution)/shard_map/all_to_all | solution.py:79
  201.8 25.7 %collective-permute-start.13 = (bf16[1024,256]{1,0:T(8,128)(2,1)S(1)}, bf16[1024,256]{1,0:T(8,128)(2,1)S(1)}, u32[]{:S(2)}, u32[]{:S(2)}) collective-permute-start(bf16[1024,256]{1,0:T(8,128)(2,1)S(1)} %slice.264), channel_id=1, source_target_pairs={{0,8},{4,12},{8,0},{12,4},{1,9},{5,13},{9,1},{13,5},{2,10},{6,14},... | collective-permute-start | bytes 1572872 | tf_op jit(solution)/shard_map/ppermute | solution.py:97
  256.1 53.2 %all-to-all-start.3 = ((bf16[4,128,2048]{2,1,0:T(8,128)(2,1)}), bf16[4,128,2048]{2,1,0:T(8,128)(2,1)}, u32[]{:S(2)}, u32[]{:S(2)}) async-start(bf16[4,128,2048]{2,1,0:T(8,128)(2,1)} %broadcast_in_dim.106), calls=%async_computation.3 | async-start | bytes 4194304 | tf_op jit(solution)/shard_map/all_to_all | solution.py:79
  342.4 51.2 %all-to-all-start.4 = ((bf16[4,128,2048]{2,1,0:T(8,128)(2,1)}), bf16[4,128,2048]{2,1,0:T(8,128)(2,1)}, u32[]{:S(2)}, u32[]{:S(2)}) async-start(bf16[4,128,2048]{2,1,0:T(8,128)(2,1)} %bitcast.313), calls=%async_computation.4 | async-start | bytes 4194304 | tf_op jit(solution)/shard_map/all_to_all | solution.py:79
  347.0 267.1 %reduce-scatter.3.cloned.1.call-start = ((), (), s32[]{:S(2)}) async-start(), calls=%async_computation.15 | async-start | bytes 9437184 | tf_op jit(solution)/shard_map/reduce_scatter | solution.py:843
  462.8 30.5 %collective-permute-start.20 = (bf16[128,256]{1,0:T(8,128)(2,1)S(1)}, bf16[128,256]{1,0:T(8,128)(2,1)S(1)}, u32[]{:S(2)}, u32[]{:S(2)}) collective-permute-start(bf16[128,256]{1,0:T(8,128)(2,1)S(1)} %get-tuple-element.136), channel_id=1, source_target_pairs={{0,3},{1,0},{2,1},{3,2},{4,7},{5,4},{6,5},{7,6},{8,11},{9,8},{10,9... | collective-permute-start | bytes 196616 | tf_op jit(solution)/shard_map/ppermute | solution.py:517
  464.3 29.0 %collective-permute-start.19 = (bf16[128,256]{1,0:T(8,128)(2,1)S(1)}, bf16[128,256]{1,0:T(8,128)(2,1)S(1)}, u32[]{:S(2)}, u32[]{:S(2)}) collective-permute-start(bf16[128,256]{1,0:T(8,128)(2,1)S(1)} %get-tuple-element.136), channel_id=1, source_target_pairs={{0,2},{1,3},{2,0},{3,1},{4,6},{5,7},{6,4},{7,5},{8,10},{9,11},{10,... | collective-permute-start | bytes 196616 | tf_op jit(solution)/shard_map/ppermute | solution.py:517
  464.5 28.8 %collective-permute-start.18 = (bf16[128,256]{1,0:T(8,128)(2,1)S(1)}, bf16[128,256]{1,0:T(8,128)(2,1)}, u32[]{:S(2)}, u32[]{:S(2)}) collective-permute-start(bf16[128,256]{1,0:T(8,128)(2,1)S(1)} %get-tuple-element.136), channel_id=1, source_target_pairs={{0,1},{1,2},{2,3},{3,0},{4,5},{5,6},{6,7},{7,4},{8,9},{9,10},{10,1... | collective-permute-start | bytes 196616 | tf_op jit(solution)/shard_map/ppermute | solution.py:517
  498.0 51.0 %all-to-all-start.6 = ((bf16[4,128,2048]{2,1,0:T(8,128)(2,1)}), bf16[4,128,2048]{2,1,0:T(8,128)(2,1)}, u32[]{:S(2)}, u32[]{:S(2)}) async-start(bf16[4,128,2048]{2,1,0:T(8,128)(2,1)} %bitcast.310), calls=%async_computation.6 | async-start | bytes 4194304 | tf_op jit(solution)/shard_map/all_to_all | solution.py:79
  502.6 180.9 %reduce-scatter.5.cloned.1.call-start = ((), (), s32[]{:S(2)}) async-start(), calls=%async_computation.16 | async-start | bytes 18874368 | tf_op jit(solution)/shard_map/reduce_scatter | solution.py:873
  502.6 16.8 %collective-permute-start.21 = (bf16[512,256]{1,0:T(8,128)(2,1)S(1)}, bf16[512,256]{1,0:T(8,128)(2,1)}, u32[]{:S(2)}, u32[]{:S(2)}) collective-permute-start(bf16[512,256]{1,0:T(8,128)(2,1)S(1)} %bitcast.319), channel_id=1, source_target_pairs={{0,4},{4,0},{8,12},{12,8},{1,5},{5,1},{9,13},{13,9},{2,6},{6,2},{1... | collective-permute-start | bytes 786440 | tf_op jit(solution)/shard_map/ppermute | solution.py:97
  561.5 52.6 %all-to-all-start.7 = ((bf16[4,128,2048]{2,1,0:T(8,128)(2,1)}), bf16[4,128,2048]{2,1,0:T(8,128)(2,1)}, u32[]{:S(2)}, u32[]{:S(2)}) async-start(bf16[4,128,2048]{2,1,0:T(8,128)(2,1)} %broadcast_in_dim.194), calls=%async_computation.7 | async-start | bytes 4194304 | tf_op jit(solution)/shard_map/all_to_all | solution.py:79
  567.7 13.4 %collective-permute-start.22 = (bf16[1024,256]{1,0:T(8,128)(2,1)}, bf16[1024,256]{1,0:T(8,128)(2,1)}, u32[]{:S(2)}, u32[]{:S(2)}) collective-permute-start(bf16[1024,256]{1,0:T(8,128)(2,1)} %pad_maximum_fusion.14), channel_id=1, source_target_pairs={{0,8},{4,12},{8,0},{12,4},{1,9},{5,13},{9,1},{13,5},{2,10},{6,14},... | collective-permute-start | bytes 1572872 | tf_op jit(solution)/shard_map/ppermute | solution.py:97
  630.5 32.3 %all-to-all-start.8 = ((bf16[4,512,512]{2,1,0:T(8,128)(2,1)}), bf16[4,512,512]{2,1,0:T(8,128)(2,1)}, u32[]{:S(2)}, u32[]{:S(2)}) async-start(bf16[4,512,512]{2,1,0:T(8,128)(2,1)} %bitcast.309), calls=%async_computation.9 | async-start | bytes 4194304 | tf_op jit(solution)/shard_map/all_to_all | solution.py:79
  635.1 117.5 %all-gather.9.cloned.1.call-start = ((), (), s32[]{:S(2)}) async-start(), calls=%async_computation.17 | async-start | bytes 9437184 | tf_op jit(solution)/shard_map/all_gather | solution.py:885
  635.2 8.3 collective-permute-start.23
  638.8 224.9 %all-gather.13.cloned.1.call-start = ((), (), s32[]{:S(2)}) async-start(), calls=%async_computation.19 | async-start | bytes 18874368 | tf_op jit(solution)/shard_map/all_gather | solution.py:950
  700.7 7.9 collective-permute-start.24
  702.6 17.5 %collective-permute-start.29 = (bf16[2,512,256]{1,2,0:T(8,128)(2,1)S(1)}, bf16[2,512,256]{1,2,0:T(8,128)(2,1)S(1)}, u32[]{:S(2)}, u32[]{:S(2)}) collective-permute-start(bf16[2,512,256]{1,2,0:T(8,128)(2,1)S(1)} %bitcast.338), channel_id=1, source_target_pairs={{0,3},{1,0},{2,1},{3,2},{4,7},{5,4},{6,5},{7,6},{8,11},{9,8},{10,9... | collective-permute-start | bytes 1572872 | tf_op jit(solution)/shard_map/ppermute | solution.py:517
  705.4 45.6 %collective-permute-start.28 = (bf16[2,512,256]{1,2,0:T(8,128)(2,1)S(1)}, bf16[2,512,256]{1,2,0:T(8,128)(2,1)S(1)}, u32[]{:S(2)}, u32[]{:S(2)}) collective-permute-start(bf16[2,512,256]{1,2,0:T(8,128)(2,1)S(1)} %bitcast.336), channel_id=1, source_target_pairs={{0,2},{1,3},{2,0},{3,1},{4,6},{5,7},{6,4},{7,5},{8,10},{9,11},{10,... | collective-permute-start | bytes 1572872 | tf_op jit(solution)/shard_map/ppermute | solution.py:517
  705.4 45.6 %collective-permute-start.27 = (bf16[2,512,256]{1,2,0:T(8,128)(2,1)S(1)}, bf16[2,512,256]{1,2,0:T(8,128)(2,1)S(1)}, u32[]{:S(2)}, u32[]{:S(2)}) collective-permute-start(bf16[2,512,256]{1,2,0:T(8,128)(2,1)S(1)} %bitcast.335), channel_id=1, source_target_pairs={{0,1},{1,2},{2,3},{3,0},{4,5},{5,6},{6,7},{7,4},{8,9},{9,10},{10,1... | collective-permute-start | bytes 1572872 | tf_op jit(solution)/shard_map/ppermute | solution.py:517
  714.5 38.1 %collective-permute-start.26 = (bf16[32,8704]{1,0:T(8,128)(2,1)}, bf16[32,8704]{1,0:T(8,128)(2,1)}, u32[]{:S(2)}, u32[]{:S(2)}) collective-permute-start(bf16[32,8704]{1,0:T(8,128)(2,1)} %get-tuple-element.322), channel_id=1, source_target_pairs={{0,8},{4,12},{8,0},{12,4},{1,9},{5,13},{9,1},{13,5},{2,10},{6,14},... | collective-permute-start | bytes 1671176 | tf_op jit(solution)/shard_map/ppermute | solution.py:97
  716.4 36.3 %collective-permute-start.25 = (bf16[32,8704]{1,0:T(8,128)(2,1)}, bf16[32,8704]{1,0:T(8,128)(2,1)}, u32[]{:S(2)}, u32[]{:S(2)}) collective-permute-start(bf16[32,8704]{1,0:T(8,128)(2,1)} %get-tuple-element.323), channel_id=1, source_target_pairs={{0,4},{4,0},{8,12},{12,8},{1,5},{5,1},{9,13},{13,9},{2,6},{6,2},{1... | collective-permute-start | bytes 1671176 | tf_op jit(solution)/shard_map/ppermute | solution.py:97
  762.3 52.3 %all-to-all-start.9 = ((bf16[4,128,2048]{2,1,0:T(8,128)(2,1)}), bf16[4,128,2048]{2,1,0:T(8,128)(2,1)S(1)}, u32[]{:S(2)}, u32[]{:S(2)}) async-start(bf16[4,128,2048]{2,1,0:T(8,128)(2,1)} %bitcast.306), calls=%async_computation.11 | async-start | bytes 4194304 | tf_op jit(solution)/shard_map/all_to_all | solution.py:79
  770.6 44.4 %collective-permute-start.31 = (bf16[64,8704]{1,0:T(8,128)(2,1)}, bf16[64,8704]{1,0:T(8,128)(2,1)S(1)}, u32[]{:S(2)}, u32[]{:S(2)}) collective-permute-start(bf16[64,8704]{1,0:T(8,128)(2,1)} %pad_maximum_fusion.4), channel_id=1, source_target_pairs={{0,8},{4,12},{8,0},{12,4},{1,9},{5,13},{9,1},{13,5},{2,10},{6,14},... | collective-permute-start | bytes 3342344 | tf_op jit(solution)/shard_map/ppermute | solution.py:97
  772.8 43.2 %collective-permute-start.30 = (bf16[64,8704]{1,0:T(8,128)(2,1)}, bf16[64,8704]{1,0:T(8,128)(2,1)}, u32[]{:S(2)}, u32[]{:S(2)}) collective-permute-start(bf16[64,8704]{1,0:T(8,128)(2,1)} %pad_maximum_fusion.3), channel_id=1, source_target_pairs={{0,4},{4,0},{8,12},{12,8},{1,5},{5,1},{9,13},{13,9},{2,6},{6,2},{1... | collective-permute-start | bytes 3342344 | tf_op jit(solution)/shard_map/ppermute | solution.py:97
  820.2 23.7 %collective-permute-start.34 = (bf16[64,1664]{1,0:T(8,128)(2,1)}, bf16[64,1664]{1,0:T(8,128)(2,1)S(1)}, u32[]{:S(2)}, u32[]{:S(2)}) collective-permute-start(bf16[64,1664]{1,0:T(8,128)(2,1)} %get-tuple-element.318), channel_id=1, source_target_pairs={{0,3},{1,0},{2,1},{3,2},{4,7},{5,4},{6,5},{7,6},{8,11},{9,8},{10,9... | collective-permute-start | bytes 638984 | tf_op jit(solution)/shard_map/ppermute | solution.py:517
  823.9 20.0 %collective-permute-start.33 = (bf16[64,1664]{1,0:T(8,128)(2,1)}, bf16[64,1664]{1,0:T(8,128)(2,1)S(1)}, u32[]{:S(2)}, u32[]{:S(2)}) collective-permute-start(bf16[64,1664]{1,0:T(8,128)(2,1)} %get-tuple-element.319), channel_id=1, source_target_pairs={{0,2},{1,3},{2,0},{3,1},{4,6},{5,7},{6,4},{7,5},{8,10},{9,11},{10,... | collective-permute-start | bytes 638984 | tf_op jit(solution)/shard_map/ppermute | solution.py:517
  824.0 20.0 %collective-permute-start.32 = (bf16[64,1664]{1,0:T(8,128)(2,1)}, bf16[64,1664]{1,0:T(8,128)(2,1)}, u32[]{:S(2)}, u32[]{:S(2)}) collective-permute-start(bf16[64,1664]{1,0:T(8,128)(2,1)} %get-tuple-element.320), channel_id=1, source_target_pairs={{0,1},{1,2},{2,3},{3,0},{4,5},{5,6},{6,7},{7,4},{8,9},{9,10},{10,1... | collective-permute-start | bytes 638984 | tf_op jit(solution)/shard_map/ppermute | solution.py:517
  863.7 27.1 %collective-permute-start.36 = (bf16[64,5760]{1,0:T(8,128)(2,1)}, bf16[64,5760]{1,0:T(8,128)(2,1)S(1)}, u32[]{:S(2)}, u32[]{:S(2)}) collective-permute-start(bf16[64,5760]{1,0:T(8,128)(2,1)} %shard_map.328), channel_id=1, source_target_pairs={{0,8},{4,12},{8,0},{12,4},{1,9},{5,13},{9,1},{13,5},{2,10},{6,14},... | collective-permute-start | bytes 2211848 | tf_op jit(solution)/shard_map/ppermute | solution.py:97
  864.4 26.4 %collective-permute-start.35 = (bf16[64,5760]{1,0:T(8,128)(2,1)}, bf16[64,5760]{1,0:T(8,128)(2,1)}, u32[]{:S(2)}, u32[]{:S(2)}) collective-permute-start(bf16[64,5760]{1,0:T(8,128)(2,1)} %shard_map.328), channel_id=1, source_target_pairs={{0,4},{4,0},{8,12},{12,8},{1,5},{5,1},{9,13},{13,9},{2,6},{6,2},{1... | collective-permute-start | bytes 2211848 | tf_op jit(solution)/shard_map/ppermute | solution.py:97
  866.4 24.4 %all-to-all-start.11 = ((f32[8,8,512]{2,1,0:T(8,128)}), f32[8,8,512]{2,1,0:T(8,128)S(1)}, u32[]{:S(2)}, u32[]{:S(2)}) async-start(f32[8,8,512]{2,1,0:T(8,128)} %reshape.689), calls=%async_computation.13 | async-start | bytes 262144 | tf_op jit(solution)/shard_map/all_to_all | solution.py:79
  892.9 24.7 %collective-permute-start.38 = (bf16[32,5760]{1,0:T(8,128)(2,1)}, bf16[32,5760]{1,0:T(8,128)(2,1)S(1)}, u32[]{:S(2)}, u32[]{:S(2)}) collective-permute-start(bf16[32,5760]{1,0:T(8,128)(2,1)} %slice.235), channel_id=1, source_target_pairs={{0,4},{4,0},{8,12},{12,8},{1,5},{5,1},{9,13},{13,9},{2,6},{6,2},{1... | collective-permute-start | bytes 1105928 | tf_op jit(solution)/shard_map/ppermute | solution.py:97
  894.9 22.7 %collective-permute-start.37 = (bf16[32,5760]{1,0:T(8,128)(2,1)S(1)}, bf16[32,5760]{1,0:T(8,128)(2,1)}, u32[]{:S(2)}, u32[]{:S(2)}) collective-permute-start(bf16[32,5760]{1,0:T(8,128)(2,1)S(1)} %slice.234), channel_id=1, source_target_pairs={{0,8},{4,12},{8,0},{12,4},{1,9},{5,13},{9,1},{13,5},{2,10},{6,14},... | collective-permute-start | bytes 1105928 | tf_op jit(solution)/shard_map/ppermute | solution.py:97
  (122 other events, 1096.2 us)
Sparse Core Ops, SparseCore 0:
  48.3 50.8 all-gather.10
  189.3 103.1 all-gather.6
  462.9 76.5 reduce-scatter.2
  552.1 131.3 reduce-scatter.4
  685.4 65.9 all-gather.8
  756.9 106.7 all-gather.12
